TPU v7x, 32 devices: a whole 2x2x4 slice. The times are simulated.
32 devices in a mesh: fsdp: 2 (over y), ctx: 4 (over x, core), tp: 4 (over z).
Axes of the slice: x: 2, y: 2, z: 4, core: 2. Of those that a mesh axis runs over, the one named last changes fastest.
Arguments:
- hidden: bfloat16 [8192, 768], P(('fsdp', 'ctx', 'tp')), may hold values from -6 to 6
- cotangent: bfloat16 [8192, 768], P(('fsdp', 'ctx', 'tp')), may hold values from -6 to 6
- mem_pos: int32 [2, 4, 20], P('fsdp', 'ctx'), may hold values from 0 to 1023, as said below
- parents: int32 [2, 4], P('fsdp'), may hold values from 0 to 2, as said below
- memory: float32 [20, 768], replicated, may hold values from -6 to 6
- wq: bfloat16 [2, 768, 768], P(None, 'fsdp', 'tp'), may hold values from -0.5 to 0.5
- wk: bfloat16 [2, 768, 768], P(None, 'fsdp', 'tp'), may hold values from -0.21875 to 0.21875
- wv: bfloat16 [2, 768, 768], P(None, 'fsdp', 'tp'), may hold values from -0.21875 to 0.21875
- wo: bfloat16 [2, 768, 768], P(None, 'tp', 'fsdp'), may hold values from -0.625 to 0.625
- w1: bfloat16 [2, 768, 3072], P(None, 'fsdp', 'tp'), may hold values from -0.21875 to 0.21875
- w2: bfloat16 [2, 3072, 768], P(None, 'tp', 'fsdp'), may hold values from -0.109375 to 0.109375
- head_bias: float32 [2, 2, 768], P(None, None, 'tp'), may hold values from -3 to 3
- ffn_bias: float32 [2, 3072], P(None, 'tp'), may hold values from -3 to 3
- out_bias: float32 [2, 2, 768], replicated, may hold values from -3 to 3
- norm_gains: float32 [2, 2, 768], replicated, may hold values from 0.5 to 1.5
- norm_shifts: float32 [2, 2, 768], replicated, may hold values from -2 to 2
Outputs:
- output: bfloat16 [8192, 768], P(('fsdp', 'ctx', 'tp'))
- hidden_grad: bfloat16 [8192, 768], P(('fsdp', 'ctx', 'tp'))
- memory_grad: float32 [20, 768], replicated
- wq_grad: float32 [2, 768, 768], P(None, 'fsdp', 'tp')
- wk_grad: float32 [2, 768, 768], P(None, 'fsdp', 'tp')
- wv_grad: float32 [2, 768, 768], P(None, 'fsdp', 'tp')
- wo_grad: float32 [2, 768, 768], P(None, 'tp', 'fsdp')
- w1_grad: float32 [2, 768, 3072], P(None, 'fsdp', 'tp')
- w2_grad: float32 [2, 3072, 768], P(None, 'tp', 'fsdp')
- head_bias_grad: float32 [2, 2, 768], P(None, None, 'tp')
- ffn_bias_grad: float32 [2, 3072], P(None, 'tp')
- out_bias_grad: float32 [2, 2, 768], replicated
- norm_gains_grad: float32 [2, 2, 768], replicated
- norm_shifts_grad: float32 [2, 2, 768], replicated
Inputs may be any that keep to these rules, and one draw needn't show every extreme that they name: `mem_pos`: in each segment the 10 read rows and 10 write rows sit at distinct positions; every segment has one memory row at position 0 and one at 1023. parents[t, 0] = 0 and every other segment's parent is an earlier segment; in one tree each segment's parent is the one before it.
All inputs are finite; a program needn't handle non-finite values.
Results may differ from a plain program's by a relative error of at most 0.035.
Values may be sent and summed in bfloat16 or wider, within the bound.
A program may use at most 192 MiB of HBM per device.

v0:
```python
import jax
import jax.numpy as jnp
from jax import lax
from jax.sharding import PartitionSpec as P

HEAD = 64


EPSILON = 1e-05
MASKED = -1000000000.0


def norm_rows(summed, gain_row, shift_row):
    row_mean = jnp.mean(summed, axis=-1, keepdims=True)
    centered = summed - row_mean
    variance = jnp.mean(centered * centered, axis=-1, keepdims=True)
    return centered * lax.rsqrt(variance + EPSILON) * gain_row + shift_row


def gelu_exact(values):
    return jax.nn.gelu(values, approximate=False)


def ancestry(parent_row):
    seg_count = parent_row.shape[0]
    segment_ids = jnp.arange(seg_count, dtype=jnp.int32)
    parent_hop = (parent_row[:, None] == segment_ids[None, :]).astype(jnp.int32)
    reached = (segment_ids[:, None] == segment_ids[None, :]).astype(jnp.int32)
    on_path = reached
    for hop_number in range(seg_count - 1):
        reached = jnp.dot(reached, parent_hop)
        on_path = jnp.maximum(on_path, reached)
    return on_path


def product(left_side, right_side):
    return jnp.dot(left_side, right_side, preferred_element_type=jnp.float32)


def product_tn(left_side, right_side):
    return lax.dot_general(
        left_side, right_side, (((0,), (0,)), ((), ())), preferred_element_type=jnp.float32
    )


def product_nt(left_side, right_side):
    return lax.dot_general(
        left_side, right_side, (((1,), (1,)), ((), ())), preferred_element_type=jnp.float32
    )


def block_scores(queries, key_rows):
    return jnp.einsum("qhe,khe->hqk", queries, key_rows, preferred_element_type=jnp.float32)


def keep_same(carried):
    return carried


def split_blocks(whole_rows, block_total, head_count):
    key_width = whole_rows.shape[0] // block_total
    return [
        whole_rows[block_no * key_width : (block_no + 1) * key_width].reshape(
            key_width, head_count, HEAD
        )
        for block_no in range(block_total)
    ]


def attend(queries, key_all, value_all, allowed):
    row_count, head_count, head_size = queries.shape
    block_total = allowed.shape[0]
    key_blocks = split_blocks(key_all, block_total, head_count)
    value_blocks = split_blocks(value_all, block_total, head_count)
    biggest = jnp.full((head_count, row_count, 1), MASKED, jnp.float32)
    row_total = jnp.zeros((head_count, row_count, 1), jnp.float32)
    for block_no in range(block_total):

        def visit(state_pair, key_rows=key_blocks[block_no]):
            old_max, old_sum = state_pair
            scores = block_scores(queries, key_rows)
            new_max = jnp.maximum(old_max, jnp.max(scores, axis=-1, keepdims=True))
            new_sum = old_sum * jnp.exp(old_max - new_max) + jnp.sum(
                jnp.exp(scores - new_max), axis=-1, keepdims=True
            )
            return (new_max, new_sum)

        biggest, row_total = lax.cond(allowed[block_no] > 0, visit, keep_same, (biggest, row_total))
    log_total = biggest + jnp.log(row_total)
    attended = jnp.zeros((row_count, head_count, head_size), jnp.float32)
    for block_no in range(block_total):

        def collect(running, key_rows=key_blocks[block_no], value_rows=value_blocks[block_no]):
            probs = jnp.exp(block_scores(queries, key_rows) - log_total).astype(jnp.bfloat16)
            return running + jnp.einsum(
                "hqk,khe->qhe", probs, value_rows, preferred_element_type=jnp.float32
            )

        attended = lax.cond(allowed[block_no] > 0, collect, keep_same, attended)
    return (attended, log_total)


def attend_back(queries, key_all, value_all, allowed, log_total, grad_out):
    row_count, head_count, head_size = queries.shape
    block_total = allowed.shape[0]
    key_blocks = split_blocks(key_all, block_total, head_count)
    value_blocks = split_blocks(value_all, block_total, head_count)
    key_width = key_blocks[0].shape[0]
    delta = jnp.zeros((head_count, row_count, 1), jnp.float32)
    for block_no in range(block_total):

        def weigh(running, key_rows=key_blocks[block_no], value_rows=value_blocks[block_no]):
            probs = jnp.exp(block_scores(queries, key_rows) - log_total)
            grad_probs = jnp.einsum(
                "qhe,khe->hqk", grad_out, value_rows, preferred_element_type=jnp.float32
            )
            return running + jnp.sum(probs * grad_probs, axis=-1, keepdims=True)

        delta = lax.cond(allowed[block_no] > 0, weigh, keep_same, delta)
    grad_query = jnp.zeros((row_count, head_count, head_size), jnp.float32)
    key_grads = []
    value_grads = []
    for block_no in range(block_total):

        def spread_back(running, key_rows=key_blocks[block_no], value_rows=value_blocks[block_no]):
            probs = jnp.exp(block_scores(queries, key_rows) - log_total)
            grad_probs = jnp.einsum(
                "qhe,khe->hqk", grad_out, value_rows, preferred_element_type=jnp.float32
            )
            grad_scores = (probs * (grad_probs - delta)).astype(jnp.bfloat16)
            new_query = running + jnp.einsum(
                "hqk,khe->qhe", grad_scores, key_rows, preferred_element_type=jnp.float32
            )
            grad_keys = jnp.einsum(
                "hqk,qhe->khe", grad_scores, queries, preferred_element_type=jnp.float32
            )
            grad_values = jnp.einsum(
                "hqk,qhe->khe",
                probs.astype(jnp.bfloat16),
                grad_out,
                preferred_element_type=jnp.float32,
            )
            return (new_query, grad_keys, grad_values)

        def skip_back(running):
            nothing = jnp.zeros((key_width, head_count, head_size), jnp.float32)
            return (running, nothing, nothing)

        grad_query, grad_keys, grad_values = lax.cond(
            allowed[block_no] > 0, spread_back, skip_back, grad_query
        )
        key_grads.append(grad_keys.reshape(key_width, -1))
        value_grads.append(grad_values.reshape(key_width, -1))
    return (grad_query, jnp.concatenate(key_grads, axis=0), jnp.concatenate(value_grads, axis=0))


def spread_rows(values):
    return lax.all_gather(values, "tp", axis=0, tiled=True)


def collect_rows(partial_sum):
    return lax.psum_scatter(
        partial_sum.astype(jnp.bfloat16), "tp", scatter_dimension=0, tiled=True
    ).astype(jnp.float32)


def spread_grads(values):
    return lax.all_gather(values, "tp", axis=0, tiled=True)


def collect_grads(partial_sum):
    return lax.psum_scatter(
        partial_sum.astype(jnp.bfloat16), "tp", scatter_dimension=0, tiled=True
    ).astype(jnp.float32)


def reduce_weights(grad_query_w, grad_key_w, grad_value_w, grad_out_w, grad_up_w, grad_down_w):
    whole_sums = (
        lax.psum(grad_query_w.astype(jnp.bfloat16), "ctx").astype(jnp.float32),
        lax.psum(grad_key_w.astype(jnp.bfloat16), "ctx").astype(jnp.float32),
        lax.psum(grad_value_w.astype(jnp.bfloat16), "ctx").astype(jnp.float32),
        lax.psum(grad_out_w.astype(jnp.bfloat16), "ctx").astype(jnp.float32),
        lax.psum(grad_up_w.astype(jnp.bfloat16), "ctx").astype(jnp.float32),
        lax.psum(grad_down_w.astype(jnp.bfloat16), "ctx").astype(jnp.float32),
    )
    return (
        lax.psum_scatter(
            whole_sums[0].astype(jnp.bfloat16), "fsdp", scatter_dimension=0, tiled=True
        ).astype(jnp.float32),
        lax.psum_scatter(
            whole_sums[1].astype(jnp.bfloat16), "fsdp", scatter_dimension=0, tiled=True
        ).astype(jnp.float32),
        lax.psum_scatter(
            whole_sums[2].astype(jnp.bfloat16), "fsdp", scatter_dimension=0, tiled=True
        ).astype(jnp.float32),
        lax.psum_scatter(
            whole_sums[3].astype(jnp.bfloat16), "fsdp", scatter_dimension=1, tiled=True
        ).astype(jnp.float32),
        lax.psum_scatter(
            whole_sums[4].astype(jnp.bfloat16), "fsdp", scatter_dimension=0, tiled=True
        ).astype(jnp.float32),
        lax.psum_scatter(
            whole_sums[5].astype(jnp.bfloat16), "fsdp", scatter_dimension=1, tiled=True
        ).astype(jnp.float32),
    )


def shards(
    hidden,
    cotangent,
    mem_pos,
    parents,
    memory,
    wq,
    wk,
    wv,
    wo,
    w1,
    w2,
    head_bias,
    ffn_bias,
    out_bias,
    norm_gains,
    norm_shifts,
):
    tp_count = lax.axis_size("tp")
    ctx_count = lax.axis_size("ctx")
    tp_place = lax.axis_index("tp")
    ctx_place = lax.axis_index("ctx")
    share_rows = hidden.shape[0]
    seg_rows = share_rows * tp_count
    layer_total = wq.shape[0]
    positions = tp_place * share_rows + jnp.arange(share_rows, dtype=jnp.int32)
    mem_marks = (mem_pos[0, 0][None, :] == positions[:, None]).astype(jnp.float32)
    stream = hidden.astype(jnp.float32) + jnp.dot(
        mem_marks, memory, precision=lax.Precision.HIGHEST, preferred_element_type=jnp.float32
    )
    on_path = ancestry(parents[0])
    segment_ids = jnp.arange(ctx_count, dtype=jnp.int32)
    allowed = jnp.sum(on_path * (segment_ids == ctx_place).astype(jnp.int32)[:, None], axis=0)
    saved = []
    for layer_no in range(layer_total):
        full_w = (
            lax.all_gather(wq[layer_no], "fsdp", axis=0, tiled=True),
            lax.all_gather(wk[layer_no], "fsdp", axis=0, tiled=True),
            lax.all_gather(wv[layer_no], "fsdp", axis=0, tiled=True),
            lax.all_gather(wo[layer_no], "fsdp", axis=1, tiled=True),
            lax.all_gather(w1[layer_no], "fsdp", axis=0, tiled=True),
            lax.all_gather(w2[layer_no], "fsdp", axis=1, tiled=True),
        )
        query_w, key_w, value_w, out_w, up_w, down_w = full_w
        rounded = spread_rows(stream.astype(jnp.bfloat16))
        queries = ((product(rounded, query_w) + head_bias[layer_no, 0]) * 0.125).astype(
            jnp.bfloat16
        )
        key_local = product(rounded, key_w).astype(jnp.bfloat16)
        value_local = (product(rounded, value_w) + head_bias[layer_no, 1]).astype(jnp.bfloat16)
        key_all, value_all = (
            lax.all_gather(key_local, "ctx", axis=0, tiled=True),
            lax.all_gather(value_local, "ctx", axis=0, tiled=True),
        )
        head_queries = queries.reshape(seg_rows, -1, HEAD)
        attended, log_total = attend(head_queries, key_all, value_all, allowed)
        attended = attended.reshape(seg_rows, -1).astype(jnp.bfloat16)
        summed_one = stream + collect_rows(product(attended, out_w)) + out_bias[layer_no, 0]
        normed_one = norm_rows(summed_one, norm_gains[layer_no, 0], norm_shifts[layer_no, 0])
        rounded_two = spread_rows(normed_one.astype(jnp.bfloat16))
        hidden_pre = product(rounded_two, up_w) + ffn_bias[layer_no]
        active = gelu_exact(hidden_pre).astype(jnp.bfloat16)
        summed_two = normed_one + collect_rows(product(active, down_w)) + out_bias[layer_no, 1]
        stream = norm_rows(summed_two, norm_gains[layer_no, 1], norm_shifts[layer_no, 1])
        saved.append(
            (
                full_w,
                rounded,
                head_queries,
                key_all,
                value_all,
                attended,
                log_total,
                summed_one,
                rounded_two,
                hidden_pre,
                active,
                summed_two,
            )
        )
    output = stream.astype(jnp.bfloat16)
    grad_stream = cotangent.astype(jnp.float32)
    matrix_grads = [None] * layer_total
    head_grads = [None] * layer_total
    ffn_grads = [None] * layer_total
    out_grads = [None] * layer_total
    gain_grads = [None] * layer_total
    shift_grads = [None] * layer_total
    for layer_no in reversed(range(layer_total)):
        (
            full_w,
            rounded,
            head_queries,
            key_all,
            value_all,
            attended,
            log_total,
            summed_one,
            rounded_two,
            hidden_pre,
            active,
            summed_two,
        ) = saved[layer_no]
        query_w, key_w, value_w, out_w, up_w, down_w = full_w
        norm_out, norm_pull = jax.vjp(
            norm_rows, summed_two, norm_gains[layer_no, 1], norm_shifts[layer_no, 1]
        )
        back_two, gain_two, shift_two = norm_pull(grad_stream)
        grad_ffn = back_two.astype(jnp.bfloat16)
        bias_two = jnp.sum(grad_ffn.astype(jnp.float32), axis=0)
        grad_ffn_full = spread_grads(grad_ffn)
        grad_down_w = product_tn(active, grad_ffn_full)
        grad_active = product_nt(grad_ffn_full, down_w)
        gelu_out, gelu_pull = jax.vjp(gelu_exact, hidden_pre)
        grad_up = gelu_pull(grad_active)[0].astype(jnp.bfloat16)
        ffn_bias_part = jnp.sum(grad_up.astype(jnp.float32), axis=0)
        grad_up_w = product_tn(rounded_two, grad_up)
        grad_normed = collect_grads(product_nt(grad_up, up_w)) + back_two
        norm_out, norm_pull = jax.vjp(
            norm_rows, summed_one, norm_gains[layer_no, 0], norm_shifts[layer_no, 0]
        )
        back_one, gain_one, shift_one = norm_pull(grad_normed)
        grad_attn = back_one.astype(jnp.bfloat16)
        bias_one = jnp.sum(grad_attn.astype(jnp.float32), axis=0)
        grad_attn_full = spread_grads(grad_attn)
        grad_out_w = product_tn(attended, grad_attn_full)
        grad_attended = product_nt(grad_attn_full, out_w).astype(jnp.bfloat16)
        grad_query, key_terms, value_terms = attend_back(
            head_queries,
            key_all,
            value_all,
            allowed,
            log_total,
            grad_attended.reshape(seg_rows, -1, HEAD),
        )
        key_sums, value_sums = (
            lax.psum_scatter(
                key_terms.astype(jnp.bfloat16), "ctx", scatter_dimension=0, tiled=True
            ).astype(jnp.float32),
            lax.psum_scatter(
                value_terms.astype(jnp.bfloat16), "ctx", scatter_dimension=0, tiled=True
            ).astype(jnp.float32),
        )
        grad_queries = grad_query.reshape(seg_rows, -1).astype(jnp.bfloat16) * 0.125
        grad_keys = key_sums.astype(jnp.bfloat16)
        grad_values = value_sums.astype(jnp.bfloat16)
        grad_query_w = product_tn(rounded, grad_queries)
        grad_key_w = product_tn(rounded, grad_keys)
        grad_value_w = product_tn(rounded, grad_values)
        head_grads[layer_no] = jnp.stack(
            [
                jnp.sum(grad_queries.astype(jnp.float32), axis=0),
                jnp.sum(grad_values.astype(jnp.float32), axis=0),
            ]
        )
        ffn_grads[layer_no] = ffn_bias_part
        out_grads[layer_no] = jnp.stack([bias_one, bias_two])
        gain_grads[layer_no] = jnp.stack([gain_one, gain_two])
        shift_grads[layer_no] = jnp.stack([shift_one, shift_two])
        grad_rounded = (
            product_nt(grad_queries, query_w)
            + product_nt(grad_keys, key_w)
            + product_nt(grad_values, value_w)
        )
        grad_stream = collect_grads(grad_rounded) + back_one
        matrix_grads[layer_no] = reduce_weights(
            grad_query_w, grad_key_w, grad_value_w, grad_out_w, grad_up_w, grad_down_w
        )
    hidden_grad = grad_stream.astype(jnp.bfloat16)
    memory_part = lax.dot_general(
        mem_marks,
        grad_stream,
        (((0,), (0,)), ((), ())),
        precision=lax.Precision.HIGHEST,
        preferred_element_type=jnp.float32,
    )
    tp_mark = (jnp.arange(tp_count, dtype=jnp.int32) == tp_place).astype(jnp.float32)
    head_stack = jnp.stack(head_grads)
    ffn_stack = jnp.stack(ffn_grads)
    padded_head = (head_stack[:, :, None, :] * tp_mark[None, None, :, None]).reshape(
        layer_total, 2, -1
    )
    padded_ffn = (ffn_stack[:, None, :] * tp_mark[None, :, None]).reshape(layer_total, -1)
    totals = lax.psum(
        (
            padded_head,
            padded_ffn,
            jnp.stack(out_grads),
            jnp.stack(gain_grads),
            jnp.stack(shift_grads),
            memory_part,
        ),
        ("fsdp", "ctx", "tp"),
    )
    head_bias_grad = jnp.sum(
        totals[0].reshape(layer_total, 2, tp_count, -1) * tp_mark[None, None, :, None], axis=2
    )
    ffn_bias_grad = jnp.sum(
        totals[1].reshape(layer_total, tp_count, -1) * tp_mark[None, :, None], axis=1
    )
    wq_grad = jnp.stack([matrix_grads[layer_no][0] for layer_no in range(layer_total)])
    wk_grad = jnp.stack([matrix_grads[layer_no][1] for layer_no in range(layer_total)])
    wv_grad = jnp.stack([matrix_grads[layer_no][2] for layer_no in range(layer_total)])
    wo_grad = jnp.stack([matrix_grads[layer_no][3] for layer_no in range(layer_total)])
    w1_grad = jnp.stack([matrix_grads[layer_no][4] for layer_no in range(layer_total)])
    w2_grad = jnp.stack([matrix_grads[layer_no][5] for layer_no in range(layer_total)])
    return (
        output,
        hidden_grad,
        totals[5],
        wq_grad,
        wk_grad,
        wv_grad,
        wo_grad,
        w1_grad,
        w2_grad,
        head_bias_grad,
        ffn_bias_grad,
        totals[2],
        totals[3],
        totals[4],
    )


def solution(mesh):
    return jax.shard_map(
        shards,
        mesh=mesh,
        in_specs=(
            P(("fsdp", "ctx", "tp"), None),
            P(("fsdp", "ctx", "tp"), None),
            P("fsdp", "ctx", None),
            P("fsdp", None),
            P(),
            P(None, "fsdp", "tp"),
            P(None, "fsdp", "tp"),
            P(None, "fsdp", "tp"),
            P(None, "tp", "fsdp"),
            P(None, "fsdp", "tp"),
            P(None, "tp", "fsdp"),
            P(None, None, "tp"),
            P(None, "tp"),
            P(),
            P(),
            P(),
        ),
        out_specs=(
            P(("fsdp", "ctx", "tp"), None),
            P(("fsdp", "ctx", "tp"), None),
            P(),
            P(None, "fsdp", "tp"),
            P(None, "fsdp", "tp"),
            P(None, "fsdp", "tp"),
            P(None, "tp", "fsdp"),
            P(None, "fsdp", "tp"),
            P(None, "tp", "fsdp"),
            P(None, None, "tp"),
            P(None, "tp"),
            P(),
            P(),
            P(),
        ),
        check_vma=False,
    )
```

profile of v0, /device:TPU:0, one launch (start us, length us, event | category | flops | bytes accessed | tf_op | source)
XLA Modules:
  0.0 1543.9 jit_solution(4745679741600282460)
XLA Ops:
  13.2 7.5 all-gather.1
  20.7 30.7 %all-gather.29.cloned.1.call-done = bf16[1024,768]{1,0:T(8,128)(2,1)} async-done(((bf16[256,768]{1,0:T(8,128)(2,1)}), bf16[1024,768]{1,0:T(8,128)(2,1)}) %all-gather.29.cloned.1.call-update) | async-done | bytes 1572880 | tf_op jit(solution)/shard_map/all_gather | solution.py:158
  55.1 6.1 all-gather.2
  87.0 7.9 all-gather.33.cloned.1.call-done
  108.4 50.8 %reduce-scatter.45.cloned.1.call-done = bf16[256,768]{1,0:T(8,128)(2,1)} async-done(((bf16[1024,768]{1,0:T(8,128)(2,1)}), bf16[256,768]{1,0:T(8,128)(2,1)}) %reduce-scatter.45.cloned.1.call-update) | async-done | bytes 393232 | tf_op jit(solution)/shard_map/reduce_scatter | solution.py:162
  164.5 33.2 %all-gather.35.cloned.1.call-done = bf16[1024,768]{1,0:T(8,128)(2,1)} async-done(((bf16[256,768]{1,0:T(8,128)(2,1)}), bf16[1024,768]{1,0:T(8,128)(2,1)}) %all-gather.35.cloned.1.call-update) | async-done | bytes 1572880 | tf_op jit(solution)/shard_map/all_gather | solution.py:158
  197.7 10.8 multiply_convert_fusion.9
  208.6 12.6 all-gather.55.cloned.1.call-done
  225.1 35.4 %reduce-scatter.47.cloned.1.call-done = bf16[256,768]{1,0:T(8,128)(2,1)} async-done(((bf16[1024,768]{1,0:T(8,128)(2,1)}), bf16[256,768]{1,0:T(8,128)(2,1)}) %reduce-scatter.47.cloned.1.call-update) | async-done | bytes 393232 | tf_op jit(solution)/shard_map/reduce_scatter | solution.py:162
  269.3 29.8 %all-gather.37.cloned.1.call-done = bf16[1024,768]{1,0:T(8,128)(2,1)} async-done(((bf16[256,768]{1,0:T(8,128)(2,1)}), bf16[1024,768]{1,0:T(8,128)(2,1)}) %all-gather.37.cloned.1.call-update) | async-done | bytes 1572880 | tf_op jit(solution)/shard_map/all_gather | solution.py:158
  330.8 11.5 all-gather.41.cloned.1.call-done
  357.4 49.3 %reduce-scatter.49.cloned.1.call-done = bf16[256,768]{1,0:T(8,128)(2,1)} async-done(((bf16[1024,768]{1,0:T(8,128)(2,1)}), bf16[256,768]{1,0:T(8,128)(2,1)}) %reduce-scatter.49.cloned.1.call-update) | async-done | bytes 393232 | tf_op jit(solution)/shard_map/reduce_scatter | solution.py:162
  409.9 20.3 %all-gather.57.cloned.1.call-done = bf16[1,768,768]{2,1,0:T(8,128)(2,1)} async-done(((bf16[1,384,768]{2,1,0:T(8,128)(2,1)}), bf16[1,768,768]{2,1,0:T(8,128)(2,1)}) %all-gather.57.cloned.1.call-update) | async-done | bytes 1179664 | tf_op jit(solution)/shard_map/all_gather | solution.py:248
  430.1 39.0 %all-gather.43.cloned.1.call-done = bf16[1024,768]{1,0:T(8,128)(2,1)} async-done(((bf16[256,768]{1,0:T(8,128)(2,1)}), bf16[1024,768]{1,0:T(8,128)(2,1)}) %all-gather.43.cloned.1.call-update) | async-done | bytes 1572880 | tf_op jit(solution)/shard_map/all_gather | solution.py:158
  469.1 11.1 multiply_convert_fusion.8
  480.3 12.4 all-gather.59.cloned.1.call-done
  497.0 35.4 %reduce-scatter.51.cloned.1.call-done = bf16[256,768]{1,0:T(8,128)(2,1)} async-done(((bf16[1024,768]{1,0:T(8,128)(2,1)}), bf16[256,768]{1,0:T(8,128)(2,1)}) %reduce-scatter.51.cloned.1.call-update) | async-done | bytes 393232 | tf_op jit(solution)/shard_map/reduce_scatter | solution.py:162
  540.9 35.8 %all-gather.45.cloned.1.call-done = bf16[1024,768]{1,0:T(8,128)(2,1)} async-done(((bf16[256,768]{1,0:T(8,128)(2,1)}), bf16[1024,768]{1,0:T(8,128)(2,1)}) %all-gather.45.cloned.1.call-update) | async-done | bytes 1572880 | tf_op jit(solution)/shard_map/all_gather | solution.py:168
  576.7 6.5 convert_reduce_fusion
  587.1 34.2 %reduce-scatter.53.cloned.1.call-done = bf16[256,768]{1,0:T(8,128)(2,1)} async-done(((bf16[1024,768]{1,0:T(8,128)(2,1)}), bf16[256,768]{1,0:T(8,128)(2,1)}) %reduce-scatter.53.cloned.1.call-update) | async-done | bytes 393232 | tf_op jit(solution)/shard_map/reduce_scatter | solution.py:172
  627.5 36.1 %all-gather.47.cloned.1.call-done = bf16[1024,768]{1,0:T(8,128)(2,1)} async-done(((bf16[256,768]{1,0:T(8,128)(2,1)}), bf16[1024,768]{1,0:T(8,128)(2,1)}) %all-gather.47.cloned.1.call-update) | async-done | bytes 1572880 | tf_op jit(solution)/shard_map/all_gather | solution.py:168
  672.4 15.2 conditional.52
  695.0 6.7 conditional.55
  710.5 51.6 %reduce-scatter.55.cloned.1.call-done = bf16[1024,192]{0,1:T(8,128)(2,1)} async-done(((bf16[4096,192]{0,1:T(8,128)(2,1)}), bf16[1024,192]{0,1:T(8,128)(2,1)}) %reduce-scatter.55.cloned.1.call-update) | async-done | bytes 393232 | tf_op jit(solution)/shard_map/reduce_scatter | solution.py:344
  765.5 27.5 %reduce-scatter.57.cloned.1.call-done = bf16[1024,192]{0,1:T(8,128)(2,1)} async-done(((bf16[4096,192]{0,1:T(8,128)(2,1)}), bf16[1024,192]{0,1:T(8,128)(2,1)}) %reduce-scatter.57.cloned.1.call-update) | async-done | bytes 393232 | tf_op jit(solution)/shard_map/reduce_scatter | solution.py:347
  797.9 35.3 %reduce-scatter.59.cloned.1.call-done = bf16[256,768]{1,0:T(8,128)(2,1)} async-done(((bf16[1024,768]{1,0:T(8,128)(2,1)}), bf16[256,768]{1,0:T(8,128)(2,1)}) %reduce-scatter.59.cloned.1.call-update) | async-done | bytes 393232 | tf_op jit(solution)/shard_map/reduce_scatter | solution.py:172
  838.5 35.7 %all-gather.49.cloned.1.call-done = bf16[1024,768]{1,0:T(8,128)(2,1)} async-done(((bf16[256,768]{1,0:T(8,128)(2,1)}), bf16[1024,768]{1,0:T(8,128)(2,1)}) %all-gather.49.cloned.1.call-update) | async-done | bytes 1572880 | tf_op jit(solution)/shard_map/all_gather | solution.py:168
  874.2 6.5 convert_reduce_fusion.1
  884.5 34.2 %reduce-scatter.61.cloned.1.call-done = bf16[256,768]{1,0:T(8,128)(2,1)} async-done(((bf16[1024,768]{1,0:T(8,128)(2,1)}), bf16[256,768]{1,0:T(8,128)(2,1)}) %reduce-scatter.61.cloned.1.call-update) | async-done | bytes 393232 | tf_op jit(solution)/shard_map/reduce_scatter | solution.py:172
  924.0 36.1 %all-gather.51.cloned.1.call-done = bf16[1024,768]{1,0:T(8,128)(2,1)} async-done(((bf16[256,768]{1,0:T(8,128)(2,1)}), bf16[1024,768]{1,0:T(8,128)(2,1)}) %all-gather.51.cloned.1.call-update) | async-done | bytes 1572880 | tf_op jit(solution)/shard_map/all_gather | solution.py:168
  969.2 15.1 conditional.60
  991.8 6.9 conditional.63
  1028.8 29.7 %reduce-scatter.63.cloned.1.call-done = bf16[1024,192]{0,1:T(8,128)(2,1)} async-done(((bf16[4096,192]{0,1:T(8,128)(2,1)}), bf16[1024,192]{0,1:T(8,128)(2,1)}) %reduce-scatter.63.cloned.1.call-update) | async-done | bytes 393232 | tf_op jit(solution)/shard_map/reduce_scatter | solution.py:344
  1060.9 28.3 %reduce-scatter.65.cloned.1.call-done = bf16[1024,192]{0,1:T(8,128)(2,1)} async-done(((bf16[4096,192]{0,1:T(8,128)(2,1)}), bf16[1024,192]{0,1:T(8,128)(2,1)}) %reduce-scatter.65.cloned.1.call-update) | async-done | bytes 393232 | tf_op jit(solution)/shard_map/reduce_scatter | solution.py:347
  1100.5 12.6 reduce-scatter.91.cloned.1.call-done
  1115.2 13.2 reduce-scatter.87.cloned.1.call-done
  1130.2 14.1 reduce-scatter.75.cloned.1.call-done
  1146.0 14.2 reduce-scatter.79.cloned.1.call-done
  1161.9 13.7 reduce-scatter.83.cloned.1.call-done
  1177.3 22.2 %reduce-scatter.89.cloned.1.call-done = bf16[384,768]{1,0:T(8,128)(2,1)} async-done(((bf16[768,768]{1,0:T(8,128)(2,1)}), bf16[384,768]{1,0:T(8,128)(2,1)}) %reduce-scatter.89.cloned.1.call-update) | async-done | bytes 589840
  1201.7 13.3 reduce-scatter.85.cloned.1.call-done
  1216.7 14.4 reduce-scatter.73.cloned.1.call-done
  1232.7 14.3 reduce-scatter.77.cloned.1.call-done
  1248.7 13.6 reduce-scatter.81.cloned.1.call-done
  1264.0 22.9 %reduce-scatter.71.cloned.1.call-done = bf16[384,768]{1,0:T(8,128)(2,1)} async-done(((bf16[768,768]{1,0:T(8,128)(2,1)}), bf16[384,768]{1,0:T(8,128)(2,1)}) %reduce-scatter.71.cloned.1.call-update) | async-done | bytes 589840 | tf_op jit(solution)/shard_map/reduce_scatter | solution.py:199
  1286.9 24.5 %reduce-scatter.69.cloned.1.call-done = bf16[384,768]{1,0:T(8,128)(2,1)} async-done(((bf16[768,768]{1,0:T(8,128)(2,1)}), bf16[384,768]{1,0:T(8,128)(2,1)}) %reduce-scatter.69.cloned.1.call-update) | async-done | bytes 589840 | tf_op jit(solution)/shard_map/reduce_scatter | solution.py:199
  1318.7 73.4 %all-reduce.7.cloned.1.call-done = (bf16[384,192]{0,1:T(8,128)(2,1)}, bf16[384,192]{0,1:T(8,128)(2,1)}, bf16[384,192]{0,1:T(8,128)(2,1)}, bf16[384,192]{0,1:T(8,...) async-done(((bf16[384,192]{0,1:T(8,128)(2,1)}, ...) | async-done | bytes 3538960 | tf_op jit(solution)/shard_map/psum | solution.py:179
  1405.5 122.1 %all-reduce.5.cloned.1.call-done = (f32[20,768]{1,0:T(8,128)}, f32[2,2,4,192]{3,2,1,0:T(4,128)}, f32[2,4,768]{2,1,0:T(4,128)}, f32[2,2,768]{2,1,0:T(2,128)}, f32[2,2,768]{2,1,0:T(2,128)}, /*index=5*/f32[2,2,768]{2,1,0:T(2,128)}) async-done(((f32[20,768]{1,0:T(8,128)}, f32[2,2,4,192]{3,2,1,0:T(4,128)}, f32[2,4,768]{2,1,0:T(4,128)}, f32[2,2,768]{2,1,0:T(2,128)}, f32[2,2,768]{2,1,0:T(2,128)}, ...) | async-done | bytes 135184 | tf_op jit(solution)/shard_map/psum | solution.py:391
  (654 shorter events, 339.8 us)
Async XLA Ops:
  8.0 43.4 %all-gather.29.cloned.1.call-start = ((), (), s32[]{:S(2)}) async-start(), calls=%async_computation.24 | async-start | bytes 1966080 | tf_op jit(solution)/shard_map/all_gather | solution.py:158
  11.5 69.6 %all-gather.31.cloned.1.call-start = ((), (), s32[]{:S(2)}) async-start(), calls=%async_computation.25 | async-start | bytes 1966080 | tf_op jit(solution)/shard_map/all_gather | solution.py:259
  54.4 40.5 %all-gather.33.cloned.1.call-start = ((), (), s32[]{:S(2)}) async-start(), calls=%async_computation.26 | async-start | bytes 1966080 | tf_op jit(solution)/shard_map/all_gather | solution.py:260
  63.5 95.8 %reduce-scatter.45.cloned.1.call-start = ((), (), s32[]{:S(2)}) async-start(), calls=%async_computation.27 | async-start | bytes 1966080 | tf_op jit(solution)/shard_map/reduce_scatter | solution.py:162
  107.0 57.5 %all-gather.53.cloned.1.call-start = ((), (), s32[]{:S(2)}) async-start(), calls=%async_computation.48 | async-start | bytes 1769472 | tf_op jit(solution)/shard_map/all_gather | solution.py:248
  108.2 89.5 %all-gather.35.cloned.1.call-start = ((), (), s32[]{:S(2)}) async-start(), calls=%async_computation.28 | async-start | bytes 1966080 | tf_op jit(solution)/shard_map/all_gather | solution.py:158
  108.4 152.1 %copy-start.109 = (f32[768]{0:T(1024)}, f32[768]{0:T(1024)S(1)}, u32[]{:S(2)}) copy-start(f32[768]{0:T(1024)S(1)} %get-tuple-element.1048) | copy-start | bytes 9220
  108.4 298.2 %copy-start.111 = (f32[768]{0:T(1024)}, f32[768]{0:T(1024)S(1)}, u32[]{:S(2)}) copy-start(f32[768]{0:T(1024)S(1)} %get-tuple-element.1047) | copy-start | bytes 9220
  161.7 59.5 %all-gather.55.cloned.1.call-start = ((), (), s32[]{:S(2)}) async-start(), calls=%async_computation.49 | async-start | bytes 1769472 | tf_op jit(solution)/shard_map/all_gather | solution.py:249
  164.4 96.1 %reduce-scatter.47.cloned.1.call-start = ((), (), s32[]{:S(2)}) async-start(), calls=%async_computation.29 | async-start | bytes 1966080 | tf_op jit(solution)/shard_map/reduce_scatter | solution.py:162
  225.1 74.0 %all-gather.37.cloned.1.call-start = ((), (), s32[]{:S(2)}) async-start(), calls=%async_computation.30 | async-start | bytes 1966080 | tf_op jit(solution)/shard_map/all_gather | solution.py:158
  261.9 144.8 %copy-start.6 = (f32[256,768]{1,0:T(8,128)}, f32[256,768]{1,0:T(8,128)S(1)}, u32[]{:S(2)}) copy-start(f32[256,768]{1,0:T(8,128)S(1)} %get-tuple-element.1109) | copy-start | bytes 2359300
  261.9 144.7 %copy-start.115 = (f32[256]{0:T(256)}, f32[256]{0:T(256)S(1)}, u32[]{:S(2)}) copy-start(f32[256]{0:T(256)S(1)} %broadcast_multiply_fusion.4) | copy-start | bytes 3076
  262.2 144.5 %copy-start.119 = (f32[256]{0:T(256)}, f32[256]{0:T(256)S(1)}, u32[]{:S(2)}) copy-start(f32[256]{0:T(256)S(1)} %fusion.188) | copy-start | bytes 3076
  263.1 62.0 %all-gather.39.cloned.1.call-start = ((), (), s32[]{:S(2)}) async-start(), calls=%async_computation.31 | async-start | bytes 1966080 | tf_op jit(solution)/shard_map/all_gather | solution.py:259
  301.9 40.4 %all-gather.41.cloned.1.call-start = ((), (), s32[]{:S(2)}) async-start(), calls=%async_computation.32 | async-start | bytes 1966080 | tf_op jit(solution)/shard_map/all_gather | solution.py:260
  311.4 95.2 %reduce-scatter.49.cloned.1.call-start = ((), (), s32[]{:S(2)}) async-start(), calls=%async_computation.33 | async-start | bytes 1966080 | tf_op jit(solution)/shard_map/reduce_scatter | solution.py:162
  356.7 73.4 %all-gather.57.cloned.1.call-start = ((), (), s32[]{:S(2)}) async-start(), calls=%async_computation.50 | async-start | bytes 1769472 | tf_op jit(solution)/shard_map/all_gather | solution.py:248
  357.3 111.8 %all-gather.43.cloned.1.call-start = ((), (), s32[]{:S(2)}) async-start(), calls=%async_computation.34 | async-start | bytes 1966080 | tf_op jit(solution)/shard_map/all_gather | solution.py:158
  409.2 83.4 %all-gather.59.cloned.1.call-start = ((), (), s32[]{:S(2)}) async-start(), calls=%async_computation.51 | async-start | bytes 1769472 | tf_op jit(solution)/shard_map/all_gather | solution.py:249
  409.8 122.5 %reduce-scatter.51.cloned.1.call-start = ((), (), s32[]{:S(2)}) async-start(), calls=%async_computation.35 | async-start | bytes 1966080 | tf_op jit(solution)/shard_map/reduce_scatter | solution.py:162
  496.9 79.8 %all-gather.45.cloned.1.call-start = ((), (), s32[]{:S(2)}) async-start(), calls=%async_computation.36 | async-start | bytes 1966080 | tf_op jit(solution)/shard_map/all_gather | solution.py:168
  540.5 80.8 %reduce-scatter.53.cloned.1.call-start = ((), (), s32[]{:S(2)}) async-start(), calls=%async_computation.37 | async-start | bytes 1966080 | tf_op jit(solution)/shard_map/reduce_scatter | solution.py:172
  587.0 76.6 %all-gather.47.cloned.1.call-start = ((), (), s32[]{:S(2)}) async-start(), calls=%async_computation.38 | async-start | bytes 1966080 | tf_op jit(solution)/shard_map/all_gather | solution.py:168
  627.5 134.6 %reduce-scatter.55.cloned.1.call-start = ((), (), s32[]{:S(2)}) async-start(), calls=%async_computation.39 | async-start | bytes 1966080 | tf_op jit(solution)/shard_map/reduce_scatter | solution.py:344
  704.2 88.9 %reduce-scatter.57.cloned.1.call-start = ((), (), s32[]{:S(2)}) async-start(), calls=%async_computation.40 | async-start | bytes 1966080 | tf_op jit(solution)/shard_map/reduce_scatter | solution.py:347
  706.5 126.7 %reduce-scatter.59.cloned.1.call-start = ((), (), s32[]{:S(2)}) async-start(), calls=%async_computation.41 | async-start | bytes 1966080 | tf_op jit(solution)/shard_map/reduce_scatter | solution.py:172
  797.8 76.4 %all-gather.49.cloned.1.call-start = ((), (), s32[]{:S(2)}) async-start(), calls=%async_computation.42 | async-start | bytes 1966080 | tf_op jit(solution)/shard_map/all_gather | solution.py:168
  838.3 80.5 %reduce-scatter.61.cloned.1.call-start = ((), (), s32[]{:S(2)}) async-start(), calls=%async_computation.43 | async-start | bytes 1966080 | tf_op jit(solution)/shard_map/reduce_scatter | solution.py:172
  884.5 75.6 %all-gather.51.cloned.1.call-start = ((), (), s32[]{:S(2)}) async-start(), calls=%async_computation.44 | async-start | bytes 1966080 | tf_op jit(solution)/shard_map/all_gather | solution.py:168
  923.9 134.5 %reduce-scatter.63.cloned.1.call-start = ((), (), s32[]{:S(2)}) async-start(), calls=%async_computation.45 | async-start | bytes 1966080 | tf_op jit(solution)/shard_map/reduce_scatter | solution.py:344
  1001.1 88.1 %reduce-scatter.65.cloned.1.call-start = ((), (), s32[]{:S(2)}) async-start(), calls=%async_computation.46 | async-start | bytes 1966080 | tf_op jit(solution)/shard_map/reduce_scatter | solution.py:347
  1003.5 109.6 %reduce-scatter.91.cloned.1.call-start = ((), (), s32[]{:S(2)}) async-start(), calls=%async_computation.63 | async-start | bytes 1769472
  1010.4 118.0 %reduce-scatter.87.cloned.1.call-start = ((), (), s32[]{:S(2)}) async-start(), calls=%async_computation.61 | async-start | bytes 589824
  1013.4 130.9 %reduce-scatter.75.cloned.1.call-start = ((), (), s32[]{:S(2)}) async-start(), calls=%async_computation.55 | async-start | bytes 589824
  1014.9 145.3 %reduce-scatter.79.cloned.1.call-start = ((), (), s32[]{:S(2)}) async-start(), calls=%async_computation.57 | async-start | bytes 589824
  1017.4 158.2 %reduce-scatter.83.cloned.1.call-start = ((), (), s32[]{:S(2)}) async-start(), calls=%async_computation.59 | async-start | bytes 589824
  1018.9 180.6 %reduce-scatter.89.cloned.1.call-start = ((), (), s32[]{:S(2)}) async-start(), calls=%async_computation.62 | async-start | bytes 1769472
  1024.1 190.9 %reduce-scatter.85.cloned.1.call-start = ((), (), s32[]{:S(2)}) async-start(), calls=%async_computation.60 | async-start | bytes 589824
  1027.1 203.9 %reduce-scatter.73.cloned.1.call-start = ((), (), s32[]{:S(2)}) async-start(), calls=%async_computation.54 | async-start | bytes 589824
  1028.7 218.3 %reduce-scatter.77.cloned.1.call-start = ((), (), s32[]{:S(2)}) async-start(), calls=%async_computation.56 | async-start | bytes 589824
  1060.9 201.4 %reduce-scatter.81.cloned.1.call-start = ((), (), s32[]{:S(2)}) async-start(), calls=%async_computation.58 | async-start | bytes 589824
  1091.7 195.3 %reduce-scatter.71.cloned.1.call-start = ((), (), s32[]{:S(2)}) async-start(), calls=%async_computation.53 | async-start | bytes 1769472 | tf_op jit(solution)/shard_map/reduce_scatter | solution.py:199
  1096.2 215.3 %reduce-scatter.69.cloned.1.call-start = ((), (), s32[]{:S(2)}) async-start(), calls=%async_computation.52 | async-start | bytes 1769472 | tf_op jit(solution)/shard_map/reduce_scatter | solution.py:199
  1100.4 291.7 %all-reduce.7.cloned.1.call-start = ((), (), s32[]{:S(2)}) async-start(), calls=%async_computation.65 | async-start | bytes 7077888 | tf_op jit(solution)/shard_map/psum | solution.py:179
  1311.5 89.9 %reduce-scatter.67.cloned.1.call-start = ((), (), s32[]{:S(2)}) async-start(), calls=%async_computation.47 | async-start | bytes 1966080 | tf_op jit(solution)/shard_map/reduce_scatter | solution.py:172
  1315.2 212.5 %all-reduce.5.cloned.1.call-start = ((), (), s32[]{:S(2)}) async-start(), calls=%async_computation.64 | async-start | bytes 303104 | tf_op jit(solution)/shard_map/psum | solution.py:391
  1399.8 136.1 %copy-start.1 = (f32[20,768]{1,0:T(8,128)S(1)}, f32[20,768]{1,0:T(8,128)}, u32[]{:S(2)}) copy-start(f32[20,768]{1,0:T(8,128)} %param.84) | copy-start | bytes 184324
  (151 other events, 3627.1 us)
Sparse Core Ops, SparseCore 0:
  11.6 39.7 all-gather.28
  54.5 18.5 all-gather.30
  75.2 19.6 all-gather.32
  107.2 52.0 reduce-scatter.44
  302.0 18.5 all-gather.38
  322.6 19.6 all-gather.40
  497.0 35.2 reduce-scatter.50
  540.6 36.0 all-gather.44
  627.6 35.9 all-gather.46
  704.3 57.7 reduce-scatter.54
  764.8 28.1 reduce-scatter.56
  924.0 35.9 all-gather.50
  1001.2 57.1 reduce-scatter.62
  1061.0 28.1 reduce-scatter.64
  1091.3 21.7 reduce-scatter.90
  1115.3 13.1 reduce-scatter.86
  1131.1 13.1 reduce-scatter.74
  1147.0 13.1 reduce-scatter.78
  1162.4 13.1 reduce-scatter.82
  1177.8 21.7 reduce-scatter.88
  1201.8 13.1 reduce-scatter.84
  1217.9 13.1 reduce-scatter.72
  1233.8 13.1 reduce-scatter.76
  1249.2 13.1 reduce-scatter.80
  1265.1 21.7 reduce-scatter.70
  1289.7 21.7 reduce-scatter.68
  1315.2 76.8 all-reduce.6
Sparse Core Ops, SparseCore 1:
  109.6 39.3 all-gather.52
  161.8 35.9 all-gather.34
  199.7 21.5 all-gather.54
  225.2 35.3 reduce-scatter.46
  263.2 35.8 all-gather.36
  356.8 49.8 reduce-scatter.48
  408.6 21.5 all-gather.56
  432.1 36.9 all-gather.42
  471.1 21.5 all-gather.58
  587.1 34.1 reduce-scatter.52
  797.9 35.3 reduce-scatter.58
  838.4 35.8 all-gather.48
  884.6 34.1 reduce-scatter.60
  1315.3 35.3 reduce-scatter.66
  1403.7 123.9 all-reduce.4
where the time goes:
time: 1550 us; the launch traced here: 1540 us
  waiting for transfers between devices  1140 us (74%)
  matrix products  159 us (10%)
  local copies, waits for them, and re-layouts  73.4 us (5%)
  other arithmetic  61.6 us (4%)
  blocking collectives  48.7 us (3%)
  loops' own time  33.5 us (2%)
  between operations  21.4 us (1%)
    reduce_scatter x4, waiting for transfers between devices, collect_rows(): lax.psum_scatter(partial_sum.astype(jnp.bfloat16), 'tp', scatter_dimensio...  171 us
    unnamed x52, waiting for transfers between devices  147 us
    all_gather x4, waiting for transfers between devices, spread_grads(): return lax.all_gather(values, 'tp', axis=0, tiled=True)  144 us
    all_gather x4, waiting for transfers between devices, spread_rows(): return lax.all_gather(values, 'tp', axis=0, tiled=True)  133 us
    psum x1, waiting for transfers between devices, shards(): lax.psum((padded_head, padded_ffn, jnp.stack(out_grads), jnp.stack(gain_g...  122 us
    reduce_scatter x4, waiting for transfers between devices, collect_grads(): lax.psum_scatter(partial_sum.astype(jnp.bfloat16), 'tp', scatter_dimensio...  104 us
    reduce_scatter x2, waiting for transfers between devices, shards(): lax.psum_scatter(key_terms.astype(jnp.bfloat16), 'ctx', scatter_dimension...  81.3 us
    psum x1, waiting for transfers between devices, reduce_weights(): lax.psum(grad_query_w.astype(jnp.bfloat16), 'ctx').astype(jnp.float32)  73.4 us
  transfers between devices with their start and end apart: 42, of which 38 were waited for; matrix products, arithmetic and copies ran while one was open for 9% of the time, Pallas kernels for 0%

commit v1 on v0

v1 whole, which is shorter than its diff:
```python
import functools

import jax
import jax.numpy as jnp
from jax import lax
from jax.experimental import pallas as pl
from jax.experimental.pallas import tpu as pltpu
from jax.sharding import PartitionSpec as P

HEAD = 64
EPSILON = 1e-05
MASKED = -1000000000.0
MESH = pl.DeviceIdType.MESH
F32 = jnp.float32
BF16 = jnp.bfloat16
NEAR = (0, 1)
ORDER = ((0, 1), (1, 0), (2, 2), (3, 3))


def mm(left, right):
    return jnp.dot(left, right, preferred_element_type=F32)


def mm_nt(left, right):
    return lax.dot_general(left, right, (((1,), (1,)), ((), ())), preferred_element_type=F32)


def mm_tn(left, right):
    return lax.dot_general(left, right, (((0,), (0,)), ((), ())), preferred_element_type=F32)


def rcopy(src, dst, send_sem, recv_sem, device):
    return pltpu.make_async_remote_copy(
        src_ref=src,
        dst_ref=dst,
        send_sem=send_sem,
        recv_sem=recv_sem,
        device_id=device,
        device_id_type=MESH,
    )


def mate_of(c):
    return c + 1 - 2 * (c % 2)


def across_of(c):
    return (c + 2) % 4


def signal(sem, device):
    pl.semaphore_signal(sem, inc=1, device_id=device, device_id_type=MESH)


def ordered(place, step):
    half = place // 2
    inner = place + half * (3 - 2 * place)
    first, second = ORDER[step]
    chunk = first + inner * (second - first)
    return chunk + half * (3 - 2 * chunk)


def dma(*shape):
    return pltpu.SemaphoreType.DMA(shape)


def call(kernel, out_shapes, scratch, collective_id, name, n_in, cost, vmem=None, smem=()):
    params = dict(vmem_limit_bytes=56 * 1024 * 1024)
    if collective_id is not None:
        params.update(collective_id=collective_id, has_side_effects=True)
    return pl.pallas_call(
        kernel,
        out_shape=out_shapes,
        in_specs=[
            pl.BlockSpec(memory_space=pltpu.SMEM if i in smem else pltpu.VMEM) for i in range(n_in)
        ],
        out_specs=[pl.BlockSpec(memory_space=pltpu.VMEM)] * len(out_shapes),
        scratch_shapes=scratch,
        compiler_params=pltpu.CompilerParams(**params),
        cost_estimate=pl.CostEstimate(flops=cost[0], bytes_accessed=cost[1], transcendentals=cost[2]),
        name=name,
    )


def sds(*shape, dtype=BF16):
    return jax.ShapeDtypeStruct(shape, dtype)


def project_kernel(
    x_ref, w_ref, b_ref, xg_ref, qw_ref, kv_ref,
    qbuf, x_recv, x_right, x_left, k1_send, k1_recv, k2_send, k2_recv, kf_send, kf_recv, q_send, q_recv,
):
    c = lax.axis_index("ctx")
    t = lax.axis_index("tp")
    barrier = pltpu.get_barrier_semaphore()
    for device in (mate_of(c), across_of(c), 3 - c):
        signal(barrier, {"ctx": device})

    @pl.when(t > 0)
    def _():
        signal(barrier, {"tp": t - 1})

    @pl.when(t < 3)
    def _():
        signal(barrier, {"tp": t + 1})

    ends = (t // 3) + (3 - t) // 3
    pl.semaphore_wait(barrier, 5 - ends)

    def right(src, chunk, step):
        return rcopy(src, xg_ref.at[chunk], x_right.at[step], x_recv.at[chunk], {"tp": t + 1})

    def left(src, chunk, step):
        return rcopy(src, xg_ref.at[chunk], x_left.at[step], x_recv.at[chunk], {"tp": t - 1})

    def arrived(chunk):
        rcopy(xg_ref.at[chunk], xg_ref.at[chunk], x_right.at[0], x_recv.at[chunk], {"tp": t}).wait_recv()

    @pl.when(t < 3)
    def _():
        right(x_ref, t, 0).start()

    @pl.when(t > 0)
    def _():
        left(x_ref, t, 0).start()

    def mate(chunk):
        return rcopy(kv_ref.at[c, chunk], kv_ref.at[c, chunk], k1_send.at[chunk], k1_recv.at[chunk], {"ctx": mate_of(c)})

    def across(chunk):
        return rcopy(kv_ref.at[c, chunk], kv_ref.at[c, chunk], k2_send.at[chunk], k2_recv.at[chunk], {"ctx": across_of(c)})

    def onward(chunk):
        return rcopy(
            kv_ref.at[across_of(c), chunk], kv_ref.at[across_of(c), chunk], kf_send.at[chunk], kf_recv.at[chunk], {"ctx": mate_of(c)}
        )

    def partner(slot):
        return rcopy(qbuf.at[slot], qw_ref.at[slot + 2], q_send.at[slot], q_recv.at[slot], {"ctx": 3 - c})

    for step in range(4):
        if step == 0:
            xg_ref[t] = x_ref[...]
        else:

            @pl.when(t - step >= 0)
            def _():
                arrived(t - step)

                @pl.when(t < 3)
                def _():
                    right(xg_ref.at[t - step], t - step, step).start()

            @pl.when(t + step <= 3)
            def _():
                arrived(t + step)

                @pl.when(t > 0)
                def _():
                    left(xg_ref.at[t + step], t + step, step).start()

        chunk = ordered(t, step)
        made = mm(xg_ref[chunk], w_ref[...]) + b_ref[...]
        kv_ref[c, chunk] = made[:, 256:].astype(BF16)
        mate(chunk).start()
        across(chunk).start()
        query = (made[:, :256] * 0.125).astype(BF16)

        @pl.when(chunk < 2)
        def _():
            qw_ref[chunk] = query

        @pl.when(chunk >= 2)
        def _():
            qbuf[chunk - 2] = query
            partner(chunk - 2).start()

        if step >= 1:
            before = ordered(t, step - 1)
            across(before).wait_recv()
            onward(before).start()
    last = ordered(t, 3)
    across(last).wait_recv()
    onward(last).start()
    for chunk in range(4):
        mate(chunk).wait()
        across(chunk).wait_send()
        onward(chunk).wait()
    for slot in range(2):
        partner(slot).wait()

    @pl.when(t < 3)
    def _():
        right(x_ref, t, 0).wait_send()

    @pl.when(t > 0)
    def _():
        left(x_ref, t, 0).wait_send()

    for step in (1, 2):

        @pl.when((t - step >= 0) & (t < 3))
        def _():
            right(xg_ref.at[t - step], t - step, step).wait_send()

        @pl.when((t + step <= 3) & (t > 0))
        def _():
            left(xg_ref.at[t + step], t + step, step).wait_send()


def project(x, w, b, cid):
    outs = [sds(4, 256, 768), sds(4, 256, 256), sds(4, 4, 256, 384)]
    scratch = [
        pltpu.VMEM((2, 256, 256), BF16),
        dma(4), dma(3), dma(3),
        dma(4), dma(4), dma(4), dma(4), dma(4), dma(4), dma(2), dma(2),
    ]
    xg, qw, kv = call(project_kernel, outs, scratch, cid, "project", 3, (2 * 1024 * 768 * 640, 8 << 20, 0))(x, w, b)
    return xg.reshape(1024, 768), qw.reshape(1024, 256), kv.reshape(4, 1024, 384)


def norm_stats(summed):
    row_mean = jnp.mean(summed, axis=-1, keepdims=True)
    centered = summed - row_mean
    variance = jnp.mean(centered * centered, axis=-1, keepdims=True)
    scale = lax.rsqrt(variance + EPSILON)
    return centered * scale, scale


def norm_back(grad, xhat, scale, gain):
    scaled = grad * gain
    first = jnp.mean(scaled, axis=-1, keepdims=True)
    second = jnp.mean(scaled * xhat, axis=-1, keepdims=True)
    return scale * (scaled - first - xhat * second)


def gelu_both(up):
    phi = 0.5 * (1.0 + lax.erf(up * 0.7071067811865476))
    slope = phi + up * jnp.exp(-0.5 * up * up) * 0.3989422804014327
    return (up * phi).astype(BF16), slope.astype(BF16)


Q_TILE = 256
K_TILE = 256


def attend_kernel(flag_ref, qw_ref, kv_ref, o_ref, lse_ref, qm_ref, m_ref, l_ref, acc_ref):
    c = lax.axis_index("ctx")
    low = lax.broadcasted_iota(jnp.int32, (Q_TILE, 128), 1) < 64
    per_half = 512 // Q_TILE

    @pl.loop(0, 1024 // Q_TILE)
    def _(tile):
        half = tile // per_half
        segment = c + half * (3 - 2 * c)
        rows = pl.ds(pl.multiple_of(tile * Q_TILE, Q_TILE), Q_TILE)
        pair = qw_ref[rows, 0:128]
        qm_ref[0] = jnp.where(low, pair, jnp.zeros_like(pair))
        qm_ref[1] = jnp.where(low, jnp.zeros_like(pair), pair)
        qm_ref[2] = qw_ref[rows, 128:256]
        m_ref[...] = jnp.full_like(m_ref, MASKED)
        l_ref[...] = jnp.zeros_like(l_ref)
        acc_ref[...] = jnp.zeros_like(acc_ref)

        @pl.loop(0, segment + 1)
        def _(block):
            @pl.when(flag_ref[half, block] > 0)
            def _():
                keys = pl.ds(pl.multiple_of(block * 1024, 1024), 1024)
                for head in range(3):
                    k_at = 0 if head < 2 else 128
                    v_at = 256 if head < 2 else 128
                    scores = mm_nt(qm_ref[head], kv_ref[keys, k_at : k_at + 128])
                    old = m_ref[head]
                    new = jnp.maximum(old, jnp.max(scores, axis=-1, keepdims=True))
                    probs = jnp.exp(scores - new)
                    keep = jnp.exp(old - new)
                    m_ref[head] = new
                    l_ref[head] = l_ref[head] * keep + jnp.sum(probs, axis=-1, keepdims=True)
                    acc_ref[head] = acc_ref[head] * keep + mm(
                        probs.astype(BF16), kv_ref[keys, v_at : v_at + 128]
                    )

        first = acc_ref[0] / l_ref[0]
        second = acc_ref[1] / l_ref[1]
        o_ref[rows, 0:128] = jnp.where(low, first, second).astype(BF16)
        o_ref[rows, 128:192] = (acc_ref[2] / l_ref[2])[:, :64].astype(BF16)
        lane = lax.broadcasted_iota(jnp.int32, (Q_TILE, 128), 1)
        totals = [m_ref[head] + jnp.log(l_ref[head]) for head in range(3)]
        lse_ref[rows, :] = jnp.where(lane == 0, totals[0], jnp.where(lane == 1, totals[1], totals[2]))


def attend(qw, kv, flags):
    outs = [sds(1024, 192), sds(1024, 128, dtype=F32)]
    scratch = [
        pltpu.VMEM((3, Q_TILE, 128), BF16),
        pltpu.VMEM((3, Q_TILE, 1), F32),
        pltpu.VMEM((3, Q_TILE, 1), F32),
        pltpu.VMEM((3, Q_TILE, 128), F32),
    ]
    cost = (5 * 512 * 1024 * 64 * 4 * 3, 6 << 20, 5 * 512 * 1024 * 3)
    return call(attend_kernel, outs, scratch, None, "attend", 3, cost, smem=(0,))(
        flags, qw, kv.reshape(4096, 384)
    )


def attend_back_kernel(
    flag_ref, qw_ref, kv_ref, do_ref, o_ref, lse_ref, dq_ref, dkv_ref,
    qm_ref, dm_ref, row_ref, acc_ref, key_ref,
):
    c = lax.axis_index("ctx")
    low = lax.broadcasted_iota(jnp.int32, (1024, 128), 1) < 64
    pair = qw_ref[:, 0:128]
    none = jnp.zeros_like(pair)
    qm_ref[0] = jnp.where(low, pair, none)
    qm_ref[1] = jnp.where(low, none, pair)
    qm_ref[2] = qw_ref[:, 128:256]
    pair = do_ref[:, 0:128]
    dm_ref[0] = jnp.where(low, pair, none)
    dm_ref[1] = jnp.where(low, none, pair)
    dm_ref[2] = jnp.concatenate([do_ref[:, 128:192], none[:, :64]], axis=1)
    turned = jnp.transpose(lse_ref[...], (1, 0))
    row_ref[0:8] = turned[0:8]
    product = do_ref[...].astype(F32) * o_ref[...].astype(F32)
    head_row = lax.broadcasted_iota(jnp.int32, (8, 192), 0)
    head_of = lax.broadcasted_iota(jnp.int32, (8, 192), 1) // 64
    marks = (head_row == head_of).astype(F32)
    row_ref[8:16] = lax.dot_general(
        marks, product, (((1,), (1,)), ((), ())),
        precision=lax.Precision.HIGHEST, preferred_element_type=F32,
    )
    acc_ref[...] = jnp.zeros_like(acc_ref)
    low_keys = lax.broadcasted_iota(jnp.int32, (K_TILE, 128), 1) < 64

    @pl.loop(0, 4)
    def _(block):
        @pl.loop(0, 1024 // K_TILE)
        def _(tile):
            keys = pl.ds(pl.multiple_of(block * 1024 + tile * K_TILE, K_TILE), K_TILE)
            key_ref[...] = jnp.zeros_like(key_ref)
            key_pair = kv_ref[keys, 0:128]
            nothing = jnp.zeros_like(key_pair)
            key_parts = (
                jnp.where(low_keys, key_pair, nothing),
                jnp.where(low_keys, nothing, key_pair),
                jnp.where(low_keys, nothing, kv_ref[keys, 128:256]),
            )
            for half in range(2):
                segment = c if half == 0 else 3 - c

                @pl.when((block <= segment) & (flag_ref[half, block] > 0))
                def _():
                    rows = pl.ds(half * 512, 512)
                    for head in range(3):
                        k_at = 0 if head < 2 else 128
                        v_at = 256 if head < 2 else 128
                        query = qm_ref[head, rows]
                        grads = dm_ref[head, rows]
                        scores = mm_nt(kv_ref[keys, k_at : k_at + 128], query)
                        probs = jnp.exp(scores - row_ref[head : head + 1, rows])
                        grad_probs = mm_nt(kv_ref[keys, v_at : v_at + 128], grads)
                        grad_scores = (probs * (grad_probs - row_ref[8 + head : 9 + head, rows])).astype(BF16)
                        key_ref[:, v_at : v_at + 128] += mm(probs.astype(BF16), grads)
                        key_ref[:, k_at : k_at + 128] += mm(grad_scores, query)
                        q_at = 0 if head < 2 else 128
                        acc_ref[rows, q_at : q_at + 128] += mm_tn(grad_scores, key_parts[head])

            dkv_ref[keys, :] = key_ref[...].astype(BF16)

    dq_ref[...] = (acc_ref[...].astype(BF16).astype(F32) * 0.125).astype(BF16)


def attend_back(qw, kv, do, o, lse, flags):
    outs = [sds(1024, 256), sds(4096, 384)]
    scratch = [
        pltpu.VMEM((3, 1024, 128), BF16),
        pltpu.VMEM((3, 1024, 128), BF16),
        pltpu.VMEM((16, 1024), F32),
        pltpu.VMEM((1024, 256), F32),
        pltpu.VMEM((K_TILE, 384), F32),
    ]
    cost = (5 * 512 * 1024 * 64 * 10 * 3, 12 << 20, 5 * 512 * 1024 * 3)
    dq, dkv = call(attend_back_kernel, outs, scratch, None, "attend_back", 6, cost, smem=(0,))(
        flags, qw, kv.reshape(4096, 384), do, o, lse
    )
    return dq, dkv.reshape(4, 1024, 384)


def block_kernel(
    o_ref, wo_ref, w1_ref, w2_ref, b1_ref, vec_ref, stream_ref,
    out_ref, low_ref, xhat1_ref, r1_ref, xhat2_ref, r2_ref, xg_ref, act_ref, slope_ref, rows_ref,
    mine_ref, send_ref, got_ref, o_send, o_recv, a_send, a_recv, s_send, s_recv,
):
    c = lax.axis_index("ctx")
    t = lax.axis_index("tp")
    barrier = pltpu.get_barrier_semaphore()
    for place in range(4):

        @pl.when((t < 2) & (t != place))
        def _():
            signal(barrier, {"tp": place})

        @pl.when(t >= 2)
        def _():
            signal(barrier, {"ctx": 3 - c, "tp": place})

    signal(barrier, {"ctx": mate_of(c)})
    signal(barrier, {"ctx": across_of(c)})
    pl.semaphore_wait(barrier, 5 + t // 2)

    def give(quarter):
        device = {"tp": quarter} if quarter < 2 else {"ctx": 3 - c, "tp": quarter}
        return rcopy(o_ref.at[quarter], rows_ref.at[t], o_send.at[quarter], o_recv.at[t], device)

    def given(group):
        rcopy(rows_ref.at[group], rows_ref.at[group], o_send.at[0], o_recv.at[group], {"tp": t}).wait_recv()

    for quarter in (3, 2, 1, 0):
        if quarter < 2:

            @pl.when(t != quarter)
            def _():
                give(quarter).start()

            @pl.when(t == quarter)
            def _():
                rows_ref[quarter] = o_ref[quarter]

        else:
            give(quarter).start()
    branch = stream_ref[...] + vec_ref[0:1]
    for group in range(4):

        @pl.when((t >= 2) | (t != group))
        def _():
            given(group)

        branch += mm(rows_ref[group], wo_ref[group * 192 : (group + 1) * 192])
    xhat, scale = norm_stats(branch)
    xhat1_ref[...] = xhat
    r1_ref[...] = jnp.broadcast_to(scale, r1_ref.shape)
    normed = xhat * vec_ref[2:3] + vec_ref[3:4]
    xg_ref[c] = normed.astype(BF16)
    mate, across, far = mate_of(c), across_of(c), 3 - c

    def gather(slot, index, device):
        return rcopy(xg_ref.at[slot], xg_ref.at[slot], a_send.at[index], a_recv.at[index], {"ctx": device})

    gather(c, 1, across).start()
    gather(c, 0, mate).start()

    def feed(segment):
        up = mm(xg_ref[segment], w1_ref[...]) + b1_ref[...]
        act, slope = gelu_both(up)
        act_ref[segment] = act
        slope_ref[segment] = slope
        return mm(act, w2_ref[...])

    mine_ref[...] = feed(c) + normed + vec_ref[1:2]
    gather(mate, 0, mate).wait_recv()

    def scatter(index, device):
        return rcopy(send_ref.at[index], got_ref.at[index], s_send.at[index], s_recv.at[index], {"ctx": device})

    send_ref[0] = feed(mate).astype(BF16)
    scatter(0, mate).start()
    gather(across, 1, across).wait_recv()
    gather(across, 2, mate).start()
    own_across = feed(across)
    gather(far, 2, mate).wait_recv()
    send_ref[1] = feed(far).astype(BF16)
    scatter(1, mate).start()
    scatter(1, mate).wait_recv()
    send_ref[2] = (own_across + got_ref[1].astype(F32)).astype(BF16)
    scatter(2, across).start()
    scatter(0, mate).wait_recv()
    scatter(2, across).wait_recv()
    summed = mine_ref[...] + got_ref[0].astype(F32) + got_ref[2].astype(F32)
    xhat, scale = norm_stats(summed)
    xhat2_ref[...] = xhat
    r2_ref[...] = jnp.broadcast_to(scale, r2_ref.shape)
    out = xhat * vec_ref[4:5] + vec_ref[5:6]
    out_ref[...] = out
    low_ref[...] = out.astype(BF16)
    for quarter in range(4):
        if quarter < 2:

            @pl.when(t != quarter)
            def _():
                give(quarter).wait_send()

        else:
            give(quarter).wait_send()
    gather(c, 0, mate).wait_send()
    gather(c, 1, across).wait_send()
    gather(across, 2, mate).wait_send()
    for index in range(3):
        scatter(index, mate).wait_send()


def block(o, wo, w1, w2, b1, vecs, stream, cid):
    f = functools.partial(sds, dtype=F32)
    outs = [
        f(256, 768), sds(256, 768), f(256, 768), f(256, 128), f(256, 768), f(256, 128),
        sds(4, 256, 768), sds(4, 256, 768), sds(4, 256, 768), sds(4, 256, 192),
    ]
    scratch = [
        pltpu.VMEM((256, 768), F32),
        pltpu.VMEM((3, 256, 768), BF16),
        pltpu.VMEM((3, 256, 768), BF16),
        dma(4), dma(4), dma(3), dma(3), dma(3), dma(3),
    ]
    cost = (2 * 256 * 768 * 768 + 4 * 1024 * 768 * 768, 16 << 20, 1 << 20)
    res = call(block_kernel, outs, scratch, cid, "block", 7, cost)(
        o.reshape(4, 256, 192), wo, w1, w2, b1, vecs, stream
    )
    flat = lambda a: a.reshape(1024, 768)
    return tuple(res[:6]) + (flat(res[6]), flat(res[7]), flat(res[8]), res[9])


def block_back_kernel(
    grad_ref, xhat2_ref, r2_ref, xhat1_ref, r1_ref, vec_ref, slope_ref, w1_ref, w2_ref, wo_ref,
    gg_ref, gu_ref, back_ref, g1_ref, do_ref, stat_ref,
    mine_ref, send_ref, got_ref, dsend_ref, d_send, d_recv, a_send, a_recv, s_send, s_recv,
):
    c = lax.axis_index("ctx")
    t = lax.axis_index("tp")
    barrier = pltpu.get_barrier_semaphore()
    for place in range(4):
        if place < 2:

            @pl.when(t != place)
            def _():
                signal(barrier, {"tp": place})

        else:
            signal(barrier, {"ctx": 3 - c, "tp": place})
    signal(barrier, {"ctx": mate_of(c)})
    signal(barrier, {"ctx": across_of(c)})
    pl.semaphore_wait(barrier, 5 + t // 2)
    mate, across, far = mate_of(c), across_of(c), 3 - c

    def row(values):
        return jnp.sum(values, axis=0, keepdims=True)

    grad = grad_ref[...]
    back_two = norm_back(grad, xhat2_ref[...], r2_ref[:, 0:1], vec_ref[4:5])
    g2 = back_two.astype(BF16)
    gg_ref[c] = g2

    def gather(slot, index, device):
        return rcopy(gg_ref.at[slot], gg_ref.at[slot], a_send.at[index], a_recv.at[index], {"ctx": device})

    gather(c, 1, across).start()
    gather(c, 0, mate).start()
    stat_ref[1:2] = row(grad * xhat2_ref[...])
    stat_ref[3:4] = row(grad)
    stat_ref[5:6] = row(g2.astype(F32))
    stat_ref[7:8] = jnp.zeros((1, 768), F32)

    def feed(segment):
        gu = (mm_nt(gg_ref[segment], w2_ref[...]) * slope_ref[segment].astype(F32)).astype(BF16)
        gu_ref[segment] = gu
        return mm_nt(gu, w1_ref[...]), row(gu.astype(F32))

    part, bias = feed(c)
    mine_ref[...] = part + back_two
    gather(mate, 0, mate).wait_recv()

    def scatter(index, device):
        return rcopy(send_ref.at[index], got_ref.at[index], s_send.at[index], s_recv.at[index], {"ctx": device})

    part, more = feed(mate)
    bias += more
    send_ref[0] = part.astype(BF16)
    scatter(0, mate).start()
    gather(across, 1, across).wait_recv()
    gather(across, 2, mate).start()
    own_across, more = feed(across)
    bias += more
    gather(far, 2, mate).wait_recv()
    part, more = feed(far)
    bias += more
    stat_ref[6:7] = bias
    send_ref[1] = part.astype(BF16)
    scatter(1, mate).start()
    scatter(1, mate).wait_recv()
    send_ref[2] = (own_across + got_ref[1].astype(F32)).astype(BF16)
    scatter(2, across).start()
    scatter(0, mate).wait_recv()
    scatter(2, across).wait_recv()
    grad_normed = mine_ref[...] + got_ref[0].astype(F32) + got_ref[2].astype(F32)
    back_one = norm_back(grad_normed, xhat1_ref[...], r1_ref[:, 0:1], vec_ref[2:3])
    back_ref[...] = back_one
    g1 = back_one.astype(BF16)
    g1_ref[...] = g1

    def give_near(group):
        return rcopy(dsend_ref.at[group], do_ref.at[t], d_send.at[group], d_recv.at[t], {"tp": group})

    def give_far(group):
        return rcopy(dsend_ref.at[group], do_ref.at[t], d_send.at[group], d_recv.at[t], {"ctx": 3 - c, "tp": group})

    for group in range(4):
        dsend_ref[group] = mm_nt(g1, wo_ref[group * 192 : (group + 1) * 192]).astype(BF16)

        @pl.when((t < 2) & (t == group))
        def _():
            do_ref[t] = dsend_ref[group]

        @pl.when((t < 2) & (t != group))
        def _():
            give_near(group).start()

        @pl.when(t >= 2)
        def _():
            give_far(group).start()

    stat_ref[0:1] = row(grad_normed * xhat1_ref[...])
    stat_ref[2:3] = row(grad_normed)
    stat_ref[4:5] = row(g1.astype(F32))
    for quarter in range(4):

        def taken():
            rcopy(do_ref.at[quarter], do_ref.at[quarter], d_send.at[0], d_recv.at[quarter], {"tp": t}).wait_recv()

        if quarter < 2:
            pl.when(t != quarter)(taken)
        else:
            taken()
    for group in range(4):

        @pl.when((t >= 2) | (t != group))
        def _():
            give_near(group).wait_send()

    gather(c, 0, mate).wait_send()
    gather(c, 1, across).wait_send()
    gather(across, 2, mate).wait_send()
    for index in range(3):
        scatter(index, mate).wait_send()


def block_back(grad, xhat2, r2, xhat1, r1, vecs, slope, w1, w2, wo, cid):
    f = functools.partial(sds, dtype=F32)
    outs = [sds(4, 256, 768), sds(4, 256, 768), f(256, 768), sds(256, 768), sds(4, 256, 192), f(8, 768)]
    scratch = [
        pltpu.VMEM((256, 768), F32),
        pltpu.VMEM((3, 256, 768), BF16),
        pltpu.VMEM((3, 256, 768), BF16),
        pltpu.VMEM((4, 256, 192), BF16),
        dma(4), dma(4), dma(3), dma(3), dma(3), dma(3),
    ]
    cost = (2 * 256 * 768 * 768 + 4 * 1024 * 768 * 768, 16 << 20, 1 << 10)
    gg, gu, back, g1, do, stats = call(block_back_kernel, outs, scratch, cid, "block_back", 10, cost)(
        grad, xhat2, r2, xhat1, r1, vecs, slope.reshape(4, 256, 768), w1, w2, wo
    )
    return gg.reshape(1024, 768), gu.reshape(1024, 768), back, g1, do.reshape(1024, 192), stats


def project_back_kernel(
    dqw_ref, dkv_ref, w_ref, back_ref, dq_ref, own_ref, grad_ref,
    part_ref, near_ref, join_ref, sum_ref, far_ref, pass_ref, take_ref,
    q_send, q_recv, n_send, n_recv, j_send, j_recv, f_send, f_recv, p_send, p_recv,
):
    c = lax.axis_index("ctx")
    t = lax.axis_index("tp")
    barrier = pltpu.get_barrier_semaphore()
    for device in (mate_of(c), across_of(c), 3 - c):
        signal(barrier, {"ctx": device})

    @pl.when(t > 0)
    def _():
        signal(barrier, {"tp": t - 1})

    @pl.when(t < 3)
    def _():
        signal(barrier, {"tp": t + 1})

    ends = (t // 3) + (3 - t) // 3
    pl.semaphore_wait(barrier, 5 - ends)
    mate, across, far = mate_of(c), across_of(c), 3 - c

    def partner(slot):
        return rcopy(dqw_ref.at[slot + 2], dq_ref.at[slot + 2], q_send.at[slot], q_recv.at[slot], {"ctx": far})

    def near(chunk):
        return rcopy(dkv_ref.at[mate, chunk], near_ref.at[chunk], n_send.at[chunk], n_recv.at[chunk], {"ctx": mate})

    def join(chunk):
        return rcopy(dkv_ref.at[far, chunk], join_ref.at[chunk], j_send.at[chunk], j_recv.at[chunk], {"ctx": mate})

    def cross(chunk):
        return rcopy(sum_ref.at[chunk], far_ref.at[chunk], f_send.at[chunk], f_recv.at[chunk], {"ctx": across})

    chunks = [ordered(t, 3 - k) for k in range(4)]
    for chunk in chunks:
        join(chunk).start()
    for slot in range(2):
        partner(slot).start()
    for chunk in chunks:
        near(chunk).start()
    for quarter in range(2):
        dq_ref[quarter] = dqw_ref[quarter]
    for chunk in chunks:
        join(chunk).wait_recv()
        sum_ref[chunk] = (dkv_ref[across, chunk].astype(F32) + join_ref[chunk].astype(F32)).astype(BF16)
        cross(chunk).start()

    def lower(chunk):
        return rcopy(pass_ref.at[chunk], take_ref.at[0, chunk], p_send.at[chunk], p_recv.at[0, chunk], {"tp": t - 1})

    def upper(chunk):
        return rcopy(pass_ref.at[chunk], take_ref.at[1, chunk], p_send.at[chunk], p_recv.at[1, chunk], {"tp": t + 1})

    def passed(side, chunk):
        rcopy(
            take_ref.at[side, chunk], take_ref.at[side, chunk], p_send.at[0], p_recv.at[side, chunk], {"tp": t}
        ).wait_recv()

    def relay(chunk):
        @pl.when(chunk < t)
        def _():
            @pl.when(t < 3)
            def _():
                passed(0, chunk)
                pass_ref[chunk] = (part_ref[chunk] + take_ref[0, chunk].astype(F32)).astype(BF16)

            @pl.when(t == 3)
            def _():
                pass_ref[chunk] = part_ref[chunk].astype(BF16)

            lower(chunk).start()

        @pl.when(chunk > t)
        def _():
            @pl.when(t > 0)
            def _():
                passed(1, chunk)
                pass_ref[chunk] = (part_ref[chunk] + take_ref[1, chunk].astype(F32)).astype(BF16)

            @pl.when(t == 0)
            def _():
                pass_ref[chunk] = part_ref[chunk].astype(BF16)

            upper(chunk).start()

    at_end = (t == 0) | (t == 3)
    for step, chunk in enumerate(chunks):

        @pl.when(chunk >= 2)
        def _():
            partner(chunk - 2).wait_recv()

        near(chunk).wait_recv()
        cross(chunk).wait_recv()
        own = (
            dkv_ref[c, chunk].astype(F32) + near_ref[chunk].astype(F32) + far_ref[chunk].astype(F32)
        ).astype(BF16)
        own_ref[chunk] = own
        part_ref[chunk] = mm_nt(dq_ref[chunk], w_ref[:, 0:256]) + mm_nt(own, w_ref[:, 256:640])
        if step < 3:

            @pl.when(at_end)
            def _():
                relay(chunk)

    for chunk in chunks[:3]:

        @pl.when(jnp.logical_not(at_end))
        def _():
            relay(chunk)

    grad_ref[...] = part_ref[t] + back_ref[...]

    @pl.when(t < 3)
    def _():
        passed(0, t)
        grad_ref[...] += take_ref[0, t].astype(F32)

    @pl.when(t > 0)
    def _():
        passed(1, t)
        grad_ref[...] += take_ref[1, t].astype(F32)

    for chunk in range(4):
        join(chunk).wait_send()
        near(chunk).wait_send()
        cross(chunk).wait_send()

        @pl.when(t != chunk)
        def _():
            upper(chunk).wait_send()

    for slot in range(2):
        partner(slot).wait_send()


def project_back(dqw, dkv, w, back_one, cid):
    outs = [sds(4, 256, 256), sds(4, 256, 384), sds(256, 768, dtype=F32)]
    scratch = [
        pltpu.VMEM((4, 256, 768), F32),
        pltpu.VMEM((4, 256, 384), BF16), pltpu.VMEM((4, 256, 384), BF16),
        pltpu.VMEM((4, 256, 384), BF16), pltpu.VMEM((4, 256, 384), BF16),
        pltpu.VMEM((4, 256, 768), BF16), pltpu.VMEM((2, 4, 256, 768), BF16),
        dma(2), dma(2), dma(4), dma(4), dma(4), dma(4), dma(4), dma(4), dma(4), dma(2, 4),
    ]
    cost = (2 * 1024 * 768 * 640, 8 << 20, 0)
    dq, own, grad = call(project_back_kernel, outs, scratch, cid, "project_back", 4, cost)(
        dqw.reshape(4, 256, 256), dkv.reshape(4, 4, 256, 384), w, back_one
    )
    return dq.reshape(1024, 256), own.reshape(1024, 384), grad


FLIP = (0, 2, 1, 3)


def ancestry(parent_row):
    seg_count = parent_row.shape[0]
    segment_ids = jnp.arange(seg_count, dtype=jnp.int32)
    parent_hop = (parent_row[:, None] == segment_ids[None, :]).astype(jnp.int32)
    reached = (segment_ids[:, None] == segment_ids[None, :]).astype(jnp.int32)
    on_path = reached
    for hop_number in range(seg_count - 1):
        reached = jnp.dot(reached, parent_hop)
        on_path = jnp.maximum(on_path, reached)
    return on_path


def flip_units(values):
    pairs = [(c * 4 + t, c * 4 + (t ^ FLIP[c])) for c in range(4) for t in range(4)]
    return lax.ppermute(values, ("ctx", "tp"), pairs)


def joined(query, key, value, gap):
    return jnp.concatenate(
        [
            query[..., :128], gap, query[..., 128:],
            key[..., :128], value[..., 128:], key[..., 128:], value[..., :128],
        ],
        axis=-1,
    )


def parted(grads):
    query = jnp.concatenate([grads[..., :128], grads[..., 192:256]], axis=-1)
    key = jnp.concatenate([grads[..., 256:384], grads[..., 448:512]], axis=-1)
    value = jnp.concatenate([grads[..., 512:640], grads[..., 384:448]], axis=-1)
    return query, key, value


def shards(
    hidden, cotangent, mem_pos, parents, memory, wq, wk, wv, wo, w1, w2,
    head_bias, ffn_bias, out_bias, norm_gains, norm_shifts,
):
    c = lax.axis_index("ctx")
    t = lax.axis_index("tp")
    layers = wq.shape[0]
    share_rows = hidden.shape[0]
    positions = t * share_rows + jnp.arange(share_rows, dtype=jnp.int32)
    marks = (mem_pos[0, 0][None, :] == positions[:, None]).astype(F32)
    stream = hidden.astype(F32) + jnp.dot(
        marks, memory, precision=lax.Precision.HIGHEST, preferred_element_type=F32
    )
    on_path = ancestry(parents[0])
    ids = jnp.arange(4, dtype=jnp.int32)
    pick = lambda seg: jnp.sum(on_path * (ids == seg).astype(jnp.int32)[:, None], axis=0)
    flags = jnp.stack([pick(c), pick(3 - c)])

    gap = jnp.zeros(wq.shape[:2] + (64,), BF16)
    local_in = joined(wq, wk, wv, gap)
    zeros = jnp.zeros((layers, 64), F32)
    none = jnp.zeros((layers, 192), F32)
    in_bias = joined(head_bias[:, 0], none, head_bias[:, 1], zeros)
    w1_flip = flip_units(w1)
    w2_flip = flip_units(w2)
    ffn_flip = flip_units(ffn_bias)
    piece = wo.shape[1] // 4
    wo_piece = lax.dynamic_slice_in_dim(wo, c * piece, piece, axis=1)
    weights = []
    for n in range(layers):
        w_in = lax.all_gather(local_in[n], "fsdp", axis=0, tiled=True)
        w_up = lax.all_gather(w1_flip[n], "fsdp", axis=0, tiled=True)
        w_down = lax.all_gather(w2_flip[n], "fsdp", axis=1, tiled=True)
        w_out = lax.all_gather(wo_piece[n], "fsdp", axis=1, tiled=True)
        w_out = lax.all_gather(w_out[None], "tp", axis=0, tiled=True)
        w_out = lax.all_gather(w_out, "ctx", axis=1, tiled=True).reshape(768, 768)
        vecs = jnp.concatenate(
            [
                out_bias[n],
                jnp.stack([norm_gains[n, 0], norm_shifts[n, 0], norm_gains[n, 1], norm_shifts[n, 1]]),
                jnp.zeros((2, 768), F32),
            ]
        )
        weights.append((w_in, w_up, w_down, w_out, vecs))
    saved = []
    rounded = stream.astype(BF16)
    for n in range(layers):
        w_in, w_up, w_down, w_out, vecs = weights[n]
        xg, qw, kv = project(rounded, w_in, in_bias[n][None], 8 * n)
        o, lse = attend(qw, kv, flags)
        stream, rounded, xhat1, r1, xhat2, r2, xg2, act, slope, rows = block(
            o, w_out, w_up, w_down, ffn_flip[n][None], vecs, stream, 8 * n + 1
        )
        saved.append((xg, qw, kv, o, lse, xhat1, r1, xhat2, r2, xg2, act, slope, rows))
    output = rounded
    grad = cotangent.astype(F32)
    matrix = [None] * layers
    small = [None] * layers
    heads = [None] * layers
    for n in reversed(range(layers)):
        w_in, w_up, w_down, w_out, vecs = weights[n]
        xg, qw, kv, o, lse, xhat1, r1, xhat2, r2, xg2, act, slope, rows = saved[n]
        gg, gu, back_one, g1, do, stats = block_back(
            grad, xhat2, r2, xhat1, r1, vecs, slope, w_up, w_down, w_out, 8 * n + 2
        )
        small[n] = stats
        d_up = mm_tn(xg2, gu).astype(BF16)
        d_down = mm_tn(act, gg).astype(BF16)
        d_out = jnp.stack([mm_tn(rows[g], g1) for g in range(4)]).astype(BF16)
        d_up = lax.psum_scatter(d_up, "fsdp", scatter_dimension=0, tiled=True)
        d_down = lax.psum_scatter(d_down, "fsdp", scatter_dimension=1, tiled=True)
        d_up = lax.psum(flip_units(d_up), "ctx").astype(F32)
        d_down = lax.psum(flip_units(d_down), "ctx").astype(F32)
        d_out = lax.psum_scatter(d_out, "ctx", scatter_dimension=1, tiled=True)
        d_out = lax.psum_scatter(d_out, "tp", scatter_dimension=0, tiled=True)
        d_out = lax.psum_scatter(d_out, "fsdp", scatter_dimension=2, tiled=True)
        d_out = lax.all_gather(d_out[0], "ctx", axis=0, tiled=True).astype(F32)
        dqw, dkv = attend_back(qw, kv, do, o, lse, flags)
        dq, own, grad = project_back(dqw, dkv, w_in, back_one, 8 * n + 3)
        both = jnp.concatenate([dq, own], axis=1)
        d_in = mm_tn(xg, both).astype(BF16)
        d_in = lax.psum_scatter(d_in, "fsdp", scatter_dimension=0, tiled=True)
        d_in = lax.psum(d_in, "ctx").astype(F32)
        sums = jnp.sum(both.astype(F32), axis=0)
        d_query_bias, _, d_value_bias = parted(sums)
        heads[n] = jnp.stack([d_query_bias, d_value_bias])
        matrix[n] = parted(d_in) + (d_out, d_up, d_down)
    hidden_grad = grad.astype(BF16)
    memory_part = lax.dot_general(
        marks, grad, (((0,), (0,)), ((), ())),
        precision=lax.Precision.HIGHEST, preferred_element_type=F32,
    )
    small = jnp.stack(small)
    heads = jnp.stack(heads)
    tp_mark = (ids == t).astype(F32)
    flipped = sum(((c == n) * (t ^ FLIP[n]) for n in range(4)), 0)
    unit_mark = (ids == flipped).astype(F32)
    padded_head = (heads[:, :, None, :] * tp_mark[None, None, :, None]).reshape(layers, 2, -1)
    padded_ffn = (small[:, 6][:, None, :] * unit_mark[None, :, None]).reshape(layers, -1)
    totals = lax.psum((padded_head, padded_ffn, small[:, :6], memory_part), ("fsdp", "ctx", "tp"))
    head_grad = jnp.sum(totals[0].reshape(layers, 2, 4, -1) * tp_mark[None, None, :, None], axis=2)
    ffn_grad = jnp.sum(totals[1].reshape(layers, 4, -1) * tp_mark[None, :, None], axis=1)
    stack = lambda k: jnp.stack([matrix[n][k] for n in range(layers)])
    return (
        output, hidden_grad, totals[3],
        stack(0), stack(1), stack(2), stack(3), stack(4), stack(5),
        head_grad, ffn_grad, totals[2][:, 4:6], totals[2][:, 0:2], totals[2][:, 2:4],
    )


def solution(mesh):
    rows = P(("fsdp", "ctx", "tp"), None)
    inner = P(None, "fsdp", "tp")
    outer = P(None, "tp", "fsdp")
    weights = (inner, inner, inner, outer, inner, outer)
    biases = (P(None, None, "tp"), P(None, "tp"), P(), P(), P())
    return jax.shard_map(
        shards,
        mesh=mesh,
        in_specs=(rows, rows, P("fsdp", "ctx", None), P("fsdp", None), P()) + weights + biases,
        out_specs=(rows, rows, P()) + weights + biases,
        check_vma=False,
    )
```

time: 1550 us -> 1080 us (0.70)
  waiting for transfers between devices: 1140 us -> 365 us
  Pallas kernels: 0 us -> 510 us
  matrix products: 159 us -> 27.5 us
  blocking collectives: 48.7 us -> 100 us
  other arithmetic: 61.6 us -> 14.3 us
  local copies, waits for them, and re-layouts: 73.4 us -> 32.7 us
  loops' own time: 33.5 us -> 0 us
    pallas_call x0 -> x12, Pallas kernels: none -> 510 us  [the longest x2 122 us: project(): call(project_kernel, outs, scratch, cid, 'project', 3, (2 * 1024 * 768 *...]
    all_gather x16 -> x6, waiting for transfers between devices: 341 us -> 0.01 us  [the longest x2 0.01 us: shards(): w_out = lax.all_gather(w_out, 'ctx', axis=1, tiled=True).reshape(768, 768)]
    reduce_scatter x14 -> x8, waiting for transfers between devices: 459 us -> 149 us  [the longest x2 68.7 us: shards(): d_out = lax.psum_scatter(d_out, 'tp', scatter_dimension=0, tiled=True)]
    dot_general x56 -> x16, matrix products: 159 us -> 26.9 us  [the longest x14 24.3 us: mm_tn(): lax.dot_general(left, right, (((0,), (0,)), ((), ())), preferred_element_...]
    unnamed x52 -> x24, waiting for transfers between devices: 147 us -> 24 us
    all_gather x8, blocking collectives: 48.7 us -> 100 us  [the longest x2 59.6 us: shards(): w_out = lax.all_gather(w_out[None], 'tp', axis=0, tiled=True)]
    another operation x32 -> x0, loops' own time: 33.5 us -> none  [the longest x8 30.1 us: attend_back(): lax.cond(allowed[block_no] > 0, spread_back, skip_back, grad_query)]
    unnamed x332 -> x100, local copies, waits for them, and re-layouts: 53.1 us -> 21.1 us
  transfers between devices with their start and end apart: 42 -> 27, of which waited for: 38 -> 10; matrix products, arithmetic and copies ran while one was open for 9% -> 5% of each run, Pallas kernels for 0% -> 27%
where the time goes in v1:
time: 1080 us
  Pallas kernels  510 us (47%)
  waiting for transfers between devices  365 us (34%)
  blocking collectives  100 us (9%)
  local copies, waits for them, and re-layouts  32.7 us (3%)
  matrix products  27.5 us (3%)
  between operations  15.7 us (1%)
  other arithmetic  14.3 us (1%)
  starting transfers between devices  12.4 us (1%)
    psum x1, waiting for transfers between devices, shards(): lax.psum((padded_head, padded_ffn, small[:, :6], memory_part), ('fsdp', '...  128 us
    pallas_call x2, Pallas kernels, project(): call(project_kernel, outs, scratch, cid, 'project', 3, (2 * 1024 * 768 *...  122 us
    pallas_call x2, Pallas kernels, project_back(): call(project_back_kernel, outs, scratch, cid, 'project_back', 4, cost)  122 us
    pallas_call x2, Pallas kernels, block(): call(block_kernel, outs, scratch, cid, 'block', 7, cost)  99.1 us
    pallas_call x2, Pallas kernels, block_back(): call(block_back_kernel, outs, scratch, cid, 'block_back', 10, cost)  89.8 us
    reduce_scatter x2, waiting for transfers between devices, shards(): d_out = lax.psum_scatter(d_out, 'tp', scatter_dimension=0, tiled=True)  68.7 us
    psum x1, waiting for transfers between devices, shards(): d_in = lax.psum(d_in, 'ctx').astype(F32)  63.5 us
    all_gather x2, blocking collectives, shards(): w_out = lax.all_gather(w_out[None], 'tp', axis=0, tiled=True)  59.6 us
  transfers between devices with their start and end apart: 27, of which 10 were waited for; matrix products, arithmetic and copies ran while one was open for 5% of the time, Pallas kernels for 27%

profile of v1, /device:TPU:0, one launch (start us, length us, event | category | flops | bytes accessed | tf_op | source)
XLA Modules:
  0.0 1077.7 jit_solution(3657657819616900379)
XLA Ops:
  8.0 5.6 all-gather.1
  13.6 15.4 %all-gather.2 = bf16[4,48,768]{2,1,0:T(8,128)(2,1)} all-gather(bf16[1,48,768]{2,1,0:T(8,128)(2,1)S(1)} %all-gather.1), channel_id=4, replica_groups=mesh['fsdp'=2,'ctx'=4,'tp'=4] {'tp'}, dimensions={0}, use_global_device_ids=true | all-gather | bytes 368640 | tf_op jit(solution)/shard_map/all_gather | solution.py:886
  29.1 1.9 collective-permute-start
  31.1 1.9 collective-permute-start.1
  35.4 4.6 all-gather.7
  40.0 44.2 %all-gather.8 = bf16[4,48,768]{2,1,0:T(8,128)(2,1)} all-gather(bf16[1,48,768]{2,1,0:T(8,128)(2,1)S(1)} %all-gather.7), channel_id=10, replica_groups=mesh['fsdp'=2,'ctx'=4,'tp'=4] {'tp'}, dimensions={0}, use_global_device_ids=true | all-gather | bytes 368640 | tf_op jit(solution)/shard_map/all_gather | solution.py:886
  89.3 9.7 all-gather
  99.1 9.6 all-gather.6
  108.7 1.5 fusion.53
  110.3 77.1 %project.2 = (bf16[4,256,768]{2,1,0:T(8,128)(2,1)}, bf16[4,256,256]{2,1,0:T(8,128)(2,1)}, bf16[4,4,256,384]{3,2,1,0:T(8,128)(2,1)}) custom-call(bf16[256,768]{1,0:T(8,128)(2,1)} %get-tuple-element.217.x_ref, bf16[768,640]{1,0:T(8,128)(2,1)} %bitcast.174, f32[1,640]{1,0:T(1,128)} %get-tuple-element.206.b_ref), custom_call_target="tpu_custom_call" | custom-call | flops 1006632960 | bytes 8388608 | tf_op jit(solution)/shard_map/project/pallas_call | solution.py:218
  187.6 16.4 %attend.2 = (bf16[1024,192]{1,0:T(8,128)(2,1)}, f32[1024,128]{1,0:T(8,128)}) custom-call(s32[2,4]{1,0:T(2,128)} %pad_add_fusion.flag_ref, bf16[1024,256]{1,0:T(8,128)(2,1)} %bitcast.235, bf16[4096,384]{1,0:T(8,128)(2,1)} %bitcast.229), custom_call_target="tpu_custom_call" | custom-call | flops 2013265920 | bytes 6291456 | tf_op jit(solution)/shard_map/attend/pallas_call | solution.py:302
  206.8 50.9 %block.2 = (f32[256,768]{1,0:T(8,128)}, bf16[256,768]{1,0:T(8,128)(2,1)}, f32[256,768]{1,0:T(8,128)}, f32[256,128]{1,0:T(8,128)}, f32[256,768]{1,0:T(8,128)}, /*...) custom-call(bf16[4,256,192]{2,1,0:T(8,128)(2,1)} %bitcast.237, ...), custom_call_target="tpu_custom_call" | custom-call | flops 2717908992 | bytes 16777216 | tf_op jit(solution)/shard_map/block/pallas_call | solution.py:514
  257.8 44.7 %project.3 = (bf16[4,256,768]{2,1,0:T(8,128)(2,1)}, bf16[4,256,256]{2,1,0:T(8,128)(2,1)}, bf16[4,4,256,384]{3,2,1,0:T(8,128)(2,1)}) custom-call(bf16[256,768]{1,0:T(8,128)(2,1)} %get-tuple-element.68.x_ref, bf16[768,640]{1,0:T(8,128)(2,1)} %bitcast.176, f32[1,640]{1,0:T(1,128)} %get-tuple-element.205.b_ref), custom_call_target="tpu_custom_call" | custom-call | flops 1006632960 | bytes 8388608 | tf_op jit(solution)/shard_map/project/pallas_call | solution.py:218
  302.5 16.3 %attend.3 = (bf16[1024,192]{1,0:T(8,128)(2,1)}, f32[1024,128]{1,0:T(8,128)}) custom-call(s32[2,4]{1,0:T(2,128)} %pad_add_fusion.flag_ref, bf16[1024,256]{1,0:T(8,128)(2,1)} %bitcast.239, bf16[4096,384]{1,0:T(8,128)(2,1)} %bitcast.231), custom_call_target="tpu_custom_call" | custom-call | flops 2013265920 | bytes 6291456 | tf_op jit(solution)/shard_map/attend/pallas_call | solution.py:302
  318.8 48.1 %block.3 = (f32[256,768]{1,0:T(8,128)}, bf16[256,768]{1,0:T(8,128)(2,1)}, f32[256,768]{1,0:T(8,128)}, f32[256,128]{1,0:T(8,128)}, f32[256,768]{1,0:T(8,128)}, /*...) custom-call(bf16[4,256,192]{2,1,0:T(8,128)(2,1)} %bitcast.241, ...), custom_call_target="tpu_custom_call" | custom-call | flops 2717908992 | bytes 16777216 | tf_op jit(solution)/shard_map/block/pallas_call | solution.py:514
  366.9 42.5 %block_back.2 = (bf16[4,256,768]{2,1,0:T(8,128)(2,1)}, bf16[4,256,768]{2,1,0:T(8,128)(2,1)}, f32[256,768]{1,0:T(8,128)}, bf16[256,768]{1,0:T(8,128)(2,1)}, bf16[...) custom-call(f32[256,768]{1,0:T(8,128)} %convert_element_type.96.grad_ref, f32[256,768]{1,0:T(8,128)} %get-tuple-element.74.xhat2_ref, ...), custom_call_target="tpu_custom_call" | custom-call | flops 2717908992 | bytes 16777216 | tf_op jit(solution)/shard_map/block_back/pallas_call | solution.py:655
  409.4 22.6 %attend_back.2 = (bf16[1024,256]{1,0:T(8,128)(2,1)}, bf16[4096,384]{1,0:T(8,128)(2,1)}) custom-call(s32[2,4]{1,0:T(2,128)} %pad_add_fusion.flag_ref, bf16[1024,256]{1,0:T(8,128)(2,1)} %bitcast.240, bf16[4096,384]{1,0:T(8,128)(2,1)} %bitcast.232, bf16[1024,192]{1,0:T(8,128)(2,1)} %bitcast.242, bf16[1024,192]{1,0:T(8,128)(2,1)} %get-tuple-element.71.o_ref, ...), custom_call_target="tpu_custom_call" | custom-call | flops 5033164800 | bytes 12582912 | tf_op jit(solution)/shard_map/attend_back/pallas_call | solution.py:383
  432.1 61.5 %project_back.2 = (bf16[4,256,256]{2,1,0:T(8,128)(2,1)}, bf16[4,256,384]{2,1,0:T(8,128)(2,1)}, f32[256,768]{1,0:T(8,128)}) custom-call(bf16[4,256,256]{2,1,0:T(8,128)(2,1)} %bitcast.199, bf16[4,4,256,384]{3,2,1,0:T(8,128)(2,1)} %bitcast.179, bf16[768,640]{1,0:T(8,128)(2,1)} %bitcast.177, f32[256,768]{1,0:T(8,128)} %get-tuple-element.83.back_ref), custom_call_target="tpu_custom_call" | custom-call | flops 1006632960 | bytes 8388608 | tf_op jit(solution)/shard_map/project_back/pallas_call | solution.py:809
  493.6 47.3 %block_back.3 = (bf16[4,256,768]{2,1,0:T(8,128)(2,1)}, bf16[4,256,768]{2,1,0:T(8,128)(2,1)}, f32[256,768]{1,0:T(8,128)}, bf16[256,768]{1,0:T(8,128)(2,1)}, bf16[...) custom-call(f32[256,768]{1,0:T(8,128)} %get-tuple-element.84.grad_ref, f32[256,768]{1,0:T(8,128)} %get-tuple-element.85.xhat2_ref, ...), custom_call_target="tpu_custom_call" | custom-call | flops 2717908992 | bytes 16777216 | tf_op jit(solution)/shard_map/block_back/pallas_call | solution.py:655
  548.3 2.8 bitcast_convert_fusion.1
  552.7 2.8 bitcast_convert_fusion
  557.1 4.0 bitcast_convert_fusion.3
  561.4 4.5 bitcast_convert_fusion.2
  566.0 12.3 %reduce-scatter.25.cloned.1.call-done = bf16[4,48,768]{2,1,0:T(8,128)(2,1)} async-done(((bf16[4,192,768]{2,1,0:T(8,128)(2,1)}), bf16[4,48,768]{2,1,0:T(8,128)(2,1)}) %reduce-scatter.25.cloned.1.call-update) | async-done | bytes 294928 | tf_op jit(solution)/shard_map/reduce_scatter | solution.py:925
  578.4 28.4 %reduce-scatter.29.cloned.1.call-done = bf16[4,48,768]{2,1,0:T(8,128)(2,1)} async-done(((bf16[4,192,768]{2,1,0:T(8,128)(2,1)}), bf16[4,48,768]{2,1,0:T(8,128)(2,1)}) %reduce-scatter.29.cloned.1.call-update) | async-done | bytes 294928 | tf_op jit(solution)/shard_map/reduce_scatter | solution.py:925
  607.1 2.4 convolution_convert_fusion
  610.6 22.7 %attend_back.3 = (bf16[1024,256]{1,0:T(8,128)(2,1)}, bf16[4096,384]{1,0:T(8,128)(2,1)}) custom-call(s32[2,4]{1,0:T(2,128)} %pad_add_fusion.flag_ref, bf16[1024,256]{1,0:T(8,128)(2,1)} %bitcast.236, bf16[4096,384]{1,0:T(8,128)(2,1)} %bitcast.230, bf16[1024,192]{1,0:T(8,128)(2,1)} %bitcast.238, bf16[1024,192]{1,0:T(8,128)(2,1)} %get-tuple-element.67.o_ref, ...), custom_call_target="tpu_custom_call" | custom-call | flops 5033164800 | bytes 12582912 | tf_op jit(solution)/shard_map/attend_back/pallas_call | solution.py:383
  633.2 60.1 %project_back.3 = (bf16[4,256,256]{2,1,0:T(8,128)(2,1)}, bf16[4,256,384]{2,1,0:T(8,128)(2,1)}, f32[256,768]{1,0:T(8,128)}) custom-call(bf16[4,256,256]{2,1,0:T(8,128)(2,1)} %bitcast.198, bf16[4,4,256,384]{3,2,1,0:T(8,128)(2,1)} %bitcast.178, bf16[768,640]{1,0:T(8,128)(2,1)} %bitcast.175, f32[256,768]{1,0:T(8,128)} %get-tuple-element.94.back_ref), custom_call_target="tpu_custom_call" | custom-call | flops 1006632960 | bytes 8388608 | tf_op jit(solution)/shard_map/project_back/pallas_call | solution.py:809
  694.9 3.7 convolution_convert_fusion.1
  700.3 2.1 copy.84
  702.4 1.7 collective-permute-start.5
  704.1 2.1 copy.86
  706.3 1.7 collective-permute-start.6
  708.0 1.7 collective-permute-start.3
  709.7 1.7 collective-permute-start.4
  712.5 27.5 %reduce-scatter.27.cloned.1.call-done = bf16[1,48,768]{2,1,0:T(8,128)(2,1)} async-done(((bf16[4,48,768]{2,1,0:T(8,128)(2,1)}), bf16[1,48,768]{2,1,0:T(8,128)(2,1)}) %reduce-scatter.27.cloned.1.call-update) | async-done | bytes 73744 | tf_op jit(solution)/shard_map/reduce_scatter | solution.py:926
  742.0 41.1 %reduce-scatter.31.cloned.1.call-done = bf16[1,48,768]{2,1,0:T(8,128)(2,1)} async-done(((bf16[4,48,768]{2,1,0:T(8,128)(2,1)}), bf16[1,48,768]{2,1,0:T(8,128)(2,1)}) %reduce-scatter.31.cloned.1.call-update) | async-done | bytes 73744 | tf_op jit(solution)/shard_map/reduce_scatter | solution.py:926
  785.1 18.0 %reduce-scatter.23.cloned.1.call-done = bf16[384,640]{1,0:T(8,128)(2,1)} async-done(((bf16[768,640]{1,0:T(8,128)(2,1)}), bf16[384,640]{1,0:T(8,128)(2,1)}) %reduce-scatter.23.cloned.1.call-update) | async-done | bytes 491536 | tf_op jit(solution)/shard_map/reduce_scatter | solution.py:933
  803.1 21.8 %reduce-scatter.21.cloned.1.call-done = bf16[384,640]{1,0:T(8,128)(2,1)} async-done(((bf16[768,640]{1,0:T(8,128)(2,1)}), bf16[384,640]{1,0:T(8,128)(2,1)}) %reduce-scatter.21.cloned.1.call-update) | async-done | bytes 491536 | tf_op jit(solution)/shard_map/reduce_scatter | solution.py:933
  827.1 127.9 %all-reduce.5.cloned.1.call-done = (f32[20,768]{1,0:T(8,128)}, f32[2,2,4,192]{3,2,1,0:T(4,128)}, f32[2,4,768]{2,1,0:T(4,128)}, f32[2,6,768]{2,1,0:T(8,128)}) async-done(((f32[20,768]{1,0:T(8,128)}, f32[2,2,4,192]{3,2,1,0:T(4,128)}, f32[2,4,768]{2,1,0:T(4,128)}, f32[2,6,768]{2,1,0:T(8,128)}), (f32[20,768]{1,0:T(8,128)}, f32[2,2,4,192]{3,2,1,0:T(4,128)}, f32[2,4,768]{2,1,0:T(4,128)}, ...) | async-done | bytes 135184 | tf_op jit(solution)/shard_map/psum | solution.py:951
  957.9 1.5 fusion.45
  959.4 11.0 %reduce-scatter.37.cloned.1.call-done = bf16[384,48]{1,0:T(8,128)(2,1)} async-done(((bf16[768,48]{1,0:T(8,128)(2,1)}), bf16[384,48]{1,0:T(8,128)(2,1)}) %reduce-scatter.37.cloned.1.call-update) | async-done | bytes 36880
  971.5 12.7 %reduce-scatter.39.cloned.1.call-done = bf16[384,48]{1,0:T(8,128)(2,1)} async-done(((bf16[768,48]{1,0:T(8,128)(2,1)}), bf16[384,48]{1,0:T(8,128)(2,1)}) %reduce-scatter.39.cloned.1.call-update) | async-done | bytes 36880
  985.2 5.5 all-gather.12
  990.7 5.5 all-gather.13
  997.0 63.5 %all-reduce.7.cloned.1.call-done = (bf16[384,640]{1,0:T(8,128)(2,1)}, bf16[384,640]{1,0:T(8,128)(2,1)}, bf16[1,384,768]{2,1,0:T(8,128)(2,1)}, bf16[1,384,768]{2,...) async-done(((bf16[384,640]{1,0:T(8,128)(2,1)}, bf16[384,640]{1,0:T(8,128)(2,1)}, bf16[1,384,768]{2,1,0:T(8,128)(2,1)}, ...) | async-done | bytes 3342352 | tf_op jit(solution)/shard_map/psum | solution.py:934
  1065.8 1.6 maximum_convert_fusion.1
  1067.4 1.6 maximum_convert_fusion
  (252 shorter events, 45.9 us)
Async XLA Ops:
  7.2 101.5 %copy-start = (f32[20,768]{1,0:T(8,128)S(1)}, f32[20,768]{1,0:T(8,128)}, u32[]{:S(2)}) copy-start(f32[20,768]{1,0:T(8,128)} %param.20) | copy-start | bytes 184324
  7.2 199.6 %all-gather.21.cloned.1.call-start = ((), (), s32[]{:S(2)}) async-start(), calls=%async_computation.20 | async-start | bytes 1474560 | tf_op jit(solution)/shard_map/all_gather | solution.py:887
  29.1 177.7 %all-gather.23.cloned.1.call-start = ((), (), s32[]{:S(2)}) async-start(), calls=%async_computation.21 | async-start | bytes 1769472 | tf_op jit(solution)/shard_map/all_gather | solution.py:883
  29.1 3.9 collective-permute-start
  31.1 3.1 collective-permute-start.1
  34.1 50.2 %copy-start.30 = (f32[2,768]{1,0:T(2,128)S(1)}, f32[2,768]{1,0:T(2,128)}, u32[]{:S(2)}) copy-start(f32[2,768]{1,0:T(2,128)} %param.28) | copy-start | bytes 18436
  34.1 50.9 %copy-start.28 = (f32[2,2,192]{2,1,0:T(2,128)S(1)}, f32[2,2,192]{2,1,0:T(2,128)}, u32[]{:S(2)}) copy-start(f32[2,2,192]{2,1,0:T(2,128)} %param.27) | copy-start | bytes 9220
  34.1 51.1 %copy-start.31 = (s32[1,4]{1,0:T(1,128)S(1)}, s32[1,4]{1,0:T(1,128)}, u32[]{:S(2)}) copy-start(s32[1,4]{1,0:T(1,128)} %param.19) | copy-start | bytes 52
  34.1 52.3 %copy-start.25 = (f32[2,2,768]{2,1,0:T(2,128)S(1)}, f32[2,2,768]{2,1,0:T(2,128)}, u32[]{:S(2)}) copy-start(f32[2,2,768]{2,1,0:T(2,128)} %param.29) | copy-start | bytes 36868
  34.1 172.7 %all-gather.25.cloned.1.call-start = ((), (), s32[]{:S(2)}) async-start(), calls=%async_computation.22 | async-start | bytes 1769472 | tf_op jit(solution)/shard_map/all_gather | solution.py:884
  35.4 283.4 %all-gather.27.cloned.1.call-start = ((), (), s32[]{:S(2)}) async-start(), calls=%async_computation.23 | async-start | bytes 1474560 | tf_op jit(solution)/shard_map/all_gather | solution.py:887
  84.3 234.5 %all-gather.29.cloned.1.call-start = ((), (), s32[]{:S(2)}) async-start(), calls=%async_computation.24 | async-start | bytes 1769472 | tf_op jit(solution)/shard_map/all_gather | solution.py:883
  84.3 121.9 %collective-permute-start.2 = (f32[2,768]{1,0:T(2,128)S(1)}, f32[2,768]{1,0:T(2,128)S(1)}, u32[]{:S(2)}, u32[]{:S(2)}) collective-permute-start(f32[2,768]{1,0:T(2,128)S(1)} %copy-done.30), channel_id=1, source_target_pairs={{0,0},{1,1},{2,2},{3,3},{4,6},{5,7},{6,4},{7,5},{8,9},{9,8},{10,11... | collective-permute-start | bytes 18440 | tf_op jit(solution)/shard_map/ppermute | solution.py:832
  86.4 232.3 %all-gather.31.cloned.1.call-start = ((), (), s32[]{:S(2)}) async-start(), calls=%async_computation.25 | async-start | bytes 1769472 | tf_op jit(solution)/shard_map/all_gather | solution.py:884
  89.3 19.4 %copy-start.20 = (bf16[256,768]{1,0:T(8,128)(2,1)S(1)}, bf16[256,768]{1,0:T(8,128)(2,1)}, u32[]{:S(2)}) copy-start(bf16[256,768]{1,0:T(8,128)(2,1)} %param.16) | copy-start | bytes 1179652
  89.3 19.4 %copy-start.29 = (s32[1,1,20]{2,1,0:T(1,128)S(1)}, s32[1,1,20]{2,1,0:T(1,128)}, u32[]{:S(2)}) copy-start(s32[1,1,20]{2,1,0:T(1,128)} %param.18) | copy-start | bytes 244
  110.3 468.0 %reduce-scatter.25.cloned.1.call-start = ((), (), s32[]{:S(2)}) async-start(), calls=%async_computation.14 | async-start | bytes 1474560 | tf_op jit(solution)/shard_map/reduce_scatter | solution.py:925
  110.3 77.2 %copy-start.26 = (f32[2,2,768]{2,1,0:T(2,128)S(1)}, f32[2,2,768]{2,1,0:T(2,128)}, u32[]{:S(2)}) copy-start(f32[2,2,768]{2,1,0:T(2,128)} %param.31) | copy-start | bytes 36868
  110.3 77.2 %copy-start.27 = (f32[2,2,768]{2,1,0:T(2,128)S(1)}, f32[2,2,768]{2,1,0:T(2,128)}, u32[]{:S(2)}) copy-start(f32[2,2,768]{2,1,0:T(2,128)} %param.30) | copy-start | bytes 36868
  187.5 16.4 %copy-start.21 = (bf16[256,768]{1,0:T(8,128)(2,1)S(1)}, bf16[256,768]{1,0:T(8,128)(2,1)}, u32[]{:S(2)}) copy-start(bf16[256,768]{1,0:T(8,128)(2,1)} %param.17) | copy-start | bytes 1179652
  493.5 47.3 %copy-start.16 = (bf16[4,256,192]{2,1,0:T(8,128)(2,1)S(1)}, bf16[4,256,192]{2,1,0:T(8,128)(2,1)}, u32[]{:S(2)}) copy-start(bf16[4,256,192]{2,1,0:T(8,128)(2,1)} %get-tuple-element.102) | copy-start | bytes 1179652
  540.9 2.6 copy-start.3
  545.3 61.5 %reduce-scatter.29.cloned.1.call-start = ((), (), s32[]{:S(2)}) async-start(), calls=%async_computation.16 | async-start | bytes 1474560 | tf_op jit(solution)/shard_map/reduce_scatter | solution.py:925
  547.7 152.6 %reduce-scatter.41.cloned.1.call-start = ((), (), s32[]{:S(2)}) async-start(), calls=%async_computation.28 | async-start | bytes 1769472
  552.6 151.5 %reduce-scatter.43.cloned.1.call-start = ((), (), s32[]{:S(2)}) async-start(), calls=%async_computation.29 | async-start | bytes 1769472
  557.1 150.9 %reduce-scatter.33.cloned.1.call-start = ((), (), s32[]{:S(2)}) async-start(), calls=%async_computation.18 | async-start | bytes 1769472 | tf_op jit(solution)/shard_map/reduce_scatter | solution.py:921
  561.1 148.6 %reduce-scatter.35.cloned.1.call-start = ((), (), s32[]{:S(2)}) async-start(), calls=%async_computation.19 | async-start | bytes 1769472 | tf_op jit(solution)/shard_map/reduce_scatter | solution.py:921
  561.4 45.7 %copy-start.33 = (bf16[4,256,768]{2,1,0:T(8,128)(2,1)S(1)}, bf16[4,256,768]{2,1,0:T(8,128)(2,1)}, u32[]{:S(2)}) copy-start(bf16[4,256,768]{2,1,0:T(8,128)(2,1)} %get-tuple-element.99) | copy-start | bytes 4718596
  565.9 41.2 %copy-start.22 = (f32[8,768]{1,0:T(8,128)S(1)}, f32[8,768]{1,0:T(8,128)}, u32[]{:S(2)}) copy-start(f32[8,768]{1,0:T(8,128)} %get-tuple-element.115) | copy-start | bytes 73732
  565.9 41.2 %copy-start.23 = (f32[8,768]{1,0:T(8,128)S(1)}, f32[8,768]{1,0:T(8,128)}, u32[]{:S(2)}) copy-start(f32[8,768]{1,0:T(8,128)} %get-tuple-element.114) | copy-start | bytes 73732
  565.9 41.2 %copy-start.7 = (bf16[4,256,384]{2,1,0:T(8,128)(2,1)S(1)}, bf16[4,256,384]{2,1,0:T(8,128)(2,1)}, u32[]{:S(2)}) copy-start(bf16[4,256,384]{2,1,0:T(8,128)(2,1)} %get-tuple-element.101) | copy-start | bytes 2359300
  565.9 41.3 %copy-start.18 = (bf16[4,256,256]{2,1,0:T(8,128)(2,1)S(1)}, bf16[4,256,256]{2,1,0:T(8,128)(2,1)}, u32[]{:S(2)}) copy-start(bf16[4,256,256]{2,1,0:T(8,128)(2,1)} %get-tuple-element.100) | copy-start | bytes 1572868
  565.9 174.2 %reduce-scatter.27.cloned.1.call-start = ((), (), s32[]{:S(2)}) async-start(), calls=%async_computation.15 | async-start | bytes 368640 | tf_op jit(solution)/shard_map/reduce_scatter | solution.py:926
  578.3 204.8 %reduce-scatter.31.cloned.1.call-start = ((), (), s32[]{:S(2)}) async-start(), calls=%async_computation.17 | async-start | bytes 368640 | tf_op jit(solution)/shard_map/reduce_scatter | solution.py:926
  606.8 196.3 %reduce-scatter.23.cloned.1.call-start = ((), (), s32[]{:S(2)}) async-start(), calls=%async_computation.13 | async-start | bytes 1474560 | tf_op jit(solution)/shard_map/reduce_scatter | solution.py:933
  609.6 215.4 %reduce-scatter.21.cloned.1.call-start = ((), (), s32[]{:S(2)}) async-start(), calls=%async_computation.12 | async-start | bytes 1474560 | tf_op jit(solution)/shard_map/reduce_scatter | solution.py:933
  633.2 61.6 %copy-start.32 = (bf16[4,256,768]{2,1,0:T(8,128)(2,1)S(1)}, bf16[4,256,768]{2,1,0:T(8,128)(2,1)}, u32[]{:S(2)}) copy-start(bf16[4,256,768]{2,1,0:T(8,128)(2,1)} %get-tuple-element.96) | copy-start | bytes 4718596
  698.5 12.9 %copy-start.4 = (f32[256,768]{1,0:T(8,128)S(1)}, f32[256,768]{1,0:T(8,128)}, u32[]{:S(2)}) copy-start(f32[256,768]{1,0:T(8,128)} %get-tuple-element.95) | copy-start | bytes 2359300
  698.6 256.5 %all-reduce.5.cloned.1.call-start = ((), (), s32[]{:S(2)}) async-start(), calls=%async_computation.30 | async-start | bytes 327680 | tf_op jit(solution)/shard_map/psum | solution.py:951
  702.4 122.5 %collective-permute-start.5 = (bf16[768,384]{1,0:T(8,128)(2,1)}, bf16[768,384]{1,0:T(8,128)(2,1)S(1)}, u32[]{:S(2)}, u32[]{:S(2)}) collective-permute-start(bf16[768,384]{1,0:T(8,128)(2,1)} %copy.84), channel_id=1, source_target_pairs={{0,0},{1,1},{2,2},{3,3},{4,6},{5,7},{6,4},{7,5},{8,9},{9,8},{10,11... | collective-permute-start | bytes 1769480 | tf_op jit(solution)/shard_map/ppermute | solution.py:832
  706.3 118.7 %collective-permute-start.6 = (bf16[768,384]{1,0:T(8,128)(2,1)}, bf16[768,384]{1,0:T(8,128)(2,1)S(1)}, u32[]{:S(2)}, u32[]{:S(2)}) collective-permute-start(bf16[768,384]{1,0:T(8,128)(2,1)} %copy.86), channel_id=1, source_target_pairs={{0,0},{1,1},{2,2},{3,3},{4,6},{5,7},{6,4},{7,5},{8,9},{9,8},{10,11... | collective-permute-start | bytes 1769480 | tf_op jit(solution)/shard_map/ppermute | solution.py:832
  708.0 117.0 %collective-permute-start.3 = (bf16[384,768]{1,0:T(8,128)(2,1)}, bf16[384,768]{1,0:T(8,128)(2,1)S(1)}, u32[]{:S(2)}, u32[]{:S(2)}) collective-permute-start(bf16[384,768]{1,0:T(8,128)(2,1)} %reduce-scatter.33.cloned.1.call-done), channel_id=1, source_target_pairs={{0,0},{1,1},{2,2},{3,3},{4,6},{5,7},{6,4},{7,5},{8,9},{9,8},{10,11... | collective-permute-start | bytes 1769480 | tf_op jit(solution)/shard_map/ppermute | solution.py:832
  709.7 115.3 %collective-permute-start.4 = (bf16[384,768]{1,0:T(8,128)(2,1)}, bf16[384,768]{1,0:T(8,128)(2,1)S(1)}, u32[]{:S(2)}, u32[]{:S(2)}) collective-permute-start(bf16[384,768]{1,0:T(8,128)(2,1)} %reduce-scatter.35.cloned.1.call-done), channel_id=1, source_target_pairs={{0,0},{1,1},{2,2},{3,3},{4,6},{5,7},{6,4},{7,5},{8,9},{9,8},{10,11... | collective-permute-start | bytes 1769480 | tf_op jit(solution)/shard_map/ppermute | solution.py:832
  712.5 257.9 %reduce-scatter.37.cloned.1.call-start = ((), (), s32[]{:S(2)}) async-start(), calls=%async_computation.26 | async-start | bytes 294912
  742.0 242.2 %reduce-scatter.39.cloned.1.call-start = ((), (), s32[]{:S(2)}) async-start(), calls=%async_computation.27 | async-start | bytes 294912
  785.0 275.5 %all-reduce.7.cloned.1.call-start = ((), (), s32[]{:S(2)}) async-start(), calls=%async_computation.31 | async-start | bytes 6684672 | tf_op jit(solution)/shard_map/psum | solution.py:934
  1067.3 3.1 copy-start.1
  1067.4 2.3 copy-start.24
  (22 other events, 30.2 us)
Sparse Core Ops, SparseCore 0:
  29.2 18.7 all-gather.20
  50.1 43.5 all-gather.22
  95.8 32.4 all-gather.24
  129.7 22.6 all-gather.26
  154.4 23.2 all-gather.28
  179.6 22.7 all-gather.30
  545.4 32.8 reduce-scatter.24
  581.0 25.7 reduce-scatter.28
  609.0 21.7 reduce-scatter.40
  633.0 21.7 reduce-scatter.42
  657.6 21.7 reduce-scatter.32
  682.1 21.7 reduce-scatter.34
  706.2 33.8 reduce-scatter.26
  742.2 40.8 reduce-scatter.30
  785.2 17.7 reduce-scatter.22
  805.3 19.5 reduce-scatter.20
  831.4 123.5 all-reduce.4
  957.7 12.6 reduce-scatter.36
  973.2 10.9 reduce-scatter.38
  987.9 72.5 all-reduce.6

commit v2 on v1

--- a/solution.py
+++ b/solution.py
@@ -7,13 +7,11 @@
 from jax.experimental.pallas import tpu as pltpu
 from jax.sharding import PartitionSpec as P
 
-HEAD = 64
 EPSILON = 1e-05
 MASKED = -1000000000.0
 MESH = pl.DeviceIdType.MESH
 F32 = jnp.float32
 BF16 = jnp.bfloat16
-NEAR = (0, 1)
 ORDER = ((0, 1), (1, 0), (2, 2), (3, 3))
 
 
@@ -64,22 +62,485 @@
     return pltpu.SemaphoreType.DMA(shape)
 
 
-def call(kernel, out_shapes, scratch, collective_id, name, n_in, cost, vmem=None, smem=()):
+class Rider:
+    def __init__(self, array, out, make, scratch, chunks=0):
+        self.array, self.out, self.make, self.scratch, self.chunks = array, out, make, scratch, chunks
+
+
+class Copies:
+    def __init__(self, steps, here, scratch):
+        self.steps, self.here = steps, here
+        self.send, self.recv, self.leg, self.stage = scratch
+        self.turned = False
+
+    def greetings(self):
+        return [(origin, when, weight) for _, origin, _, _, when, weight in self.steps]
+
+    def copies(self):
+        for number, (to, _, source, target, when, _) in enumerate(self.steps):
+            yield rcopy(source, target, self.send.at[number], self.recv.at[number], to), when
+
+    def inward(self):
+        return pltpu.make_async_copy(self.here[0], self.stage, self.leg.at[0])
+
+    def outward(self):
+        return pltpu.make_async_copy(self.stage, self.here[1], self.leg.at[1])
+
+    def start(self):
+        for copy, when in self.copies():
+            guarded(when, copy.start)
+        guarded(self.here[2], self.inward().start)
+
+    def turn(self):
+        guarded(self.here[2], self.inward().wait)
+        guarded(self.here[2], self.outward().start)
+
+    def finish(self):
+        for copy, when in self.copies():
+            guarded(when, copy.wait)
+        guarded(self.here[2], self.outward().wait)
+
+
+class FlipGather:
+    def __init__(self, source, target, place, scratch):
+        self.source, self.target = source, target
+        self.f, self.c, self.t = place
+        self.size = target.shape[0]
+        self.send, self.recv, self.on_send, self.on_recv, self.leg, self.stage = scratch
+        self.moves = self.c > 0
+
+    def greetings(self):
+        there = {"tp": flipped_place(self.c, self.t)}
+        ring = [({"fsdp": (self.f + self.size - k) % self.size}, None, 1) for k in range(1, self.size)]
+        return [(there, self.moves, (self.c + 3) // 4)] + ring
+
+    def first(self, chunk):
+        there = {"tp": flipped_place(self.c, self.t)}
+        return rcopy(
+            self.source.at[chunk], self.target.at[self.f, chunk], self.send.at[chunk], self.recv.at[chunk], there
+        )
+
+    def second(self, chunk, k, moved):
+        source = self.target.at[self.f, chunk] if moved else self.source.at[chunk]
+        device = {"fsdp": (self.f + k) % self.size}
+        return rcopy(
+            source, self.target.at[self.f, chunk], self.on_send.at[k - 1, chunk], self.on_recv.at[k - 1, chunk], device
+        )
+
+    def inward(self):
+        return pltpu.make_async_copy(self.source, self.stage, self.leg.at[0])
+
+    def outward(self):
+        return pltpu.make_async_copy(self.stage, self.target.at[self.f], self.leg.at[1])
+
+    def start(self):
+        @pl.when(self.moves)
+        def _():
+            for chunk in range(self.source.shape[0]):
+                self.first(chunk).start()
+
+        @pl.when(self.c == 0)
+        def _():
+            self.inward().start()
+
+    def hop(self, chunk):
+        @pl.when(self.moves)
+        def _():
+            self.first(chunk).wait_recv()
+            for k in range(1, self.size):
+                self.second(chunk, k, True).start()
+
+        @pl.when(self.c == 0)
+        def _():
+            for k in range(1, self.size):
+                self.second(chunk, k, False).start()
+
+    def turn(self):
+        @pl.when(self.c == 0)
+        def _():
+            self.inward().wait()
+            self.outward().start()
+
+    def finish(self):
+        @pl.when(self.moves)
+        def _():
+            for chunk in range(self.source.shape[0]):
+                self.first(chunk).wait_send()
+
+        for chunk in range(self.source.shape[0]):
+            for k in range(1, self.size):
+                self.second(chunk, k, False).wait()
+
+        @pl.when(self.c == 0)
+        def _():
+            self.outward().wait()
+
+
+class ScatterFlip:
+    def __init__(self, source, target, place, scratch):
+        self.source, self.target = source, target
+        self.f, self.c, self.t = place
+        self.size = source.shape[1]
+        self.send, self.recv, self.on_send, self.on_recv, self.leg, self.got, self.out = scratch
+        self.moves = self.c > 0
+
+    def greetings(self):
+        there = {"tp": flipped_place(self.c, self.t)}
+        ring = [({"fsdp": (self.f + self.size - k) % self.size}, None, 1) for k in range(1, self.size)]
+        return [(there, self.moves, (self.c + 3) // 4)] + ring
+
+    def first(self, chunk, k):
+        to = (self.f + k) % self.size
+        return rcopy(
+            self.source.at[chunk // 2, to, chunk % 2], self.got.at[k, chunk],
+            self.send.at[k - 1, chunk], self.recv.at[k - 1, chunk], {"fsdp": to},
+        )
+
+    def own(self, chunk):
+        return pltpu.make_async_copy(
+            self.source.at[chunk // 2, self.f, chunk % 2], self.got.at[0, chunk], self.leg.at[chunk]
+        )
+
+    def second(self, chunk):
+        there = {"tp": flipped_place(self.c, self.t)}
+        return rcopy(self.out.at[chunk], self.target.at[chunk], self.on_send.at[chunk], self.on_recv.at[chunk], there)
+
+    def stays(self, chunk):
+        return pltpu.make_async_copy(self.out.at[chunk], self.target.at[chunk], self.on_send.at[chunk])
+
+    def start(self):
+        for chunk in range(self.target.shape[0]):
+            for k in range(1, self.size):
+                self.first(chunk, k).start()
+            self.own(chunk).start()
+
+    def hop(self, chunk):
+        self.own(chunk).wait()
+        total = self.got[0, chunk].astype(F32)
+        for k in range(1, self.size):
+            self.first(chunk, k).wait_recv()
+            total += self.got[k, chunk].astype(F32)
+        self.out[chunk] = total.astype(BF16)
+
+        @pl.when(self.moves)
+        def _():
+            self.second(chunk).start()
+
+        @pl.when(self.c == 0)
+        def _():
+            self.stays(chunk).start()
+
+    def turn(self):
+        pass
+
+    def finish(self):
+        for chunk in range(self.target.shape[0]):
+            for k in range(1, self.size):
+                self.first(chunk, k).wait_send()
+
+            @pl.when(self.moves)
+            def _():
+                self.second(chunk).wait()
+
+            @pl.when(self.c == 0)
+            def _():
+                self.stays(chunk).wait()
+
+
+class CtxGather:
+    def __init__(self, source, target, place, scratch):
+        self.source, self.target = source, target
+        self.c = place[1]
+        self.send, self.recv, self.leg, self.stage = scratch
+
+    def greetings(self):
+        return [({"ctx": mate_of(self.c)}, None, 1), ({"ctx": across_of(self.c)}, None, 1)]
+
+    def copy(self, number):
+        c = self.c
+        device = across_of(c) if number == 0 else mate_of(c)
+        source = self.target.at[across_of(c)] if number == 2 else self.source
+        slot = across_of(c) if number == 2 else c
+        return rcopy(source, self.target.at[slot], self.send.at[number], self.recv.at[number], {"ctx": device})
+
+    def inward(self):
+        return pltpu.make_async_copy(self.source, self.stage, self.leg.at[0])
+
+    def outward(self):
+        return pltpu.make_async_copy(self.stage, self.target.at[self.c], self.leg.at[1])
+
+    def start(self):
+        self.copy(0).start()
+        self.copy(1).start()
+        self.inward().start()
+
+    def turn(self):
+        self.inward().wait()
+        self.outward().start()
+        self.copy(0).wait_recv()
+        self.copy(2).start()
+
+    def finish(self):
+        self.copy(0).wait_send()
+        self.copy(1).wait()
+        self.copy(2).wait()
+        self.outward().wait()
+
+
+class CtxScatter:
+    def __init__(self, pick, source, target, place, scratch):
+        self.source, self.target, self.pick = source, target, pick
+        self.c = place[1]
+        self.send, self.recv, self.leg, self.stage, self.cross, self.far, self.total = scratch
+
+    def greetings(self):
+        return [({"ctx": mate_of(self.c)}, None, 1), ({"ctx": across_of(self.c)}, None, 1)]
+
+    def copy(self, number):
+        c = self.c
+        device = across_of(c) if number == 2 else mate_of(c)
+        source = (self.pick(self.source, 3 - c), self.pick(self.source, mate_of(c)), self.total)[number]
+        target = (self.far, self.target.at[1], self.target.at[2])[number]
+        return rcopy(source, target, self.send.at[number], self.recv.at[number], {"ctx": device})
+
+    def inward(self):
+        return pltpu.make_async_copy(self.pick(self.source, self.c), self.stage, self.leg.at[0])
+
+    def outward(self):
+        return pltpu.make_async_copy(self.stage, self.target.at[0], self.leg.at[1])
+
+    def beside(self):
+        return pltpu.make_async_copy(self.pick(self.source, across_of(self.c)), self.cross, self.leg.at[2])
+
+    def start(self):
+        self.copy(0).start()
+        self.beside().start()
+        self.copy(1).start()
+        self.inward().start()
+
+    def turn(self):
+        self.copy(0).wait_recv()
+        self.beside().wait()
+        self.total[...] = (self.cross[...].astype(F32) + self.far[...].astype(F32)).astype(self.total.dtype)
+        self.copy(2).start()
+        self.inward().wait()
+        self.outward().start()
+
+    def finish(self):
+        self.copy(0).wait_send()
+        self.copy(1).wait()
+        self.copy(2).wait()
+        self.outward().wait()
+
+
+class Riding:
+    def __init__(self, riders, sources, targets, scratch):
+        place = tuple(lax.axis_index(axis) for axis in ("fsdp", "ctx", "tp"))
+        scratch = list(scratch)
+        self.rides, self.hops = [], []
+        self.turned = False
+        for rider, source, target in zip(riders, sources, targets):
+            own = [scratch.pop(0) for _ in rider.scratch]
+            ride = rider.make(source, target, place, own)
+            self.rides.append(ride)
+            self.hops += [(ride, chunk) for chunk in range(rider.chunks)]
+
+    def greet(self, barrier):
+        count = 0
+        for ride in self.rides:
+            for origin, when, weight in ride.greetings():
+                guarded(when, functools.partial(signal, barrier, origin))
+                count = count + weight
+        return count
+
+    def start(self):
+        for ride in self.rides:
+            ride.start()
+
+    def hop(self, number):
+        if isinstance(number, int):
+            if number < len(self.hops):
+                ride, chunk = self.hops[number]
+                ride.hop(chunk)
+            return
+        for at, (ride, chunk) in enumerate(self.hops):
+            pl.when(number == at)(functools.partial(ride.hop, chunk))
+
+    def turn(self):
+        self.turned = True
+        for ride in self.rides:
+            ride.turn()
+
+    def finish(self):
+        if not self.turned:
+            self.turn()
+        for ride in self.rides:
+            ride.finish()
+
+
+def guarded(when, action):
+    if when is None:
+        action()
+    else:
+        pl.when(when)(action)
+
+
+def call(kernel, operands, out_shapes, scratch, collective_id, name, cost, riders=(), smem=(), any_in=(), any_out=()):
+    n_in, n_out, n_scratch, n_ride = len(operands), len(out_shapes), len(scratch), len(riders)
+
+    def body(*refs):
+        refs = list(refs)
+        take = lambda n: [refs.pop(0) for _ in range(n)]
+        ins, sources, outs, targets, own = take(n_in), take(n_ride), take(n_out), take(n_ride), take(n_scratch)
+        kernel(Riding(riders, sources, targets, refs), *ins, *outs, *own)
+
     params = dict(vmem_limit_bytes=56 * 1024 * 1024)
     if collective_id is not None:
         params.update(collective_id=collective_id, has_side_effects=True)
-    return pl.pallas_call(
-        kernel,
-        out_shape=out_shapes,
+    extra = [item for rider in riders for item in rider.scratch]
+    anywhere = pl.BlockSpec(memory_space=pl.ANY)
+    whole = pl.BlockSpec(memory_space=pltpu.VMEM)
+    results = pl.pallas_call(
+        body,
+        out_shape=list(out_shapes) + [rider.out for rider in riders],
         in_specs=[
-            pl.BlockSpec(memory_space=pltpu.SMEM if i in smem else pltpu.VMEM) for i in range(n_in)
-        ],
-        out_specs=[pl.BlockSpec(memory_space=pltpu.VMEM)] * len(out_shapes),
-        scratch_shapes=scratch,
+            pl.BlockSpec(memory_space=pltpu.SMEM) if i in smem else anywhere if i in any_in else whole
+            for i in range(n_in)
+        ]
+        + [anywhere] * n_ride,
+        out_specs=[anywhere if i in any_out else whole for i in range(n_out)] + [anywhere] * n_ride,
+        scratch_shapes=list(scratch) + extra,
         compiler_params=pltpu.CompilerParams(**params),
         cost_estimate=pl.CostEstimate(flops=cost[0], bytes_accessed=cost[1], transcendentals=cost[2]),
         name=name,
-    )
+    )(*operands, *[rider.array for rider in riders])
+    return results[:n_out], results[n_out:]
+
+
+def copies_rider(array, out, steps, stage, plan):
+    def make(source, target, place, scratch):
+        return Copies(*plan(source, target, *place), scratch)
+
+    scratch = [dma(steps), dma(steps), dma(2), pltpu.VMEM(stage, array.dtype)]
+    return Rider(array, out, make, scratch)
+
+
+def flip_gather(own, size):
+    own = own.reshape(2, own.shape[0] // 2, own.shape[1])
+    scratch = [dma(2), dma(2), dma(size - 1, 2), dma(size - 1, 2), dma(2), pltpu.VMEM(own.shape, own.dtype)]
+    return Rider(own, sds(size, *own.shape), FlipGather, scratch, chunks=2)
+
+
+def scatter_flip(parts):
+    n, size = parts.shape[0], parts.shape[1]
+    shape = (2 * n, *parts.shape[3:])
+    scratch = [
+        dma(size - 1, 2 * n), dma(size - 1, 2 * n), dma(2 * n), dma(2 * n), dma(2 * n),
+        pltpu.VMEM((size, *shape), BF16), pltpu.VMEM(shape, BF16),
+    ]
+    return Rider(parts, sds(*shape), ScatterFlip, scratch, chunks=2 * n)
+
+
+def fsdp_gather(own, size):
+    def make(source, target, f, c, t):
+        steps = [
+            ({"fsdp": (f + k) % size}, {"fsdp": (f + size - k) % size}, source, target.at[f], None, 1)
+            for k in range(1, size)
+        ]
+        return steps, (source, target.at[f], None)
+
+    return copies_rider(own, sds(size, *own.shape, dtype=own.dtype), size - 1, own.shape, make)
+
+
+def fsdp_scatter(parts, size):
+    out = sds(size, parts.shape[0], *parts.shape[2:], dtype=parts.dtype)
+
+    def make(source, target, f, c, t):
+        steps = [
+            (
+                {"fsdp": (f + k) % size}, {"fsdp": (f + size - k) % size},
+                source.at[:, (f + k) % size], target.at[k], None, 1,
+            )
+            for k in range(1, size)
+        ]
+        return steps, (source.at[:, f], target.at[0], None)
+
+    return copies_rider(parts, out, size - 1, out.shape[1:], make)
+
+
+def ctx_gather(own):
+    scratch = [dma(3), dma(3), dma(2), pltpu.VMEM(own.shape, own.dtype)]
+    return Rider(own, sds(4, *own.shape, dtype=own.dtype), CtxGather, scratch)
+
+
+def ctx_scatter(parts, axis=0):
+    shape = parts.shape[:axis] + parts.shape[axis + 1 :]
+
+    def pick(ref, slot):
+        return ref.at[slot] if axis == 0 else ref.at[:, :, slot]
+
+    buffer = pltpu.VMEM(shape, parts.dtype)
+    scratch = [dma(3), dma(3), dma(3), buffer, buffer, buffer, buffer]
+    return Rider(parts, sds(3, *shape, dtype=parts.dtype), functools.partial(CtxScatter, pick), scratch)
+
+
+def flipped_place(c, t):
+    return 2 * ((t // 2 + c % 2) % 2) + (t % 2 + c // 2) % 2
+
+
+def tp_flip(own):
+    def make(source, target, f, c, t):
+        other = {"tp": flipped_place(c, t)}
+        return [(other, other, source, target, c > 0, (c + 3) // 4)], (source, target, c == 0)
+
+    return copies_rider(own, sds(*own.shape, dtype=own.dtype), 1, own.shape, make)
+
+
+def plane(size):
+    return [(kt, kf) for kt in (2, 3, 1, 0) for kf in range(size) if kt + kf > 0]
+
+
+def plane_gather(own, size):
+    def make(source, target, f, c, t):
+        steps = [
+            (
+                {"fsdp": (f + kf) % size, "tp": (t + kt) % 4},
+                {"fsdp": (f + size - kf) % size, "tp": (t + 4 - kt) % 4},
+                source, target.at[t, f], None, 1,
+            )
+            for kt, kf in plane(size)
+        ]
+        return steps, (source, target.at[t, f], None)
+
+    return copies_rider(own, sds(4, size, *own.shape, dtype=own.dtype), 4 * size - 1, own.shape, make)
+
+
+def plane_scatter(parts, size):
+    def make(source, target, f, c, t):
+        steps = [
+            (
+                {"fsdp": (f + kf) % size, "tp": (t + kt) % 4},
+                {"fsdp": (f + size - kf) % size, "tp": (t + 4 - kt) % 4},
+                source.at[(t + kt) % 4, (f + kf) % size], target.at[kt, kf], None, 1,
+            )
+            for kt, kf in plane(size)
+        ]
+        return steps, (source.at[t, f], target.at[0, 0], None)
+
+    return copies_rider(parts, sds(*parts.shape, dtype=parts.dtype), 4 * size - 1, parts.shape[2:], make)
+
+
+def carry_kernel(ride):
+    barrier = pltpu.get_barrier_semaphore()
+    pl.semaphore_wait(barrier, ride.greet(barrier))
+    ride.start()
+    for number in range(len(ride.hops)):
+        ride.hop(number)
+    ride.finish()
+
+
+def carry(riders, cid):
+    return call(carry_kernel, (), (), (), cid, "carry", (1 << 20, 1 << 20, 0), riders)[1]
 
 
 def sds(*shape, dtype=BF16):
@@ -87,9 +548,13 @@
 
 
 def project_kernel(
-    x_ref, w_ref, b_ref, xg_ref, qw_ref, kv_ref,
-    qbuf, x_recv, x_right, x_left, k1_send, k1_recv, k2_send, k2_recv, kf_send, kf_recv, q_send, q_recv,
+    fetch, ride, x_ref, w_ref, b_ref, xg_ref, qw_ref, kv_ref, *rest
 ):
+    if fetch:
+        full_ref, w_send, w_recv, *rest = rest
+    (
+        qbuf, x_recv, x_right, x_left, k1_send, k1_recv, k2_send, k2_recv, kf_send, kf_recv, q_send, q_recv,
+    ) = rest
     c = lax.axis_index("ctx")
     t = lax.axis_index("tp")
     barrier = pltpu.get_barrier_semaphore()
@@ -104,8 +569,12 @@
     def _():
         signal(barrier, {"tp": t + 1})
 
+    f, size = lax.axis_index("fsdp"), lax.axis_size("fsdp")
+    if fetch:
+        for k in range(1, size):
+            signal(barrier, {"fsdp": (f + size - k) % size})
     ends = (t // 3) + (3 - t) // 3
-    pl.semaphore_wait(barrier, 5 - ends)
+    pl.semaphore_wait(barrier, 5 - ends + ride.greet(barrier) + (size - 1 if fetch else 0))
 
     def right(src, chunk, step):
         return rcopy(src, xg_ref.at[chunk], x_right.at[step], x_recv.at[chunk], {"tp": t + 1})
@@ -123,6 +592,18 @@
     @pl.when(t > 0)
     def _():
         left(x_ref, t, 0).start()
+
+    def weight(k):
+        device = {"fsdp": (f + k) % size}
+        return rcopy(w_ref, full_ref.at[f], w_send.at[k - 1], w_recv.at[k - 1], device)
+
+    if fetch:
+        for k in range(1, size):
+            weight(k).start()
+        full_ref[f] = w_ref[...]
+        for k in range(1, size):
+            weight(k).wait_recv()
+    ride.start()
 
     def mate(chunk):
         return rcopy(kv_ref.at[c, chunk], kv_ref.at[c, chunk], k1_send.at[chunk], k1_recv.at[chunk], {"ctx": mate_of(c)})
@@ -160,7 +641,8 @@
                     left(xg_ref.at[t + step], t + step, step).start()
 
         chunk = ordered(t, step)
-        made = mm(xg_ref[chunk], w_ref[...]) + b_ref[...]
+        w = full_ref[...].reshape(768, 640) if fetch else w_ref[...]
+        made = mm(xg_ref[chunk], w) + b_ref[...]
         kv_ref[c, chunk] = made[:, 256:].astype(BF16)
         mate(chunk).start()
         across(chunk).start()
@@ -207,16 +689,29 @@
         def _():
             left(xg_ref.at[t + step], t + step, step).wait_send()
 
-
-def project(x, w, b, cid):
+    if fetch:
+        for k in range(1, size):
+            weight(k).wait_send()
+    ride.finish()
+
+
+def project(x, w, b, cid, riders=(), fetch=False):
     outs = [sds(4, 256, 768), sds(4, 256, 256), sds(4, 4, 256, 384)]
     scratch = [
         pltpu.VMEM((2, 256, 256), BF16),
         dma(4), dma(3), dma(3),
         dma(4), dma(4), dma(4), dma(4), dma(4), dma(4), dma(2), dma(2),
     ]
-    xg, qw, kv = call(project_kernel, outs, scratch, cid, "project", 3, (2 * 1024 * 768 * 640, 8 << 20, 0))(x, w, b)
-    return xg.reshape(1024, 768), qw.reshape(1024, 256), kv.reshape(4, 1024, 384)
+    if fetch:
+        size = lax.axis_size("fsdp")
+        outs.append(sds(size, *w.shape))
+        scratch = [dma(size - 1), dma(size - 1)] + scratch
+    cost = (2 * 1024 * 768 * 640, 8 << 20, 0)
+    kernel = functools.partial(project_kernel, fetch)
+    res, ridden = call(kernel, (x, w, b), outs, scratch, cid, "project", cost, riders)
+    xg, qw, kv = res[:3]
+    full = res[3].reshape(768, 640) if fetch else w
+    return xg.reshape(1024, 768), qw.reshape(1024, 256), kv.reshape(4, 1024, 384), full, ridden
 
 
 def norm_stats(summed):
@@ -244,8 +739,16 @@
 K_TILE = 256
 
 
-def attend_kernel(flag_ref, qw_ref, kv_ref, o_ref, lse_ref, qm_ref, m_ref, l_ref, acc_ref):
+def open_up(ride):
+    if ride.rides:
+        barrier = pltpu.get_barrier_semaphore()
+        pl.semaphore_wait(barrier, ride.greet(barrier))
+        ride.start()
+
+
+def attend_kernel(ride, flag_ref, qw_ref, kv_ref, o_ref, lse_ref, qm_ref, m_ref, l_ref, acc_ref):
     c = lax.axis_index("ctx")
+    open_up(ride)
     low = lax.broadcasted_iota(jnp.int32, (Q_TILE, 128), 1) < 64
     per_half = 512 // Q_TILE
 
@@ -264,22 +767,22 @@
 
         @pl.loop(0, segment + 1)
         def _(block):
-            @pl.when(flag_ref[half, block] > 0)
-            def _():
-                keys = pl.ds(pl.multiple_of(block * 1024, 1024), 1024)
-                for head in range(3):
-                    k_at = 0 if head < 2 else 128
-                    v_at = 256 if head < 2 else 128
-                    scores = mm_nt(qm_ref[head], kv_ref[keys, k_at : k_at + 128])
-                    old = m_ref[head]
-                    new = jnp.maximum(old, jnp.max(scores, axis=-1, keepdims=True))
-                    probs = jnp.exp(scores - new)
-                    keep = jnp.exp(old - new)
-                    m_ref[head] = new
-                    l_ref[head] = l_ref[head] * keep + jnp.sum(probs, axis=-1, keepdims=True)
-                    acc_ref[head] = acc_ref[head] * keep + mm(
-                        probs.astype(BF16), kv_ref[keys, v_at : v_at + 128]
-                    )
+            seen = flag_ref[half, block] > 0
+            keys = pl.ds(pl.multiple_of(block * 1024, 1024), 1024)
+            for head in range(3):
+                k_at = 0 if head < 2 else 128
+                v_at = 256 if head < 2 else 128
+                scores = mm_nt(qm_ref[head], kv_ref[keys, k_at : k_at + 128])
+                scores = jnp.where(seen, scores, MASKED)
+                old = m_ref[head]
+                new = jnp.maximum(old, jnp.max(scores, axis=-1, keepdims=True))
+                probs = jnp.exp(scores - new)
+                keep = jnp.exp(old - new)
+                m_ref[head] = new
+                l_ref[head] = l_ref[head] * keep + jnp.sum(probs, axis=-1, keepdims=True)
+                acc_ref[head] = acc_ref[head] * keep + mm(
+                    probs.astype(BF16), kv_ref[keys, v_at : v_at + 128]
+                )
 
         first = acc_ref[0] / l_ref[0]
         second = acc_ref[1] / l_ref[1]
@@ -288,9 +791,12 @@
         lane = lax.broadcasted_iota(jnp.int32, (Q_TILE, 128), 1)
         totals = [m_ref[head] + jnp.log(l_ref[head]) for head in range(3)]
         lse_ref[rows, :] = jnp.where(lane == 0, totals[0], jnp.where(lane == 1, totals[1], totals[2]))
-
-
-def attend(qw, kv, flags):
+        ride.hop(tile)
+
+    ride.finish()
+
+
+def attend(qw, kv, flags, cid, riders=()):
     outs = [sds(1024, 192), sds(1024, 128, dtype=F32)]
     scratch = [
         pltpu.VMEM((3, Q_TILE, 128), BF16),
@@ -299,16 +805,18 @@
         pltpu.VMEM((3, Q_TILE, 128), F32),
     ]
     cost = (5 * 512 * 1024 * 64 * 4 * 3, 6 << 20, 5 * 512 * 1024 * 3)
-    return call(attend_kernel, outs, scratch, None, "attend", 3, cost, smem=(0,))(
-        flags, qw, kv.reshape(4096, 384)
-    )
+    operands = (flags, qw, kv.reshape(4096, 384))
+    cid = cid if riders else None
+    res, ridden = call(attend_kernel, operands, outs, scratch, cid, "attend", cost, riders, smem=(0,))
+    return res[0], res[1], ridden
 
 
 def attend_back_kernel(
-    flag_ref, qw_ref, kv_ref, do_ref, o_ref, lse_ref, dq_ref, dkv_ref,
+    ride, flag_ref, qw_ref, kv_ref, do_ref, o_ref, lse_ref, dq_ref, dkv_ref,
     qm_ref, dm_ref, row_ref, acc_ref, key_ref,
 ):
     c = lax.axis_index("ctx")
+    open_up(ride)
     low = lax.broadcasted_iota(jnp.int32, (1024, 128), 1) < 64
     pair = qw_ref[:, 0:128]
     none = jnp.zeros_like(pair)
@@ -348,8 +856,9 @@
             for half in range(2):
                 segment = c if half == 0 else 3 - c
 
-                @pl.when((block <= segment) & (flag_ref[half, block] > 0))
+                @pl.when(block <= segment)
                 def _():
+                    seen = flag_ref[half, block] > 0
                     rows = pl.ds(half * 512, 512)
                     for head in range(3):
                         k_at = 0 if head < 2 else 128
@@ -357,6 +866,7 @@
                         query = qm_ref[head, rows]
                         grads = dm_ref[head, rows]
                         scores = mm_nt(kv_ref[keys, k_at : k_at + 128], query)
+                        scores = jnp.where(seen, scores, MASKED)
                         probs = jnp.exp(scores - row_ref[head : head + 1, rows])
                         grad_probs = mm_nt(kv_ref[keys, v_at : v_at + 128], grads)
                         grad_scores = (probs * (grad_probs - row_ref[8 + head : 9 + head, rows])).astype(BF16)
@@ -367,10 +877,13 @@
 
             dkv_ref[keys, :] = key_ref[...].astype(BF16)
 
+        ride.hop(block)
+
     dq_ref[...] = (acc_ref[...].astype(BF16).astype(F32) * 0.125).astype(BF16)
-
-
-def attend_back(qw, kv, do, o, lse, flags):
+    ride.finish()
+
+
+def attend_back(qw, kv, do, o, lse, flags, cid, riders=()):
     outs = [sds(1024, 256), sds(4096, 384)]
     scratch = [
         pltpu.VMEM((3, 1024, 128), BF16),
@@ -380,14 +893,14 @@
         pltpu.VMEM((K_TILE, 384), F32),
     ]
     cost = (5 * 512 * 1024 * 64 * 10 * 3, 12 << 20, 5 * 512 * 1024 * 3)
-    dq, dkv = call(attend_back_kernel, outs, scratch, None, "attend_back", 6, cost, smem=(0,))(
-        flags, qw, kv.reshape(4096, 384), do, o, lse
-    )
-    return dq, dkv.reshape(4, 1024, 384)
+    operands = (flags, qw, kv.reshape(4096, 384), do, o, lse)
+    cid = cid if riders else None
+    res, ridden = call(attend_back_kernel, operands, outs, scratch, cid, "attend_back", cost, riders, smem=(0,))
+    return res[0], res[1].reshape(4, 1024, 384), ridden
 
 
 def block_kernel(
-    o_ref, wo_ref, w1_ref, w2_ref, b1_ref, vec_ref, stream_ref,
+    ride, o_ref, wo_ref, w1_ref, w2_ref, b1_ref, vec_ref, stream_ref,
     out_ref, low_ref, xhat1_ref, r1_ref, xhat2_ref, r2_ref, xg_ref, act_ref, slope_ref, rows_ref,
     mine_ref, send_ref, got_ref, o_send, o_recv, a_send, a_recv, s_send, s_recv,
 ):
@@ -406,7 +919,7 @@
 
     signal(barrier, {"ctx": mate_of(c)})
     signal(barrier, {"ctx": across_of(c)})
-    pl.semaphore_wait(barrier, 5 + t // 2)
+    pl.semaphore_wait(barrier, 5 + t // 2 + ride.greet(barrier))
 
     def give(quarter):
         device = {"tp": quarter} if quarter < 2 else {"ctx": 3 - c, "tp": quarter}
@@ -435,7 +948,8 @@
         def _():
             given(group)
 
-        branch += mm(rows_ref[group], wo_ref[group * 192 : (group + 1) * 192])
+        branch += mm_nt(rows_ref[group], wo_ref[group])
+    ride.start()
     xhat, scale = norm_stats(branch)
     xhat1_ref[...] = xhat
     r1_ref[...] = jnp.broadcast_to(scale, r1_ref.shape)
@@ -454,7 +968,7 @@
         act, slope = gelu_both(up)
         act_ref[segment] = act
         slope_ref[segment] = slope
-        return mm(act, w2_ref[...])
+        return mm_nt(act, w2_ref[...])
 
     mine_ref[...] = feed(c) + normed + vec_ref[1:2]
     gather(mate, 0, mate).wait_recv()
@@ -473,6 +987,7 @@
     scatter(1, mate).wait_recv()
     send_ref[2] = (own_across + got_ref[1].astype(F32)).astype(BF16)
     scatter(2, across).start()
+    ride.turn()
     scatter(0, mate).wait_recv()
     scatter(2, across).wait_recv()
     summed = mine_ref[...] + got_ref[0].astype(F32) + got_ref[2].astype(F32)
@@ -496,9 +1011,10 @@
     gather(across, 2, mate).wait_send()
     for index in range(3):
         scatter(index, mate).wait_send()
-
-
-def block(o, wo, w1, w2, b1, vecs, stream, cid):
+    ride.finish()
+
+
+def block(o, wo, w1, w2, b1, vecs, stream, cid, riders=()):
     f = functools.partial(sds, dtype=F32)
     outs = [
         f(256, 768), sds(256, 768), f(256, 768), f(256, 128), f(256, 768), f(256, 128),
@@ -511,17 +1027,16 @@
         dma(4), dma(4), dma(3), dma(3), dma(3), dma(3),
     ]
     cost = (2 * 256 * 768 * 768 + 4 * 1024 * 768 * 768, 16 << 20, 1 << 20)
-    res = call(block_kernel, outs, scratch, cid, "block", 7, cost)(
-        o.reshape(4, 256, 192), wo, w1, w2, b1, vecs, stream
-    )
+    operands = (o.reshape(4, 256, 192), wo, w1, w2, b1, vecs, stream)
+    res, ridden = call(block_kernel, operands, outs, scratch, cid, "block", cost, riders)
     flat = lambda a: a.reshape(1024, 768)
-    return tuple(res[:6]) + (flat(res[6]), flat(res[7]), flat(res[8]), res[9])
+    return tuple(res[:6]) + (flat(res[6]), flat(res[7]), flat(res[8]), res[9], ridden)
 
 
 def block_back_kernel(
-    grad_ref, xhat2_ref, r2_ref, xhat1_ref, r1_ref, vec_ref, slope_ref, w1_ref, w2_ref, wo_ref,
-    gg_ref, gu_ref, back_ref, g1_ref, do_ref, stat_ref,
-    mine_ref, send_ref, got_ref, dsend_ref, d_send, d_recv, a_send, a_recv, s_send, s_recv,
+    ride, grad_ref, xhat2_ref, r2_ref, xhat1_ref, r1_ref, vec_ref, slope_ref, w1_ref, w2_ref, wo_ref,
+    xg_ref, act_ref, rows_ref, back_ref, do_ref, stat_ref, dffn_ref, dout_ref,
+    gg_ref, gu_ref, mine_ref, send_ref, got_ref, dsend_ref, d_send, d_recv, a_send, a_recv, s_send, s_recv,
 ):
     c = lax.axis_index("ctx")
     t = lax.axis_index("tp")
@@ -537,7 +1052,7 @@
             signal(barrier, {"ctx": 3 - c, "tp": place})
     signal(barrier, {"ctx": mate_of(c)})
     signal(barrier, {"ctx": across_of(c)})
-    pl.semaphore_wait(barrier, 5 + t // 2)
+    pl.semaphore_wait(barrier, 5 + t // 2 + ride.greet(barrier))
     mate, across, far = mate_of(c), across_of(c), 3 - c
 
     def row(values):
@@ -553,13 +1068,14 @@
 
     gather(c, 1, across).start()
     gather(c, 0, mate).start()
+    ride.start()
     stat_ref[1:2] = row(grad * xhat2_ref[...])
     stat_ref[3:4] = row(grad)
     stat_ref[5:6] = row(g2.astype(F32))
     stat_ref[7:8] = jnp.zeros((1, 768), F32)
 
     def feed(segment):
-        gu = (mm_nt(gg_ref[segment], w2_ref[...]) * slope_ref[segment].astype(F32)).astype(BF16)
+        gu = (mm(gg_ref[segment], w2_ref[...]) * slope_ref[segment].astype(F32)).astype(BF16)
         gu_ref[segment] = gu
         return mm_nt(gu, w1_ref[...]), row(gu.astype(F32))
 
@@ -587,13 +1103,20 @@
     scatter(1, mate).wait_recv()
     send_ref[2] = (own_across + got_ref[1].astype(F32)).astype(BF16)
     scatter(2, across).start()
+    tall = lambda ref: ref[...].reshape(1024, 768)
+
+    @pl.loop(0, 3)
+    def _(tile):
+        cols = pl.ds(pl.multiple_of(tile * 256, 256), 256)
+        dffn_ref[0, cols] = mm_tn(xg_ref[:, cols], tall(gu_ref)).astype(BF16)
+        dffn_ref[1, cols] = mm_tn(gg_ref[:, :, cols].reshape(1024, 256), act_ref[...]).astype(BF16)
+
     scatter(0, mate).wait_recv()
     scatter(2, across).wait_recv()
     grad_normed = mine_ref[...] + got_ref[0].astype(F32) + got_ref[2].astype(F32)
     back_one = norm_back(grad_normed, xhat1_ref[...], r1_ref[:, 0:1], vec_ref[2:3])
     back_ref[...] = back_one
     g1 = back_one.astype(BF16)
-    g1_ref[...] = g1
 
     def give_near(group):
         return rcopy(dsend_ref.at[group], do_ref.at[t], d_send.at[group], d_recv.at[t], {"tp": group})
@@ -602,7 +1125,7 @@
         return rcopy(dsend_ref.at[group], do_ref.at[t], d_send.at[group], d_recv.at[t], {"ctx": 3 - c, "tp": group})
 
     for group in range(4):
-        dsend_ref[group] = mm_nt(g1, wo_ref[group * 192 : (group + 1) * 192]).astype(BF16)
+        dsend_ref[group] = mm(g1, wo_ref[group]).astype(BF16)
 
         @pl.when((t < 2) & (t == group))
         def _():
@@ -619,6 +1142,8 @@
     stat_ref[0:1] = row(grad_normed * xhat1_ref[...])
     stat_ref[2:3] = row(grad_normed)
     stat_ref[4:5] = row(g1.astype(F32))
+    for group in range(4):
+        dout_ref[group] = mm_tn(g1, rows_ref[group]).astype(BF16)
     for quarter in range(4):
 
         def taken():
@@ -639,28 +1164,31 @@
     gather(across, 2, mate).wait_send()
     for index in range(3):
         scatter(index, mate).wait_send()
-
-
-def block_back(grad, xhat2, r2, xhat1, r1, vecs, slope, w1, w2, wo, cid):
+    ride.finish()
+
+
+def block_back(grad, xhat2, r2, xhat1, r1, vecs, slope, w1, w2, wo, xg, act, rows, cid, riders=()):
     f = functools.partial(sds, dtype=F32)
-    outs = [sds(4, 256, 768), sds(4, 256, 768), f(256, 768), sds(256, 768), sds(4, 256, 192), f(8, 768)]
+    outs = [f(256, 768), sds(4, 256, 192), f(8, 768), sds(2, 768, 768), sds(4, 768, 192)]
     scratch = [
+        pltpu.VMEM((4, 256, 768), BF16),
+        pltpu.VMEM((4, 256, 768), BF16),
         pltpu.VMEM((256, 768), F32),
         pltpu.VMEM((3, 256, 768), BF16),
         pltpu.VMEM((3, 256, 768), BF16),
         pltpu.VMEM((4, 256, 192), BF16),
         dma(4), dma(4), dma(3), dma(3), dma(3), dma(3),
     ]
-    cost = (2 * 256 * 768 * 768 + 4 * 1024 * 768 * 768, 16 << 20, 1 << 10)
-    gg, gu, back, g1, do, stats = call(block_back_kernel, outs, scratch, cid, "block_back", 10, cost)(
-        grad, xhat2, r2, xhat1, r1, vecs, slope.reshape(4, 256, 768), w1, w2, wo
-    )
-    return gg.reshape(1024, 768), gu.reshape(1024, 768), back, g1, do.reshape(1024, 192), stats
+    cost = (4 * 256 * 768 * 768 + 8 * 1024 * 768 * 768, 20 << 20, 1 << 10)
+    operands = (grad, xhat2, r2, xhat1, r1, vecs, slope.reshape(4, 256, 768), w1, w2, wo, xg, act, rows)
+    res, ridden = call(block_back_kernel, operands, outs, scratch, cid, "block_back", cost, riders)
+    back, do, stats, d_ffn, d_out = res
+    return back, do.reshape(1024, 192), stats, d_ffn, d_out, ridden
 
 
 def project_back_kernel(
-    dqw_ref, dkv_ref, w_ref, back_ref, dq_ref, own_ref, grad_ref,
-    part_ref, near_ref, join_ref, sum_ref, far_ref, pass_ref, take_ref,
+    ride, dqw_ref, dkv_ref, w_ref, back_ref, xg_ref, grad_ref, din_ref, sum_out_ref,
+    dq_ref, own_ref, part_ref, near_ref, join_ref, sum_ref, far_ref, pass_ref, take_ref,
     q_send, q_recv, n_send, n_recv, j_send, j_recv, f_send, f_recv, p_send, p_recv,
 ):
     c = lax.axis_index("ctx")
@@ -678,7 +1206,7 @@
         signal(barrier, {"tp": t + 1})
 
     ends = (t // 3) + (3 - t) // 3
-    pl.semaphore_wait(barrier, 5 - ends)
+    pl.semaphore_wait(barrier, 5 - ends + ride.greet(barrier))
     mate, across, far = mate_of(c), across_of(c), 3 - c
 
     def partner(slot):
@@ -765,12 +1293,24 @@
             def _():
                 relay(chunk)
 
+    ride.start()
     for chunk in chunks[:3]:
 
         @pl.when(jnp.logical_not(at_end))
         def _():
             relay(chunk)
 
+    query, own = dq_ref[...].reshape(1024, 256), own_ref[...].reshape(1024, 384)
+    sum_out_ref[0:1, 0:256] = jnp.sum(query.astype(F32), axis=0, keepdims=True)
+    sum_out_ref[0:1, 256:640] = jnp.sum(own.astype(F32), axis=0, keepdims=True)
+
+    @pl.loop(0, 3)
+    def _(tile):
+        cols = pl.ds(pl.multiple_of(tile * 256, 256), 256)
+        din_ref[cols, 0:256] = mm_tn(xg_ref[:, cols], dq_ref[...].reshape(1024, 256)).astype(BF16)
+        din_ref[cols, 256:640] = mm_tn(xg_ref[:, cols], own_ref[...].reshape(1024, 384)).astype(BF16)
+
+    ride.turn()
     grad_ref[...] = part_ref[t] + back_ref[...]
 
     @pl.when(t < 3)
@@ -794,25 +1334,23 @@
 
     for slot in range(2):
         partner(slot).wait_send()
-
-
-def project_back(dqw, dkv, w, back_one, cid):
-    outs = [sds(4, 256, 256), sds(4, 256, 384), sds(256, 768, dtype=F32)]
+    ride.finish()
+
+
+def project_back(dqw, dkv, w, back_one, xg, cid, riders=()):
+    outs = [sds(256, 768, dtype=F32), sds(768, 640), sds(8, 640, dtype=F32)]
     scratch = [
+        pltpu.VMEM((4, 256, 256), BF16), pltpu.VMEM((4, 256, 384), BF16),
         pltpu.VMEM((4, 256, 768), F32),
         pltpu.VMEM((4, 256, 384), BF16), pltpu.VMEM((4, 256, 384), BF16),
         pltpu.VMEM((4, 256, 384), BF16), pltpu.VMEM((4, 256, 384), BF16),
         pltpu.VMEM((4, 256, 768), BF16), pltpu.VMEM((2, 4, 256, 768), BF16),
         dma(2), dma(2), dma(4), dma(4), dma(4), dma(4), dma(4), dma(4), dma(4), dma(2, 4),
     ]
-    cost = (2 * 1024 * 768 * 640, 8 << 20, 0)
-    dq, own, grad = call(project_back_kernel, outs, scratch, cid, "project_back", 4, cost)(
-        dqw.reshape(4, 256, 256), dkv.reshape(4, 4, 256, 384), w, back_one
-    )
-    return dq.reshape(1024, 256), own.reshape(1024, 384), grad
-
-
-FLIP = (0, 2, 1, 3)
+    cost = (4 * 1024 * 768 * 640, 12 << 20, 0)
+    operands = (dqw.reshape(4, 256, 256), dkv.reshape(4, 4, 256, 384), w, back_one, xg)
+    res, ridden = call(project_back_kernel, operands, outs, scratch, cid, "project_back", cost, riders)
+    return res[0], res[1], res[2][0], ridden
 
 
 def ancestry(parent_row):
@@ -827,11 +1365,6 @@
     return on_path
 
 
-def flip_units(values):
-    pairs = [(c * 4 + t, c * 4 + (t ^ FLIP[c])) for c in range(4) for t in range(4)]
-    return lax.ppermute(values, ("ctx", "tp"), pairs)
-
-
 def joined(query, key, value, gap):
     return jnp.concatenate(
         [
@@ -849,15 +1382,26 @@
     return query, key, value
 
 
+def added(terms, axes=(0,)):
+    return jnp.sum(terms.astype(F32), axis=axes)
+
+
+def low(values):
+    return values.astype(BF16)
+
+
 def shards(
     hidden, cotangent, mem_pos, parents, memory, wq, wk, wv, wo, w1, w2,
     head_bias, ffn_bias, out_bias, norm_gains, norm_shifts,
 ):
     c = lax.axis_index("ctx")
     t = lax.axis_index("tp")
+    size = lax.axis_size("fsdp")
     layers = wq.shape[0]
-    share_rows = hidden.shape[0]
-    positions = t * share_rows + jnp.arange(share_rows, dtype=jnp.int32)
+    share = hidden.shape[0]
+    depth = wq.shape[1]
+    piece = depth // 4
+    positions = t * share + jnp.arange(share, dtype=jnp.int32)
     marks = (mem_pos[0, 0][None, :] == positions[:, None]).astype(F32)
     stream = hidden.astype(F32) + jnp.dot(
         marks, memory, precision=lax.Precision.HIGHEST, preferred_element_type=F32
@@ -868,94 +1412,129 @@
     flags = jnp.stack([pick(c), pick(3 - c)])
 
     gap = jnp.zeros(wq.shape[:2] + (64,), BF16)
-    local_in = joined(wq, wk, wv, gap)
-    zeros = jnp.zeros((layers, 64), F32)
+    own_in = joined(wq, wk, wv, gap)
     none = jnp.zeros((layers, 192), F32)
-    in_bias = joined(head_bias[:, 0], none, head_bias[:, 1], zeros)
-    w1_flip = flip_units(w1)
-    w2_flip = flip_units(w2)
-    ffn_flip = flip_units(ffn_bias)
-    piece = wo.shape[1] // 4
-    wo_piece = lax.dynamic_slice_in_dim(wo, c * piece, piece, axis=1)
-    weights = []
+    in_bias = joined(head_bias[:, 0], none, head_bias[:, 1], jnp.zeros((layers, 64), F32))
+    down_turned = jnp.swapaxes(w2, 1, 2)
+    out_turned = jnp.swapaxes(wo, 1, 2).reshape(layers, 4, piece, 192)
+    out_piece = lax.dynamic_index_in_dim(out_turned, c, axis=1, keepdims=False)
+
+    def out_whole(gathered):
+        return jnp.transpose(gathered, (1, 2, 0, 3, 4)).reshape(4, 768, 192)
+
+    def vectors(n):
+        norms = [norm_gains[n, 0], norm_shifts[n, 0], norm_gains[n, 1], norm_shifts[n, 1]]
+        return jnp.concatenate([out_bias[n], jnp.stack(norms), jnp.zeros((2, 768), F32)])
+
+    saved, weights = [], []
+    rounded = low(stream)
+    riders = [plane_gather(out_piece[0], size), tp_flip(ffn_bias)]
+    xg, qw, kv, w_in, (out, units) = project(
+        rounded, own_in[0], in_bias[0][None], 0, riders, fetch=True
+    )
     for n in range(layers):
-        w_in = lax.all_gather(local_in[n], "fsdp", axis=0, tiled=True)
-        w_up = lax.all_gather(w1_flip[n], "fsdp", axis=0, tiled=True)
-        w_down = lax.all_gather(w2_flip[n], "fsdp", axis=1, tiled=True)
-        w_out = lax.all_gather(wo_piece[n], "fsdp", axis=1, tiled=True)
-        w_out = lax.all_gather(w_out[None], "tp", axis=0, tiled=True)
-        w_out = lax.all_gather(w_out, "ctx", axis=1, tiled=True).reshape(768, 768)
-        vecs = jnp.concatenate(
-            [
-                out_bias[n],
-                jnp.stack([norm_gains[n, 0], norm_shifts[n, 0], norm_gains[n, 1], norm_shifts[n, 1]]),
-                jnp.zeros((2, 768), F32),
+        last = n == layers - 1
+        riders = [ctx_gather(out)]
+        if n == 0:
+            riders += [flip_gather(w1[0], size), flip_gather(down_turned[0], size)]
+        else:
+            riders += [fsdp_gather(up, size), fsdp_gather(down, size)]
+        o, lse, got = attend(qw, kv, flags, 16 * n + 1, riders)
+        w_out = out_whole(got[0])
+        w_up, w_down = got[1:]
+        w_up, w_down = w_up.reshape(768, 768), w_down.reshape(768, 768)
+        vecs = vectors(n)
+        weights.append((w_in, w_up, w_down, w_out, vecs))
+        riders = []
+        if not last:
+            riders = [
+                tp_flip(w1[n + 1]), tp_flip(down_turned[n + 1]),
+                plane_gather(out_piece[n + 1], size), fsdp_gather(own_in[n + 1], size),
             ]
-        )
-        weights.append((w_in, w_up, w_down, w_out, vecs))
-    saved = []
-    rounded = stream.astype(BF16)
-    for n in range(layers):
-        w_in, w_up, w_down, w_out, vecs = weights[n]
-        xg, qw, kv = project(rounded, w_in, in_bias[n][None], 8 * n)
-        o, lse = attend(qw, kv, flags)
-        stream, rounded, xhat1, r1, xhat2, r2, xg2, act, slope, rows = block(
-            o, w_out, w_up, w_down, ffn_flip[n][None], vecs, stream, 8 * n + 1
+        stream, rounded, xhat1, r1, xhat2, r2, xg2, act, slope, rows, got = block(
+            o, w_out, w_up, w_down, units[n][None], vecs, stream, 16 * n + 2, riders
         )
         saved.append((xg, qw, kv, o, lse, xhat1, r1, xhat2, r2, xg2, act, slope, rows))
+        if not last:
+            up, down, out, w_in = got
+            xg, qw, kv, w_in, _ = project(rounded, w_in.reshape(768, 640), in_bias[n + 1][None], 16 * n + 16)
     output = rounded
+
     grad = cotangent.astype(F32)
-    matrix = [None] * layers
-    small = [None] * layers
-    heads = [None] * layers
+    small, heads = [None] * layers, [None] * layers
+    done = [None] * layers
+    above = None
     for n in reversed(range(layers)):
         w_in, w_up, w_down, w_out, vecs = weights[n]
         xg, qw, kv, o, lse, xhat1, r1, xhat2, r2, xg2, act, slope, rows = saved[n]
-        gg, gu, back_one, g1, do, stats = block_back(
-            grad, xhat2, r2, xhat1, r1, vecs, slope, w_up, w_down, w_out, 8 * n + 2
+        riders = []
+        if above is not None:
+            riders = [plane_scatter(above["out"], size), fsdp_scatter(above["in"], size)]
+        back_one, do, small[n], d_ffn, d_out, got = block_back(
+            grad, xhat2, r2, xhat1, r1, vecs, slope, w_up, w_down, w_out, xg2, act, rows, 16 * n + 3, riders
         )
-        small[n] = stats
-        d_up = mm_tn(xg2, gu).astype(BF16)
-        d_down = mm_tn(act, gg).astype(BF16)
-        d_out = jnp.stack([mm_tn(rows[g], g1) for g in range(4)]).astype(BF16)
-        d_up = lax.psum_scatter(d_up, "fsdp", scatter_dimension=0, tiled=True)
-        d_down = lax.psum_scatter(d_down, "fsdp", scatter_dimension=1, tiled=True)
-        d_up = lax.psum(flip_units(d_up), "ctx").astype(F32)
-        d_down = lax.psum(flip_units(d_down), "ctx").astype(F32)
-        d_out = lax.psum_scatter(d_out, "ctx", scatter_dimension=1, tiled=True)
-        d_out = lax.psum_scatter(d_out, "tp", scatter_dimension=0, tiled=True)
-        d_out = lax.psum_scatter(d_out, "fsdp", scatter_dimension=2, tiled=True)
-        d_out = lax.all_gather(d_out[0], "ctx", axis=0, tiled=True).astype(F32)
-        dqw, dkv = attend_back(qw, kv, do, o, lse, flags)
-        dq, own, grad = project_back(dqw, dkv, w_in, back_one, 8 * n + 3)
-        both = jnp.concatenate([dq, own], axis=1)
-        d_in = mm_tn(xg, both).astype(BF16)
-        d_in = lax.psum_scatter(d_in, "fsdp", scatter_dimension=0, tiled=True)
-        d_in = lax.psum(d_in, "ctx").astype(F32)
-        sums = jnp.sum(both.astype(F32), axis=0)
+        if above is not None:
+            above["out"] = low(added(got[0], (0, 1)))
+            above["in"] = low(added(got[1])).reshape(4, depth // 4, 640)
+        d_ffn = d_ffn.reshape(2, size, 2, depth // 2, 768)
+        riders = [scatter_flip(d_ffn), ctx_scatter(d_out.reshape(4, size, 4, piece, 192), axis=2)]
+        if above is not None:
+            riders += [ctx_scatter(above["ffn"]), ctx_scatter(above["in"]), ctx_gather(above["out"])]
+        dqw, dkv, got = attend_back(qw, kv, do, o, lse, flags, 16 * n + 4, riders)
+        d_ffn = got[0]
+        d_out = low(added(got[1]))
+        riders = []
+        if above is not None:
+            above["out"] = got[4]
+            riders = [ctx_gather(low(added(got[2]))), ctx_gather(low(added(got[3])))]
+        if n == 0:
+            riders += [ctx_scatter(d_ffn), plane_scatter(d_out, size)]
+        grad, d_in, sums, got = project_back(dqw, dkv, w_in, back_one, xg, 16 * n + 5, riders)
+        if above is not None:
+            done[n + 1] = (got[1], above["out"], got[0])
+        d_in = d_in.reshape(1, size, depth, 640)
         d_query_bias, _, d_value_bias = parted(sums)
         heads[n] = jnp.stack([d_query_bias, d_value_bias])
-        matrix[n] = parted(d_in) + (d_out, d_up, d_down)
-    hidden_grad = grad.astype(BF16)
+        above = {"ffn": d_ffn, "out": d_out, "in": d_in}
+    hidden_grad = low(grad)
     memory_part = lax.dot_general(
         marks, grad, (((0,), (0,)), ((), ())),
         precision=lax.Precision.HIGHEST, preferred_element_type=F32,
     )
+    ffn0 = low(added(got[-2]))
+    out0 = low(added(got[-1], (0, 1)))
     small = jnp.stack(small)
-    heads = jnp.stack(heads)
-    tp_mark = (ids == t).astype(F32)
-    flipped = sum(((c == n) * (t ^ FLIP[n]) for n in range(4)), 0)
-    unit_mark = (ids == flipped).astype(F32)
-    padded_head = (heads[:, :, None, :] * tp_mark[None, None, :, None]).reshape(layers, 2, -1)
-    padded_ffn = (small[:, 6][:, None, :] * unit_mark[None, :, None]).reshape(layers, -1)
-    totals = lax.psum((padded_head, padded_ffn, small[:, :6], memory_part), ("fsdp", "ctx", "tp"))
-    head_grad = jnp.sum(totals[0].reshape(layers, 2, 4, -1) * tp_mark[None, None, :, None], axis=2)
-    ffn_grad = jnp.sum(totals[1].reshape(layers, 4, -1) * tp_mark[None, :, None], axis=1)
-    stack = lambda k: jnp.stack([matrix[n][k] for n in range(layers)])
+    place = (ids == t).astype(F32)
+    unit = (ids == flipped_place(c, t)).astype(F32)
+    head_rows = (jnp.stack(heads)[:, :, None, :] * place[None, None, :, None]).reshape(2 * layers, 768)
+    unit_rows = (small[:, 6][:, None, :] * unit[None, :, None]).reshape(4 * layers, 768)
+    stat_rows = small[:, :6].reshape(6 * layers, 768)
+    short = 48 - 12 * layers - memory_part.shape[0]
+    sums = jnp.concatenate([stat_rows, unit_rows, head_rows, memory_part, jnp.zeros((short, 768), F32)])
+    got = carry(
+        [fsdp_scatter(d_in, size), ctx_gather(ffn0), ctx_gather(out0), ctx_scatter(sums.reshape(4, 12, 768))], 6
+    )
+    d_in = low(added(got[0])).reshape(4, depth // 4, 640)
+    ffn0, out0 = got[1:3]
+    got = carry([ctx_scatter(d_in), plane_gather(added(got[3]), size)], 7)
+    got = carry([ctx_gather(low(added(got[0]))), ctx_gather(added(got[1], (0, 1)))], 8)
+    done[0] = (got[0], out0, ffn0)
+    totals = got[1].reshape(48, 768)
+    stats = totals[: 6 * layers].reshape(layers, 6, 768)
+    at = 6 * layers
+    ffn_rows = totals[at : at + 4 * layers].reshape(layers, 4, 768)
+    ffn_grad = jnp.sum(ffn_rows * place[None, :, None], axis=1)
+    at += 4 * layers
+    head_sums = totals[at : at + 2 * layers].reshape(layers, 2, 4, 192)
+    head_grad = jnp.sum(head_sums * place[None, None, :, None], axis=2)
+    at += 2 * layers
+    memory_grad = totals[at : at + memory_part.shape[0]]
+    d_in = jnp.stack([part[0].reshape(depth, 640) for part in done]).astype(F32)
+    d_out = jnp.stack([jnp.swapaxes(part[1].reshape(depth, 192), 0, 1) for part in done]).astype(F32)
+    d_ffn = jnp.stack([part[2].reshape(2, depth, 768) for part in done]).astype(F32)
     return (
-        output, hidden_grad, totals[3],
-        stack(0), stack(1), stack(2), stack(3), stack(4), stack(5),
-        head_grad, ffn_grad, totals[2][:, 4:6], totals[2][:, 0:2], totals[2][:, 2:4],
+        output, hidden_grad, memory_grad, *parted(d_in), d_out, d_ffn[:, 0], jnp.swapaxes(d_ffn[:, 1], 1, 2),
+        head_grad, ffn_grad, stats[:, 4:6], stats[:, 0:2], stats[:, 2:4],
     )
 
 

time: 1080 us -> 683 us (0.63)
  waiting for transfers between devices: 365 us -> 0 us
  Pallas kernels: 510 us -> 616 us
  blocking collectives: 100 us -> 0 us
  matrix products: 27.5 us -> 5.63 us
  between operations: 15.7 us -> 1.94 us
  starting transfers between devices: 12.4 us -> 0 us
  other arithmetic: 14.3 us -> 26.1 us
    psum x2 -> x0, waiting for transfers between devices: 191 us -> none  [the longest x1 128 us: shards(): lax.psum((padded_head, padded_ffn, small[:, :6], memory_part), ('fsdp', '...]
    reduce_scatter x8 -> x0, waiting for transfers between devices: 149 us -> none  [the longest x2 68.7 us: shards(): d_out = lax.psum_scatter(d_out, 'tp', scatter_dimension=0, tiled=True)]
    pallas_call x12 -> x15, Pallas kernels: 510 us -> 616 us  [call(): pl.pallas_call(body, out_shape=list(out_shapes) + [rider.out for rider in...]
    all_gather x8 -> x0, blocking collectives: 100 us -> none  [the longest x2 59.6 us: shards(): w_out = lax.all_gather(w_out[None], 'tp', axis=0, tiled=True)]
    dot_general x14 -> x0, matrix products: 24.3 us -> none  [mm_tn(): lax.dot_general(left, right, (((0,), (0,)), ((), ())), preferred_element_...]
    unnamed x24 -> x0, waiting for transfers between devices: 24 us -> none
    unnamed x100 -> x66, local copies, waits for them, and re-layouts: 21.1 us -> 5.24 us
    reduce_sum x4 -> x14, other arithmetic: 4.59 us -> 18.4 us  [the longest x12 17.1 us: added(): return jnp.sum(terms.astype(F32), axis=axes)]
  transfers between devices with their start and end apart: 27 -> 0, of which waited for: 10 -> 0; matrix products, arithmetic and copies ran while one was open for 5% -> 0% of each run, Pallas kernels for 27% -> 0%
where the time goes in v2:
time: 683 us; the launch traced here: 677 us
  Pallas kernels  616 us (90%)
  local copies, waits for them, and re-layouts  27.3 us (4%)
  other arithmetic  26.1 us (4%)
    pallas_call x15, Pallas kernels, call(): pl.pallas_call(body, out_shape=list(out_shapes) + [rider.out for rider in...  616 us
    reduce_sum x12, other arithmetic, added(): return jnp.sum(terms.astype(F32), axis=axes)  17.1 us

profile of v2, /device:TPU:0, one launch (start us, length us, event | category | flops | bytes accessed | tf_op | source)
XLA Modules:
  0.0 676.9 jit_solution(14431143915362194208)
XLA Ops:
  0.7 0.9 fusion.8
  1.6 0.8 fusion.7
  2.5 0.9 multiply_reduce_fusion.3
  3.9 2.6 fusion.17
  8.4 1.0 slice_bitcast_fusion.4
  11.0 56.5 %project.2 = (bf16[4,256,768]{2,1,0:T(8,128)(2,1)}, bf16[4,256,256]{2,1,0:T(8,128)(2,1)}, bf16[4,4,256,384]{3,2,1,0:T(8,128)(2,1)}, bf16[2,384,640]{2,1,0:T(8,12...) custom-call(bf16[256,768]{1,0:T(8,128)(2,1)} %get-tuple-element.238.refs_0_, ...), custom_call_target="tpu_custom_call" | custom-call | flops 1006632960 | bytes 8388608 | tf_op jit(solution)/shard_map/project/pallas_call | solution.py:403
  68.8 1.4 slice_bitcast_fusion.2
  70.3 42.1 %attend.2 = (bf16[1024,192]{1,0:T(8,128)(2,1)}, f32[1024,128]{1,0:T(8,128)}, bf16[4,4,2,96,192]{4,3,2,1,0:T(8,128)(2,1)}, bf16[2,2,192,768]{3,2,1,0:T(8,128)(2,1)}, bf16[2,2,192,768]{3,2,1,0:T(8,128)(2,1)}) custom-call(s32[2,4]{1,0:T(2,128)} %pad_add_fusion.refs_0_, bf16[1024,256]{1,0:T(8,128)(2,1)} %bitcast.203, bf16[4096,384]{1,0:T(8,128)(2,1)} %bitcast.178, ...), custom_call_target="tpu_custom_call" | custom-call | flops 2013265920 | bytes 6291456 | tf_op jit(solution)/shard_map/attend/pallas_call | solution.py:403
  112.4 2.7 copy.58
  116.4 48.3 %block.2 = (f32[256,768]{1,0:T(8,128)}, bf16[256,768]{1,0:T(8,128)(2,1)}, f32[256,768]{1,0:T(8,128)}, f32[256,128]{1,0:T(8,128)}, f32[256,768]{1,0:T(8,128)}, /*...) custom-call(bf16[4,256,192]{2,1,0:T(8,128)(2,1)} %bitcast.205, ...), custom_call_target="tpu_custom_call" | custom-call | flops 2717908992 | bytes 16777216 | tf_op jit(solution)/shard_map/block/pallas_call | solution.py:403
  164.7 50.9 %project.3 = (bf16[4,256,768]{2,1,0:T(8,128)(2,1)}, bf16[4,256,256]{2,1,0:T(8,128)(2,1)}, bf16[4,4,256,384]{3,2,1,0:T(8,128)(2,1)}) custom-call(bf16[256,768]{1,0:T(8,128)(2,1)} %get-tuple-element.105.refs_0_, bf16[768,640]{1,0:T(8,128)(2,1)} %bitcast.200, f32[1,640]{1,0:T(1,128)} %get-tuple-element.234.refs_2_), custom_call_target="tpu_custom_call" | custom-call | flops 1006632960 | bytes 8388608 | tf_op jit(solution)/shard_map/project/pallas_call | solution.py:403
  215.6 32.4 %attend.3 = (bf16[1024,192]{1,0:T(8,128)(2,1)}, f32[1024,128]{1,0:T(8,128)}, bf16[4,4,2,96,192]{4,3,2,1,0:T(8,128)(2,1)}, bf16[2,384,768]{2,1,0:T(8,128)(2,1)}, bf16[2,384,768]{2,1,0:T(8,128)(2,1)}) custom-call(s32[2,4]{1,0:T(2,128)} %pad_add_fusion.refs_0_, bf16[1024,256]{1,0:T(8,128)(2,1)} %bitcast.206, bf16[4096,384]{1,0:T(8,128)(2,1)} %bitcast.180, ...), custom_call_target="tpu_custom_call" | custom-call | flops 2013265920 | bytes 6291456 | tf_op jit(solution)/shard_map/attend/pallas_call | solution.py:403
  248.0 2.7 copy.59
  251.4 45.0 %block.3 = (f32[256,768]{1,0:T(8,128)}, bf16[256,768]{1,0:T(8,128)(2,1)}, f32[256,768]{1,0:T(8,128)}, f32[256,128]{1,0:T(8,128)}, f32[256,768]{1,0:T(8,128)}, /*...) custom-call(bf16[4,256,192]{2,1,0:T(8,128)(2,1)} %bitcast.208, ...), custom_call_target="tpu_custom_call" | custom-call | flops 2717908992 | bytes 16777216 | tf_op jit(solution)/shard_map/block/pallas_call | solution.py:403
  296.3 0.9 convert_element_type.83.refs_0_
  297.3 42.8 %block_back.2 = (f32[256,768]{1,0:T(8,128)}, bf16[4,256,192]{2,1,0:T(8,128)(2,1)}, f32[8,768]{1,0:T(8,128)}, bf16[2,768,768]{2,1,0:T(8,128)(2,1)}, bf16[4,768,192]{2,1,0:T(8,128)(2,1)}) custom-call(f32[256,768]{1,0:T(8,128)} %convert_element_type.83.refs_0_, f32[256,768]{1,0:T(8,128)} %get-tuple-element.118.refs_1_, f32[256,128]{1,0:T(8,128)} %get-tuple-element.119.refs_2_, ...), custom_call_target="tpu_custom_call" | custom-call | flops 5435817984 | bytes 20971520 | tf_op jit(solution)/shard_map/block_back/pallas_call | solution.py:403
  340.1 50.0 %attend_back.2 = (bf16[1024,256]{1,0:T(8,128)(2,1)}, bf16[4096,384]{1,0:T(8,128)(2,1)}, bf16[4,192,768]{2,1,0:T(8,128)(2,1)}, bf16[3,4,2,96,192]{4,3,2,1,0:T(8,128)(2,1)}) custom-call(s32[2,4]{1,0:T(2,128)} %pad_add_fusion.refs_0_, bf16[1024,256]{1,0:T(8,128)(2,1)} %bitcast.207, bf16[4096,384]{1,0:T(8,128)(2,1)} %bitcast.181, bf16[1024,192]{1,0:T(8,128)(2,1)} %bitcast.210, ...), custom_call_target="tpu_custom_call" | custom-call | flops 5033164800 | bytes 12582912 | tf_op jit(solution)/shard_map/attend_back/pallas_call | solution.py:403
  390.0 52.3 %project_back.2 = (f32[256,768]{1,0:T(8,128)}, bf16[768,640]{1,0:T(8,128)(2,1)}, f32[8,640]{1,0:T(8,128)}) custom-call(bf16[4,256,256]{2,1,0:T(8,128)(2,1)} %bitcast.211, bf16[4,4,256,384]{3,2,1,0:T(8,128)(2,1)} %bitcast.182, bf16[768,640]{1,0:T(8,128)(2,1)} %bitcast.201, f32[256,768]{1,0:T(8,128)} %get-tuple-element.132.refs_3_, bf16[1024,768]{1,0:T(8,128)(2,1)} %bitcast.187), custom_call_target="tpu_custom_call" | custom-call | flops 2013265920 | bytes 12582912 | tf_op jit(solution)/shard_map/project_back/pallas_call | solution.py:403
  442.4 1.1 reduce_sum.176.refs_13_
  443.5 43.3 %block_back.3 = (f32[256,768]{1,0:T(8,128)}, bf16[4,256,192]{2,1,0:T(8,128)(2,1)}, f32[8,768]{1,0:T(8,128)}, bf16[2,768,768]{2,1,0:T(8,128)(2,1)}, bf16[4,768,19...) custom-call(f32[256,768]{1,0:T(8,128)} %get-tuple-element.134.refs_0_, ...), custom_call_target="tpu_custom_call" | custom-call | flops 5435817984 | bytes 20971520 | tf_op jit(solution)/shard_map/block_back/pallas_call | solution.py:403
  486.8 2.3 reduce_sum.177
  489.8 60.3 %attend_back.3 = (bf16[1024,256]{1,0:T(8,128)(2,1)}, bf16[4096,384]{1,0:T(8,128)(2,1)}, bf16[4,192,768]{2,1,0:T(8,128)(2,1)}, bf16[3,4,2,96,192]{4,3,2,1,0:T(8,1...) custom-call(s32[2,4]{1,0:T(2,128)} %pad_add_fusion.refs_0_, ...), custom_call_target="tpu_custom_call" | custom-call | flops 5033164800 | bytes 12582912 | tf_op jit(solution)/shard_map/attend_back/pallas_call | solution.py:403
  550.1 2.2 reduce_sum.179.refs_5_
  552.3 1.7 reduce_sum.180.refs_6_
  554.0 1.1 reduce_sum.181.refs_8_
  555.1 57.9 %project_back.3 = (f32[256,768]{1,0:T(8,128)}, bf16[768,640]{1,0:T(8,128)(2,1)}, f32[8,640]{1,0:T(8,128)}, bf16[4,192,768]{2,1,0:T(8,128)(2,1)}, bf16[4,96,640]{...) custom-call(bf16[4,256,256]{2,1,0:T(8,128)(2,1)} %bitcast.155, ...), custom_call_target="tpu_custom_call" | custom-call | flops 2013265920 | bytes 12582912 | tf_op jit(solution)/shard_map/project_back/pallas_call | solution.py:403
  613.1 2.1 convert_element_type.84
  615.2 0.9 reduce_sum.182.refs_1_
  616.1 0.7 reduce_sum.183.refs_2_
  617.1 0.7 slice_bitcast_fusion.18
  618.6 0.8 slice_bitcast_fusion.22
  619.4 0.7 slice_bitcast_fusion.23
  621.0 0.7 reshape.232.refs_3_
  621.6 13.7 %carry.3 = (bf16[2,1,384,640]{3,2,1,0:T(8,128)(2,1)}, bf16[4,192,768]{2,1,0:T(8,128)(2,1)}, bf16[4,96,192]{2,1,0:T(8,128)(2,1)}, f32[3,12,768]{2,1,0:T(8,128)}) custom-call(bf16[1,2,384,640]{3,2,1,0:T(8,128)(2,1)} %bitcast.148, bf16[192,768]{1,0:T(8,128)(2,1)} %reduce_sum.182.refs_1_, bf16[96,192]{1,0:T(8,128)(2,1)} %reduce_sum.183.refs_2_, ...), custom_call_target="tpu_custom_call" | custom-call | flops 1048576 | bytes 1048576 | tf_op jit(solution)/shard_map/carry/pallas_call | solution.py:403
  635.4 2.4 reduce_sum.184
  638.4 12.8 %carry.4 = (bf16[3,96,640]{2,1,0:T(8,128)(2,1)}, f32[4,2,12,768]{3,2,1,0:T(8,128)}) custom-call(bf16[4,96,640]{2,1,0:T(8,128)(2,1)} %bitcast.138, f32[12,768]{1,0:T(8,128)} %reduce_sum.185.refs_1_), custom_call_target="tpu_custom_call" | custom-call | flops 1048576 | bytes 1048576 | tf_op jit(solution)/shard_map/carry/pallas_call | solution.py:403
  651.2 1.7 reduce_sum.186.refs_0_
  652.9 1.6 reduce_sum.187.refs_1_
  654.6 7.6 %carry.5 = (bf16[4,96,640]{2,1,0:T(8,128)(2,1)}, f32[4,12,768]{2,1,0:T(8,128)}) custom-call(bf16[96,640]{1,0:T(8,128)(2,1)} %reduce_sum.186.refs_0_, f32[12,768]{1,0:T(8,128)} %reduce_sum.187.refs_1_), custom_call_target="tpu_custom_call" | custom-call | flops 1048576 | bytes 1048576 | tf_op jit(solution)/shard_map/carry/pallas_call | solution.py:403
  662.2 1.0 reshape.234
  664.7 0.9 pad_maximum_fusion
  665.5 0.9 pad_maximum_fusion.1
  666.4 0.9 pad_maximum_fusion.2
  667.7 0.9 maximum_convert_fusion.2
  668.9 1.8 slice_bitcast_fusion
  670.8 1.9 copy.66
  674.2 0.8 slice.281
  675.6 0.7 copy.81
  (145 shorter events, 14.6 us)
Async XLA Ops:
  0.6 3.3 copy-start
  0.7 5.8 slice-start
  0.7 6.0 slice-start.1
  3.9 3.0 slice-start.2
  3.9 3.1 slice-start.4
  6.5 0.9 slice-start.3
  6.5 1.1 slice-start.5
  8.4 1.1 copy-start.26
  8.4 1.8 copy-start.16
  11.0 56.6 %copy-start.5 = (bf16[2,768,384]{2,1,0:T(8,128)(2,1)S(1)}, bf16[2,768,384]{2,1,0:T(8,128)(2,1)}, u32[]{:S(2)}) copy-start(bf16[2,768,384]{2,1,0:T(8,128)(2,1)} %param.26) | copy-start | bytes 3538948
  67.6 1.3 copy-start.8
  112.4 2.7 copy-start.25
  112.4 3.3 copy-start.22
  112.4 3.3 copy-start.23
  112.4 3.3 copy-start.24
  251.4 45.0 %copy-start.15 = (bf16[256,768]{1,0:T(8,128)(2,1)S(1)}, bf16[256,768]{1,0:T(8,128)(2,1)}, u32[]{:S(2)}) copy-start(bf16[256,768]{1,0:T(8,128)(2,1)} %param.17) | copy-start | bytes 1179652
  390.0 52.3 %copy-start.7 = (bf16[3,4,2,96,192]{4,3,2,1,0:T(8,128)(2,1)S(1)}, bf16[3,4,2,96,192]{4,3,2,1,0:T(8,128)(2,1)}, u32[]{:S(2)}) copy-start(bf16[3,4,2,96,192]{4,3,2,1,0:T(8,128)(2,1)} %get-tuple-element.143) | copy-start | bytes 2654212
  486.8 2.3 copy-start.13
  550.1 3.9 copy-start.6
  613.1 2.1 copy-start.9
  613.1 3.0 copy-start.14
  613.1 3.7 copy-start.20
  613.1 3.7 copy-start.21
  613.1 7.3 %copy-start.2 = (f32[256,768]{1,0:T(8,128)S(1)}, f32[256,768]{1,0:T(8,128)}, u32[]{:S(2)}) copy-start(f32[256,768]{1,0:T(8,128)} %get-tuple-element.161) | copy-start | bytes 2359300
  613.1 7.3 %copy-start.27 = (s32[1,1,20]{2,1,0:T(1,128)S(1)}, s32[1,1,20]{2,1,0:T(1,128)}, u32[]{:S(2)}) copy-start(s32[1,1,20]{2,1,0:T(1,128)} %param.18) | copy-start | bytes 244
  635.4 2.4 copy-start.19
  635.4 28.5 %copy-start.10 = (bf16[4,96,640]{2,1,0:T(8,128)(2,1)S(1)}, bf16[4,96,640]{2,1,0:T(8,128)(2,1)}, u32[]{:S(2)}) copy-start(bf16[4,96,640]{2,1,0:T(8,128)(2,1)} %get-tuple-element.175) | copy-start | bytes 1474564
  662.2 1.9 copy-start.11
  666.4 0.9 copy-start.17
  666.4 1.2 copy-start.18
  666.4 2.2 copy-start.3
  666.4 2.2 copy-start.4
  670.8 4.9 copy-start.12
  670.8 5.6 copy-start.1

commit v3 on v2

--- a/solution.py
+++ b/solution.py
@@ -65,6 +65,11 @@
 class Rider:
     def __init__(self, array, out, make, scratch, chunks=0):
         self.array, self.out, self.make, self.scratch, self.chunks = array, out, make, scratch, chunks
+        self.late = False
+
+    def after(self):
+        self.late = True
+        return self
 
 
 class Copies:
@@ -334,16 +339,37 @@
 
 
 class Riding:
-    def __init__(self, riders, sources, targets, scratch):
+    def __init__(self, riders, sources, targets, scratch, fetches, results, puts):
+        self.fetches, self.results, self.puts = fetches, results, puts
+        self.gone = [False] * len(puts)
         place = tuple(lax.axis_index(axis) for axis in ("fsdp", "ctx", "tp"))
         scratch = list(scratch)
-        self.rides, self.hops = [], []
+        self.rides, self.hops, self.late = [], [], []
         self.turned = False
         for rider, source, target in zip(riders, sources, targets):
             own = [scratch.pop(0) for _ in rider.scratch]
             ride = rider.make(source, target, place, own)
             self.rides.append(ride)
+            if rider.late:
+                self.late.append(ride)
             self.hops += [(ride, chunk) for chunk in range(rider.chunks)]
+
+    def ready(self):
+        for fetch in self.fetches:
+            fetch.wait()
+
+    def put(self, *refs):
+        for ref in refs:
+            slot = [ref is result for result in self.results].index(True)
+            self.gone[slot] = True
+            self.puts[slot].start()
+
+    def close(self):
+        for slot, put in enumerate(self.puts):
+            if not self.gone[slot]:
+                put.start()
+        for put in self.puts:
+            put.wait()
 
     def greet(self, barrier):
         count = 0
@@ -355,16 +381,23 @@
 
     def start(self):
         for ride in self.rides:
-            ride.start()
+            if ride not in self.late:
+                ride.start()
+
+    def one_hop(self, at):
+        ride, chunk = self.hops[at]
+        ride.hop(chunk)
+        if at == len(self.hops) - 1:
+            for ride in self.late:
+                ride.start()
 
     def hop(self, number):
-        if isinstance(number, int):
-            if number < len(self.hops):
-                ride, chunk = self.hops[number]
-                ride.hop(chunk)
-            return
-        for at, (ride, chunk) in enumerate(self.hops):
-            pl.when(number == at)(functools.partial(ride.hop, chunk))
+        for at in range(len(self.hops)):
+            pl.when(number == at)(functools.partial(self.one_hop, at))
+
+    def turn_at(self, number, at):
+        if self.rides:
+            pl.when(number == at)(self.turn)
 
     def turn(self):
         self.turned = True
@@ -385,31 +418,41 @@
         pl.when(when)(action)
 
 
-def call(kernel, operands, out_shapes, scratch, collective_id, name, cost, riders=(), smem=(), any_in=(), any_out=()):
+def call(kernel, operands, out_shapes, scratch, collective_id, name, cost, riders=(), smem=()):
     n_in, n_out, n_scratch, n_ride = len(operands), len(out_shapes), len(scratch), len(riders)
+    large = [i for i in range(n_in) if i not in smem]
 
     def body(*refs):
         refs = list(refs)
         take = lambda n: [refs.pop(0) for _ in range(n)]
-        ins, sources, outs, targets, own = take(n_in), take(n_ride), take(n_out), take(n_ride), take(n_scratch)
-        kernel(Riding(riders, sources, targets, refs), *ins, *outs, *own)
-
-    params = dict(vmem_limit_bytes=56 * 1024 * 1024)
+        ins, sources, outs, targets = take(n_in), take(n_ride), take(n_out), take(n_ride)
+        near_ins, near_outs, (in_sem, out_sem), own = take(len(large)), take(n_out), take(2), take(n_scratch)
+        fetches = [
+            pltpu.make_async_copy(ins[i], near, in_sem.at[slot]) for slot, (i, near) in enumerate(zip(large, near_ins))
+        ]
+        for fetch in fetches:
+            fetch.start()
+        for i, near in zip(large, near_ins):
+            ins[i] = near
+        puts = [pltpu.make_async_copy(near, far, out_sem.at[i]) for i, (near, far) in enumerate(zip(near_outs, outs))]
+        ride = Riding(riders, sources, targets, refs, fetches, near_outs, puts)
+        kernel(ride, *ins, *near_outs, *own)
+        ride.close()
+
+    params = dict(vmem_limit_bytes=60 * 1024 * 1024)
     if collective_id is not None:
         params.update(collective_id=collective_id, has_side_effects=True)
     extra = [item for rider in riders for item in rider.scratch]
     anywhere = pl.BlockSpec(memory_space=pl.ANY)
-    whole = pl.BlockSpec(memory_space=pltpu.VMEM)
+    near = [pltpu.VMEM(operands[i].shape, operands[i].dtype) for i in large]
+    near += [pltpu.VMEM(out.shape, out.dtype) for out in out_shapes]
     results = pl.pallas_call(
         body,
         out_shape=list(out_shapes) + [rider.out for rider in riders],
-        in_specs=[
-            pl.BlockSpec(memory_space=pltpu.SMEM) if i in smem else anywhere if i in any_in else whole
-            for i in range(n_in)
-        ]
+        in_specs=[pl.BlockSpec(memory_space=pltpu.SMEM) if i in smem else anywhere for i in range(n_in)]
         + [anywhere] * n_ride,
-        out_specs=[anywhere if i in any_out else whole for i in range(n_out)] + [anywhere] * n_ride,
-        scratch_shapes=list(scratch) + extra,
+        out_specs=[anywhere] * (n_out + n_ride),
+        scratch_shapes=near + [dma(max(len(large), 1)), dma(max(n_out, 1))] + list(scratch) + extra,
         compiler_params=pltpu.CompilerParams(**params),
         cost_estimate=pl.CostEstimate(flops=cost[0], bytes_accessed=cost[1], transcendentals=cost[2]),
         name=name,
@@ -530,12 +573,29 @@
     return copies_rider(parts, sds(*parts.shape, dtype=parts.dtype), 4 * size - 1, parts.shape[2:], make)
 
 
+def all_gather(own, size):
+    others = [(kt, kc, kf) for kt in (2, 3, 1, 0) for kc in (2, 3, 1, 0) for kf in range(size)][:-size] + [
+        (0, 0, kf) for kf in range(1, size)
+    ]
+
+    def make(source, target, f, c, t):
+        steps = [
+            (
+                {"fsdp": (f + kf) % size, "ctx": (c + kc) % 4, "tp": (t + kt) % 4},
+                {"fsdp": (f + size - kf) % size, "ctx": (c + 4 - kc) % 4, "tp": (t + 4 - kt) % 4},
+                source, target.at[c, t, f], None, 1,
+            )
+            for kt, kc, kf in others
+        ]
+        return steps, (source, target.at[c, t, f], None)
+
+    return copies_rider(own, sds(4, 4, size, *own.shape, dtype=own.dtype), 16 * size - 1, own.shape, make)
+
+
 def carry_kernel(ride):
     barrier = pltpu.get_barrier_semaphore()
     pl.semaphore_wait(barrier, ride.greet(barrier))
     ride.start()
-    for number in range(len(ride.hops)):
-        ride.hop(number)
     ride.finish()
 
 
@@ -574,7 +634,9 @@
         for k in range(1, size):
             signal(barrier, {"fsdp": (f + size - k) % size})
     ends = (t // 3) + (3 - t) // 3
-    pl.semaphore_wait(barrier, 5 - ends + ride.greet(barrier) + (size - 1 if fetch else 0))
+    count = 5 - ends + ride.greet(barrier) + (size - 1 if fetch else 0)
+    ride.ready()
+    pl.semaphore_wait(barrier, count)
 
     def right(src, chunk, step):
         return rcopy(src, xg_ref.at[chunk], x_right.at[step], x_recv.at[chunk], {"tp": t + 1})
@@ -661,6 +723,8 @@
             before = ordered(t, step - 1)
             across(before).wait_recv()
             onward(before).start()
+    ride.put(xg_ref)
+    ride.turn()
     last = ordered(t, 3)
     across(last).wait_recv()
     onward(last).start()
@@ -736,21 +800,27 @@
 
 
 Q_TILE = 256
+FAR = 1e30
 K_TILE = 256
 
 
 def open_up(ride):
     if ride.rides:
         barrier = pltpu.get_barrier_semaphore()
-        pl.semaphore_wait(barrier, ride.greet(barrier))
+        count = ride.greet(barrier)
+        pl.semaphore_wait(barrier, count)
         ride.start()
-
-
-def attend_kernel(ride, flag_ref, qw_ref, kv_ref, o_ref, lse_ref, qm_ref, m_ref, l_ref, acc_ref):
+    ride.ready()
+
+
+def attend_kernel(ride, flag_ref, qw_ref, kv_ref, o_ref, lse_ref, qm_ref, m_ref, acc_ref, vo_ref):
     c = lax.axis_index("ctx")
     open_up(ride)
     low = lax.broadcasted_iota(jnp.int32, (Q_TILE, 128), 1) < 64
     per_half = 512 // Q_TILE
+    for side, at in enumerate((128, 256)):
+        vo_ref[side, :, 0:128] = kv_ref[:, at : at + 128]
+        vo_ref[side, :, 128:256] = jnp.ones((4096, 128), BF16)
 
     @pl.loop(0, 1024 // Q_TILE)
     def _(tile):
@@ -762,36 +832,34 @@
         qm_ref[1] = jnp.where(low, jnp.zeros_like(pair), pair)
         qm_ref[2] = qw_ref[rows, 128:256]
         m_ref[...] = jnp.full_like(m_ref, MASKED)
-        l_ref[...] = jnp.zeros_like(l_ref)
         acc_ref[...] = jnp.zeros_like(acc_ref)
 
         @pl.loop(0, segment + 1)
         def _(block):
             seen = flag_ref[half, block] > 0
+            penalty = jnp.where(seen, 0.0, FAR)
             keys = pl.ds(pl.multiple_of(block * 1024, 1024), 1024)
             for head in range(3):
                 k_at = 0 if head < 2 else 128
-                v_at = 256 if head < 2 else 128
                 scores = mm_nt(qm_ref[head], kv_ref[keys, k_at : k_at + 128])
-                scores = jnp.where(seen, scores, MASKED)
                 old = m_ref[head]
-                new = jnp.maximum(old, jnp.max(scores, axis=-1, keepdims=True))
-                probs = jnp.exp(scores - new)
+                most = jnp.max(scores, axis=-1, keepdims=True)
+                new = jnp.maximum(old, jnp.where(seen, most, MASKED))
+                probs = jnp.exp(scores - (new + penalty)).astype(BF16)
                 keep = jnp.exp(old - new)
                 m_ref[head] = new
-                l_ref[head] = l_ref[head] * keep + jnp.sum(probs, axis=-1, keepdims=True)
-                acc_ref[head] = acc_ref[head] * keep + mm(
-                    probs.astype(BF16), kv_ref[keys, v_at : v_at + 128]
-                )
-
-        first = acc_ref[0] / l_ref[0]
-        second = acc_ref[1] / l_ref[1]
+                acc_ref[head] = acc_ref[head] * keep + mm(probs, vo_ref[1 if head < 2 else 0, keys])
+
+        whole = [acc_ref[head][:, 128:256] for head in range(3)]
+        first = acc_ref[0][:, 0:128] / whole[0]
+        second = acc_ref[1][:, 0:128] / whole[1]
         o_ref[rows, 0:128] = jnp.where(low, first, second).astype(BF16)
-        o_ref[rows, 128:192] = (acc_ref[2] / l_ref[2])[:, :64].astype(BF16)
+        o_ref[rows, 128:192] = (acc_ref[2][:, 0:128] / whole[2])[:, :64].astype(BF16)
         lane = lax.broadcasted_iota(jnp.int32, (Q_TILE, 128), 1)
-        totals = [m_ref[head] + jnp.log(l_ref[head]) for head in range(3)]
+        totals = [m_ref[head] + jnp.log(whole[head]) for head in range(3)]
         lse_ref[rows, :] = jnp.where(lane == 0, totals[0], jnp.where(lane == 1, totals[1], totals[2]))
         ride.hop(tile)
+        ride.turn_at(tile, 2)
 
     ride.finish()
 
@@ -801,8 +869,8 @@
     scratch = [
         pltpu.VMEM((3, Q_TILE, 128), BF16),
         pltpu.VMEM((3, Q_TILE, 1), F32),
-        pltpu.VMEM((3, Q_TILE, 1), F32),
-        pltpu.VMEM((3, Q_TILE, 128), F32),
+        pltpu.VMEM((3, Q_TILE, 256), F32),
+        pltpu.VMEM((2, 4096, 256), BF16),
     ]
     cost = (5 * 512 * 1024 * 64 * 4 * 3, 6 << 20, 5 * 512 * 1024 * 3)
     operands = (flags, qw, kv.reshape(4096, 384))
@@ -858,7 +926,7 @@
 
                 @pl.when(block <= segment)
                 def _():
-                    seen = flag_ref[half, block] > 0
+                    penalty = jnp.where(flag_ref[half, block] > 0, 0.0, FAR)
                     rows = pl.ds(half * 512, 512)
                     for head in range(3):
                         k_at = 0 if head < 2 else 128
@@ -866,8 +934,7 @@
                         query = qm_ref[head, rows]
                         grads = dm_ref[head, rows]
                         scores = mm_nt(kv_ref[keys, k_at : k_at + 128], query)
-                        scores = jnp.where(seen, scores, MASKED)
-                        probs = jnp.exp(scores - row_ref[head : head + 1, rows])
+                        probs = jnp.exp(scores - (row_ref[head : head + 1, rows] + penalty))
                         grad_probs = mm_nt(kv_ref[keys, v_at : v_at + 128], grads)
                         grad_scores = (probs * (grad_probs - row_ref[8 + head : 9 + head, rows])).astype(BF16)
                         key_ref[:, v_at : v_at + 128] += mm(probs.astype(BF16), grads)
@@ -878,6 +945,7 @@
             dkv_ref[keys, :] = key_ref[...].astype(BF16)
 
         ride.hop(block)
+        ride.turn_at(block, 0)
 
     dq_ref[...] = (acc_ref[...].astype(BF16).astype(F32) * 0.125).astype(BF16)
     ride.finish()
@@ -899,10 +967,71 @@
     return res[0], res[1].reshape(4, 1024, 384), ridden
 
 
+PIECE = 128
+
+
+def exchange(c, ref, feed, mine_ref, part_ref, send_ref, got_ref, a_send, a_recv, s_send, s_recv, meanwhile):
+    mate, across, far = mate_of(c), across_of(c), 3 - c
+    pieces = (pl.ds(0, PIECE), pl.ds(PIECE, PIECE))
+
+    def gather(slot, index, p, device):
+        part = ref.at[slot, pieces[p]]
+        return rcopy(part, part, a_send.at[index, p], a_recv.at[index, p], {"ctx": device})
+
+    def scatter(index, p, device):
+        source, target = send_ref.at[index, pieces[p]], got_ref.at[index, pieces[p]]
+        return rcopy(source, target, s_send.at[index, p], s_recv.at[index, p], {"ctx": device})
+
+    for p in range(2):
+        gather(c, 1, p, across).start()
+    for p in range(2):
+        gather(c, 0, p, mate).start()
+    mine_ref[...] += feed(c, pl.ds(0, 2 * PIECE))
+    for p in range(2):
+        gather(mate, 0, p, mate).wait_recv()
+    send_ref[0] = feed(mate, pl.ds(0, 2 * PIECE)).astype(BF16)
+    for p in range(2):
+        scatter(0, p, mate).start()
+
+    def take_across(p):
+        gather(across, 1, p, across).wait_recv()
+        gather(across, 2, p, mate).start()
+        part_ref[pieces[p]] = feed(across, pieces[p])
+
+    def take_far(p):
+        gather(far, 2, p, mate).wait_recv()
+        send_ref[1, pieces[p]] = feed(far, pieces[p]).astype(BF16)
+        scatter(1, p, mate).start()
+
+    def join(p):
+        scatter(1, p, mate).wait_recv()
+        send_ref[2, pieces[p]] = (part_ref[pieces[p]] + got_ref[1, pieces[p]].astype(F32)).astype(BF16)
+        scatter(2, p, across).start()
+
+    take_across(0)
+    take_far(0)
+    take_across(1)
+    join(0)
+    take_far(1)
+    join(1)
+    meanwhile()
+    for p in range(2):
+        scatter(0, p, mate).wait_recv()
+        scatter(2, p, across).wait_recv()
+
+    def settle():
+        for p in range(2):
+            for index in range(3):
+                gather(c, index, p, mate).wait_send()
+                scatter(index, p, mate).wait_send()
+
+    return mine_ref[...] + got_ref[0].astype(F32) + got_ref[2].astype(F32), settle
+
+
 def block_kernel(
     ride, o_ref, wo_ref, w1_ref, w2_ref, b1_ref, vec_ref, stream_ref,
-    out_ref, low_ref, xhat1_ref, r1_ref, xhat2_ref, r2_ref, xg_ref, act_ref, slope_ref, rows_ref,
-    mine_ref, send_ref, got_ref, o_send, o_recv, a_send, a_recv, s_send, s_recv,
+    out_ref, low_ref, xhat1_ref, r1_ref, xhat2_ref, r2_ref, xg_ref, act_ref, slope_ref, rows_ref, down_ref,
+    w_send, w_recv, mine_ref, part_ref, send_ref, got_ref, o_send, o_recv, a_send, a_recv, s_send, s_recv,
 ):
     c = lax.axis_index("ctx")
     t = lax.axis_index("tp")
@@ -919,7 +1048,16 @@
 
     signal(barrier, {"ctx": mate_of(c)})
     signal(barrier, {"ctx": across_of(c)})
-    pl.semaphore_wait(barrier, 5 + t // 2 + ride.greet(barrier))
+    f, size = lax.axis_index("fsdp"), lax.axis_size("fsdp")
+    for k in range(1, size):
+        signal(barrier, {"fsdp": (f + size - k) % size})
+    count = 5 + t // 2 + size - 1 + ride.greet(barrier)
+    ride.ready()
+    pl.semaphore_wait(barrier, count)
+
+    def weight(k):
+        device = {"fsdp": (f + k) % size}
+        return rcopy(w2_ref, down_ref.at[f], w_send.at[k - 1], w_recv.at[k - 1], device)
 
     def give(quarter):
         device = {"tp": quarter} if quarter < 2 else {"ctx": 3 - c, "tp": quarter}
@@ -941,6 +1079,9 @@
 
         else:
             give(quarter).start()
+    for k in range(1, size):
+        weight(k).start()
+    down_ref[f] = w2_ref[...]
     branch = stream_ref[...] + vec_ref[0:1]
     for group in range(4):
 
@@ -955,48 +1096,31 @@
     r1_ref[...] = jnp.broadcast_to(scale, r1_ref.shape)
     normed = xhat * vec_ref[2:3] + vec_ref[3:4]
     xg_ref[c] = normed.astype(BF16)
-    mate, across, far = mate_of(c), across_of(c), 3 - c
-
-    def gather(slot, index, device):
-        return rcopy(xg_ref.at[slot], xg_ref.at[slot], a_send.at[index], a_recv.at[index], {"ctx": device})
-
-    gather(c, 1, across).start()
-    gather(c, 0, mate).start()
-
-    def feed(segment):
-        up = mm(xg_ref[segment], w1_ref[...]) + b1_ref[...]
+    mine_ref[...] = normed + vec_ref[1:2]
+    for k in range(1, size):
+        weight(k).wait_recv()
+
+    def feed(segment, rows):
+        up = mm(xg_ref[segment, rows], w1_ref[...]) + b1_ref[...]
         act, slope = gelu_both(up)
-        act_ref[segment] = act
-        slope_ref[segment] = slope
-        return mm_nt(act, w2_ref[...])
-
-    mine_ref[...] = feed(c) + normed + vec_ref[1:2]
-    gather(mate, 0, mate).wait_recv()
-
-    def scatter(index, device):
-        return rcopy(send_ref.at[index], got_ref.at[index], s_send.at[index], s_recv.at[index], {"ctx": device})
-
-    send_ref[0] = feed(mate).astype(BF16)
-    scatter(0, mate).start()
-    gather(across, 1, across).wait_recv()
-    gather(across, 2, mate).start()
-    own_across = feed(across)
-    gather(far, 2, mate).wait_recv()
-    send_ref[1] = feed(far).astype(BF16)
-    scatter(1, mate).start()
-    scatter(1, mate).wait_recv()
-    send_ref[2] = (own_across + got_ref[1].astype(F32)).astype(BF16)
-    scatter(2, across).start()
-    ride.turn()
-    scatter(0, mate).wait_recv()
-    scatter(2, across).wait_recv()
-    summed = mine_ref[...] + got_ref[0].astype(F32) + got_ref[2].astype(F32)
+        act_ref[segment, rows] = act
+        slope_ref[segment, rows] = slope
+        return mm_nt(act, down_ref[...].reshape(768, 768))
+
+    def meanwhile():
+        ride.turn()
+        ride.put(xhat1_ref, r1_ref, xg_ref, act_ref, slope_ref, rows_ref, down_ref)
+
+    summed, settle = exchange(
+        c, xg_ref, feed, mine_ref, part_ref, send_ref, got_ref, a_send, a_recv, s_send, s_recv, meanwhile
+    )
     xhat, scale = norm_stats(summed)
     xhat2_ref[...] = xhat
     r2_ref[...] = jnp.broadcast_to(scale, r2_ref.shape)
     out = xhat * vec_ref[4:5] + vec_ref[5:6]
     out_ref[...] = out
     low_ref[...] = out.astype(BF16)
+    ride.put(out_ref, low_ref, xhat2_ref, r2_ref)
     for quarter in range(4):
         if quarter < 2:
 
@@ -1006,37 +1130,38 @@
 
         else:
             give(quarter).wait_send()
-    gather(c, 0, mate).wait_send()
-    gather(c, 1, across).wait_send()
-    gather(across, 2, mate).wait_send()
-    for index in range(3):
-        scatter(index, mate).wait_send()
+    for k in range(1, size):
+        weight(k).wait_send()
+    settle()
     ride.finish()
 
 
 def block(o, wo, w1, w2, b1, vecs, stream, cid, riders=()):
+    size = lax.axis_size("fsdp")
     f = functools.partial(sds, dtype=F32)
     outs = [
         f(256, 768), sds(256, 768), f(256, 768), f(256, 128), f(256, 768), f(256, 128),
-        sds(4, 256, 768), sds(4, 256, 768), sds(4, 256, 768), sds(4, 256, 192),
+        sds(4, 256, 768), sds(4, 256, 768), sds(4, 256, 768), sds(4, 256, 192), sds(size, *w2.shape),
     ]
     scratch = [
+        dma(size - 1), dma(size - 1),
+        pltpu.VMEM((256, 768), F32),
         pltpu.VMEM((256, 768), F32),
         pltpu.VMEM((3, 256, 768), BF16),
         pltpu.VMEM((3, 256, 768), BF16),
-        dma(4), dma(4), dma(3), dma(3), dma(3), dma(3),
+        dma(4), dma(4), dma(3, 2), dma(3, 2), dma(3, 2), dma(3, 2),
     ]
     cost = (2 * 256 * 768 * 768 + 4 * 1024 * 768 * 768, 16 << 20, 1 << 20)
     operands = (o.reshape(4, 256, 192), wo, w1, w2, b1, vecs, stream)
     res, ridden = call(block_kernel, operands, outs, scratch, cid, "block", cost, riders)
     flat = lambda a: a.reshape(1024, 768)
-    return tuple(res[:6]) + (flat(res[6]), flat(res[7]), flat(res[8]), res[9], ridden)
+    return tuple(res[:6]) + (flat(res[6]), flat(res[7]), flat(res[8]), res[9], res[10].reshape(768, 768), ridden)
 
 
 def block_back_kernel(
     ride, grad_ref, xhat2_ref, r2_ref, xhat1_ref, r1_ref, vec_ref, slope_ref, w1_ref, w2_ref, wo_ref,
-    xg_ref, act_ref, rows_ref, back_ref, do_ref, stat_ref, dffn_ref, dout_ref,
-    gg_ref, gu_ref, mine_ref, send_ref, got_ref, dsend_ref, d_send, d_recv, a_send, a_recv, s_send, s_recv,
+    xg_ref, act_ref, rows_ref, back_ref, do_ref, stat_ref, dup_ref, ddown_ref, dout_ref,
+    w_send, w_recv, term_ref, all_up_ref, gg_ref, gu_ref, mine_ref, part_ref, send_ref, got_ref, dsend_ref, d_send, d_recv, a_send, a_recv, s_send, s_recv,
 ):
     c = lax.axis_index("ctx")
     t = lax.axis_index("tp")
@@ -1052,8 +1177,13 @@
             signal(barrier, {"ctx": 3 - c, "tp": place})
     signal(barrier, {"ctx": mate_of(c)})
     signal(barrier, {"ctx": across_of(c)})
-    pl.semaphore_wait(barrier, 5 + t // 2 + ride.greet(barrier))
-    mate, across, far = mate_of(c), across_of(c), 3 - c
+    f, size = lax.axis_index("fsdp"), lax.axis_size("fsdp")
+    depth = dup_ref.shape[0]
+    for k in range(1, size):
+        signal(barrier, {"fsdp": (f + size - k) % size})
+    count = 5 + t // 2 + size - 1 + ride.greet(barrier)
+    ride.ready()
+    pl.semaphore_wait(barrier, count)
 
     def row(values):
         return jnp.sum(values, axis=0, keepdims=True)
@@ -1062,58 +1192,50 @@
     back_two = norm_back(grad, xhat2_ref[...], r2_ref[:, 0:1], vec_ref[4:5])
     g2 = back_two.astype(BF16)
     gg_ref[c] = g2
-
-    def gather(slot, index, device):
-        return rcopy(gg_ref.at[slot], gg_ref.at[slot], a_send.at[index], a_recv.at[index], {"ctx": device})
-
-    gather(c, 1, across).start()
-    gather(c, 0, mate).start()
+    mine_ref[...] = back_two
     ride.start()
     stat_ref[1:2] = row(grad * xhat2_ref[...])
     stat_ref[3:4] = row(grad)
     stat_ref[5:6] = row(g2.astype(F32))
-    stat_ref[7:8] = jnp.zeros((1, 768), F32)
-
-    def feed(segment):
-        gu = (mm(gg_ref[segment], w2_ref[...]) * slope_ref[segment].astype(F32)).astype(BF16)
-        gu_ref[segment] = gu
-        return mm_nt(gu, w1_ref[...]), row(gu.astype(F32))
-
-    part, bias = feed(c)
-    mine_ref[...] = part + back_two
-    gather(mate, 0, mate).wait_recv()
-
-    def scatter(index, device):
-        return rcopy(send_ref.at[index], got_ref.at[index], s_send.at[index], s_recv.at[index], {"ctx": device})
-
-    part, more = feed(mate)
-    bias += more
-    send_ref[0] = part.astype(BF16)
-    scatter(0, mate).start()
-    gather(across, 1, across).wait_recv()
-    gather(across, 2, mate).start()
-    own_across, more = feed(across)
-    bias += more
-    gather(far, 2, mate).wait_recv()
-    part, more = feed(far)
-    bias += more
-    stat_ref[6:7] = bias
-    send_ref[1] = part.astype(BF16)
-    scatter(1, mate).start()
-    scatter(1, mate).wait_recv()
-    send_ref[2] = (own_across + got_ref[1].astype(F32)).astype(BF16)
-    scatter(2, across).start()
+    stat_ref[6:8] = jnp.zeros((2, 768), F32)
+
+    def feed(segment, rows):
+        gu = (mm(gg_ref[segment, rows], w2_ref[...]) * slope_ref[segment, rows].astype(F32)).astype(BF16)
+        gu_ref[segment, rows] = gu
+        stat_ref[6:7] += row(gu.astype(F32))
+        return mm_nt(gu, w1_ref[...])
+
     tall = lambda ref: ref[...].reshape(1024, 768)
 
-    @pl.loop(0, 3)
-    def _(tile):
-        cols = pl.ds(pl.multiple_of(tile * 256, 256), 256)
-        dffn_ref[0, cols] = mm_tn(xg_ref[:, cols], tall(gu_ref)).astype(BF16)
-        dffn_ref[1, cols] = mm_tn(gg_ref[:, :, cols].reshape(1024, 256), act_ref[...]).astype(BF16)
-
-    scatter(0, mate).wait_recv()
-    scatter(2, across).wait_recv()
-    grad_normed = mine_ref[...] + got_ref[0].astype(F32) + got_ref[2].astype(F32)
+    def slice_of(place):
+        return pl.ds(pl.multiple_of(place * depth, depth), depth)
+
+    def term(k):
+        to = (f + k) % size
+        return rcopy(
+            all_up_ref.at[slice_of(to)], term_ref.at[k - 1], w_send.at[k - 1], w_recv.at[k - 1], {"fsdp": to}
+        )
+
+    def meanwhile():
+        @pl.loop(0, 3)
+        def _(tile):
+            cols = pl.ds(pl.multiple_of(tile * 256, 256), 256)
+            all_up_ref[cols] = mm_tn(xg_ref[:, cols], tall(gu_ref)).astype(BF16)
+
+        for k in range(1, size):
+            term(k).start()
+
+        @pl.loop(0, 3)
+        def _(tile):
+            cols = pl.ds(pl.multiple_of(tile * 256, 256), 256)
+            ddown_ref[cols] = mm_tn(gg_ref[:, :, cols].reshape(1024, 256), act_ref[...]).astype(BF16)
+
+        ride.put(ddown_ref)
+        ride.turn()
+
+    grad_normed, settle = exchange(
+        c, gg_ref, feed, mine_ref, part_ref, send_ref, got_ref, a_send, a_recv, s_send, s_recv, meanwhile
+    )
     back_one = norm_back(grad_normed, xhat1_ref[...], r1_ref[:, 0:1], vec_ref[2:3])
     back_ref[...] = back_one
     g1 = back_one.astype(BF16)
@@ -1144,6 +1266,13 @@
     stat_ref[4:5] = row(g1.astype(F32))
     for group in range(4):
         dout_ref[group] = mm_tn(g1, rows_ref[group]).astype(BF16)
+    ride.put(back_ref, stat_ref, dout_ref)
+    total = all_up_ref[slice_of(f)].astype(F32)
+    for k in range(1, size):
+        term(k).wait_recv()
+        total += term_ref[k - 1].astype(F32)
+    dup_ref[...] = total.astype(BF16)
+    ride.put(dup_ref)
     for quarter in range(4):
 
         def taken():
@@ -1159,36 +1288,40 @@
         def _():
             give_near(group).wait_send()
 
-    gather(c, 0, mate).wait_send()
-    gather(c, 1, across).wait_send()
-    gather(across, 2, mate).wait_send()
-    for index in range(3):
-        scatter(index, mate).wait_send()
+    for k in range(1, size):
+        term(k).wait_send()
+    settle()
     ride.finish()
 
 
 def block_back(grad, xhat2, r2, xhat1, r1, vecs, slope, w1, w2, wo, xg, act, rows, cid, riders=()):
     f = functools.partial(sds, dtype=F32)
-    outs = [f(256, 768), sds(4, 256, 192), f(8, 768), sds(2, 768, 768), sds(4, 768, 192)]
+    size = lax.axis_size("fsdp")
+    depth = 768 // size
+    outs = [
+        f(256, 768), sds(4, 256, 192), f(8, 768), sds(depth, 768), sds(768, 768), sds(4, 768, 192),
+    ]
     scratch = [
+        dma(size - 1), dma(size - 1), pltpu.VMEM((size - 1, depth, 768), BF16), pltpu.VMEM((768, 768), BF16),
         pltpu.VMEM((4, 256, 768), BF16),
         pltpu.VMEM((4, 256, 768), BF16),
+        pltpu.VMEM((256, 768), F32),
         pltpu.VMEM((256, 768), F32),
         pltpu.VMEM((3, 256, 768), BF16),
         pltpu.VMEM((3, 256, 768), BF16),
         pltpu.VMEM((4, 256, 192), BF16),
-        dma(4), dma(4), dma(3), dma(3), dma(3), dma(3),
+        dma(4), dma(4), dma(3, 2), dma(3, 2), dma(3, 2), dma(3, 2),
     ]
     cost = (4 * 256 * 768 * 768 + 8 * 1024 * 768 * 768, 20 << 20, 1 << 10)
     operands = (grad, xhat2, r2, xhat1, r1, vecs, slope.reshape(4, 256, 768), w1, w2, wo, xg, act, rows)
     res, ridden = call(block_back_kernel, operands, outs, scratch, cid, "block_back", cost, riders)
-    back, do, stats, d_ffn, d_out = res
-    return back, do.reshape(1024, 192), stats, d_ffn, d_out, ridden
+    back, do, stats, d_up, d_down, d_out = res
+    return back, do.reshape(1024, 192), stats, d_up, d_down, d_out, ridden
 
 
 def project_back_kernel(
-    ride, dqw_ref, dkv_ref, w_ref, back_ref, xg_ref, grad_ref, din_ref, sum_out_ref,
-    dq_ref, own_ref, part_ref, near_ref, join_ref, sum_ref, far_ref, pass_ref, take_ref,
+    ride, dqw_ref, dkv_ref, w_ref, back_ref, xg_ref, mark_ref, grad_ref, low_ref, din_ref, sum_out_ref, mem_ref,
+    w_send, w_recv, term_ref, all_in_ref, dq_ref, own_ref, part_ref, near_ref, join_ref, sum_ref, far_ref, pass_ref, take_ref,
     q_send, q_recv, n_send, n_recv, j_send, j_recv, f_send, f_recv, p_send, p_recv,
 ):
     c = lax.axis_index("ctx")
@@ -1206,7 +1339,13 @@
         signal(barrier, {"tp": t + 1})
 
     ends = (t // 3) + (3 - t) // 3
-    pl.semaphore_wait(barrier, 5 - ends + ride.greet(barrier))
+    f, size = lax.axis_index("fsdp"), lax.axis_size("fsdp")
+    depth = din_ref.shape[0]
+    for k in range(1, size):
+        signal(barrier, {"fsdp": (f + size - k) % size})
+    count = 5 - ends + size - 1 + ride.greet(barrier)
+    ride.ready()
+    pl.semaphore_wait(barrier, count)
     mate, across, far = mate_of(c), across_of(c), 3 - c
 
     def partner(slot):
@@ -1294,23 +1433,35 @@
                 relay(chunk)
 
     ride.start()
-    for chunk in chunks[:3]:
+
+    def slice_of(place):
+        return pl.ds(pl.multiple_of(place * depth, depth), depth)
+
+    spans = (pl.ds(0, 256), pl.ds(256, 256), pl.ds(512, 128))
+
+    def term(k, span):
+        to, cols = (f + k) % size, spans[span]
+        return rcopy(
+            all_in_ref.at[slice_of(to), cols], term_ref.at[k - 1, :, cols],
+            w_send.at[k - 1, span], w_recv.at[k - 1, span], {"fsdp": to},
+        )
+
+    query, own = dq_ref[...].reshape(1024, 256), own_ref[...].reshape(1024, 384)
+    made = (query, own[:, 0:256], own[:, 256:384])
+    for span, chunk in enumerate(chunks[:3]):
 
         @pl.when(jnp.logical_not(at_end))
         def _():
             relay(chunk)
 
-    query, own = dq_ref[...].reshape(1024, 256), own_ref[...].reshape(1024, 384)
+        all_in_ref[:, spans[span]] = mm_tn(xg_ref[...], made[span]).astype(BF16)
+        for k in range(1, size):
+            term(k, span).start()
+
+    ride.turn()
     sum_out_ref[0:1, 0:256] = jnp.sum(query.astype(F32), axis=0, keepdims=True)
     sum_out_ref[0:1, 256:640] = jnp.sum(own.astype(F32), axis=0, keepdims=True)
-
-    @pl.loop(0, 3)
-    def _(tile):
-        cols = pl.ds(pl.multiple_of(tile * 256, 256), 256)
-        din_ref[cols, 0:256] = mm_tn(xg_ref[:, cols], dq_ref[...].reshape(1024, 256)).astype(BF16)
-        din_ref[cols, 256:640] = mm_tn(xg_ref[:, cols], own_ref[...].reshape(1024, 384)).astype(BF16)
-
-    ride.turn()
+    ride.put(sum_out_ref)
     grad_ref[...] = part_ref[t] + back_ref[...]
 
     @pl.when(t < 3)
@@ -1323,6 +1474,23 @@
         passed(1, t)
         grad_ref[...] += take_ref[1, t].astype(F32)
 
+    low_ref[...] = grad_ref[...].astype(BF16)
+    ride.put(grad_ref, low_ref)
+    mem_ref[...] = lax.dot_general(
+        mark_ref[...], grad_ref[...], (((0,), (0,)), ((), ())),
+        precision=lax.Precision.HIGHEST, preferred_element_type=F32,
+    )
+    ride.put(mem_ref)
+    total = all_in_ref[slice_of(f)].astype(F32)
+    for k in range(1, size):
+        for span in range(3):
+            term(k, span).wait_recv()
+        total += term_ref[k - 1].astype(F32)
+    din_ref[...] = total.astype(BF16)
+    ride.put(din_ref)
+    for k in range(1, size):
+        for span in range(3):
+            term(k, span).wait_send()
     for chunk in range(4):
         join(chunk).wait_send()
         near(chunk).wait_send()
@@ -1337,9 +1505,13 @@
     ride.finish()
 
 
-def project_back(dqw, dkv, w, back_one, xg, cid, riders=()):
-    outs = [sds(256, 768, dtype=F32), sds(768, 640), sds(8, 640, dtype=F32)]
+def project_back(dqw, dkv, w, back_one, xg, marks, cid, riders=()):
+    size = lax.axis_size("fsdp")
+    depth = 768 // size
+    f = functools.partial(sds, dtype=F32)
+    outs = [f(256, 768), sds(256, 768), sds(depth, 640), f(8, 640), f(marks.shape[1], 768)]
     scratch = [
+        dma(size - 1, 3), dma(size - 1, 3), pltpu.VMEM((size - 1, depth, 640), BF16), pltpu.VMEM((768, 640), BF16),
         pltpu.VMEM((4, 256, 256), BF16), pltpu.VMEM((4, 256, 384), BF16),
         pltpu.VMEM((4, 256, 768), F32),
         pltpu.VMEM((4, 256, 384), BF16), pltpu.VMEM((4, 256, 384), BF16),
@@ -1348,9 +1520,9 @@
         dma(2), dma(2), dma(4), dma(4), dma(4), dma(4), dma(4), dma(4), dma(4), dma(2, 4),
     ]
     cost = (4 * 1024 * 768 * 640, 12 << 20, 0)
-    operands = (dqw.reshape(4, 256, 256), dkv.reshape(4, 4, 256, 384), w, back_one, xg)
+    operands = (dqw.reshape(4, 256, 256), dkv.reshape(4, 4, 256, 384), w, back_one, xg, marks)
     res, ridden = call(project_back_kernel, operands, outs, scratch, cid, "project_back", cost, riders)
-    return res[0], res[1], res[2][0], ridden
+    return (*res[:3], res[3][0], res[4], ridden)
 
 
 def ancestry(parent_row):
@@ -1436,28 +1608,32 @@
         last = n == layers - 1
         riders = [ctx_gather(out)]
         if n == 0:
-            riders += [flip_gather(w1[0], size), flip_gather(down_turned[0], size)]
-        else:
-            riders += [fsdp_gather(up, size), fsdp_gather(down, size)]
+            riders += [flip_gather(w1[0], size)]
+        riders += [tp_flip(down_turned[n])]
+        if n == 0:
+            riders[-1].after()
         o, lse, got = attend(qw, kv, flags, 16 * n + 1, riders)
         w_out = out_whole(got[0])
-        w_up, w_down = got[1:]
-        w_up, w_down = w_up.reshape(768, 768), w_down.reshape(768, 768)
+        if n == 0:
+            w_up = got[1]
+        w_up, down = w_up.reshape(768, 768), got[-1]
         vecs = vectors(n)
-        weights.append((w_in, w_up, w_down, w_out, vecs))
         riders = []
         if not last:
             riders = [
-                tp_flip(w1[n + 1]), tp_flip(down_turned[n + 1]),
+                tp_flip(w1[n + 1]),
                 plane_gather(out_piece[n + 1], size), fsdp_gather(own_in[n + 1], size),
             ]
-        stream, rounded, xhat1, r1, xhat2, r2, xg2, act, slope, rows, got = block(
-            o, w_out, w_up, w_down, units[n][None], vecs, stream, 16 * n + 2, riders
+        stream, rounded, xhat1, r1, xhat2, r2, xg2, act, slope, rows, w_down, got = block(
+            o, w_out, w_up, down, units[n][None], vecs, stream, 16 * n + 2, riders
         )
+        weights.append((w_in, w_up, w_down, w_out, vecs))
         saved.append((xg, qw, kv, o, lse, xhat1, r1, xhat2, r2, xg2, act, slope, rows))
         if not last:
-            up, down, out, w_in = got
-            xg, qw, kv, w_in, _ = project(rounded, w_in.reshape(768, 640), in_bias[n + 1][None], 16 * n + 16)
+            up, out, w_in = got
+            xg, qw, kv, w_in, (w_up,) = project(
+                rounded, w_in.reshape(768, 640), in_bias[n + 1][None], 16 * n + 16, [fsdp_gather(up, size)]
+            )
     output = rounded
 
     grad = cotangent.astype(F32)
@@ -1469,39 +1645,37 @@
         xg, qw, kv, o, lse, xhat1, r1, xhat2, r2, xg2, act, slope, rows = saved[n]
         riders = []
         if above is not None:
-            riders = [plane_scatter(above["out"], size), fsdp_scatter(above["in"], size)]
-        back_one, do, small[n], d_ffn, d_out, got = block_back(
+            riders = [plane_scatter(above["out"], size)]
+        back_one, do, small[n], d_up, d_down, d_out, got = block_back(
             grad, xhat2, r2, xhat1, r1, vecs, slope, w_up, w_down, w_out, xg2, act, rows, 16 * n + 3, riders
         )
         if above is not None:
             above["out"] = low(added(got[0], (0, 1)))
-            above["in"] = low(added(got[1])).reshape(4, depth // 4, 640)
-        d_ffn = d_ffn.reshape(2, size, 2, depth // 2, 768)
-        riders = [scatter_flip(d_ffn), ctx_scatter(d_out.reshape(4, size, 4, piece, 192), axis=2)]
+        d_down = d_down.reshape(1, size, 2, depth // 2, 768)
+        riders = [tp_flip(d_up), scatter_flip(d_down), ctx_scatter(d_out.reshape(4, size, 4, piece, 192), axis=2)]
         if above is not None:
-            riders += [ctx_scatter(above["ffn"]), ctx_scatter(above["in"]), ctx_gather(above["out"])]
+            riders += [ctx_scatter(part) for part in above["ffn"]]
+            riders += [ctx_scatter(above["in"]), ctx_gather(above["out"])]
         dqw, dkv, got = attend_back(qw, kv, do, o, lse, flags, 16 * n + 4, riders)
-        d_ffn = got[0]
-        d_out = low(added(got[1]))
+        d_ffn = [got[0].reshape(4, depth // 4, 768), got[1].reshape(4, depth // 4, 768)]
+        d_out = low(added(got[2]))
         riders = []
         if above is not None:
-            above["out"] = got[4]
-            riders = [ctx_gather(low(added(got[2]))), ctx_gather(low(added(got[3])))]
+            above["out"] = got[6]
+            riders = [ctx_gather(low(added(part))) for part in got[3:6]]
         if n == 0:
-            riders += [ctx_scatter(d_ffn), plane_scatter(d_out, size)]
-        grad, d_in, sums, got = project_back(dqw, dkv, w_in, back_one, xg, 16 * n + 5, riders)
+            riders += [ctx_scatter(part) for part in d_ffn] + [plane_scatter(d_out, size)]
+        grad, low_grad, d_in, sums, memory_part, got = project_back(
+            dqw, dkv, w_in, back_one, xg, marks, 16 * n + 5, riders
+        )
         if above is not None:
-            done[n + 1] = (got[1], above["out"], got[0])
-        d_in = d_in.reshape(1, size, depth, 640)
+            done[n + 1] = (got[2], above["out"], got[0], got[1])
+        d_in = d_in.reshape(4, depth // 4, 640)
         d_query_bias, _, d_value_bias = parted(sums)
         heads[n] = jnp.stack([d_query_bias, d_value_bias])
         above = {"ffn": d_ffn, "out": d_out, "in": d_in}
-    hidden_grad = low(grad)
-    memory_part = lax.dot_general(
-        marks, grad, (((0,), (0,)), ((), ())),
-        precision=lax.Precision.HIGHEST, preferred_element_type=F32,
-    )
-    ffn0 = low(added(got[-2]))
+    hidden_grad = low_grad
+    up0, down0 = (low(added(part)) for part in got[-3:-1])
     out0 = low(added(got[-1], (0, 1)))
     small = jnp.stack(small)
     place = (ids == t).astype(F32)
@@ -1509,17 +1683,19 @@
     head_rows = (jnp.stack(heads)[:, :, None, :] * place[None, None, :, None]).reshape(2 * layers, 768)
     unit_rows = (small[:, 6][:, None, :] * unit[None, :, None]).reshape(4 * layers, 768)
     stat_rows = small[:, :6].reshape(6 * layers, 768)
-    short = 48 - 12 * layers - memory_part.shape[0]
-    sums = jnp.concatenate([stat_rows, unit_rows, head_rows, memory_part, jnp.zeros((short, 768), F32)])
+    filled = 12 * layers + memory_part.shape[0]
+    slices = 4 * size
+    width = -(-filled // slices)
+    rest = jnp.zeros((width * slices - filled, 768), F32)
+    sums = jnp.concatenate([stat_rows, unit_rows, head_rows, memory_part, rest])
+    sums = sums.reshape(4, size, width, 768)
     got = carry(
-        [fsdp_scatter(d_in, size), ctx_gather(ffn0), ctx_gather(out0), ctx_scatter(sums.reshape(4, 12, 768))], 6
+        [ctx_scatter(d_in), plane_scatter(sums, size), ctx_gather(up0), ctx_gather(down0), ctx_gather(out0)], 6
     )
-    d_in = low(added(got[0])).reshape(4, depth // 4, 640)
-    ffn0, out0 = got[1:3]
-    got = carry([ctx_scatter(d_in), plane_gather(added(got[3]), size)], 7)
-    got = carry([ctx_gather(low(added(got[0]))), ctx_gather(added(got[1], (0, 1)))], 8)
-    done[0] = (got[0], out0, ffn0)
-    totals = got[1].reshape(48, 768)
+    up0, down0, out0 = got[2:]
+    got = carry([ctx_gather(low(added(got[0]))), all_gather(added(got[1], (0, 1)), size)], 7)
+    done[0] = (got[0], out0, up0, down0)
+    totals = added(got[1]).reshape(width * slices, 768)
     stats = totals[: 6 * layers].reshape(layers, 6, 768)
     at = 6 * layers
     ffn_rows = totals[at : at + 4 * layers].reshape(layers, 4, 768)
@@ -1531,9 +1707,10 @@
     memory_grad = totals[at : at + memory_part.shape[0]]
     d_in = jnp.stack([part[0].reshape(depth, 640) for part in done]).astype(F32)
     d_out = jnp.stack([jnp.swapaxes(part[1].reshape(depth, 192), 0, 1) for part in done]).astype(F32)
-    d_ffn = jnp.stack([part[2].reshape(2, depth, 768) for part in done]).astype(F32)
+    d_up = jnp.stack([part[2].reshape(depth, 768) for part in done]).astype(F32)
+    d_down = jnp.stack([jnp.swapaxes(part[3].reshape(depth, 768), 0, 1) for part in done]).astype(F32)
     return (
-        output, hidden_grad, memory_grad, *parted(d_in), d_out, d_ffn[:, 0], jnp.swapaxes(d_ffn[:, 1], 1, 2),
+        output, hidden_grad, memory_grad, *parted(d_in), d_out, d_up, d_down,
         head_grad, ffn_grad, stats[:, 4:6], stats[:, 0:2], stats[:, 2:4],
     )
 

time: 683 us -> 590 us (0.86)
  Pallas kernels: 616 us -> 523 us
    pallas_call x15 -> x14, Pallas kernels: 616 us -> 523 us  [call(): pl.pallas_call(body, out_shape=list(out_shapes) + [rider.out for rider in...]
where the time goes in v3:
time: 590 us; the launch traced here: 581 us
  Pallas kernels  523 us (89%)
  other arithmetic  26.6 us (5%)
  local copies, waits for them, and re-layouts  24.7 us (4%)
    pallas_call x14, Pallas kernels, call(): pl.pallas_call(body, out_shape=list(out_shapes) + [rider.out for rider in...  523 us
    reduce_sum x12, other arithmetic, added(): return jnp.sum(terms.astype(F32), axis=axes)  16 us

profile of v3, /device:TPU:0, one launch (start us, length us, event | category | flops | bytes accessed | tf_op | source)
XLA Modules:
  0.0 581.4 jit_solution(10477597286713091183)
XLA Ops:
  0.7 0.9 fusion.4
  1.6 0.8 fusion.3
  2.5 0.9 multiply_reduce_fusion.3
  3.9 2.6 fusion.13
  8.4 1.0 slice_bitcast_fusion.3
  11.0 54.1 %project.2 = (bf16[4,256,768]{2,1,0:T(8,128)(2,1)}, bf16[4,256,256]{2,1,0:T(8,128)(2,1)}, bf16[4,4,256,384]{3,2,1,0:T(8,128)(2,1)}, bf16[2,384,640]{2,1,0:T(8,12...) custom-call(bf16[256,768]{1,0:T(8,128)(2,1)} %get-tuple-element.236.refs_0_, ...), custom_call_target="tpu_custom_call" | custom-call | flops 1006632960 | bytes 8388608 | tf_op jit(solution)/shard_map/project/pallas_call | solution.py:449
  65.2 1.1 slice_bitcast_fusion.2
  67.5 1.1 slice_bitcast_fusion
  68.6 25.8 %attend.2 = (bf16[1024,192]{1,0:T(8,128)(2,1)}, f32[1024,128]{1,0:T(8,128)}, bf16[4,4,2,96,192]{4,3,2,1,0:T(8,128)(2,1)}, bf16[2,2,192,768]{3,2,1,0:T(8,128)(2,1)}, bf16[384,768]{1,0:T(8,128)(2,1)}) custom-call(s32[2,4]{1,0:T(2,128)} %pad_add_fusion.refs_0_, bf16[1024,256]{1,0:T(8,128)(2,1)} %bitcast.207, bf16[4096,384]{1,0:T(8,128)(2,1)} %bitcast.183, ...), custom_call_target="tpu_custom_call" | custom-call | flops 2013265920 | bytes 6291456 | tf_op jit(solution)/shard_map/attend/pallas_call | solution.py:449
  94.4 2.7 copy.58
  98.4 48.0 %block.2 = (f32[256,768]{1,0:T(8,128)}, bf16[256,768]{1,0:T(8,128)(2,1)}, f32[256,768]{1,0:T(8,128)}, f32[256,128]{1,0:T(8,128)}, f32[256,768]{1,0:T(8,128)}, /*...) custom-call(bf16[4,256,192]{2,1,0:T(8,128)(2,1)} %bitcast.209, ...), custom_call_target="tpu_custom_call" | custom-call | flops 2717908992 | bytes 16777216 | tf_op jit(solution)/shard_map/block/pallas_call | solution.py:449
  146.4 42.0 %project.3 = (bf16[4,256,768]{2,1,0:T(8,128)(2,1)}, bf16[4,256,256]{2,1,0:T(8,128)(2,1)}, bf16[4,4,256,384]{3,2,1,0:T(8,128)(2,1)}, bf16[2,384,768]{2,1,0:T(8,128)(2,1)}) custom-call(bf16[256,768]{1,0:T(8,128)(2,1)} %get-tuple-element.112.refs_0_, bf16[768,640]{1,0:T(8,128)(2,1)} %bitcast.203, f32[1,640]{1,0:T(1,128)} %get-tuple-element.232.refs_2_, ...), custom_call_target="tpu_custom_call" | custom-call | flops 1006632960 | bytes 8388608 | tf_op jit(solution)/shard_map/project/pallas_call | solution.py:449
  188.4 21.9 %attend.3 = (bf16[1024,192]{1,0:T(8,128)(2,1)}, f32[1024,128]{1,0:T(8,128)}, bf16[4,4,2,96,192]{4,3,2,1,0:T(8,128)(2,1)}, bf16[384,768]{1,0:T(8,128)(2,1)}) custom-call(s32[2,4]{1,0:T(2,128)} %pad_add_fusion.refs_0_, bf16[1024,256]{1,0:T(8,128)(2,1)} %bitcast.210, bf16[4096,384]{1,0:T(8,128)(2,1)} %bitcast.185, ...), custom_call_target="tpu_custom_call" | custom-call | flops 2013265920 | bytes 6291456 | tf_op jit(solution)/shard_map/attend/pallas_call | solution.py:449
  210.3 2.7 copy.59
  213.7 40.6 %block.3 = (f32[256,768]{1,0:T(8,128)}, bf16[256,768]{1,0:T(8,128)(2,1)}, f32[256,768]{1,0:T(8,128)}, f32[256,128]{1,0:T(8,128)}, f32[256,768]{1,0:T(8,128)}, /*...) custom-call(bf16[4,256,192]{2,1,0:T(8,128)(2,1)} %bitcast.212, ...), custom_call_target="tpu_custom_call" | custom-call | flops 2717908992 | bytes 16777216 | tf_op jit(solution)/shard_map/block/pallas_call | solution.py:449
  254.3 1.0 convert_element_type.85.refs_0_
  255.3 36.2 %block_back.2 = (f32[256,768]{1,0:T(8,128)}, bf16[4,256,192]{2,1,0:T(8,128)(2,1)}, f32[8,768]{1,0:T(8,128)}, bf16[384,768]{1,0:T(8,128)(2,1)}, bf16[768,768]{1,0:T(8,128)(2,1)}, /*index=5*/bf16[4,768,192]{2,1,0:T(8,128)(2,1)}) custom-call(f32[256,768]{1,0:T(8,128)} %convert_element_type.85.refs_0_, f32[256,768]{1,0:T(8,128)} %get-tuple-element.124.refs_1_, ...), custom_call_target="tpu_custom_call" | custom-call | flops 5435817984 | bytes 20971520 | tf_op jit(solution)/shard_map/block_back/pallas_call | solution.py:449
  291.5 34.4 %attend_back.2 = (bf16[1024,256]{1,0:T(8,128)(2,1)}, bf16[4096,384]{1,0:T(8,128)(2,1)}, bf16[384,768]{1,0:T(8,128)(2,1)}, bf16[2,192,768]{2,1,0:T(8,128)(2,1)}, bf16[3,4,2,96,192]{4,3,2,1,0:T(8,128)(2,1)}) custom-call(s32[2,4]{1,0:T(2,128)} %pad_add_fusion.refs_0_, bf16[1024,256]{1,0:T(8,128)(2,1)} %bitcast.211, bf16[4096,384]{1,0:T(8,128)(2,1)} %bitcast.186, ...), custom_call_target="tpu_custom_call" | custom-call | flops 5033164800 | bytes 12582912 | tf_op jit(solution)/shard_map/attend_back/pallas_call | solution.py:449
  325.9 0.8 compare_convert_fusion.refs_5_
  326.7 51.0 %project_back.2 = (f32[256,768]{1,0:T(8,128)}, bf16[256,768]{1,0:T(8,128)(2,1)}, bf16[384,640]{1,0:T(8,128)(2,1)}, f32[8,640]{1,0:T(8,128)}, f32[20,768]{1,0:T(8,128)}) custom-call(bf16[4,256,256]{2,1,0:T(8,128)(2,1)} %bitcast.215, bf16[4,4,256,384]{3,2,1,0:T(8,128)(2,1)} %bitcast.187, bf16[768,640]{1,0:T(8,128)(2,1)} %bitcast.204, ...), custom_call_target="tpu_custom_call" | custom-call | flops 2013265920 | bytes 12582912 | tf_op jit(solution)/shard_map/project_back/pallas_call | solution.py:449
  377.7 1.1 reduce_sum.176.refs_13_
  378.8 40.7 %block_back.3 = (f32[256,768]{1,0:T(8,128)}, bf16[4,256,192]{2,1,0:T(8,128)(2,1)}, f32[8,768]{1,0:T(8,128)}, bf16[384,768]{1,0:T(8,128)(2,1)}, bf16[768,768]{1,0...) custom-call(f32[256,768]{1,0:T(8,128)} %get-tuple-element.142.refs_0_, ...), custom_call_target="tpu_custom_call" | custom-call | flops 5435817984 | bytes 20971520 | tf_op jit(solution)/shard_map/block_back/pallas_call | solution.py:449
  419.5 1.7 reduce_sum.177.refs_12_
  421.2 36.9 %attend_back.3 = (bf16[1024,256]{1,0:T(8,128)(2,1)}, bf16[4096,384]{1,0:T(8,128)(2,1)}, bf16[384,768]{1,0:T(8,128)(2,1)}, bf16[2,192,768]{2,1,0:T(8,128)(2,1)}, ...) custom-call(s32[2,4]{1,0:T(2,128)} %pad_add_fusion.refs_0_, ...), custom_call_target="tpu_custom_call" | custom-call | flops 5033164800 | bytes 12582912 | tf_op jit(solution)/shard_map/attend_back/pallas_call | solution.py:449
  458.1 1.9 reduce_sum.178.refs_6_
  460.0 1.8 reduce_sum.179.refs_7_
  461.8 1.7 reduce_sum.180.refs_8_
  463.5 1.1 reduce_sum.181.refs_11_
  464.6 57.5 %project_back.3 = (f32[256,768]{1,0:T(8,128)}, bf16[256,768]{1,0:T(8,128)(2,1)}, bf16[384,640]{1,0:T(8,128)(2,1)}, f32[8,640]{1,0:T(8,128)}, f32[20,768]{1,0:T(8...) custom-call(bf16[4,256,256]{2,1,0:T(8,128)(2,1)} %bitcast.160, ...), custom_call_target="tpu_custom_call" | custom-call | flops 2013265920 | bytes 12582912 | tf_op jit(solution)/shard_map/project_back/pallas_call | solution.py:449
  522.6 0.8 slice_bitcast_fusion.18
  524.0 0.8 slice_bitcast_fusion.22
  525.8 1.0 concatenate.44
  526.8 0.7 reshape.243.refs_1_
  527.5 0.7 reduce_sum.182.refs_2_
  528.3 0.7 reduce_sum.183.refs_3_
  529.7 14.4 %carry.2 = (bf16[3,96,640]{2,1,0:T(8,128)(2,1)}, f32[4,2,6,768]{3,2,1,0:T(8,128)}, bf16[4,96,768]{2,1,0:T(8,128)(2,1)}, bf16[4,96,768]{2,1,0:T(8,128)(2,1)}, bf16[4,96,192]{2,1,0:T(8,128)(2,1)}) custom-call(bf16[4,96,640]{2,1,0:T(8,128)(2,1)} %bitcast.162, f32[4,2,6,768]{3,2,1,0:T(8,128)} %reshape.243.refs_1_, bf16[96,768]{1,0:T(8,128)(2,1)} %reduce_sum.182.refs_2_, ...), custom_call_target="tpu_custom_call" | custom-call | flops 1048576 | bytes 1048576 | tf_op jit(solution)/shard_map/carry/pallas_call | solution.py:449
  544.2 1.7 reduce_sum.185.refs_0_
  545.9 1.6 reduce_sum.186.refs_1_
  547.4 19.7 %carry.3 = (bf16[4,96,640]{2,1,0:T(8,128)(2,1)}, f32[4,4,2,6,768]{4,3,2,1,0:T(8,128)}) custom-call(bf16[96,640]{1,0:T(8,128)(2,1)} %reduce_sum.185.refs_0_, f32[6,768]{1,0:T(8,128)} %reduce_sum.186.refs_1_), custom_call_target="tpu_custom_call" | custom-call | flops 1048576 | bytes 1048576 | tf_op jit(solution)/shard_map/carry/pallas_call | solution.py:449
  567.1 1.3 reduce_sum.187
  569.8 0.9 pad_maximum_fusion
  570.7 0.9 pad_maximum_fusion.1
  571.6 0.9 pad_maximum_fusion.2
  572.9 0.9 maximum_convert_fusion.3
  573.8 1.6 maximum_convert_fusion
  576.0 1.6 maximum_convert_fusion.1
  579.7 0.7 copy.81
  580.4 0.7 copy.82
  (147 shorter events, 14.4 us)
Async XLA Ops:
  0.6 3.3 copy-start
  0.7 5.8 %slice-start = ((bf16[2,384,192]{1,2,0:T(8,128)(2,1)}), bf16[2,384,128]{1,2,0:T(8,128)(2,1)S(1)}, s32[]{:S(2)}) async-start(bf16[2,384,192]{1,2,0:T(8,128)(2,1)} %param.21), calls=%async_computation | async-start | bytes 393216 | tf_op jit(solution)/shard_map/slice | solution.py:1543
  0.7 6.0 %slice-start.1 = ((bf16[2,384,192]{1,2,0:T(8,128)(2,1)}), bf16[2,384,64]{1,2,0:T(8,128)(2,1)S(1)}, s32[]{:S(2)}) async-start(bf16[2,384,192]{1,2,0:T(8,128)(2,1)} %param.21), calls=%async_computation.1 | async-start | bytes 196608 | tf_op jit(solution)/shard_map/slice | solution.py:1543
  3.9 3.0 slice-start.2
  3.9 3.1 slice-start.4
  6.5 0.9 slice-start.3
  6.5 1.1 slice-start.5
  8.4 1.1 copy-start.27
  8.4 1.8 copy-start.18
  11.0 54.1 %copy-start.2 = (bf16[2,384,768]{2,1,0:T(8,128)(2,1)S(1)}, bf16[2,384,768]{2,1,0:T(8,128)(2,1)}, u32[]{:S(2)}) copy-start(bf16[2,384,768]{2,1,0:T(8,128)(2,1)} %param.25) | copy-start | bytes 3538948
  65.1 1.7 copy-start.3
  94.3 2.7 copy-start.26
  94.3 3.3 copy-start.23
  94.4 3.3 copy-start.24
  94.4 3.3 copy-start.25
  213.6 40.6 %copy-start.17 = (bf16[256,768]{1,0:T(8,128)(2,1)S(1)}, bf16[256,768]{1,0:T(8,128)(2,1)}, u32[]{:S(2)}) copy-start(bf16[256,768]{1,0:T(8,128)(2,1)} %param.17) | copy-start | bytes 1179652
  291.5 34.4 %copy-start.28 = (s32[1,1,20]{2,1,0:T(1,128)S(1)}, s32[1,1,20]{2,1,0:T(1,128)}, u32[]{:S(2)}) copy-start(s32[1,1,20]{2,1,0:T(1,128)} %param.18) | copy-start | bytes 244
  326.7 51.0 %copy-start.4 = (bf16[3,4,2,96,192]{4,3,2,1,0:T(8,128)(2,1)S(1)}, bf16[3,4,2,96,192]{4,3,2,1,0:T(8,128)(2,1)}, u32[]{:S(2)}) copy-start(bf16[3,4,2,96,192]{4,3,2,1,0:T(8,128)(2,1)} %get-tuple-element.152) | copy-start | bytes 2654212
  458.1 5.4 copy-start.5
  464.6 57.6 %copy-start.21 = (f32[8,768]{1,0:T(8,128)S(1)}, f32[8,768]{1,0:T(8,128)}, u32[]{:S(2)}) copy-start(f32[8,768]{1,0:T(8,128)} %get-tuple-element.176) | copy-start | bytes 73732
  464.6 57.6 %copy-start.22 = (f32[8,768]{1,0:T(8,128)S(1)}, f32[8,768]{1,0:T(8,128)}, u32[]{:S(2)}) copy-start(f32[8,768]{1,0:T(8,128)} %get-tuple-element.175) | copy-start | bytes 73732
  522.2 5.4 copy-start.13
  522.2 6.1 %copy-start.12 = (bf16[3,96,768]{2,1,0:T(8,128)(2,1)S(1)}, bf16[3,96,768]{2,1,0:T(8,128)(2,1)}, u32[]{:S(2)}) copy-start(bf16[3,96,768]{2,1,0:T(8,128)(2,1)} %get-tuple-element.181) | copy-start | bytes 1327108
  522.2 6.8 %copy-start.16 = (bf16[4,2,96,192]{3,2,1,0:T(8,128)(2,1)S(1)}, bf16[4,2,96,192]{3,2,1,0:T(8,128)(2,1)}, u32[]{:S(2)}) copy-start(bf16[4,2,96,192]{3,2,1,0:T(8,128)(2,1)} %get-tuple-element.182) | copy-start | bytes 884740
  529.7 39.3 %copy-start.10 = (bf16[4,96,640]{2,1,0:T(8,128)(2,1)S(1)}, bf16[4,96,640]{2,1,0:T(8,128)(2,1)}, u32[]{:S(2)}) copy-start(bf16[4,96,640]{2,1,0:T(8,128)(2,1)} %get-tuple-element.187) | copy-start | bytes 1474564
  567.1 2.2 copy-start.11
  571.6 0.9 copy-start.19
  571.6 1.2 copy-start.20
  571.6 2.2 copy-start.6
  571.6 2.2 copy-start.7
  573.8 1.6 copy-start.8
  573.8 1.9 copy-start.9
  576.0 3.7 copy-start.14
  576.0 4.4 copy-start.15
  576.0 5.2 copy-start.1

commit v4 on v3

--- a/solution.py
+++ b/solution.py
@@ -395,9 +395,9 @@
         for at in range(len(self.hops)):
             pl.when(number == at)(functools.partial(self.one_hop, at))
 
-    def turn_at(self, number, at):
+    def turn_when(self, when):
         if self.rides:
-            pl.when(number == at)(self.turn)
+            pl.when(when)(self.turn)
 
     def turn(self):
         self.turned = True
@@ -679,7 +679,7 @@
         )
 
     def partner(slot):
-        return rcopy(qbuf.at[slot], qw_ref.at[slot + 2], q_send.at[slot], q_recv.at[slot], {"ctx": 3 - c})
+        return rcopy(qbuf.at[slot], qw_ref.at[2 * slot + 1], q_send.at[slot], q_recv.at[slot], {"ctx": 3 - c})
 
     for step in range(4):
         if step == 0:
@@ -710,14 +710,14 @@
         across(chunk).start()
         query = (made[:, :256] * 0.125).astype(BF16)
 
-        @pl.when(chunk < 2)
+        @pl.when(chunk % 2 == 0)
         def _():
             qw_ref[chunk] = query
 
-        @pl.when(chunk >= 2)
-        def _():
-            qbuf[chunk - 2] = query
-            partner(chunk - 2).start()
+        @pl.when(chunk % 2 == 1)
+        def _():
+            qbuf[chunk // 2] = query
+            partner(chunk // 2).start()
 
         if step >= 1:
             before = ordered(t, step - 1)
@@ -801,7 +801,6 @@
 
 Q_TILE = 256
 FAR = 1e30
-K_TILE = 256
 
 
 def open_up(ride):
@@ -817,14 +816,13 @@
     c = lax.axis_index("ctx")
     open_up(ride)
     low = lax.broadcasted_iota(jnp.int32, (Q_TILE, 128), 1) < 64
-    per_half = 512 // Q_TILE
     for side, at in enumerate((128, 256)):
         vo_ref[side, :, 0:128] = kv_ref[:, at : at + 128]
         vo_ref[side, :, 128:256] = jnp.ones((4096, 128), BF16)
 
     @pl.loop(0, 1024 // Q_TILE)
     def _(tile):
-        half = tile // per_half
+        half = tile % 2
         segment = c + half * (3 - 2 * c)
         rows = pl.ds(pl.multiple_of(tile * Q_TILE, Q_TILE), Q_TILE)
         pair = qw_ref[rows, 0:128]
@@ -859,7 +857,7 @@
         totals = [m_ref[head] + jnp.log(whole[head]) for head in range(3)]
         lse_ref[rows, :] = jnp.where(lane == 0, totals[0], jnp.where(lane == 1, totals[1], totals[2]))
         ride.hop(tile)
-        ride.turn_at(tile, 2)
+        ride.turn_when(tile == 2)
 
     ride.finish()
 
@@ -879,94 +877,6 @@
     return res[0], res[1], ridden
 
 
-def attend_back_kernel(
-    ride, flag_ref, qw_ref, kv_ref, do_ref, o_ref, lse_ref, dq_ref, dkv_ref,
-    qm_ref, dm_ref, row_ref, acc_ref, key_ref,
-):
-    c = lax.axis_index("ctx")
-    open_up(ride)
-    low = lax.broadcasted_iota(jnp.int32, (1024, 128), 1) < 64
-    pair = qw_ref[:, 0:128]
-    none = jnp.zeros_like(pair)
-    qm_ref[0] = jnp.where(low, pair, none)
-    qm_ref[1] = jnp.where(low, none, pair)
-    qm_ref[2] = qw_ref[:, 128:256]
-    pair = do_ref[:, 0:128]
-    dm_ref[0] = jnp.where(low, pair, none)
-    dm_ref[1] = jnp.where(low, none, pair)
-    dm_ref[2] = jnp.concatenate([do_ref[:, 128:192], none[:, :64]], axis=1)
-    turned = jnp.transpose(lse_ref[...], (1, 0))
-    row_ref[0:8] = turned[0:8]
-    product = do_ref[...].astype(F32) * o_ref[...].astype(F32)
-    head_row = lax.broadcasted_iota(jnp.int32, (8, 192), 0)
-    head_of = lax.broadcasted_iota(jnp.int32, (8, 192), 1) // 64
-    marks = (head_row == head_of).astype(F32)
-    row_ref[8:16] = lax.dot_general(
-        marks, product, (((1,), (1,)), ((), ())),
-        precision=lax.Precision.HIGHEST, preferred_element_type=F32,
-    )
-    acc_ref[...] = jnp.zeros_like(acc_ref)
-    low_keys = lax.broadcasted_iota(jnp.int32, (K_TILE, 128), 1) < 64
-
-    @pl.loop(0, 4)
-    def _(block):
-        @pl.loop(0, 1024 // K_TILE)
-        def _(tile):
-            keys = pl.ds(pl.multiple_of(block * 1024 + tile * K_TILE, K_TILE), K_TILE)
-            key_ref[...] = jnp.zeros_like(key_ref)
-            key_pair = kv_ref[keys, 0:128]
-            nothing = jnp.zeros_like(key_pair)
-            key_parts = (
-                jnp.where(low_keys, key_pair, nothing),
-                jnp.where(low_keys, nothing, key_pair),
-                jnp.where(low_keys, nothing, kv_ref[keys, 128:256]),
-            )
-            for half in range(2):
-                segment = c if half == 0 else 3 - c
-
-                @pl.when(block <= segment)
-                def _():
-                    penalty = jnp.where(flag_ref[half, block] > 0, 0.0, FAR)
-                    rows = pl.ds(half * 512, 512)
-                    for head in range(3):
-                        k_at = 0 if head < 2 else 128
-                        v_at = 256 if head < 2 else 128
-                        query = qm_ref[head, rows]
-                        grads = dm_ref[head, rows]
-                        scores = mm_nt(kv_ref[keys, k_at : k_at + 128], query)
-                        probs = jnp.exp(scores - (row_ref[head : head + 1, rows] + penalty))
-                        grad_probs = mm_nt(kv_ref[keys, v_at : v_at + 128], grads)
-                        grad_scores = (probs * (grad_probs - row_ref[8 + head : 9 + head, rows])).astype(BF16)
-                        key_ref[:, v_at : v_at + 128] += mm(probs.astype(BF16), grads)
-                        key_ref[:, k_at : k_at + 128] += mm(grad_scores, query)
-                        q_at = 0 if head < 2 else 128
-                        acc_ref[rows, q_at : q_at + 128] += mm_tn(grad_scores, key_parts[head])
-
-            dkv_ref[keys, :] = key_ref[...].astype(BF16)
-
-        ride.hop(block)
-        ride.turn_at(block, 0)
-
-    dq_ref[...] = (acc_ref[...].astype(BF16).astype(F32) * 0.125).astype(BF16)
-    ride.finish()
-
-
-def attend_back(qw, kv, do, o, lse, flags, cid, riders=()):
-    outs = [sds(1024, 256), sds(4096, 384)]
-    scratch = [
-        pltpu.VMEM((3, 1024, 128), BF16),
-        pltpu.VMEM((3, 1024, 128), BF16),
-        pltpu.VMEM((16, 1024), F32),
-        pltpu.VMEM((1024, 256), F32),
-        pltpu.VMEM((K_TILE, 384), F32),
-    ]
-    cost = (5 * 512 * 1024 * 64 * 10 * 3, 12 << 20, 5 * 512 * 1024 * 3)
-    operands = (flags, qw, kv.reshape(4096, 384), do, o, lse)
-    cid = cid if riders else None
-    res, ridden = call(attend_back_kernel, operands, outs, scratch, cid, "attend_back", cost, riders, smem=(0,))
-    return res[0], res[1].reshape(4, 1024, 384), ridden
-
-
 PIECE = 128
 
 
@@ -1038,11 +948,11 @@
     barrier = pltpu.get_barrier_semaphore()
     for place in range(4):
 
-        @pl.when((t < 2) & (t != place))
+        @pl.when((t % 2 == 0) & (t != place))
         def _():
             signal(barrier, {"tp": place})
 
-        @pl.when(t >= 2)
+        @pl.when(t % 2 == 1)
         def _():
             signal(barrier, {"ctx": 3 - c, "tp": place})
 
@@ -1051,7 +961,7 @@
     f, size = lax.axis_index("fsdp"), lax.axis_size("fsdp")
     for k in range(1, size):
         signal(barrier, {"fsdp": (f + size - k) % size})
-    count = 5 + t // 2 + size - 1 + ride.greet(barrier)
+    count = 5 + t % 2 + size - 1 + ride.greet(barrier)
     ride.ready()
     pl.semaphore_wait(barrier, count)
 
@@ -1060,14 +970,14 @@
         return rcopy(w2_ref, down_ref.at[f], w_send.at[k - 1], w_recv.at[k - 1], device)
 
     def give(quarter):
-        device = {"tp": quarter} if quarter < 2 else {"ctx": 3 - c, "tp": quarter}
+        device = {"tp": quarter} if quarter % 2 == 0 else {"ctx": 3 - c, "tp": quarter}
         return rcopy(o_ref.at[quarter], rows_ref.at[t], o_send.at[quarter], o_recv.at[t], device)
 
     def given(group):
         rcopy(rows_ref.at[group], rows_ref.at[group], o_send.at[0], o_recv.at[group], {"tp": t}).wait_recv()
 
     for quarter in (3, 2, 1, 0):
-        if quarter < 2:
+        if quarter % 2 == 0:
 
             @pl.when(t != quarter)
             def _():
@@ -1085,7 +995,7 @@
     branch = stream_ref[...] + vec_ref[0:1]
     for group in range(4):
 
-        @pl.when((t >= 2) | (t != group))
+        @pl.when((t % 2 == 1) | (t != group))
         def _():
             given(group)
 
@@ -1122,7 +1032,7 @@
     low_ref[...] = out.astype(BF16)
     ride.put(out_ref, low_ref, xhat2_ref, r2_ref)
     for quarter in range(4):
-        if quarter < 2:
+        if quarter % 2 == 0:
 
             @pl.when(t != quarter)
             def _():
@@ -1167,7 +1077,7 @@
     t = lax.axis_index("tp")
     barrier = pltpu.get_barrier_semaphore()
     for place in range(4):
-        if place < 2:
+        if place % 2 == 0:
 
             @pl.when(t != place)
             def _():
@@ -1181,7 +1091,7 @@
     depth = dup_ref.shape[0]
     for k in range(1, size):
         signal(barrier, {"fsdp": (f + size - k) % size})
-    count = 5 + t // 2 + size - 1 + ride.greet(barrier)
+    count = 5 + t % 2 + size - 1 + ride.greet(barrier)
     ride.ready()
     pl.semaphore_wait(barrier, count)
 
@@ -1249,15 +1159,15 @@
     for group in range(4):
         dsend_ref[group] = mm(g1, wo_ref[group]).astype(BF16)
 
-        @pl.when((t < 2) & (t == group))
+        @pl.when((t % 2 == 0) & (t == group))
         def _():
             do_ref[t] = dsend_ref[group]
 
-        @pl.when((t < 2) & (t != group))
+        @pl.when((t % 2 == 0) & (t != group))
         def _():
             give_near(group).start()
 
-        @pl.when(t >= 2)
+        @pl.when(t % 2 == 1)
         def _():
             give_far(group).start()
 
@@ -1278,13 +1188,13 @@
         def taken():
             rcopy(do_ref.at[quarter], do_ref.at[quarter], d_send.at[0], d_recv.at[quarter], {"tp": t}).wait_recv()
 
-        if quarter < 2:
+        if quarter % 2 == 0:
             pl.when(t != quarter)(taken)
         else:
             taken()
     for group in range(4):
 
-        @pl.when((t >= 2) | (t != group))
+        @pl.when((t % 2 == 1) | (t != group))
         def _():
             give_near(group).wait_send()
 
@@ -1319,15 +1229,28 @@
     return back, do.reshape(1024, 192), stats, d_up, d_down, d_out, ridden
 
 
-def project_back_kernel(
-    ride, dqw_ref, dkv_ref, w_ref, back_ref, xg_ref, mark_ref, grad_ref, low_ref, din_ref, sum_out_ref, mem_ref,
-    w_send, w_recv, term_ref, all_in_ref, dq_ref, own_ref, part_ref, near_ref, join_ref, sum_ref, far_ref, pass_ref, take_ref,
+def ordered_by(place, step):
+    half = place // 2
+    inner = place + half * (3 - 2 * place)
+    chunk = step + inner * (1 - 2 * step) * ((3 - step) // 2)
+    return chunk + half * (3 - 2 * chunk)
+
+
+def inner_back_kernel(
+    ride, flag_ref, qw_ref, kv_ref, do_ref, o_ref, lse_ref, w_ref, back_ref, xg_ref, mark_ref,
+    grad_ref, low_ref, din_ref, sum_out_ref, mem_ref,
+    qm_ref, dm_ref, row_ref, acc_ref, wide_ref, dkv_ref, dqs_ref,
+    w_send, w_recv, term_ref, all_in_ref, dq_ref, own_ref, part_ref,
+    near_ref, join_ref, sum_ref, far_ref, pass_ref, take_ref,
     q_send, q_recv, n_send, n_recv, j_send, j_recv, f_send, f_recv, p_send, p_recv,
 ):
     c = lax.axis_index("ctx")
     t = lax.axis_index("tp")
+    f, size = lax.axis_index("fsdp"), lax.axis_size("fsdp")
+    depth = din_ref.shape[0]
+    mate, across, far = mate_of(c), across_of(c), 3 - c
     barrier = pltpu.get_barrier_semaphore()
-    for device in (mate_of(c), across_of(c), 3 - c):
+    for device in (mate, across, far):
         signal(barrier, {"ctx": device})
 
     @pl.when(t > 0)
@@ -1338,18 +1261,40 @@
     def _():
         signal(barrier, {"tp": t + 1})
 
-    ends = (t // 3) + (3 - t) // 3
-    f, size = lax.axis_index("fsdp"), lax.axis_size("fsdp")
-    depth = din_ref.shape[0]
     for k in range(1, size):
         signal(barrier, {"fsdp": (f + size - k) % size})
+    ends = (t // 3) + (3 - t) // 3
     count = 5 - ends + size - 1 + ride.greet(barrier)
     ride.ready()
+
+    low = lax.broadcasted_iota(jnp.int32, (1024, 128), 1) < 64
+    pair = qw_ref[:, 0:128]
+    none = jnp.zeros_like(pair)
+    qm_ref[0] = jnp.where(low, pair, none)
+    qm_ref[1] = jnp.where(low, none, pair)
+    qm_ref[2] = qw_ref[:, 128:256]
+    pair = do_ref[:, 0:128]
+    dm_ref[0] = jnp.where(low, pair, none)
+    dm_ref[1] = jnp.where(low, none, pair)
+    dm_ref[2] = jnp.concatenate([do_ref[:, 128:192], none[:, :64]], axis=1)
+    turned = jnp.transpose(lse_ref[...], (1, 0))
+    product = do_ref[...].astype(F32) * o_ref[...].astype(F32)
+    head_row = lax.broadcasted_iota(jnp.int32, (8, 192), 0)
+    head_of = lax.broadcasted_iota(jnp.int32, (8, 192), 1) // 64
+    delta = lax.dot_general(
+        (head_row == head_of).astype(F32), product, (((1,), (1,)), ((), ())),
+        precision=lax.Precision.HIGHEST, preferred_element_type=F32,
+    )
+    for quarter in range(4):
+        row_ref[quarter, 0:8] = turned[0:8, quarter * 256 : (quarter + 1) * 256]
+        row_ref[quarter, 8:16] = delta[:, quarter * 256 : (quarter + 1) * 256]
+    acc_ref[...] = jnp.zeros_like(acc_ref)
+    wide_ref[...] = jnp.zeros_like(wide_ref)
     pl.semaphore_wait(barrier, count)
-    mate, across, far = mate_of(c), across_of(c), 3 - c
+    ride.start()
 
     def partner(slot):
-        return rcopy(dqw_ref.at[slot + 2], dq_ref.at[slot + 2], q_send.at[slot], q_recv.at[slot], {"ctx": far})
+        return rcopy(dqs_ref.at[slot], dq_ref.at[2 * slot + 1], q_send.at[slot], q_recv.at[slot], {"ctx": far})
 
     def near(chunk):
         return rcopy(dkv_ref.at[mate, chunk], near_ref.at[chunk], n_send.at[chunk], n_recv.at[chunk], {"ctx": mate})
@@ -1359,20 +1304,6 @@
 
     def cross(chunk):
         return rcopy(sum_ref.at[chunk], far_ref.at[chunk], f_send.at[chunk], f_recv.at[chunk], {"ctx": across})
-
-    chunks = [ordered(t, 3 - k) for k in range(4)]
-    for chunk in chunks:
-        join(chunk).start()
-    for slot in range(2):
-        partner(slot).start()
-    for chunk in chunks:
-        near(chunk).start()
-    for quarter in range(2):
-        dq_ref[quarter] = dqw_ref[quarter]
-    for chunk in chunks:
-        join(chunk).wait_recv()
-        sum_ref[chunk] = (dkv_ref[across, chunk].astype(F32) + join_ref[chunk].astype(F32)).astype(BF16)
-        cross(chunk).start()
 
     def lower(chunk):
         return rcopy(pass_ref.at[chunk], take_ref.at[0, chunk], p_send.at[chunk], p_recv.at[0, chunk], {"tp": t - 1})
@@ -1385,39 +1316,38 @@
             take_ref.at[side, chunk], take_ref.at[side, chunk], p_send.at[0], p_recv.at[side, chunk], {"tp": t}
         ).wait_recv()
 
-    def relay(chunk):
-        @pl.when(chunk < t)
-        def _():
-            @pl.when(t < 3)
+    chunks = [ordered(t, 3 - k) for k in range(4)]
+    at_end = (t == 0) | (t == 3)
+
+    def leave(k):
+        chunk = chunks[k]
+        dkv_ref[:, chunk] = wide_ref[:, chunk].astype(BF16)
+        join(chunk).start()
+        near(chunk).start()
+        query = (acc_ref[chunk].astype(BF16).astype(F32) * 0.125).astype(BF16)
+
+        @pl.when(chunk % 2 == 0)
+        def _():
+            dq_ref[chunk] = query
+
+        @pl.when(chunk % 2 == 1)
+        def _():
+            dqs_ref[chunk // 2] = query
+            partner(chunk // 2).start()
+
+    def go_across(k):
+        chunk = chunks[k]
+        join(chunk).wait_recv()
+        sum_ref[chunk] = (dkv_ref[across, chunk].astype(F32) + join_ref[chunk].astype(F32)).astype(BF16)
+        cross(chunk).start()
+
+    def gather_up(k):
+        chunk = chunks[k]
+        if k < 3:
+
+            @pl.when(chunk % 2 == 1)
             def _():
-                passed(0, chunk)
-                pass_ref[chunk] = (part_ref[chunk] + take_ref[0, chunk].astype(F32)).astype(BF16)
-
-            @pl.when(t == 3)
-            def _():
-                pass_ref[chunk] = part_ref[chunk].astype(BF16)
-
-            lower(chunk).start()
-
-        @pl.when(chunk > t)
-        def _():
-            @pl.when(t > 0)
-            def _():
-                passed(1, chunk)
-                pass_ref[chunk] = (part_ref[chunk] + take_ref[1, chunk].astype(F32)).astype(BF16)
-
-            @pl.when(t == 0)
-            def _():
-                pass_ref[chunk] = part_ref[chunk].astype(BF16)
-
-            upper(chunk).start()
-
-    at_end = (t == 0) | (t == 3)
-    for step, chunk in enumerate(chunks):
-
-        @pl.when(chunk >= 2)
-        def _():
-            partner(chunk - 2).wait_recv()
+                partner(chunk // 2).wait_recv()
 
         near(chunk).wait_recv()
         cross(chunk).wait_recv()
@@ -1426,13 +1356,121 @@
         ).astype(BF16)
         own_ref[chunk] = own
         part_ref[chunk] = mm_nt(dq_ref[chunk], w_ref[:, 0:256]) + mm_nt(own, w_ref[:, 256:640])
-        if step < 3:
-
-            @pl.when(at_end)
+
+    def relay(k):
+        chunk = chunks[k]
+
+        @pl.when(chunk < t)
+        def _():
+            @pl.when(t < 3)
             def _():
-                relay(chunk)
-
-    ride.start()
+                passed(0, chunk)
+                pass_ref[chunk] = (part_ref[chunk] + take_ref[0, chunk].astype(F32)).astype(BF16)
+
+            @pl.when(t == 3)
+            def _():
+                pass_ref[chunk] = part_ref[chunk].astype(BF16)
+
+            lower(chunk).start()
+
+        @pl.when(chunk > t)
+        def _():
+            @pl.when(t > 0)
+            def _():
+                passed(1, chunk)
+                pass_ref[chunk] = (part_ref[chunk] + take_ref[1, chunk].astype(F32)).astype(BF16)
+
+            @pl.when(t == 0)
+            def _():
+                pass_ref[chunk] = part_ref[chunk].astype(BF16)
+
+            upper(chunk).start()
+
+    def relay_ends(k):
+        pl.when(at_end)(functools.partial(relay, k))
+
+    def relay_inner(k):
+        pl.when(jnp.logical_not(at_end))(functools.partial(relay, k))
+
+    low_keys = lax.broadcasted_iota(jnp.int32, (256, 128), 1) < 64
+
+    def one_item(item, done):
+        phase = (item + 9) // 16 + (item + 4) // 16 + (item + 1) // 16
+        number = item - phase * (8 - phase)
+        second = number // (4 - phase)
+        query_at = ordered_by(t, 3 - (phase + second * (number - 3 + phase)))
+        key_at = ordered_by(t, 3 - (phase + (1 - second) * number))
+        half = query_at % 2
+        rows = pl.ds(pl.multiple_of(query_at * 256, 256), 256)
+
+        def visit(segments):
+            queries = [qm_ref[head, rows] for head in range(3)]
+            grads = [dm_ref[head, rows] for head in range(3)]
+            made = []
+            for segment in segments:
+                penalty = jnp.where(flag_ref[half, segment] > 0, 0.0, FAR)
+                key_pair = kv_ref[segment, key_at, :, 0:128]
+                mixed = kv_ref[segment, key_at, :, 128:256]
+                value_pair = kv_ref[segment, key_at, :, 256:384]
+                for head in range(3):
+                    shift = row_ref[query_at, head : head + 1] + penalty
+                    prob = jnp.exp(mm_nt(key_pair if head < 2 else mixed, queries[head]) - shift)
+                    grad_prob = mm_nt(value_pair if head < 2 else mixed, grads[head])
+                    grad_score = (prob * (grad_prob - row_ref[query_at, 8 + head : 9 + head])).astype(BF16)
+                    made.append((prob.astype(BF16), grad_score))
+            pair_sum, mixed_sum = 0.0, 0.0
+            for number, segment in enumerate(segments):
+                (p0, g0), (p1, g1), (p2, g2) = made[3 * number : 3 * number + 3]
+                for_keys = mm(g0, queries[0]) + mm(g1, queries[1])
+                for_mixed = mm(g2, queries[2]) + mm(p2, grads[2])
+                for_values = mm(p0, grads[0]) + mm(p1, grads[1])
+                wide_ref[segment, key_at] += jnp.concatenate([for_keys, for_mixed, for_values], axis=1)
+                key_pair = kv_ref[segment, key_at, :, 0:128]
+                nothing = jnp.zeros_like(key_pair)
+                pair_sum += mm_tn(g0, jnp.where(low_keys, key_pair, nothing))
+                pair_sum += mm_tn(g1, jnp.where(low_keys, nothing, key_pair))
+                mixed_sum += mm_tn(g2, jnp.where(low_keys, nothing, kv_ref[segment, key_at, :, 128:256]))
+            acc_ref[query_at] += jnp.concatenate([pair_sum, mixed_sum], axis=1)
+
+        length = c + 1 + half * (3 - 2 * c)
+
+        @pl.loop(0, length // 2)
+        def _(two):
+            visit((2 * two, 2 * two + 1))
+
+        @pl.when(length % 2 == 1)
+        def _():
+            visit((length - 1,))
+
+        now = done + length
+
+        def at(place, action, k):
+            pl.when(item == place)(functools.partial(action, k))
+
+        def once(amount, action, k):
+            pl.when((done < amount) & (now >= amount))(functools.partial(action, k))
+
+        for n in range(len(ride.hops)):
+            once(RIDE_HOPS[n], ride.one_hop, n)
+        ride.turn_when((done < 16) & (now >= 16))
+        for k, place in enumerate((6, 11, 14)):
+            at(place, leave, k)
+        once(24, go_across, 0)
+        once(31, gather_up, 0)
+        once(31, relay_ends, 0)
+        once(32, go_across, 1)
+        once(38, gather_up, 1)
+        once(38, relay_ends, 1)
+        return now
+
+    lax.fori_loop(0, 16, one_item, 0)
+    leave(3)
+    go_across(2)
+    relay_inner(0)
+    go_across(3)
+    gather_up(2)
+    relay_ends(2)
+    relay_inner(1)
 
     def slice_of(place):
         return pl.ds(pl.multiple_of(place * depth, depth), depth)
@@ -1446,19 +1484,22 @@
             w_send.at[k - 1, span], w_recv.at[k - 1, span], {"fsdp": to},
         )
 
-    query, own = dq_ref[...].reshape(1024, 256), own_ref[...].reshape(1024, 384)
-    made = (query, own[:, 0:256], own[:, 256:384])
-    for span, chunk in enumerate(chunks[:3]):
-
-        @pl.when(jnp.logical_not(at_end))
-        def _():
-            relay(chunk)
-
-        all_in_ref[:, spans[span]] = mm_tn(xg_ref[...], made[span]).astype(BF16)
+
+    @pl.when(t % 2 == 1)
+    def _():
+        partner(t // 2).wait_recv()
+
+    query = dq_ref[...].reshape(1024, 256)
+    for span in range(3):
+        if span == 1:
+            gather_up(3)
+        own = own_ref[...].reshape(1024, 384)
+        made = (query, own[:, 0:256], own[:, 256:384])[span]
+        all_in_ref[:, spans[span]] = mm_tn(xg_ref[...], made).astype(BF16)
         for k in range(1, size):
             term(k, span).start()
 
-    ride.turn()
+    relay_inner(2)
     sum_out_ref[0:1, 0:256] = jnp.sum(query.astype(F32), axis=0, keepdims=True)
     sum_out_ref[0:1, 256:640] = jnp.sum(own.astype(F32), axis=0, keepdims=True)
     ride.put(sum_out_ref)
@@ -1505,12 +1546,18 @@
     ride.finish()
 
 
-def project_back(dqw, dkv, w, back_one, xg, marks, cid, riders=()):
+RIDE_HOPS = (10, 14)
+
+
+def inner_back(qw, kv, do, o, lse, flags, w, back_one, xg, marks, cid, riders=()):
     size = lax.axis_size("fsdp")
     depth = 768 // size
     f = functools.partial(sds, dtype=F32)
     outs = [f(256, 768), sds(256, 768), sds(depth, 640), f(8, 640), f(marks.shape[1], 768)]
     scratch = [
+        pltpu.VMEM((3, 1024, 128), BF16), pltpu.VMEM((3, 1024, 128), BF16), pltpu.VMEM((4, 16, 256), F32),
+        pltpu.VMEM((4, 256, 256), F32), pltpu.VMEM((4, 4, 256, 384), F32), pltpu.VMEM((4, 4, 256, 384), BF16),
+        pltpu.VMEM((2, 256, 256), BF16),
         dma(size - 1, 3), dma(size - 1, 3), pltpu.VMEM((size - 1, depth, 640), BF16), pltpu.VMEM((768, 640), BF16),
         pltpu.VMEM((4, 256, 256), BF16), pltpu.VMEM((4, 256, 384), BF16),
         pltpu.VMEM((4, 256, 768), F32),
@@ -1519,9 +1566,9 @@
         pltpu.VMEM((4, 256, 768), BF16), pltpu.VMEM((2, 4, 256, 768), BF16),
         dma(2), dma(2), dma(4), dma(4), dma(4), dma(4), dma(4), dma(4), dma(4), dma(2, 4),
     ]
-    cost = (4 * 1024 * 768 * 640, 12 << 20, 0)
-    operands = (dqw.reshape(4, 256, 256), dkv.reshape(4, 4, 256, 384), w, back_one, xg, marks)
-    res, ridden = call(project_back_kernel, operands, outs, scratch, cid, "project_back", cost, riders)
+    cost = (5 * 512 * 1024 * 64 * 30 + 4 * 1024 * 768 * 640, 16 << 20, 5 * 512 * 1024 * 3)
+    operands = (flags, qw, kv.reshape(4, 4, 256, 384), do, o, lse, w, back_one, xg, marks)
+    res, ridden = call(inner_back_kernel, operands, outs, scratch, cid, "inner_back", cost, riders, smem=(0,))
     return (*res[:3], res[3][0], res[4], ridden)
 
 
@@ -1646,37 +1693,28 @@
         riders = []
         if above is not None:
             riders = [plane_scatter(above["out"], size)]
+            riders += [ctx_scatter(above[part]) for part in ("up", "down", "in")]
         back_one, do, small[n], d_up, d_down, d_out, got = block_back(
             grad, xhat2, r2, xhat1, r1, vecs, slope, w_up, w_down, w_out, xg2, act, rows, 16 * n + 3, riders
         )
-        if above is not None:
-            above["out"] = low(added(got[0], (0, 1)))
         d_down = d_down.reshape(1, size, 2, depth // 2, 768)
         riders = [tp_flip(d_up), scatter_flip(d_down), ctx_scatter(d_out.reshape(4, size, 4, piece, 192), axis=2)]
         if above is not None:
-            riders += [ctx_scatter(part) for part in above["ffn"]]
-            riders += [ctx_scatter(above["in"]), ctx_gather(above["out"])]
-        dqw, dkv, got = attend_back(qw, kv, do, o, lse, flags, 16 * n + 4, riders)
-        d_ffn = [got[0].reshape(4, depth // 4, 768), got[1].reshape(4, depth // 4, 768)]
-        d_out = low(added(got[2]))
-        riders = []
-        if above is not None:
-            above["out"] = got[6]
-            riders = [ctx_gather(low(added(part))) for part in got[3:6]]
-        if n == 0:
-            riders += [ctx_scatter(part) for part in d_ffn] + [plane_scatter(d_out, size)]
-        grad, low_grad, d_in, sums, memory_part, got = project_back(
-            dqw, dkv, w_in, back_one, xg, marks, 16 * n + 5, riders
+            riders += [ctx_gather(low(added(got[0], (0, 1))))] + [ctx_gather(low(added(part))) for part in got[1:]]
+        grad, low_grad, d_in, sums, memory_part, got = inner_back(
+            qw, kv, do, o, lse, flags, w_in, back_one, xg, marks, 16 * n + 4, riders
         )
         if above is not None:
-            done[n + 1] = (got[2], above["out"], got[0], got[1])
-        d_in = d_in.reshape(4, depth // 4, 640)
+            done[n + 1] = (got[6], got[3], got[4], got[5])
         d_query_bias, _, d_value_bias = parted(sums)
         heads[n] = jnp.stack([d_query_bias, d_value_bias])
-        above = {"ffn": d_ffn, "out": d_out, "in": d_in}
+        above = {
+            "up": got[0].reshape(4, depth // 4, 768),
+            "down": got[1].reshape(4, depth // 4, 768),
+            "in": d_in.reshape(4, depth // 4, 640),
+            "out": low(added(got[2])),
+        }
     hidden_grad = low_grad
-    up0, down0 = (low(added(part)) for part in got[-3:-1])
-    out0 = low(added(got[-1], (0, 1)))
     small = jnp.stack(small)
     place = (ids == t).astype(F32)
     unit = (ids == flipped_place(c, t)).astype(F32)
@@ -1689,13 +1727,13 @@
     rest = jnp.zeros((width * slices - filled, 768), F32)
     sums = jnp.concatenate([stat_rows, unit_rows, head_rows, memory_part, rest])
     sums = sums.reshape(4, size, width, 768)
-    got = carry(
-        [ctx_scatter(d_in), plane_scatter(sums, size), ctx_gather(up0), ctx_gather(down0), ctx_gather(out0)], 6
-    )
-    up0, down0, out0 = got[2:]
-    got = carry([ctx_gather(low(added(got[0]))), all_gather(added(got[1], (0, 1)), size)], 7)
-    done[0] = (got[0], out0, up0, down0)
-    totals = added(got[1]).reshape(width * slices, 768)
+    riders = [ctx_scatter(above[part]) for part in ("up", "down", "in")]
+    got = carry(riders + [plane_scatter(above["out"], size), plane_scatter(sums, size)], 6)
+    up0, down0, in0 = (ctx_gather(low(added(part))) for part in got[:3])
+    out0 = ctx_gather(low(added(got[3], (0, 1))))
+    got = carry([up0, down0, in0, out0, all_gather(added(got[4], (0, 1)), size)], 7)
+    done[0] = (got[2], got[3], got[0], got[1])
+    totals = added(got[4]).reshape(width * slices, 768)
     stats = totals[: 6 * layers].reshape(layers, 6, 768)
     at = 6 * layers
     ffn_rows = totals[at : at + 4 * layers].reshape(layers, 4, 768)

time: 590 us -> 560 us (0.949)
  Pallas kernels: 523 us -> 494 us
    pallas_call x14 -> x12, Pallas kernels: 523 us -> 494 us  [call(): pl.pallas_call(body, out_shape=list(out_shapes) + [rider.out for rider in...]
where the time goes in v4:
time: 560 us; the launch traced here: 554 us
  Pallas kernels  494 us (88%)
  other arithmetic  29.2 us (5%)
  local copies, waits for them, and re-layouts  23.8 us (4%)
    pallas_call x12, Pallas kernels, call(): pl.pallas_call(body, out_shape=list(out_shapes) + [rider.out for rider in...  494 us
    reduce_sum x12, other arithmetic, added(): return jnp.sum(terms.astype(F32), axis=axes)  18.7 us

profile of v4, /device:TPU:0, one launch (start us, length us, event | category | flops | bytes accessed | tf_op | source)
XLA Modules:
  0.0 553.6 jit_solution(16258522203130839223)
XLA Ops:
  0.7 0.9 fusion.4
  1.6 0.8 fusion.3
  2.5 0.9 multiply_reduce_fusion.3
  3.9 2.6 fusion.13
  8.4 1.0 slice_bitcast_fusion.3
  11.0 54.1 %project.2 = (bf16[4,256,768]{2,1,0:T(8,128)(2,1)}, bf16[4,256,256]{2,1,0:T(8,128)(2,1)}, bf16[4,4,256,384]{3,2,1,0:T(8,128)(2,1)}, bf16[2,384,640]{2,1,0:T(8,12...) custom-call(bf16[256,768]{1,0:T(8,128)(2,1)} %get-tuple-element.228.refs_0_, ...), custom_call_target="tpu_custom_call" | custom-call | flops 1006632960 | bytes 8388608 | tf_op jit(solution)/shard_map/project/pallas_call | solution.py:449
  65.2 1.1 slice_bitcast_fusion.2
  67.5 1.1 slice_bitcast_fusion
  68.6 25.8 %attend.2 = (bf16[1024,192]{1,0:T(8,128)(2,1)}, f32[1024,128]{1,0:T(8,128)}, bf16[4,4,2,96,192]{4,3,2,1,0:T(8,128)(2,1)}, bf16[2,2,192,768]{3,2,1,0:T(8,128)(2,1)}, bf16[384,768]{1,0:T(8,128)(2,1)}) custom-call(s32[2,4]{1,0:T(2,128)} %pad_add_fusion.refs_0_, bf16[1024,256]{1,0:T(8,128)(2,1)} %bitcast.198, bf16[4096,384]{1,0:T(8,128)(2,1)} %bitcast.175, ...), custom_call_target="tpu_custom_call" | custom-call | flops 2013265920 | bytes 6291456 | tf_op jit(solution)/shard_map/attend/pallas_call | solution.py:449
  94.4 2.7 copy.58
  98.4 47.4 %block.2 = (f32[256,768]{1,0:T(8,128)}, bf16[256,768]{1,0:T(8,128)(2,1)}, f32[256,768]{1,0:T(8,128)}, f32[256,128]{1,0:T(8,128)}, f32[256,768]{1,0:T(8,128)}, /*...) custom-call(bf16[4,256,192]{2,1,0:T(8,128)(2,1)} %bitcast.200, ...), custom_call_target="tpu_custom_call" | custom-call | flops 2717908992 | bytes 16777216 | tf_op jit(solution)/shard_map/block/pallas_call | solution.py:449
  145.8 42.4 %project.3 = (bf16[4,256,768]{2,1,0:T(8,128)(2,1)}, bf16[4,256,256]{2,1,0:T(8,128)(2,1)}, bf16[4,4,256,384]{3,2,1,0:T(8,128)(2,1)}, bf16[2,384,768]{2,1,0:T(8,128)(2,1)}) custom-call(bf16[256,768]{1,0:T(8,128)(2,1)} %get-tuple-element.108.refs_0_, bf16[768,640]{1,0:T(8,128)(2,1)} %bitcast.194, f32[1,640]{1,0:T(1,128)} %get-tuple-element.224.refs_2_, ...), custom_call_target="tpu_custom_call" | custom-call | flops 1006632960 | bytes 8388608 | tf_op jit(solution)/shard_map/project/pallas_call | solution.py:449
  188.2 21.9 %attend.3 = (bf16[1024,192]{1,0:T(8,128)(2,1)}, f32[1024,128]{1,0:T(8,128)}, bf16[4,4,2,96,192]{4,3,2,1,0:T(8,128)(2,1)}, bf16[384,768]{1,0:T(8,128)(2,1)}) custom-call(s32[2,4]{1,0:T(2,128)} %pad_add_fusion.refs_0_, bf16[1024,256]{1,0:T(8,128)(2,1)} %bitcast.201, bf16[4096,384]{1,0:T(8,128)(2,1)} %bitcast.176, ...), custom_call_target="tpu_custom_call" | custom-call | flops 2013265920 | bytes 6291456 | tf_op jit(solution)/shard_map/attend/pallas_call | solution.py:449
  210.1 2.7 copy.59
  213.4 39.0 %block.3 = (f32[256,768]{1,0:T(8,128)}, bf16[256,768]{1,0:T(8,128)(2,1)}, f32[256,768]{1,0:T(8,128)}, f32[256,128]{1,0:T(8,128)}, f32[256,768]{1,0:T(8,128)}, /*...) custom-call(bf16[4,256,192]{2,1,0:T(8,128)(2,1)} %bitcast.203, ...), custom_call_target="tpu_custom_call" | custom-call | flops 2717908992 | bytes 16777216 | tf_op jit(solution)/shard_map/block/pallas_call | solution.py:449
  252.4 1.0 convert_element_type.85.refs_0_
  253.4 38.5 %block_back.2 = (f32[256,768]{1,0:T(8,128)}, bf16[4,256,192]{2,1,0:T(8,128)(2,1)}, f32[8,768]{1,0:T(8,128)}, bf16[384,768]{1,0:T(8,128)(2,1)}, bf16[768,768]{1,0:T(8,128)(2,1)}, /*index=5*/bf16[4,768,192]{2,1,0:T(8,128)(2,1)}) custom-call(f32[256,768]{1,0:T(8,128)} %convert_element_type.85.refs_0_, f32[256,768]{1,0:T(8,128)} %get-tuple-element.120.refs_1_, ...), custom_call_target="tpu_custom_call" | custom-call | flops 5435817984 | bytes 20971520 | tf_op jit(solution)/shard_map/block_back/pallas_call | solution.py:449
  291.8 0.8 compare_convert_fusion.refs_9_
  292.6 69.8 %inner_back.2 = (f32[256,768]{1,0:T(8,128)}, bf16[256,768]{1,0:T(8,128)(2,1)}, bf16[384,640]{1,0:T(8,128)(2,1)}, f32[8,640]{1,0:T(8,128)}, f32[20,768]{1,0:T(8,1...) custom-call(s32[2,4]{1,0:T(2,128)} %pad_add_fusion.refs_0_, ...), custom_call_target="tpu_custom_call" | custom-call | flops 7046430720 | bytes 16777216 | tf_op jit(solution)/shard_map/inner_back/pallas_call | solution.py:449
  362.4 2.3 reduce_sum.176.refs_13_
  364.8 40.0 %block_back.3 = (f32[256,768]{1,0:T(8,128)}, bf16[4,256,192]{2,1,0:T(8,128)(2,1)}, f32[8,768]{1,0:T(8,128)}, bf16[384,768]{1,0:T(8,128)(2,1)}, bf16[768,768]{1,0...) custom-call(f32[256,768]{1,0:T(8,128)} %get-tuple-element.136.refs_0, ...), custom_call_target="tpu_custom_call" | custom-call | flops 5435817984 | bytes 20971520 | tf_op jit(solution)/shard_map/block_back/pallas_call | solution.py:449
  404.8 1.7 reduce_sum.177.refs_13_
  406.5 1.8 reduce_sum.178.refs_14_
  408.3 1.8 reduce_sum.179.refs_15_
  410.1 0.7 reduce_sum.180.refs_16_
  410.8 75.0 %inner_back.3 = (f32[256,768]{1,0:T(8,128)}, bf16[256,768]{1,0:T(8,128)(2,1)}, bf16[384,640]{1,0:T(8,128)(2,1)}, f32[8,640]{1,0:T(8,128)}, f32[20,768]{1,0:T(8,1...) custom-call(s32[2,4]{1,0:T(2,128)} %pad_add_fusion.refs_0_, ...), custom_call_target="tpu_custom_call" | custom-call | flops 7046430720 | bytes 16777216 | tf_op jit(solution)/shard_map/inner_back/pallas_call | solution.py:449
  485.8 2.3 reduce_sum.181.refs_3_
  488.5 0.8 slice_bitcast_fusion.18
  490.0 0.8 slice_bitcast_fusion.22
  490.7 0.7 slice_bitcast_fusion.23
  491.9 0.7 reshape.235.refs_4_
  492.6 16.2 %carry.2 = (bf16[3,96,768]{2,1,0:T(8,128)(2,1)}, bf16[3,96,768]{2,1,0:T(8,128)(2,1)}, bf16[3,96,640]{2,1,0:T(8,128)(2,1)}, bf16[4,2,96,192]{3,2,1,0:T(8,128)(2,1)}, f32[4,2,6,768]{3,2,1,0:T(8,128)}) custom-call(bf16[4,96,768]{2,1,0:T(8,128)(2,1)} %bitcast.150, bf16[4,96,768]{2,1,0:T(8,128)(2,1)} %bitcast.151, bf16[4,96,640]{2,1,0:T(8,128)(2,1)} %bitcast.154, ...), custom_call_target="tpu_custom_call" | custom-call | flops 1048576 | bytes 1048576 | tf_op jit(solution)/shard_map/carry/pallas_call | solution.py:449
  508.8 1.8 reduce_sum.182.refs_0_
  510.7 1.8 reduce_sum.183.refs_1_
  512.4 1.8 reduce_sum.184.refs_2_
  514.2 0.7 reduce_sum.185.refs_3_
  515.5 23.8 %carry.3 = (bf16[4,96,768]{2,1,0:T(8,128)(2,1)}, bf16[4,96,768]{2,1,0:T(8,128)(2,1)}, bf16[4,96,640]{2,1,0:T(8,128)(2,1)}, bf16[4,96,192]{2,1,0:T(8,128)(2,1)}, f32[4,4,2,6,768]{4,3,2,1,0:T(8,128)}) custom-call(bf16[96,768]{1,0:T(8,128)(2,1)} %reduce_sum.182.refs_0_, bf16[96,768]{1,0:T(8,128)(2,1)} %reduce_sum.183.refs_1_, ...), custom_call_target="tpu_custom_call" | custom-call | flops 1048576 | bytes 1048576 | tf_op jit(solution)/shard_map/carry/pallas_call | solution.py:449
  539.3 1.3 reduce_sum.187
  542.1 0.9 pad_maximum_fusion
  543.0 0.9 pad_maximum_fusion.1
  543.9 0.9 pad_maximum_fusion.2
  545.2 0.9 maximum_convert_fusion.3
  546.0 1.6 maximum_convert_fusion
  548.3 1.6 maximum_convert_fusion.1
  549.9 0.7 multiply_reduce_fusion.1
  550.6 0.7 multiply_reduce_fusion
  551.9 0.7 copy.81
  552.7 0.7 copy.82
  (143 shorter events, 12.4 us)
Async XLA Ops:
  0.6 3.3 copy-start
  0.7 5.8 %slice-start = ((bf16[2,384,192]{1,2,0:T(8,128)(2,1)}), bf16[2,384,128]{1,2,0:T(8,128)(2,1)S(1)}, s32[]{:S(2)}) async-start(bf16[2,384,192]{1,2,0:T(8,128)(2,1)} %param.21), calls=%async_computation | async-start | bytes 393216 | tf_op jit(solution)/shard_map/slice | solution.py:1590
  0.7 6.0 %slice-start.1 = ((bf16[2,384,192]{1,2,0:T(8,128)(2,1)}), bf16[2,384,64]{1,2,0:T(8,128)(2,1)S(1)}, s32[]{:S(2)}) async-start(bf16[2,384,192]{1,2,0:T(8,128)(2,1)} %param.21), calls=%async_computation.1 | async-start | bytes 196608 | tf_op jit(solution)/shard_map/slice | solution.py:1590
  3.9 3.0 slice-start.2
  3.9 3.1 slice-start.4
  6.5 0.9 slice-start.3
  6.5 1.1 slice-start.5
  8.4 1.1 copy-start.26
  8.4 1.8 copy-start.15
  11.0 54.1 %copy-start.2 = (bf16[2,384,768]{2,1,0:T(8,128)(2,1)S(1)}, bf16[2,384,768]{2,1,0:T(8,128)(2,1)}, u32[]{:S(2)}) copy-start(bf16[2,384,768]{2,1,0:T(8,128)(2,1)} %param.25) | copy-start | bytes 3538948
  65.2 1.7 copy-start.3
  94.3 2.7 copy-start.25
  94.4 3.3 copy-start.22
  94.4 3.3 copy-start.23
  94.4 3.3 copy-start.24
  213.4 39.0 %copy-start.13 = (bf16[256,768]{1,0:T(8,128)(2,1)S(1)}, bf16[256,768]{1,0:T(8,128)(2,1)}, u32[]{:S(2)}) copy-start(bf16[256,768]{1,0:T(8,128)(2,1)} %param.17) | copy-start | bytes 1179652
  253.4 38.5 %copy-start.27 = (s32[1,1,20]{2,1,0:T(1,128)S(1)}, s32[1,1,20]{2,1,0:T(1,128)}, u32[]{:S(2)}) copy-start(s32[1,1,20]{2,1,0:T(1,128)} %param.18) | copy-start | bytes 244
  404.8 5.3 copy-start.14
  485.8 2.4 copy-start.19
  485.8 2.4 copy-start.20
  485.8 5.9 %copy-start.21 = (f32[20,768]{1,0:T(8,128)S(1)}, f32[20,768]{1,0:T(8,128)}, u32[]{:S(2)}) copy-start(f32[20,768]{1,0:T(8,128)} %get-tuple-element.171) | copy-start | bytes 184324
  508.8 5.4 copy-start.12
  508.8 6.1 %copy-start.16 = (f32[4,2,6,768]{3,2,1,0:T(8,128)S(1)}, f32[4,2,6,768]{3,2,1,0:T(8,128)}, u32[]{:S(2)}) copy-start(f32[4,2,6,768]{3,2,1,0:T(8,128)} %get-tuple-element.176) | copy-start | bytes 442372
  512.4 28.9 %copy-start.8 = (bf16[4,96,640]{2,1,0:T(8,128)(2,1)S(1)}, bf16[4,96,640]{2,1,0:T(8,128)(2,1)}, u32[]{:S(2)}) copy-start(bf16[4,96,640]{2,1,0:T(8,128)(2,1)} %get-tuple-element.179) | copy-start | bytes 1474564
  539.3 2.2 copy-start.9
  543.8 0.9 copy-start.17
  543.8 1.2 copy-start.18
  543.8 2.2 copy-start.4
  543.9 2.2 copy-start.5
  546.0 1.6 copy-start.6
  546.0 1.9 copy-start.7
  548.2 3.7 copy-start.10
  548.2 4.4 copy-start.11
  548.2 5.2 copy-start.1

commit v5 on v4

--- a/solution.py
+++ b/solution.py
@@ -58,6 +58,13 @@
     return chunk + half * (3 - 2 * chunk)
 
 
+def ordered_by(place, step):
+    half = place // 2
+    inner = place + half * (3 - 2 * place)
+    chunk = step + inner * (1 - 2 * step) * ((3 - step) // 2)
+    return chunk + half * (3 - 2 * chunk)
+
+
 def dma(*shape):
     return pltpu.SemaphoreType.DMA(shape)
 
@@ -65,10 +72,10 @@
 class Rider:
     def __init__(self, array, out, make, scratch, chunks=0):
         self.array, self.out, self.make, self.scratch, self.chunks = array, out, make, scratch, chunks
-        self.late = False
-
-    def after(self):
-        self.late = True
+        self.late = self.hopped = False
+
+    def later(self, hopped=False):
+        self.late, self.hopped = True, hopped
         return self
 
 
@@ -76,7 +83,7 @@
     def __init__(self, steps, here, scratch):
         self.steps, self.here = steps, here
         self.send, self.recv, self.leg, self.stage = scratch
-        self.turned = False
+        self.came = False
 
     def greetings(self):
         return [(origin, when, weight) for _, origin, _, _, when, weight in self.steps]
@@ -100,10 +107,17 @@
         guarded(self.here[2], self.inward().wait)
         guarded(self.here[2], self.outward().start)
 
+    def arrive(self):
+        self.came = True
+        for copy, when in self.copies():
+            guarded(when, copy.wait_recv)
+        guarded(self.here[2], self.outward().wait)
+
     def finish(self):
+        if not self.came:
+            self.arrive()
         for copy, when in self.copies():
-            guarded(when, copy.wait)
-        guarded(self.here[2], self.outward().wait)
+            guarded(when, copy.wait_send)
 
 
 class FlipGather:
@@ -185,7 +199,8 @@
     def __init__(self, source, target, place, scratch):
         self.source, self.target = source, target
         self.f, self.c, self.t = place
-        self.size = source.shape[1]
+        self.size = source.shape[0]
+        self.here = False
         self.send, self.recv, self.on_send, self.on_recv, self.leg, self.got, self.out = scratch
         self.moves = self.c > 0
 
@@ -197,13 +212,13 @@
     def first(self, chunk, k):
         to = (self.f + k) % self.size
         return rcopy(
-            self.source.at[chunk // 2, to, chunk % 2], self.got.at[k, chunk],
+            self.source.at[to, chunk], self.got.at[k, chunk],
             self.send.at[k - 1, chunk], self.recv.at[k - 1, chunk], {"fsdp": to},
         )
 
     def own(self, chunk):
         return pltpu.make_async_copy(
-            self.source.at[chunk // 2, self.f, chunk % 2], self.got.at[0, chunk], self.leg.at[chunk]
+            self.source.at[self.f, chunk], self.got.at[0, chunk], self.leg.at[chunk]
         )
 
     def second(self, chunk):
@@ -238,18 +253,19 @@
     def turn(self):
         pass
 
+    def arrive(self):
+        self.here = True
+        for chunk in range(self.target.shape[0]):
+            guarded(self.moves, self.second(chunk).wait_recv)
+            guarded(self.c == 0, self.stays(chunk).wait)
+
     def finish(self):
+        if not self.here:
+            self.arrive()
         for chunk in range(self.target.shape[0]):
             for k in range(1, self.size):
                 self.first(chunk, k).wait_send()
-
-            @pl.when(self.moves)
-            def _():
-                self.second(chunk).wait()
-
-            @pl.when(self.c == 0)
-            def _():
-                self.stays(chunk).wait()
+            guarded(self.moves, self.second(chunk).wait_send)
 
 
 class CtxGather:
@@ -344,14 +360,21 @@
         self.gone = [False] * len(puts)
         place = tuple(lax.axis_index(axis) for axis in ("fsdp", "ctx", "tp"))
         scratch = list(scratch)
-        self.rides, self.hops, self.late = [], [], []
-        self.turned = False
-        for rider, source, target in zip(riders, sources, targets):
+        self.rides, self.hops, self.late, self.hopped = [], [], [], []
+        self.firsts, self.seconds, self.begun, self.turned = [], [], [], []
+        for rider, target in zip(riders, targets):
             own = [scratch.pop(0) for _ in rider.scratch]
-            ride = rider.make(source, target, place, own)
+            chained = isinstance(rider.array, int)
+            ride = rider.make(targets[rider.array] if chained else sources.pop(0), target, place, own)
             self.rides.append(ride)
+            if chained:
+                self.firsts.append(self.rides[rider.array])
+                self.seconds.append(ride)
+                self.late.append(ride)
             if rider.late:
                 self.late.append(ride)
+            if rider.hopped:
+                self.hopped.append(ride)
             self.hops += [(ride, chunk) for chunk in range(rider.chunks)]
 
     def ready(self):
@@ -379,34 +402,51 @@
                 count = count + weight
         return count
 
+    def begin(self, ride):
+        self.begun.append(ride)
+        ride.start()
+
     def start(self):
         for ride in self.rides:
             if ride not in self.late:
-                ride.start()
+                self.begin(ride)
+
+    def start_late(self):
+        for ride in self.late:
+            if ride not in self.hopped + self.seconds:
+                self.begin(ride)
 
     def one_hop(self, at):
         ride, chunk = self.hops[at]
         ride.hop(chunk)
         if at == len(self.hops) - 1:
-            for ride in self.late:
-                ride.start()
-
-    def hop(self, number):
-        for at in range(len(self.hops)):
-            pl.when(number == at)(functools.partial(self.one_hop, at))
+            for ride in self.hopped:
+                self.begin(ride)
+
+    def turn(self):
+        for ride in self.begun:
+            if ride not in self.turned + self.seconds:
+                self.turned.append(ride)
+                ride.turn()
 
     def turn_when(self, when):
         if self.rides:
             pl.when(when)(self.turn)
 
-    def turn(self):
-        self.turned = True
+    def chain(self):
+        for first, second in zip(self.firsts, self.seconds):
+            first.arrive()
+            self.begin(second)
+
+    def chain_turn(self):
+        for second in self.seconds:
+            self.turned.append(second)
+            second.turn()
+
+    def finish(self):
         for ride in self.rides:
-            ride.turn()
-
-    def finish(self):
-        if not self.turned:
-            self.turn()
+            if ride not in self.turned:
+                ride.turn()
         for ride in self.rides:
             ride.finish()
 
@@ -421,11 +461,12 @@
 def call(kernel, operands, out_shapes, scratch, collective_id, name, cost, riders=(), smem=()):
     n_in, n_out, n_scratch, n_ride = len(operands), len(out_shapes), len(scratch), len(riders)
     large = [i for i in range(n_in) if i not in smem]
+    carried = [rider.array for rider in riders if not isinstance(rider.array, int)]
 
     def body(*refs):
         refs = list(refs)
         take = lambda n: [refs.pop(0) for _ in range(n)]
-        ins, sources, outs, targets = take(n_in), take(n_ride), take(n_out), take(n_ride)
+        ins, sources, outs, targets = take(n_in), take(len(carried)), take(n_out), take(n_ride)
         near_ins, near_outs, (in_sem, out_sem), own = take(len(large)), take(n_out), take(2), take(n_scratch)
         fetches = [
             pltpu.make_async_copy(ins[i], near, in_sem.at[slot]) for slot, (i, near) in enumerate(zip(large, near_ins))
@@ -450,13 +491,13 @@
         body,
         out_shape=list(out_shapes) + [rider.out for rider in riders],
         in_specs=[pl.BlockSpec(memory_space=pltpu.SMEM) if i in smem else anywhere for i in range(n_in)]
-        + [anywhere] * n_ride,
+        + [anywhere] * len(carried),
         out_specs=[anywhere] * (n_out + n_ride),
         scratch_shapes=near + [dma(max(len(large), 1)), dma(max(n_out, 1))] + list(scratch) + extra,
         compiler_params=pltpu.CompilerParams(**params),
         cost_estimate=pl.CostEstimate(flops=cost[0], bytes_accessed=cost[1], transcendentals=cost[2]),
         name=name,
-    )(*operands, *[rider.array for rider in riders])
+    )(*operands, *carried)
     return results[:n_out], results[n_out:]
 
 
@@ -475,13 +516,13 @@
 
 
 def scatter_flip(parts):
-    n, size = parts.shape[0], parts.shape[1]
-    shape = (2 * n, *parts.shape[3:])
+    size, n = parts.shape[0], parts.shape[1]
+    shape = parts.shape[1:]
     scratch = [
-        dma(size - 1, 2 * n), dma(size - 1, 2 * n), dma(2 * n), dma(2 * n), dma(2 * n),
+        dma(size - 1, n), dma(size - 1, n), dma(n), dma(n), dma(n),
         pltpu.VMEM((size, *shape), BF16), pltpu.VMEM(shape, BF16),
     ]
-    return Rider(parts, sds(*shape), ScatterFlip, scratch, chunks=2 * n)
+    return Rider(parts, sds(*shape), ScatterFlip, scratch, chunks=n)
 
 
 def fsdp_gather(own, size):
@@ -511,12 +552,13 @@
     return copies_rider(parts, out, size - 1, out.shape[1:], make)
 
 
-def ctx_gather(own):
+def ctx_gather(own, first=None):
     scratch = [dma(3), dma(3), dma(2), pltpu.VMEM(own.shape, own.dtype)]
-    return Rider(own, sds(4, *own.shape, dtype=own.dtype), CtxGather, scratch)
-
-
-def ctx_scatter(parts, axis=0):
+    array = own if first is None else first
+    return Rider(array, sds(4, *own.shape, dtype=own.dtype), CtxGather, scratch)
+
+
+def ctx_scatter(parts, axis=0, first=None):
     shape = parts.shape[:axis] + parts.shape[axis + 1 :]
 
     def pick(ref, slot):
@@ -524,7 +566,8 @@
 
     buffer = pltpu.VMEM(shape, parts.dtype)
     scratch = [dma(3), dma(3), dma(3), buffer, buffer, buffer, buffer]
-    return Rider(parts, sds(3, *shape, dtype=parts.dtype), functools.partial(CtxScatter, pick), scratch)
+    array = parts if first is None else first
+    return Rider(array, sds(3, *shape, dtype=parts.dtype), functools.partial(CtxScatter, pick), scratch)
 
 
 def flipped_place(c, t):
@@ -573,23 +616,65 @@
     return copies_rider(parts, sds(*parts.shape, dtype=parts.dtype), 4 * size - 1, parts.shape[2:], make)
 
 
-def all_gather(own, size):
-    others = [(kt, kc, kf) for kt in (2, 3, 1, 0) for kc in (2, 3, 1, 0) for kf in range(size)][:-size] + [
-        (0, 0, kf) for kf in range(1, size)
+class SmallSum:
+    def __init__(self, source, target, place, scratch):
+        self.source, self.target = source, target
+        self.f, self.c, self.t = place
+        self.size = target.shape[1]
+        self.send, self.recv, self.on_send, self.on_recv, self.leg, self.terms, self.total = scratch
+
+    def greetings(self):
+        around = [({"ctx": (self.c + 4 - k) % 4}, None, 1) for k in (1, 2, 3)]
+        return around + [
+            ({"fsdp": (self.f + self.size - kf) % self.size, "tp": (self.t + 4 - kt) % 4}, None, 1)
+            for kt, kf in plane(self.size)
+        ]
+
+    def first(self, k):
+        device = {"ctx": (self.c + k) % 4}
+        return rcopy(self.source, self.terms.at[self.c], self.send.at[k - 1], self.recv.at[k - 1], device)
+
+    def own(self):
+        return pltpu.make_async_copy(self.source, self.terms.at[self.c], self.leg.at[0])
+
+    def second(self, number):
+        kt, kf = plane(self.size)[number]
+        device = {"fsdp": (self.f + kf) % self.size, "tp": (self.t + kt) % 4}
+        target = self.target.at[self.t, self.f]
+        return rcopy(self.total, target, self.on_send.at[number], self.on_recv.at[number], device)
+
+    def stays(self):
+        return pltpu.make_async_copy(self.total, self.target.at[self.t, self.f], self.leg.at[1])
+
+    def start(self):
+        for k in (2, 3, 1):
+            self.first(k).start()
+        self.own().start()
+
+    def turn(self):
+        self.own().wait()
+        for k in (1, 2, 3):
+            self.first(k).wait_recv()
+        self.total[...] = self.terms[0] + self.terms[1] + self.terms[2] + self.terms[3]
+        for number in range(4 * self.size - 1):
+            self.second(number).start()
+        self.stays().start()
+
+    def finish(self):
+        for k in (1, 2, 3):
+            self.first(k).wait_send()
+        for number in range(4 * self.size - 1):
+            self.second(number).wait()
+        self.stays().wait()
+
+
+def small_sum(own, size):
+    many = 4 * size - 1
+    scratch = [
+        dma(3), dma(3), dma(many), dma(many), dma(2),
+        pltpu.VMEM((4, *own.shape), own.dtype), pltpu.VMEM(own.shape, own.dtype),
     ]
-
-    def make(source, target, f, c, t):
-        steps = [
-            (
-                {"fsdp": (f + kf) % size, "ctx": (c + kc) % 4, "tp": (t + kt) % 4},
-                {"fsdp": (f + size - kf) % size, "ctx": (c + 4 - kc) % 4, "tp": (t + 4 - kt) % 4},
-                source, target.at[c, t, f], None, 1,
-            )
-            for kt, kc, kf in others
-        ]
-        return steps, (source, target.at[c, t, f], None)
-
-    return copies_rider(own, sds(4, 4, size, *own.shape, dtype=own.dtype), 16 * size - 1, own.shape, make)
+    return Rider(own, sds(4, size, *own.shape, dtype=own.dtype), SmallSum, scratch)
 
 
 def carry_kernel(ride):
@@ -607,16 +692,21 @@
     return jax.ShapeDtypeStruct(shape, dtype)
 
 
-def project_kernel(
-    fetch, ride, x_ref, w_ref, b_ref, xg_ref, qw_ref, kv_ref, *rest
+FAR = 1e30
+
+
+def inner_kernel(
+    fetch, ride, flag_ref, x_ref, w_ref, b_ref, xg_ref, qw_ref, kv_ref, o_ref, lse_ref, *rest
 ):
     if fetch:
         full_ref, w_send, w_recv, *rest = rest
     (
-        qbuf, x_recv, x_right, x_left, k1_send, k1_recv, k2_send, k2_recv, kf_send, kf_recv, q_send, q_recv,
+        qbuf, qm_ref, m_ref, acc_ref, vt_ref, x_recv, x_right, x_left,
+        k1_send, k1_recv, k2_send, k2_recv, kf_send, kf_recv, q_send, q_recv,
     ) = rest
     c = lax.axis_index("ctx")
     t = lax.axis_index("tp")
+    f, size = lax.axis_index("fsdp"), lax.axis_size("fsdp")
     barrier = pltpu.get_barrier_semaphore()
     for device in (mate_of(c), across_of(c), 3 - c):
         signal(barrier, {"ctx": device})
@@ -629,12 +719,14 @@
     def _():
         signal(barrier, {"tp": t + 1})
 
-    f, size = lax.axis_index("fsdp"), lax.axis_size("fsdp")
     if fetch:
         for k in range(1, size):
             signal(barrier, {"fsdp": (f + size - k) % size})
     ends = (t // 3) + (3 - t) // 3
     count = 5 - ends + ride.greet(barrier) + (size - 1 if fetch else 0)
+    m_ref[...] = jnp.full_like(m_ref, MASKED)
+    acc_ref[...] = jnp.zeros_like(acc_ref)
+    vt_ref[:, :, :, 128:144] = jnp.ones((4, 4, 2, 16, 256), BF16)
     ride.ready()
     pl.semaphore_wait(barrier, count)
 
@@ -663,51 +755,34 @@
         for k in range(1, size):
             weight(k).start()
         full_ref[f] = w_ref[...]
+    xg_ref[t] = x_ref[...]
+    ride.start()
+    if fetch:
         for k in range(1, size):
             weight(k).wait_recv()
-    ride.start()
 
     def mate(chunk):
-        return rcopy(kv_ref.at[c, chunk], kv_ref.at[c, chunk], k1_send.at[chunk], k1_recv.at[chunk], {"ctx": mate_of(c)})
+        part = kv_ref.at[c, chunk]
+        return rcopy(part, part, k1_send.at[chunk], k1_recv.at[chunk], {"ctx": mate_of(c)})
 
     def across(chunk):
-        return rcopy(kv_ref.at[c, chunk], kv_ref.at[c, chunk], k2_send.at[chunk], k2_recv.at[chunk], {"ctx": across_of(c)})
+        part = kv_ref.at[c, chunk]
+        return rcopy(part, part, k2_send.at[chunk], k2_recv.at[chunk], {"ctx": across_of(c)})
 
     def onward(chunk):
-        return rcopy(
-            kv_ref.at[across_of(c), chunk], kv_ref.at[across_of(c), chunk], kf_send.at[chunk], kf_recv.at[chunk], {"ctx": mate_of(c)}
-        )
+        part = kv_ref.at[across_of(c), chunk]
+        return rcopy(part, part, kf_send.at[chunk], kf_recv.at[chunk], {"ctx": mate_of(c)})
 
     def partner(slot):
         return rcopy(qbuf.at[slot], qw_ref.at[2 * slot + 1], q_send.at[slot], q_recv.at[slot], {"ctx": 3 - c})
 
-    for step in range(4):
-        if step == 0:
-            xg_ref[t] = x_ref[...]
-        else:
-
-            @pl.when(t - step >= 0)
-            def _():
-                arrived(t - step)
-
-                @pl.when(t < 3)
-                def _():
-                    right(xg_ref.at[t - step], t - step, step).start()
-
-            @pl.when(t + step <= 3)
-            def _():
-                arrived(t + step)
-
-                @pl.when(t > 0)
-                def _():
-                    left(xg_ref.at[t + step], t + step, step).start()
-
+    def project(step):
         chunk = ordered(t, step)
         w = full_ref[...].reshape(768, 640) if fetch else w_ref[...]
         made = mm(xg_ref[chunk], w) + b_ref[...]
         kv_ref[c, chunk] = made[:, 256:].astype(BF16)
+        across(chunk).start()
         mate(chunk).start()
-        across(chunk).start()
         query = (made[:, :256] * 0.125).astype(BF16)
 
         @pl.when(chunk % 2 == 0)
@@ -719,21 +794,124 @@
             qbuf[chunk // 2] = query
             partner(chunk // 2).start()
 
-        if step >= 1:
-            before = ordered(t, step - 1)
-            across(before).wait_recv()
-            onward(before).start()
-    ride.put(xg_ref)
+    low = lax.broadcasted_iota(jnp.int32, (256, 128), 1) < 64
+
+    def complete(step):
+        chunk = ordered(t, step)
+        across(chunk).wait_recv()
+        onward(chunk).start()
+        mate(chunk).wait_recv()
+
+        @pl.when(chunk % 2 == 1)
+        def _():
+            partner(chunk // 2).wait_recv()
+
+        pair = qw_ref[chunk, :, 0:128]
+        none = jnp.zeros_like(pair)
+        qm_ref[0, chunk] = jnp.where(low, pair, none)
+        qm_ref[1, chunk] = jnp.where(low, none, pair)
+        qm_ref[2, chunk] = qw_ref[chunk, :, 128:256]
+        onward(chunk).wait_recv()
+        for segment in range(4):
+            vt_ref[segment, chunk, 0, 0:128] = jnp.transpose(kv_ref[segment, chunk, :, 256:384], (1, 0))
+            vt_ref[segment, chunk, 1, 0:128] = jnp.transpose(kv_ref[segment, chunk, :, 128:256], (1, 0))
+
+    def items(step):
+        @pl.loop(step * step, (step + 1) * (step + 1))
+        def _(item):
+            number = item - step * step
+            second = number // (step + 1)
+            query_at = ordered_by(t, step + second * (number - 2 * step - 1))
+            key_at = ordered_by(t, number + second * (step - number))
+            half = query_at % 2
+
+            def visit(segments):
+                seen = [flag_ref[half, segment] > 0 for segment in segments]
+                far = [jnp.where(one, 0.0, FAR) for one in seen]
+                scores, most, made = [], [], []
+                for head in range(3):
+                    query, at = qm_ref[head, query_at], 128 * (head // 2)
+                    rows = [mm_nt(kv_ref[segment, key_at, :, at : at + 128], query) for segment in segments]
+                    new = m_ref[query_at, head : head + 1]
+                    for one, row in zip(seen, rows):
+                        new = jnp.maximum(new, jnp.where(one, jnp.max(row, axis=0, keepdims=True), MASKED))
+                    scores.append(rows)
+                    most.append(new)
+                for head in range(3):
+                    total = acc_ref[query_at, head] * jnp.exp(m_ref[query_at, head : head + 1] - most[head])
+                    for segment, row, off in zip(segments, scores[head], far):
+                        probs = jnp.exp(row - (most[head] + off)).astype(BF16)
+                        total += mm(vt_ref[segment, key_at, head // 2], probs)
+                    made.append(total)
+                for head in range(3):
+                    m_ref[query_at, head : head + 1] = most[head]
+                    acc_ref[query_at, head] = made[head]
+
+            length = c + 1 + half * (3 - 2 * c)
+
+            @pl.loop(0, length // 2)
+            def _(two):
+                visit((2 * two, 2 * two + 1))
+
+            @pl.when(length % 2 == 1)
+            def _():
+                visit((length - 1,))
+
+            if step == 3:
+                for n in range(1, len(ride.hops)):
+                    pl.when(item == 9 + 2 * n)(functools.partial(ride.one_hop, n))
+
+    project(0)
+    for step in range(1, 4):
+
+        @pl.when(t - step >= 0)
+        def _():
+            arrived(t - step)
+
+            @pl.when(t < 3)
+            def _():
+                right(xg_ref.at[t - step], t - step, step).start()
+
+        @pl.when(t + step <= 3)
+        def _():
+            arrived(t + step)
+
+            @pl.when(t > 0)
+            def _():
+                left(xg_ref.at[t + step], t + step, step).start()
+
+        project(step)
+        if step == 2:
+            ride.turn()
+        if step == 3:
+            ride.start_late()
+            ride.chain()
+            ride.put(xg_ref)
+        complete(step - 1)
+        items(step - 1)
+    complete(3)
+    if ride.hops:
+        ride.one_hop(0)
     ride.turn()
-    last = ordered(t, 3)
-    across(last).wait_recv()
-    onward(last).start()
+    ride.chain_turn()
+    ride.put(qw_ref, kv_ref)
+    items(3)
+    for quarter in range(4):
+        whole = [acc_ref[quarter, head, 128:129] for head in range(3)]
+        parts = [acc_ref[quarter, head, 0:128] / whole[head] for head in range(3)]
+        pair = jnp.concatenate([parts[0][0:64], parts[1][64:128]], axis=0)
+        o_ref[quarter, :, 0:128] = jnp.transpose(pair, (1, 0)).astype(BF16)
+        o_ref[quarter, :, 128:192] = jnp.transpose(parts[2], (1, 0))[:, :64].astype(BF16)
+        for head in range(3):
+            lse_ref[quarter, head : head + 1] = m_ref[quarter, head : head + 1] + jnp.log(whole[head])
+        lse_ref[quarter, 3:8] = jnp.zeros((5, 256), F32)
+    ride.put(o_ref, lse_ref)
     for chunk in range(4):
-        mate(chunk).wait()
+        mate(chunk).wait_send()
         across(chunk).wait_send()
-        onward(chunk).wait()
+        onward(chunk).wait_send()
     for slot in range(2):
-        partner(slot).wait()
+        partner(slot).wait_send()
 
     @pl.when(t < 3)
     def _():
@@ -759,10 +937,14 @@
     ride.finish()
 
 
-def project(x, w, b, cid, riders=(), fetch=False):
-    outs = [sds(4, 256, 768), sds(4, 256, 256), sds(4, 4, 256, 384)]
+def inner(x, w, b, flags, cid, riders=(), fetch=False):
+    outs = [
+        sds(4, 256, 768), sds(4, 256, 256), sds(4, 4, 256, 384), sds(4, 256, 192), sds(4, 8, 256, dtype=F32),
+    ]
     scratch = [
         pltpu.VMEM((2, 256, 256), BF16),
+        pltpu.VMEM((3, 4, 256, 128), BF16), pltpu.VMEM((4, 8, 256), F32), pltpu.VMEM((4, 3, 144, 256), F32),
+        pltpu.VMEM((4, 4, 2, 144, 256), BF16),
         dma(4), dma(3), dma(3),
         dma(4), dma(4), dma(4), dma(4), dma(4), dma(4), dma(2), dma(2),
     ]
@@ -770,12 +952,15 @@
         size = lax.axis_size("fsdp")
         outs.append(sds(size, *w.shape))
         scratch = [dma(size - 1), dma(size - 1)] + scratch
-    cost = (2 * 1024 * 768 * 640, 8 << 20, 0)
-    kernel = functools.partial(project_kernel, fetch)
-    res, ridden = call(kernel, (x, w, b), outs, scratch, cid, "project", cost, riders)
-    xg, qw, kv = res[:3]
-    full = res[3].reshape(768, 640) if fetch else w
-    return xg.reshape(1024, 768), qw.reshape(1024, 256), kv.reshape(4, 1024, 384), full, ridden
+    cost = (2 * 1024 * 768 * 640 + 5 * 512 * 1024 * 64 * 12, 14 << 20, 5 * 512 * 1024 * 3)
+    kernel = functools.partial(inner_kernel, fetch)
+    res, ridden = call(kernel, (flags, x, w, b), outs, scratch, cid, "inner", cost, riders, smem=(0,))
+    full = res[5].reshape(768, 640) if fetch else w
+    xg, qw, kv, o, lse = res[:5]
+    return (
+        xg.reshape(1024, 768), qw.reshape(1024, 256), kv.reshape(4, 1024, 384),
+        o.reshape(1024, 192), lse, full, ridden,
+    )
 
 
 def norm_stats(summed):
@@ -797,84 +982,6 @@
     phi = 0.5 * (1.0 + lax.erf(up * 0.7071067811865476))
     slope = phi + up * jnp.exp(-0.5 * up * up) * 0.3989422804014327
     return (up * phi).astype(BF16), slope.astype(BF16)
-
-
-Q_TILE = 256
-FAR = 1e30
-
-
-def open_up(ride):
-    if ride.rides:
-        barrier = pltpu.get_barrier_semaphore()
-        count = ride.greet(barrier)
-        pl.semaphore_wait(barrier, count)
-        ride.start()
-    ride.ready()
-
-
-def attend_kernel(ride, flag_ref, qw_ref, kv_ref, o_ref, lse_ref, qm_ref, m_ref, acc_ref, vo_ref):
-    c = lax.axis_index("ctx")
-    open_up(ride)
-    low = lax.broadcasted_iota(jnp.int32, (Q_TILE, 128), 1) < 64
-    for side, at in enumerate((128, 256)):
-        vo_ref[side, :, 0:128] = kv_ref[:, at : at + 128]
-        vo_ref[side, :, 128:256] = jnp.ones((4096, 128), BF16)
-
-    @pl.loop(0, 1024 // Q_TILE)
-    def _(tile):
-        half = tile % 2
-        segment = c + half * (3 - 2 * c)
-        rows = pl.ds(pl.multiple_of(tile * Q_TILE, Q_TILE), Q_TILE)
-        pair = qw_ref[rows, 0:128]
-        qm_ref[0] = jnp.where(low, pair, jnp.zeros_like(pair))
-        qm_ref[1] = jnp.where(low, jnp.zeros_like(pair), pair)
-        qm_ref[2] = qw_ref[rows, 128:256]
-        m_ref[...] = jnp.full_like(m_ref, MASKED)
-        acc_ref[...] = jnp.zeros_like(acc_ref)
-
-        @pl.loop(0, segment + 1)
-        def _(block):
-            seen = flag_ref[half, block] > 0
-            penalty = jnp.where(seen, 0.0, FAR)
-            keys = pl.ds(pl.multiple_of(block * 1024, 1024), 1024)
-            for head in range(3):
-                k_at = 0 if head < 2 else 128
-                scores = mm_nt(qm_ref[head], kv_ref[keys, k_at : k_at + 128])
-                old = m_ref[head]
-                most = jnp.max(scores, axis=-1, keepdims=True)
-                new = jnp.maximum(old, jnp.where(seen, most, MASKED))
-                probs = jnp.exp(scores - (new + penalty)).astype(BF16)
-                keep = jnp.exp(old - new)
-                m_ref[head] = new
-                acc_ref[head] = acc_ref[head] * keep + mm(probs, vo_ref[1 if head < 2 else 0, keys])
-
-        whole = [acc_ref[head][:, 128:256] for head in range(3)]
-        first = acc_ref[0][:, 0:128] / whole[0]
-        second = acc_ref[1][:, 0:128] / whole[1]
-        o_ref[rows, 0:128] = jnp.where(low, first, second).astype(BF16)
-        o_ref[rows, 128:192] = (acc_ref[2][:, 0:128] / whole[2])[:, :64].astype(BF16)
-        lane = lax.broadcasted_iota(jnp.int32, (Q_TILE, 128), 1)
-        totals = [m_ref[head] + jnp.log(whole[head]) for head in range(3)]
-        lse_ref[rows, :] = jnp.where(lane == 0, totals[0], jnp.where(lane == 1, totals[1], totals[2]))
-        ride.hop(tile)
-        ride.turn_when(tile == 2)
-
-    ride.finish()
-
-
-def attend(qw, kv, flags, cid, riders=()):
-    outs = [sds(1024, 192), sds(1024, 128, dtype=F32)]
-    scratch = [
-        pltpu.VMEM((3, Q_TILE, 128), BF16),
-        pltpu.VMEM((3, Q_TILE, 1), F32),
-        pltpu.VMEM((3, Q_TILE, 256), F32),
-        pltpu.VMEM((2, 4096, 256), BF16),
-    ]
-    cost = (5 * 512 * 1024 * 64 * 4 * 3, 6 << 20, 5 * 512 * 1024 * 3)
-    operands = (flags, qw, kv.reshape(4096, 384))
-    cid = cid if riders else None
-    res, ridden = call(attend_kernel, operands, outs, scratch, cid, "attend", cost, riders, smem=(0,))
-    return res[0], res[1], ridden
 
 
 PIECE = 128
@@ -1229,13 +1336,6 @@
     return back, do.reshape(1024, 192), stats, d_up, d_down, d_out, ridden
 
 
-def ordered_by(place, step):
-    half = place // 2
-    inner = place + half * (3 - 2 * place)
-    chunk = step + inner * (1 - 2 * step) * ((3 - step) // 2)
-    return chunk + half * (3 - 2 * chunk)
-
-
 def inner_back_kernel(
     ride, flag_ref, qw_ref, kv_ref, do_ref, o_ref, lse_ref, w_ref, back_ref, xg_ref, mark_ref,
     grad_ref, low_ref, din_ref, sum_out_ref, mem_ref,
@@ -1277,7 +1377,6 @@
     dm_ref[0] = jnp.where(low, pair, none)
     dm_ref[1] = jnp.where(low, none, pair)
     dm_ref[2] = jnp.concatenate([do_ref[:, 128:192], none[:, :64]], axis=1)
-    turned = jnp.transpose(lse_ref[...], (1, 0))
     product = do_ref[...].astype(F32) * o_ref[...].astype(F32)
     head_row = lax.broadcasted_iota(jnp.int32, (8, 192), 0)
     head_of = lax.broadcasted_iota(jnp.int32, (8, 192), 1) // 64
@@ -1286,7 +1385,7 @@
         precision=lax.Precision.HIGHEST, preferred_element_type=F32,
     )
     for quarter in range(4):
-        row_ref[quarter, 0:8] = turned[0:8, quarter * 256 : (quarter + 1) * 256]
+        row_ref[quarter, 0:8] = lse_ref[quarter]
         row_ref[quarter, 8:16] = delta[:, quarter * 256 : (quarter + 1) * 256]
     acc_ref[...] = jnp.zeros_like(acc_ref)
     wide_ref[...] = jnp.zeros_like(wide_ref)
@@ -1452,7 +1551,7 @@
 
         for n in range(len(ride.hops)):
             once(RIDE_HOPS[n], ride.one_hop, n)
-        ride.turn_when((done < 16) & (now >= 16))
+        ride.turn_when((done < 14) & (now >= 14))
         for k, place in enumerate((6, 11, 14)):
             at(place, leave, k)
         once(24, go_across, 0)
@@ -1499,10 +1598,12 @@
         for k in range(1, size):
             term(k, span).start()
 
+    ride.chain()
     relay_inner(2)
     sum_out_ref[0:1, 0:256] = jnp.sum(query.astype(F32), axis=0, keepdims=True)
     sum_out_ref[0:1, 256:640] = jnp.sum(own.astype(F32), axis=0, keepdims=True)
     ride.put(sum_out_ref)
+    ride.chain_turn()
     grad_ref[...] = part_ref[t] + back_ref[...]
 
     @pl.when(t < 3)
@@ -1546,7 +1647,7 @@
     ride.finish()
 
 
-RIDE_HOPS = (10, 14)
+RIDE_HOPS = (8, 11, 14, 17)
 
 
 def inner_back(qw, kv, do, o, lse, flags, w, back_one, xg, marks, cid, riders=()):
@@ -1647,23 +1748,14 @@
 
     saved, weights = [], []
     rounded = low(stream)
-    riders = [plane_gather(out_piece[0], size), tp_flip(ffn_bias)]
-    xg, qw, kv, w_in, (out, units) = project(
-        rounded, own_in[0], in_bias[0][None], 0, riders, fetch=True
-    )
+    riders = [plane_gather(out_piece[0], size), ctx_gather(sds(4, size, piece, 192), first=0)]
+    riders += [flip_gather(w1[0], size).later(), tp_flip(down_turned[0]).later(hopped=True), tp_flip(ffn_bias)]
+    xg, qw, kv, o, lse, w_in, got = inner(rounded, own_in[0], in_bias[0][None], flags, 0, riders, fetch=True)
+    _, out, w_up, down, units = got
     for n in range(layers):
         last = n == layers - 1
-        riders = [ctx_gather(out)]
-        if n == 0:
-            riders += [flip_gather(w1[0], size)]
-        riders += [tp_flip(down_turned[n])]
-        if n == 0:
-            riders[-1].after()
-        o, lse, got = attend(qw, kv, flags, 16 * n + 1, riders)
-        w_out = out_whole(got[0])
-        if n == 0:
-            w_up = got[1]
-        w_up, down = w_up.reshape(768, 768), got[-1]
+        w_out = out_whole(out)
+        w_up = w_up.reshape(768, 768)
         vecs = vectors(n)
         riders = []
         if not last:
@@ -1678,8 +1770,9 @@
         saved.append((xg, qw, kv, o, lse, xhat1, r1, xhat2, r2, xg2, act, slope, rows))
         if not last:
             up, out, w_in = got
-            xg, qw, kv, w_in, (w_up,) = project(
-                rounded, w_in.reshape(768, 640), in_bias[n + 1][None], 16 * n + 16, [fsdp_gather(up, size)]
+            riders = [ctx_gather(out), tp_flip(down_turned[n + 1]).later(), fsdp_gather(up, size)]
+            xg, qw, kv, o, lse, w_in, (out, down, w_up) = inner(
+                rounded, w_in.reshape(768, 640), in_bias[n + 1][None], flags, 16 * n + 16, riders
             )
     output = rounded
 
@@ -1692,25 +1785,29 @@
         xg, qw, kv, o, lse, xhat1, r1, xhat2, r2, xg2, act, slope, rows = saved[n]
         riders = []
         if above is not None:
-            riders = [plane_scatter(above["out"], size)]
-            riders += [ctx_scatter(above[part]) for part in ("up", "down", "in")]
+            riders = [plane_scatter(above["out"], size), ctx_scatter(above["in"])]
         back_one, do, small[n], d_up, d_down, d_out, got = block_back(
             grad, xhat2, r2, xhat1, r1, vecs, slope, w_up, w_down, w_out, xg2, act, rows, 16 * n + 3, riders
         )
-        d_down = d_down.reshape(1, size, 2, depth // 2, 768)
-        riders = [tp_flip(d_up), scatter_flip(d_down), ctx_scatter(d_out.reshape(4, size, 4, piece, 192), axis=2)]
+        quarters = sds(4, depth // 4, 768)
+        riders = [
+            tp_flip(d_up.reshape(quarters.shape)), scatter_flip(d_down.reshape(size, *quarters.shape)),
+            ctx_scatter(d_out.reshape(4, size, 4, piece, 192), axis=2),
+            ctx_scatter(quarters, first=0), ctx_scatter(quarters, first=1),
+        ]
         if above is not None:
-            riders += [ctx_gather(low(added(got[0], (0, 1))))] + [ctx_gather(low(added(part))) for part in got[1:]]
+            gathered = (added(got[0], (0, 1)), above["up"], above["down"], added(got[1]))
+            riders += [ctx_gather(low(part)) for part in gathered]
         grad, low_grad, d_in, sums, memory_part, got = inner_back(
             qw, kv, do, o, lse, flags, w_in, back_one, xg, marks, 16 * n + 4, riders
         )
         if above is not None:
-            done[n + 1] = (got[6], got[3], got[4], got[5])
+            done[n + 1] = (got[8], got[5], got[6], got[7])
         d_query_bias, _, d_value_bias = parted(sums)
         heads[n] = jnp.stack([d_query_bias, d_value_bias])
         above = {
-            "up": got[0].reshape(4, depth // 4, 768),
-            "down": got[1].reshape(4, depth // 4, 768),
+            "up": low(added(got[3])),
+            "down": low(added(got[4])),
             "in": d_in.reshape(4, depth // 4, 640),
             "out": low(added(got[2])),
         }
@@ -1727,13 +1824,12 @@
     rest = jnp.zeros((width * slices - filled, 768), F32)
     sums = jnp.concatenate([stat_rows, unit_rows, head_rows, memory_part, rest])
     sums = sums.reshape(4, size, width, 768)
-    riders = [ctx_scatter(above[part]) for part in ("up", "down", "in")]
-    got = carry(riders + [plane_scatter(above["out"], size), plane_scatter(sums, size)], 6)
-    up0, down0, in0 = (ctx_gather(low(added(part))) for part in got[:3])
-    out0 = ctx_gather(low(added(got[3], (0, 1))))
-    got = carry([up0, down0, in0, out0, all_gather(added(got[4], (0, 1)), size)], 7)
-    done[0] = (got[2], got[3], got[0], got[1])
-    totals = added(got[4]).reshape(width * slices, 768)
+    riders = [ctx_scatter(above["in"]), plane_scatter(above["out"], size), plane_scatter(sums, size)]
+    got = carry(riders, 6)
+    parts = (low(added(got[0])), low(added(got[1], (0, 1))), above["up"], above["down"])
+    got = carry([ctx_gather(part) for part in parts] + [small_sum(added(got[2], (0, 1)), size)], 7)
+    done[0] = got[:4]
+    totals = got[4].reshape(width * slices, 768)
     stats = totals[: 6 * layers].reshape(layers, 6, 768)
     at = 6 * layers
     ffn_rows = totals[at : at + 4 * layers].reshape(layers, 4, 768)

time: 560 us -> 529 us (0.945)
  Pallas kernels: 494 us -> 463 us
    pallas_call x12 -> x10, Pallas kernels: 494 us -> 463 us  [call(): pl.pallas_call(body, out_shape=list(out_shapes) + [rider.out for rider in...]
    reduce_sum x12 -> x11, other arithmetic: 18.7 us -> 14.2 us  [added(): return jnp.sum(terms.astype(F32), axis=axes)]
where the time goes in v5:
time: 529 us; the launch traced here: 521 us
  Pallas kernels  463 us (88%)
  local copies, waits for them, and re-layouts  26 us (5%)
  other arithmetic  24.8 us (5%)
    pallas_call x10, Pallas kernels, call(): pl.pallas_call(body, out_shape=list(out_shapes) + [rider.out for rider in...  463 us
    reduce_sum x11, other arithmetic, added(): return jnp.sum(terms.astype(F32), axis=axes)  14.2 us

profile of v5, /device:TPU:0, one launch (start us, length us, event | category | flops | bytes accessed | tf_op | source)
XLA Modules:
  0.0 520.9 jit_solution(11459490778112434615)
XLA Ops:
  0.7 0.9 fusion.4
  1.6 0.8 fusion.3
  2.5 0.9 multiply_reduce_fusion.3
  3.9 2.6 fusion.13
  8.4 1.0 slice_bitcast_fusion.3
  10.2 1.2 copy.56
  12.1 1.1 slice_bitcast_fusion.2
  13.8 1.1 slice_bitcast_fusion
  14.9 71.2 %inner.2 = (bf16[4,256,768]{2,1,0:T(8,128)(2,1)}, bf16[4,256,256]{2,1,0:T(8,128)(2,1)}, bf16[4,4,256,384]{3,2,1,0:T(8,128)(2,1)}, bf16[4,256,192]{2,1,0:T(8,128)...) custom-call(s32[2,4]{1,0:T(2,128)} %pad_add_fusion.refs_0_, ...), custom_call_target="tpu_custom_call" | custom-call | flops 3019898880 | bytes 14680064 | tf_op jit(solution)/shard_map/inner/pallas_call | solution.py:490
  86.1 2.7 copy.58
  90.1 43.8 %block.2 = (f32[256,768]{1,0:T(8,128)}, bf16[256,768]{1,0:T(8,128)(2,1)}, f32[256,768]{1,0:T(8,128)}, f32[256,128]{1,0:T(8,128)}, f32[256,768]{1,0:T(8,128)}, /*...) custom-call(bf16[4,256,192]{2,1,0:T(8,128)(2,1)} %get-tuple-element., ...), custom_call_target="tpu_custom_call" | custom-call | flops 2717908992 | bytes 16777216 | tf_op jit(solution)/shard_map/block/pallas_call | solution.py:490
  133.9 50.8 %inner.3 = (bf16[4,256,768]{2,1,0:T(8,128)(2,1)}, bf16[4,256,256]{2,1,0:T(8,128)(2,1)}, bf16[4,4,256,384]{3,2,1,0:T(8,128)(2,1)}, bf16[4,256,192]{2,1,0:T(8,128)...) custom-call(s32[2,4]{1,0:T(2,128)} %pad_add_fusion.refs_0_, ...), custom_call_target="tpu_custom_call" | custom-call | flops 3019898880 | bytes 14680064 | tf_op jit(solution)/shard_map/inner/pallas_call | solution.py:490
  184.7 2.7 copy.59
  188.0 39.3 %block.3 = (f32[256,768]{1,0:T(8,128)}, bf16[256,768]{1,0:T(8,128)(2,1)}, f32[256,768]{1,0:T(8,128)}, f32[256,128]{1,0:T(8,128)}, f32[256,768]{1,0:T(8,128)}, /*...) custom-call(bf16[4,256,192]{2,1,0:T(8,128)(2,1)} %get-tuple-element., ...), custom_call_target="tpu_custom_call" | custom-call | flops 2717908992 | bytes 16777216 | tf_op jit(solution)/shard_map/block/pallas_call | solution.py:490
  227.3 1.0 convert_element_type.85.refs_0_
  228.3 37.1 %block_back.2 = (f32[256,768]{1,0:T(8,128)}, bf16[4,256,192]{2,1,0:T(8,128)(2,1)}, f32[8,768]{1,0:T(8,128)}, bf16[384,768]{1,0:T(8,128)(2,1)}, bf16[768,768]{1,0:T(8,128)(2,1)}, /*index=5*/bf16[4,768,192]{2,1,0:T(8,128)(2,1)}) custom-call(f32[256,768]{1,0:T(8,128)} %convert_element_type.85.refs_0_, f32[256,768]{1,0:T(8,128)} %get-tuple-element.114.refs_1_, ...), custom_call_target="tpu_custom_call" | custom-call | flops 5435817984 | bytes 20971520 | tf_op jit(solution)/shard_map/block_back/pallas_call | solution.py:490
  265.4 0.8 compare_convert_fusion.refs_9_
  266.2 72.5 %inner_back.2 = (f32[256,768]{1,0:T(8,128)}, bf16[256,768]{1,0:T(8,128)(2,1)}, bf16[384,640]{1,0:T(8,128)(2,1)}, f32[8,640]{1,0:T(8,128)}, f32[20,768]{1,0:T(8,1...) custom-call(s32[2,4]{1,0:T(2,128)} %pad_add_fusion.refs_0_, ...), custom_call_target="tpu_custom_call" | custom-call | flops 7046430720 | bytes 16777216 | tf_op jit(solution)/shard_map/inner_back/pallas_call | solution.py:490
  338.7 2.3 reduce_sum.167.refs_13_
  341.1 37.7 %block_back.3 = (f32[256,768]{1,0:T(8,128)}, bf16[4,256,192]{2,1,0:T(8,128)(2,1)}, f32[8,768]{1,0:T(8,128)}, bf16[384,768]{1,0:T(8,128)(2,1)}, bf16[768,768]{1,0...) custom-call(f32[256,768]{1,0:T(8,128)} %get-tuple-element.130.refs_0_, ...), custom_call_target="tpu_custom_call" | custom-call | flops 5435817984 | bytes 20971520 | tf_op jit(solution)/shard_map/block_back/pallas_call | solution.py:490
  378.8 1.7 reduce_sum.168.refs_13_
  380.6 0.7 reduce_sum.169.refs_14_
  381.3 0.7 reduce_sum.170.refs_15_
  382.1 0.7 reduce_sum.171.refs_16_
  382.8 69.6 %inner_back.3 = (f32[256,768]{1,0:T(8,128)}, bf16[256,768]{1,0:T(8,128)(2,1)}, bf16[384,640]{1,0:T(8,128)(2,1)}, f32[8,640]{1,0:T(8,128)}, f32[20,768]{1,0:T(8,1...) custom-call(s32[2,4]{1,0:T(2,128)} %pad_add_fusion.refs_0_, ...), custom_call_target="tpu_custom_call" | custom-call | flops 7046430720 | bytes 16777216 | tf_op jit(solution)/shard_map/inner_back/pallas_call | solution.py:490
  452.4 2.3 reduce_sum.172.refs_1_
  455.1 0.7 slice_bitcast_fusion.18
  455.8 0.7 slice_bitcast_fusion.19
  456.5 0.8 slice_bitcast_fusion.22
  457.3 0.7 slice_bitcast_fusion.23
  458.5 0.7 reshape.227.refs_2_
  459.2 18.9 %carry.2 = (bf16[3,96,640]{2,1,0:T(8,128)(2,1)}, bf16[4,2,96,192]{3,2,1,0:T(8,128)(2,1)}, f32[4,2,6,768]{3,2,1,0:T(8,128)}) custom-call(bf16[4,96,640]{2,1,0:T(8,128)(2,1)} %bitcast.148, bf16[4,2,96,192]{3,2,1,0:T(8,128)(2,1)} %reduce_sum.172.refs_1_, f32[4,2,6,768]{3,2,1,0:T(8,128)} %reshape.227.refs_2_), custom_call_target="tpu_custom_call" | custom-call | flops 1048576 | bytes 1048576 | tf_op jit(solution)/shard_map/carry/pallas_call | solution.py:490
  478.1 1.8 reduce_sum.173.refs_0_
  479.9 1.7 reduce_sum.174.refs_1_
  481.6 0.7 reduce_sum.175.refs_2_
  482.3 0.7 reduce_sum.176.refs_3_
  483.7 22.3 %carry.3 = (bf16[4,96,640]{2,1,0:T(8,128)(2,1)}, bf16[4,96,192]{2,1,0:T(8,128)(2,1)}, bf16[4,96,768]{2,1,0:T(8,128)(2,1)}, bf16[4,96,768]{2,1,0:T(8,128)(2,1)}, f32[4,2,6,768]{3,2,1,0:T(8,128)}) custom-call(bf16[96,640]{1,0:T(8,128)(2,1)} %reduce_sum.173.refs_0_, bf16[96,192]{1,0:T(8,128)(2,1)} %reduce_sum.174.refs_1_, bf16[96,768]{1,0:T(8,128)(2,1)} %reduce_sum.175.refs_2_, ...), custom_call_target="tpu_custom_call" | custom-call | flops 1048576 | bytes 1048576 | tf_op jit(solution)/shard_map/carry/pallas_call | solution.py:490
  506.1 1.0 reshape.228
  508.5 0.9 pad_maximum_fusion
  509.4 0.9 pad_maximum_fusion.1
  510.3 0.9 pad_maximum_fusion.2
  511.6 0.9 maximum_convert_fusion.3
  512.4 1.6 maximum_convert_fusion
  514.7 1.6 maximum_convert_fusion.1
  517.0 0.7 multiply_reduce_fusion
  517.7 0.8 slice_bitcast_fusion.5
  519.1 0.7 copy.81
  519.9 0.7 copy.82
  (144 shorter events, 11.6 us)
Async XLA Ops:
  0.6 3.3 copy-start
  0.7 5.8 %slice-start = ((bf16[2,384,192]{1,2,0:T(8,128)(2,1)}), bf16[2,384,128]{1,2,0:T(8,128)(2,1)S(1)}, s32[]{:S(2)}) async-start(bf16[2,384,192]{1,2,0:T(8,128)(2,1)} %param.21), calls=%async_computation | async-start | bytes 393216 | tf_op jit(solution)/shard_map/slice | solution.py:1691
  0.7 6.0 %slice-start.1 = ((bf16[2,384,192]{1,2,0:T(8,128)(2,1)}), bf16[2,384,64]{1,2,0:T(8,128)(2,1)S(1)}, s32[]{:S(2)}) async-start(bf16[2,384,192]{1,2,0:T(8,128)(2,1)} %param.21), calls=%async_computation.1 | async-start | bytes 196608 | tf_op jit(solution)/shard_map/slice | solution.py:1691
  3.9 3.0 slice-start.2
  3.9 3.1 slice-start.4
  6.5 0.9 slice-start.3
  6.5 1.1 slice-start.5
  8.4 1.1 copy-start.28
  8.4 3.7 copy-start.2
  10.2 3.0 copy-start.3
  86.1 2.7 copy-start.27
  86.1 3.3 copy-start.24
  86.1 3.3 copy-start.25
  86.1 3.3 copy-start.26
  188.0 39.3 %copy-start.16 = (bf16[256,768]{1,0:T(8,128)(2,1)S(1)}, bf16[256,768]{1,0:T(8,128)(2,1)}, u32[]{:S(2)}) copy-start(bf16[256,768]{1,0:T(8,128)(2,1)} %param.17) | copy-start | bytes 1179652
  228.3 37.1 %copy-start.29 = (s32[1,1,20]{2,1,0:T(1,128)S(1)}, s32[1,1,20]{2,1,0:T(1,128)}, u32[]{:S(2)}) copy-start(s32[1,1,20]{2,1,0:T(1,128)} %param.18) | copy-start | bytes 244
  341.1 39.5 %copy-start.13 = (bf16[3,96,768]{2,1,0:T(8,128)(2,1)S(1)}, bf16[3,96,768]{2,1,0:T(8,128)(2,1)}, u32[]{:S(2)}) copy-start(bf16[3,96,768]{2,1,0:T(8,128)(2,1)} %get-tuple-element.151) | copy-start | bytes 1327108
  341.1 40.3 %copy-start.12 = (bf16[3,96,768]{2,1,0:T(8,128)(2,1)S(1)}, bf16[3,96,768]{2,1,0:T(8,128)(2,1)}, u32[]{:S(2)}) copy-start(bf16[3,96,768]{2,1,0:T(8,128)(2,1)} %get-tuple-element.152) | copy-start | bytes 1327108
  378.8 3.3 copy-start.17
  452.3 2.4 copy-start.21
  452.4 2.4 copy-start.22
  452.4 5.9 %copy-start.23 = (f32[20,768]{1,0:T(8,128)S(1)}, f32[20,768]{1,0:T(8,128)}, u32[]{:S(2)}) copy-start(f32[20,768]{1,0:T(8,128)} %get-tuple-element.161) | copy-start | bytes 184324
  454.8 26.8 %copy-start.11 = (bf16[3,96,768]{2,1,0:T(8,128)(2,1)S(1)}, bf16[3,96,768]{2,1,0:T(8,128)(2,1)}, u32[]{:S(2)}) copy-start(bf16[3,96,768]{2,1,0:T(8,128)(2,1)} %get-tuple-element.164) | copy-start | bytes 1327108
  458.3 24.0 %copy-start.10 = (bf16[3,96,768]{2,1,0:T(8,128)(2,1)S(1)}, bf16[3,96,768]{2,1,0:T(8,128)(2,1)}, u32[]{:S(2)}) copy-start(bf16[3,96,768]{2,1,0:T(8,128)(2,1)} %get-tuple-element.165) | copy-start | bytes 1327108
  478.1 5.0 copy-start.18
  478.1 29.6 %copy-start.8 = (bf16[4,96,640]{2,1,0:T(8,128)(2,1)S(1)}, bf16[4,96,640]{2,1,0:T(8,128)(2,1)}, u32[]{:S(2)}) copy-start(bf16[4,96,640]{2,1,0:T(8,128)(2,1)} %get-tuple-element.169) | copy-start | bytes 1474564
  506.0 1.9 copy-start.9
  510.2 0.9 copy-start.19
  510.2 1.2 copy-start.20
  510.2 2.2 copy-start.4
  510.3 2.2 copy-start.5
  512.4 1.6 copy-start.6
  512.4 1.9 copy-start.7
  514.6 4.5 copy-start.14
  514.6 5.2 %copy-start.15 = (bf16[256,768]{1,0:T(8,128)(2,1)S(1)}, bf16[256,768]{1,0:T(8,128)(2,1)}, u32[]{:S(2)}) copy-start(bf16[256,768]{1,0:T(8,128)(2,1)} %get-tuple-element.243) | copy-start | bytes 1179652
  514.6 6.0 %copy-start.1 = (f32[20,768]{1,0:T(8,128)S(1)}, f32[20,768]{1,0:T(8,128)}, u32[]{:S(2)}) copy-start(f32[20,768]{1,0:T(8,128)} %param.20) | copy-start | bytes 184324

commit v6 on v5

--- a/solution.py
+++ b/solution.py
@@ -70,8 +70,9 @@
 
 
 class Rider:
-    def __init__(self, array, out, make, scratch, chunks=0):
+    def __init__(self, array, out, make, scratch, chunks=0, summed=None):
         self.array, self.out, self.make, self.scratch, self.chunks = array, out, make, scratch, chunks
+        self.summed = summed
         self.late = self.hopped = False
 
     def later(self, hopped=False):
@@ -269,8 +270,8 @@
 
 
 class CtxGather:
-    def __init__(self, source, target, place, scratch):
-        self.source, self.target = source, target
+    def __init__(self, pick, source, target, place, scratch):
+        self.source, self.target, self.pick = source, target, pick
         self.c = place[1]
         self.send, self.recv, self.leg, self.stage = scratch
 
@@ -280,15 +281,15 @@
     def copy(self, number):
         c = self.c
         device = across_of(c) if number == 0 else mate_of(c)
-        source = self.target.at[across_of(c)] if number == 2 else self.source
+        source = self.pick(self.target, across_of(c)) if number == 2 else self.source
         slot = across_of(c) if number == 2 else c
-        return rcopy(source, self.target.at[slot], self.send.at[number], self.recv.at[number], {"ctx": device})
+        return rcopy(source, self.pick(self.target, slot), self.send.at[number], self.recv.at[number], {"ctx": device})
 
     def inward(self):
         return pltpu.make_async_copy(self.source, self.stage, self.leg.at[0])
 
     def outward(self):
-        return pltpu.make_async_copy(self.stage, self.target.at[self.c], self.leg.at[1])
+        return pltpu.make_async_copy(self.stage, self.pick(self.target, self.c), self.leg.at[1])
 
     def start(self):
         self.copy(0).start()
@@ -311,7 +312,7 @@
 class CtxScatter:
     def __init__(self, pick, source, target, place, scratch):
         self.source, self.target, self.pick = source, target, pick
-        self.c = place[1]
+        self.c, self.came = place[1], False
         self.send, self.recv, self.leg, self.stage, self.cross, self.far, self.total = scratch
 
     def greetings(self):
@@ -347,11 +348,17 @@
         self.inward().wait()
         self.outward().start()
 
+    def arrive(self):
+        self.came = True
+        self.copy(1).wait_recv()
+        self.copy(2).wait_recv()
+        self.outward().wait()
+
     def finish(self):
-        self.copy(0).wait_send()
-        self.copy(1).wait()
-        self.copy(2).wait()
-        self.outward().wait()
+        if not self.came:
+            self.arrive()
+        for number in range(3):
+            self.copy(number).wait_send()
 
 
 class Riding:
@@ -361,11 +368,16 @@
         place = tuple(lax.axis_index(axis) for axis in ("fsdp", "ctx", "tp"))
         scratch = list(scratch)
         self.rides, self.hops, self.late, self.hopped = [], [], [], []
-        self.firsts, self.seconds, self.begun, self.turned = [], [], [], []
+        self.firsts, self.seconds, self.begun, self.turned, self.sums = [], [], [], [], {}
         for rider, target in zip(riders, targets):
             own = [scratch.pop(0) for _ in rider.scratch]
             chained = isinstance(rider.array, int)
-            ride = rider.make(targets[rider.array] if chained else sources.pop(0), target, place, own)
+            source = targets[rider.array] if chained else sources.pop(0)
+            if rider.summed is not None:
+                terms, total, sem = (scratch.pop(0) for _ in range(3))
+                self.sums[len(self.seconds)] = (pltpu.make_async_copy(source, terms, sem.at[0]), terms, total)
+                source = total
+            ride = rider.make(source, target, place, own)
             self.rides.append(ride)
             if chained:
                 self.firsts.append(self.rides[rider.array])
@@ -434,8 +446,14 @@
             pl.when(when)(self.turn)
 
     def chain(self):
-        for first, second in zip(self.firsts, self.seconds):
+        for number, (first, second) in enumerate(zip(self.firsts, self.seconds)):
             first.arrive()
+            if number in self.sums:
+                fetch, terms, total = self.sums[number]
+                fetch.start()
+                fetch.wait()
+                axes = tuple(range(len(terms.shape) - len(total.shape)))
+                total[...] = jnp.sum(terms[...].astype(F32), axis=axes).astype(total.dtype)
             self.begin(second)
 
     def chain_turn(self):
@@ -483,7 +501,12 @@
     params = dict(vmem_limit_bytes=60 * 1024 * 1024)
     if collective_id is not None:
         params.update(collective_id=collective_id, has_side_effects=True)
-    extra = [item for rider in riders for item in rider.scratch]
+    extra = []
+    for rider in riders:
+        extra += rider.scratch
+        if rider.summed is not None:
+            terms, total = riders[rider.array].out, rider.summed
+            extra += [pltpu.VMEM(terms.shape, terms.dtype), pltpu.VMEM(total.shape, total.dtype), dma(1)]
     anywhere = pl.BlockSpec(memory_space=pl.ANY)
     near = [pltpu.VMEM(operands[i].shape, operands[i].dtype) for i in large]
     near += [pltpu.VMEM(out.shape, out.dtype) for out in out_shapes]
@@ -552,22 +575,27 @@
     return copies_rider(parts, out, size - 1, out.shape[1:], make)
 
 
-def ctx_gather(own, first=None):
+def slot_of(axis):
+    def pick(ref, slot):
+        return ref.at[slot] if axis == 0 else ref.at[:, :, slot]
+
+    return pick
+
+
+def ctx_gather(own, axis=0, first=None, summed=False):
     scratch = [dma(3), dma(3), dma(2), pltpu.VMEM(own.shape, own.dtype)]
-    array = own if first is None else first
-    return Rider(array, sds(4, *own.shape, dtype=own.dtype), CtxGather, scratch)
+    out = sds(*own.shape[:axis], 4, *own.shape[axis:], dtype=own.dtype)
+    make = functools.partial(CtxGather, slot_of(axis))
+    return Rider(own if first is None else first, out, make, scratch, summed=own if summed else None)
 
 
 def ctx_scatter(parts, axis=0, first=None):
     shape = parts.shape[:axis] + parts.shape[axis + 1 :]
-
-    def pick(ref, slot):
-        return ref.at[slot] if axis == 0 else ref.at[:, :, slot]
 
     buffer = pltpu.VMEM(shape, parts.dtype)
     scratch = [dma(3), dma(3), dma(3), buffer, buffer, buffer, buffer]
     array = parts if first is None else first
-    return Rider(array, sds(3, *shape, dtype=parts.dtype), functools.partial(CtxScatter, pick), scratch)
+    return Rider(array, sds(3, *shape, dtype=parts.dtype), functools.partial(CtxScatter, slot_of(axis)), scratch)
 
 
 def flipped_place(c, t):
@@ -668,19 +696,25 @@
         self.stays().wait()
 
 
-def small_sum(own, size):
+def small_sum(own, size, first=None):
     many = 4 * size - 1
     scratch = [
         dma(3), dma(3), dma(many), dma(many), dma(2),
         pltpu.VMEM((4, *own.shape), own.dtype), pltpu.VMEM(own.shape, own.dtype),
     ]
-    return Rider(own, sds(4, size, *own.shape, dtype=own.dtype), SmallSum, scratch)
+    out = sds(4, size, *own.shape, dtype=own.dtype)
+    return Rider(own if first is None else first, out, SmallSum, scratch, summed=None if first is None else own)
 
 
 def carry_kernel(ride):
     barrier = pltpu.get_barrier_semaphore()
     pl.semaphore_wait(barrier, ride.greet(barrier))
     ride.start()
+    ride.turn()
+    ride.start_late()
+    ride.chain()
+    ride.turn()
+    ride.chain_turn()
     ride.finish()
 
 
@@ -726,7 +760,7 @@
     count = 5 - ends + ride.greet(barrier) + (size - 1 if fetch else 0)
     m_ref[...] = jnp.full_like(m_ref, MASKED)
     acc_ref[...] = jnp.zeros_like(acc_ref)
-    vt_ref[:, :, :, 128:144] = jnp.ones((4, 4, 2, 16, 256), BF16)
+    vt_ref[:, :, :, 64:80] = jnp.ones((4, 4, 3, 16, 256), BF16)
     ride.ready()
     pl.semaphore_wait(barrier, count)
 
@@ -813,8 +847,10 @@
         qm_ref[2, chunk] = qw_ref[chunk, :, 128:256]
         onward(chunk).wait_recv()
         for segment in range(4):
-            vt_ref[segment, chunk, 0, 0:128] = jnp.transpose(kv_ref[segment, chunk, :, 256:384], (1, 0))
-            vt_ref[segment, chunk, 1, 0:128] = jnp.transpose(kv_ref[segment, chunk, :, 128:256], (1, 0))
+            pair = jnp.transpose(kv_ref[segment, chunk, :, 256:384], (1, 0))
+            mixed = jnp.transpose(kv_ref[segment, chunk, :, 128:256], (1, 0))
+            for head, rows in enumerate((pair[0:64], pair[64:128], mixed[0:64])):
+                vt_ref[segment, chunk, head, 0:64] = rows
 
     def items(step):
         @pl.loop(step * step, (step + 1) * (step + 1))
@@ -841,7 +877,7 @@
                     total = acc_ref[query_at, head] * jnp.exp(m_ref[query_at, head : head + 1] - most[head])
                     for segment, row, off in zip(segments, scores[head], far):
                         probs = jnp.exp(row - (most[head] + off)).astype(BF16)
-                        total += mm(vt_ref[segment, key_at, head // 2], probs)
+                        total += mm(vt_ref[segment, key_at, head], probs)
                     made.append(total)
                 for head in range(3):
                     m_ref[query_at, head : head + 1] = most[head]
@@ -897,11 +933,11 @@
     ride.put(qw_ref, kv_ref)
     items(3)
     for quarter in range(4):
-        whole = [acc_ref[quarter, head, 128:129] for head in range(3)]
-        parts = [acc_ref[quarter, head, 0:128] / whole[head] for head in range(3)]
-        pair = jnp.concatenate([parts[0][0:64], parts[1][64:128]], axis=0)
-        o_ref[quarter, :, 0:128] = jnp.transpose(pair, (1, 0)).astype(BF16)
-        o_ref[quarter, :, 128:192] = jnp.transpose(parts[2], (1, 0))[:, :64].astype(BF16)
+        whole = [acc_ref[quarter, head, 64:65] for head in range(3)]
+        parts = [acc_ref[quarter, head, 0:64] / whole[head] for head in range(3)]
+        for at, pair in ((0, parts[0:2]), (128, [parts[2], jnp.zeros_like(parts[2])])):
+            turned = jnp.transpose(jnp.concatenate(pair, axis=0), (1, 0)).astype(BF16)
+            o_ref[quarter, :, at : min(at + 128, 192)] = turned[:, : min(128, 192 - at)]
         for head in range(3):
             lse_ref[quarter, head : head + 1] = m_ref[quarter, head : head + 1] + jnp.log(whole[head])
         lse_ref[quarter, 3:8] = jnp.zeros((5, 256), F32)
@@ -943,8 +979,8 @@
     ]
     scratch = [
         pltpu.VMEM((2, 256, 256), BF16),
-        pltpu.VMEM((3, 4, 256, 128), BF16), pltpu.VMEM((4, 8, 256), F32), pltpu.VMEM((4, 3, 144, 256), F32),
-        pltpu.VMEM((4, 4, 2, 144, 256), BF16),
+        pltpu.VMEM((3, 4, 256, 128), BF16), pltpu.VMEM((4, 8, 256), F32), pltpu.VMEM((4, 3, 80, 256), F32),
+        pltpu.VMEM((4, 4, 3, 80, 256), BF16),
         dma(4), dma(3), dma(3),
         dma(4), dma(4), dma(4), dma(4), dma(4), dma(4), dma(2), dma(2),
     ]
@@ -1284,6 +1320,7 @@
     for group in range(4):
         dout_ref[group] = mm_tn(g1, rows_ref[group]).astype(BF16)
     ride.put(back_ref, stat_ref, dout_ref)
+    ride.chain()
     total = all_up_ref[slice_of(f)].astype(F32)
     for k in range(1, size):
         term(k).wait_recv()
@@ -1305,6 +1342,7 @@
         def _():
             give_near(group).wait_send()
 
+    ride.chain_turn()
     for k in range(1, size):
         term(k).wait_send()
     settle()
@@ -1404,16 +1442,17 @@
     def cross(chunk):
         return rcopy(sum_ref.at[chunk], far_ref.at[chunk], f_send.at[chunk], f_recv.at[chunk], {"ctx": across})
 
-    def lower(chunk):
-        return rcopy(pass_ref.at[chunk], take_ref.at[0, chunk], p_send.at[chunk], p_recv.at[0, chunk], {"tp": t - 1})
-
-    def upper(chunk):
-        return rcopy(pass_ref.at[chunk], take_ref.at[1, chunk], p_send.at[chunk], p_recv.at[1, chunk], {"tp": t + 1})
-
-    def passed(side, chunk):
-        rcopy(
-            take_ref.at[side, chunk], take_ref.at[side, chunk], p_send.at[0], p_recv.at[side, chunk], {"tp": t}
-        ).wait_recv()
+    pieces = (pl.ds(0, PIECE), pl.ds(PIECE, PIECE))
+
+    def onward(side, chunk, p):
+        return rcopy(
+            pass_ref.at[chunk, pieces[p]], take_ref.at[side, chunk, pieces[p]],
+            p_send.at[chunk, p], p_recv.at[side, chunk, p], {"tp": t - 1 + 2 * side},
+        )
+
+    def passed(side, chunk, p):
+        part = take_ref.at[side, chunk, pieces[p]]
+        rcopy(part, part, p_send.at[0, p], p_recv.at[side, chunk, p], {"tp": t}).wait_recv()
 
     chunks = [ordered(t, 3 - k) for k in range(4)]
     at_end = (t == 0) | (t == 3)
@@ -1459,31 +1498,28 @@
     def relay(k):
         chunk = chunks[k]
 
+        def move(side, first):
+            for p in range(2):
+
+                @pl.when(jnp.logical_not(first))
+                def _():
+                    passed(side, chunk, p)
+                    total = part_ref[chunk, pieces[p]] + take_ref[side, chunk, pieces[p]].astype(F32)
+                    pass_ref[chunk, pieces[p]] = total.astype(BF16)
+
+                @pl.when(first)
+                def _():
+                    pass_ref[chunk, pieces[p]] = part_ref[chunk, pieces[p]].astype(BF16)
+
+                onward(side, chunk, p).start()
+
         @pl.when(chunk < t)
         def _():
-            @pl.when(t < 3)
-            def _():
-                passed(0, chunk)
-                pass_ref[chunk] = (part_ref[chunk] + take_ref[0, chunk].astype(F32)).astype(BF16)
-
-            @pl.when(t == 3)
-            def _():
-                pass_ref[chunk] = part_ref[chunk].astype(BF16)
-
-            lower(chunk).start()
+            move(0, t == 3)
 
         @pl.when(chunk > t)
         def _():
-            @pl.when(t > 0)
-            def _():
-                passed(1, chunk)
-                pass_ref[chunk] = (part_ref[chunk] + take_ref[1, chunk].astype(F32)).astype(BF16)
-
-            @pl.when(t == 0)
-            def _():
-                pass_ref[chunk] = part_ref[chunk].astype(BF16)
-
-            upper(chunk).start()
+            move(1, t == 0)
 
     def relay_ends(k):
         pl.when(at_end)(functools.partial(relay, k))
@@ -1590,31 +1626,30 @@
 
     query = dq_ref[...].reshape(1024, 256)
     for span in range(3):
+        if span == 0:
+            ride.chain()
         if span == 1:
+            relay_inner(2)
             gather_up(3)
+            ride.chain_turn()
         own = own_ref[...].reshape(1024, 384)
         made = (query, own[:, 0:256], own[:, 256:384])[span]
         all_in_ref[:, spans[span]] = mm_tn(xg_ref[...], made).astype(BF16)
         for k in range(1, size):
             term(k, span).start()
 
-    ride.chain()
-    relay_inner(2)
     sum_out_ref[0:1, 0:256] = jnp.sum(query.astype(F32), axis=0, keepdims=True)
     sum_out_ref[0:1, 256:640] = jnp.sum(own.astype(F32), axis=0, keepdims=True)
     ride.put(sum_out_ref)
-    ride.chain_turn()
     grad_ref[...] = part_ref[t] + back_ref[...]
 
-    @pl.when(t < 3)
-    def _():
-        passed(0, t)
-        grad_ref[...] += take_ref[0, t].astype(F32)
-
-    @pl.when(t > 0)
-    def _():
-        passed(1, t)
-        grad_ref[...] += take_ref[1, t].astype(F32)
+    for side, there in ((0, t < 3), (1, t > 0)):
+
+        @pl.when(there)
+        def _():
+            for p in range(2):
+                passed(side, t, p)
+                grad_ref[pieces[p]] += take_ref[side, t, pieces[p]].astype(F32)
 
     low_ref[...] = grad_ref[...].astype(BF16)
     ride.put(grad_ref, low_ref)
@@ -1640,7 +1675,8 @@
 
         @pl.when(t != chunk)
         def _():
-            upper(chunk).wait_send()
+            for p in range(2):
+                onward(1, chunk, p).wait_send()
 
     for slot in range(2):
         partner(slot).wait_send()
@@ -1665,7 +1701,7 @@
         pltpu.VMEM((4, 256, 384), BF16), pltpu.VMEM((4, 256, 384), BF16),
         pltpu.VMEM((4, 256, 384), BF16), pltpu.VMEM((4, 256, 384), BF16),
         pltpu.VMEM((4, 256, 768), BF16), pltpu.VMEM((2, 4, 256, 768), BF16),
-        dma(2), dma(2), dma(4), dma(4), dma(4), dma(4), dma(4), dma(4), dma(4), dma(2, 4),
+        dma(2), dma(2), dma(4), dma(4), dma(4), dma(4), dma(4), dma(4), dma(4, 2), dma(2, 4, 2),
     ]
     cost = (5 * 512 * 1024 * 64 * 30 + 4 * 1024 * 768 * 640, 16 << 20, 5 * 512 * 1024 * 3)
     operands = (flags, qw, kv.reshape(4, 4, 256, 384), do, o, lse, w, back_one, xg, marks)
@@ -1739,22 +1775,19 @@
     out_turned = jnp.swapaxes(wo, 1, 2).reshape(layers, 4, piece, 192)
     out_piece = lax.dynamic_index_in_dim(out_turned, c, axis=1, keepdims=False)
 
-    def out_whole(gathered):
-        return jnp.transpose(gathered, (1, 2, 0, 3, 4)).reshape(4, 768, 192)
-
     def vectors(n):
         norms = [norm_gains[n, 0], norm_shifts[n, 0], norm_gains[n, 1], norm_shifts[n, 1]]
         return jnp.concatenate([out_bias[n], jnp.stack(norms), jnp.zeros((2, 768), F32)])
 
     saved, weights = [], []
     rounded = low(stream)
-    riders = [plane_gather(out_piece[0], size), ctx_gather(sds(4, size, piece, 192), first=0)]
+    riders = [plane_gather(out_piece[0], size), ctx_gather(sds(4, size, piece, 192), axis=2, first=0)]
     riders += [flip_gather(w1[0], size).later(), tp_flip(down_turned[0]).later(hopped=True), tp_flip(ffn_bias)]
     xg, qw, kv, o, lse, w_in, got = inner(rounded, own_in[0], in_bias[0][None], flags, 0, riders, fetch=True)
     _, out, w_up, down, units = got
     for n in range(layers):
         last = n == layers - 1
-        w_out = out_whole(out)
+        w_out = out.reshape(4, 768, 192)
         w_up = w_up.reshape(768, 768)
         vecs = vectors(n)
         riders = []
@@ -1770,7 +1803,7 @@
         saved.append((xg, qw, kv, o, lse, xhat1, r1, xhat2, r2, xg2, act, slope, rows))
         if not last:
             up, out, w_in = got
-            riders = [ctx_gather(out), tp_flip(down_turned[n + 1]).later(), fsdp_gather(up, size)]
+            riders = [ctx_gather(out, axis=2), tp_flip(down_turned[n + 1]).later(), fsdp_gather(up, size)]
             xg, qw, kv, o, lse, w_in, (out, down, w_up) = inner(
                 rounded, w_in.reshape(768, 640), in_bias[n + 1][None], flags, 16 * n + 16, riders
             )
@@ -1786,6 +1819,8 @@
         riders = []
         if above is not None:
             riders = [plane_scatter(above["out"], size), ctx_scatter(above["in"])]
+            riders += [ctx_gather(sds(piece, 192), first=0, summed=True)]
+            riders += [ctx_gather(sds(piece, 640), first=1, summed=True)]
         back_one, do, small[n], d_up, d_down, d_out, got = block_back(
             grad, xhat2, r2, xhat1, r1, vecs, slope, w_up, w_down, w_out, xg2, act, rows, 16 * n + 3, riders
         )
@@ -1796,13 +1831,13 @@
             ctx_scatter(quarters, first=0), ctx_scatter(quarters, first=1),
         ]
         if above is not None:
-            gathered = (added(got[0], (0, 1)), above["up"], above["down"], added(got[1]))
-            riders += [ctx_gather(low(part)) for part in gathered]
+            done[n + 1] = tuple(got[2:4])
+            riders += [ctx_gather(above["up"]), ctx_gather(above["down"])]
         grad, low_grad, d_in, sums, memory_part, got = inner_back(
             qw, kv, do, o, lse, flags, w_in, back_one, xg, marks, 16 * n + 4, riders
         )
         if above is not None:
-            done[n + 1] = (got[8], got[5], got[6], got[7])
+            done[n + 1] = (done[n + 1][1], done[n + 1][0], got[5], got[6])
         d_query_bias, _, d_value_bias = parted(sums)
         heads[n] = jnp.stack([d_query_bias, d_value_bias])
         above = {
@@ -1825,10 +1860,10 @@
     sums = jnp.concatenate([stat_rows, unit_rows, head_rows, memory_part, rest])
     sums = sums.reshape(4, size, width, 768)
     riders = [ctx_scatter(above["in"]), plane_scatter(above["out"], size), plane_scatter(sums, size)]
-    got = carry(riders, 6)
-    parts = (low(added(got[0])), low(added(got[1], (0, 1))), above["up"], above["down"])
-    got = carry([ctx_gather(part) for part in parts] + [small_sum(added(got[2], (0, 1)), size)], 7)
-    done[0] = got[:4]
+    riders += [ctx_gather(above["up"]).later(), ctx_gather(above["down"]).later()]
+    riders += [ctx_gather(sds(piece, 640), first=0, summed=True), ctx_gather(sds(piece, 192), first=1, summed=True)]
+    got = carry(riders + [small_sum(sds(width, 768, dtype=F32), size, first=2)], 6)[3:]
+    done[0] = (got[2], got[3], got[0], got[1])
     totals = got[4].reshape(width * slices, 768)
     stats = totals[: 6 * layers].reshape(layers, 6, 768)
     at = 6 * layers

time: 529 us -> 504 us (0.953)
  Pallas kernels: 463 us -> 450 us
  other arithmetic: 24.8 us -> 18.3 us
    pallas_call x10 -> x9, Pallas kernels: 463 us -> 450 us  [call(): pl.pallas_call(body, out_shape=list(out_shapes) + [rider.out for rider in...]
    reduce_sum x11 -> x6, other arithmetic: 14.2 us -> 7.74 us  [added(): return jnp.sum(terms.astype(F32), axis=axes)]
    transpose x2 -> x0, local copies, waits for them, and re-layouts: 5.36 us -> none  [out_whole(): return jnp.transpose(gathered, (1, 2, 0, 3, 4)).reshape(4, 768, 192)]
where the time goes in v6:
time: 504 us; the launch traced here: 496 us
  Pallas kernels  450 us (89%)
  local copies, waits for them, and re-layouts  21.4 us (4%)
  other arithmetic  18.3 us (4%)
  matrix products  5.21 us (1%)
    pallas_call x9, Pallas kernels, call(): pl.pallas_call(body, out_shape=list(out_shapes) + [rider.out for rider in...  450 us

profile of v6, /device:TPU:0, one launch (start us, length us, event | category | flops | bytes accessed | tf_op | source)
XLA Modules:
  0.0 496.4 jit_solution(11216851193584566638)
XLA Ops:
  0.7 0.9 fusion.4
  1.6 0.8 fusion.3
  2.5 0.9 multiply_reduce_fusion.3
  3.9 2.6 fusion.13
  8.4 1.1 slice_bitcast_fusion.3
  10.2 1.2 copy.54
  11.5 0.7 dynamic-slice_bitcast_fusion
  12.1 1.1 slice_bitcast_fusion.2
  13.2 0.6 copy.55
  13.8 1.1 slice_bitcast_fusion
  14.9 71.0 %inner.2 = (bf16[4,256,768]{2,1,0:T(8,128)(2,1)}, bf16[4,256,256]{2,1,0:T(8,128)(2,1)}, bf16[4,4,256,384]{3,2,1,0:T(8,128)(2,1)}, bf16[4,256,192]{2,1,0:T(8,128)...) custom-call(s32[2,4]{1,0:T(2,128)} %pad_add_fusion.refs_0_, ...), custom_call_target="tpu_custom_call" | custom-call | flops 3019898880 | bytes 14680064 | tf_op jit(solution)/shard_map/inner/pallas_call | solution.py:513
  85.9 1.4 fusion.10
  87.3 0.6 concatenate.38.refs_5_
  88.0 43.8 %block.2 = (f32[256,768]{1,0:T(8,128)}, bf16[256,768]{1,0:T(8,128)(2,1)}, f32[256,768]{1,0:T(8,128)}, f32[256,128]{1,0:T(8,128)}, f32[256,768]{1,0:T(8,128)}, /*...) custom-call(bf16[4,256,192]{2,1,0:T(8,128)(2,1)} %get-tuple-element., ...), custom_call_target="tpu_custom_call" | custom-call | flops 2717908992 | bytes 16777216 | tf_op jit(solution)/shard_map/block/pallas_call | solution.py:513
  131.8 50.1 %inner.3 = (bf16[4,256,768]{2,1,0:T(8,128)(2,1)}, bf16[4,256,256]{2,1,0:T(8,128)(2,1)}, bf16[4,4,256,384]{3,2,1,0:T(8,128)(2,1)}, bf16[4,256,192]{2,1,0:T(8,128)...) custom-call(s32[2,4]{1,0:T(2,128)} %pad_add_fusion.refs_0_, ...), custom_call_target="tpu_custom_call" | custom-call | flops 3019898880 | bytes 14680064 | tf_op jit(solution)/shard_map/inner/pallas_call | solution.py:513
  182.0 0.6 concatenate.39.refs_5_
  182.6 39.5 %block.3 = (f32[256,768]{1,0:T(8,128)}, bf16[256,768]{1,0:T(8,128)(2,1)}, f32[256,768]{1,0:T(8,128)}, f32[256,128]{1,0:T(8,128)}, f32[256,768]{1,0:T(8,128)}, /*...) custom-call(bf16[4,256,192]{2,1,0:T(8,128)(2,1)} %get-tuple-element., ...), custom_call_target="tpu_custom_call" | custom-call | flops 2717908992 | bytes 16777216 | tf_op jit(solution)/shard_map/block/pallas_call | solution.py:513
  222.1 0.9 convert_element_type.77.refs_0_
  223.0 37.0 %block_back.2 = (f32[256,768]{1,0:T(8,128)}, bf16[4,256,192]{2,1,0:T(8,128)(2,1)}, f32[8,768]{1,0:T(8,128)}, bf16[384,768]{1,0:T(8,128)(2,1)}, bf16[768,768]{1,0:T(8,128)(2,1)}, /*index=5*/bf16[4,768,192]{2,1,0:T(8,128)(2,1)}) custom-call(f32[256,768]{1,0:T(8,128)} %convert_element_type.77.refs_0_, f32[256,768]{1,0:T(8,128)} %get-tuple-element.109.refs_1_, ...), custom_call_target="tpu_custom_call" | custom-call | flops 5435817984 | bytes 20971520 | tf_op jit(solution)/shard_map/block_back/pallas_call | solution.py:513
  260.0 0.8 compare_convert_fusion.refs_9_
  260.8 69.3 %inner_back.2 = (f32[256,768]{1,0:T(8,128)}, bf16[256,768]{1,0:T(8,128)(2,1)}, bf16[384,640]{1,0:T(8,128)(2,1)}, f32[8,640]{1,0:T(8,128)}, f32[20,768]{1,0:T(8,1...) custom-call(s32[2,4]{1,0:T(2,128)} %pad_add_fusion.refs_0_, ...), custom_call_target="tpu_custom_call" | custom-call | flops 7046430720 | bytes 16777216 | tf_op jit(solution)/shard_map/inner_back/pallas_call | solution.py:513
  330.1 2.3 reduce_sum.110.refs_13_
  332.5 43.4 %block_back.3 = (f32[256,768]{1,0:T(8,128)}, bf16[4,256,192]{2,1,0:T(8,128)(2,1)}, f32[8,768]{1,0:T(8,128)}, bf16[384,768]{1,0:T(8,128)(2,1)}, bf16[768,768]{1,0...) custom-call(f32[256,768]{1,0:T(8,128)} %get-tuple-element.125.refs_0, ...), custom_call_target="tpu_custom_call" | custom-call | flops 5435817984 | bytes 20971520 | tf_op jit(solution)/shard_map/block_back/pallas_call | solution.py:513
  375.8 0.7 reduce_sum.111.refs_13_
  376.6 0.7 reduce_sum.112.refs_14_
  377.3 66.6 %inner_back.3 = (f32[256,768]{1,0:T(8,128)}, bf16[256,768]{1,0:T(8,128)(2,1)}, bf16[384,640]{1,0:T(8,128)(2,1)}, f32[8,640]{1,0:T(8,128)}, f32[20,768]{1,0:T(8,1...) custom-call(s32[2,4]{1,0:T(2,128)} %pad_add_fusion.refs_0_, ...), custom_call_target="tpu_custom_call" | custom-call | flops 7046430720 | bytes 16777216 | tf_op jit(solution)/shard_map/inner_back/pallas_call | solution.py:513
  444.0 2.4 reduce_sum.113.refs_1_
  446.8 0.8 slice_bitcast_fusion.18
  447.5 0.7 slice_bitcast_fusion.19
  448.2 0.8 slice_bitcast_fusion.22
  449.0 0.7 slice_bitcast_fusion.23
  450.2 0.7 reshape.227.refs_2_
  450.9 0.7 reduce_sum.114.refs_3_
  451.6 0.7 reduce_sum.115.refs_4_
  452.4 29.0 %carry.1 = (bf16[3,96,640]{2,1,0:T(8,128)(2,1)}, bf16[4,2,96,192]{3,2,1,0:T(8,128)(2,1)}, f32[4,2,6,768]{3,2,1,0:T(8,128)}, bf16[4,96,768]{2,1,0:T(8,128)(2,1)},...) custom-call(bf16[4,96,640]{2,1,0:T(8,128)(2,1)} %bitcast.141, ...), custom_call_target="tpu_custom_call" | custom-call | flops 1048576 | bytes 1048576 | tf_op jit(solution)/shard_map/carry/pallas_call | solution.py:513
  481.4 1.0 reshape.228
  482.4 0.6 slice.289
  483.8 0.9 pad_maximum_fusion
  484.7 0.9 pad_maximum_fusion.1
  485.6 0.9 pad_maximum_fusion.2
  486.9 0.9 maximum_convert_fusion.3
  487.7 1.6 maximum_convert_fusion
  490.0 1.6 maximum_convert_fusion.1
  491.6 0.7 multiply_reduce_fusion.1
  492.3 0.7 multiply_reduce_fusion
  493.0 0.8 slice_bitcast_fusion.5
  494.4 0.7 copy.77
  495.2 0.7 copy.78
  (130 shorter events, 6.5 us)
Async XLA Ops:
  0.6 3.3 copy-start
  0.7 5.8 %slice-start = ((bf16[2,384,192]{1,2,0:T(8,128)(2,1)}), bf16[2,384,128]{1,2,0:T(8,128)(2,1)S(1)}, s32[]{:S(2)}) async-start(bf16[2,384,192]{1,2,0:T(8,128)(2,1)} %param.21), calls=%async_computation | async-start | bytes 393216 | tf_op jit(solution)/shard_map/slice | solution.py:1727
  0.7 6.0 %slice-start.1 = ((bf16[2,384,192]{1,2,0:T(8,128)(2,1)}), bf16[2,384,64]{1,2,0:T(8,128)(2,1)S(1)}, s32[]{:S(2)}) async-start(bf16[2,384,192]{1,2,0:T(8,128)(2,1)} %param.21), calls=%async_computation.1 | async-start | bytes 196608 | tf_op jit(solution)/shard_map/slice | solution.py:1727
  3.9 3.0 slice-start.2
  3.9 3.1 slice-start.4
  6.5 0.9 slice-start.3
  6.5 1.1 slice-start.5
  8.4 1.1 copy-start.25
  8.4 3.7 copy-start.2
  10.2 3.0 copy-start.3
  14.9 72.3 %copy-start.22 = (f32[2,2,768]{2,1,0:T(2,128)S(1)}, f32[2,2,768]{2,1,0:T(2,128)}, u32[]{:S(2)}) copy-start(f32[2,2,768]{2,1,0:T(2,128)} %param.29) | copy-start | bytes 36868
  14.9 72.4 %copy-start.23 = (f32[2,2,768]{2,1,0:T(2,128)S(1)}, f32[2,2,768]{2,1,0:T(2,128)}, u32[]{:S(2)}) copy-start(f32[2,2,768]{2,1,0:T(2,128)} %param.31) | copy-start | bytes 36868
  14.9 72.4 %copy-start.24 = (f32[2,2,768]{2,1,0:T(2,128)S(1)}, f32[2,2,768]{2,1,0:T(2,128)}, u32[]{:S(2)}) copy-start(f32[2,2,768]{2,1,0:T(2,128)} %param.30) | copy-start | bytes 36868
  182.6 39.5 %copy-start.16 = (bf16[256,768]{1,0:T(8,128)(2,1)S(1)}, bf16[256,768]{1,0:T(8,128)(2,1)}, u32[]{:S(2)}) copy-start(bf16[256,768]{1,0:T(8,128)(2,1)} %param.17) | copy-start | bytes 1179652
  223.0 37.0 %copy-start.26 = (s32[1,1,20]{2,1,0:T(1,128)S(1)}, s32[1,1,20]{2,1,0:T(1,128)}, u32[]{:S(2)}) copy-start(s32[1,1,20]{2,1,0:T(1,128)} %param.18) | copy-start | bytes 244
  332.5 43.4 %copy-start.13 = (bf16[3,96,768]{2,1,0:T(8,128)(2,1)S(1)}, bf16[3,96,768]{2,1,0:T(8,128)(2,1)}, u32[]{:S(2)}) copy-start(bf16[3,96,768]{2,1,0:T(8,128)(2,1)} %get-tuple-element.145) | copy-start | bytes 1327108
  332.5 44.1 %copy-start.12 = (bf16[3,96,768]{2,1,0:T(8,128)(2,1)S(1)}, bf16[3,96,768]{2,1,0:T(8,128)(2,1)}, u32[]{:S(2)}) copy-start(bf16[3,96,768]{2,1,0:T(8,128)(2,1)} %get-tuple-element.146) | copy-start | bytes 1327108
  443.9 2.5 copy-start.19
  444.0 2.5 copy-start.20
  444.0 6.0 %copy-start.21 = (f32[20,768]{1,0:T(8,128)S(1)}, f32[20,768]{1,0:T(8,128)}, u32[]{:S(2)}) copy-start(f32[20,768]{1,0:T(8,128)} %get-tuple-element.154) | copy-start | bytes 184324
  444.0 6.9 %copy-start.11 = (bf16[3,96,768]{2,1,0:T(8,128)(2,1)S(1)}, bf16[3,96,768]{2,1,0:T(8,128)(2,1)}, u32[]{:S(2)}) copy-start(bf16[3,96,768]{2,1,0:T(8,128)(2,1)} %get-tuple-element.155) | copy-start | bytes 1327108
  444.0 7.6 %copy-start.10 = (bf16[3,96,768]{2,1,0:T(8,128)(2,1)S(1)}, bf16[3,96,768]{2,1,0:T(8,128)(2,1)}, u32[]{:S(2)}) copy-start(bf16[3,96,768]{2,1,0:T(8,128)(2,1)} %get-tuple-element.156) | copy-start | bytes 1327108
  450.9 32.1 %copy-start.8 = (bf16[4,96,640]{2,1,0:T(8,128)(2,1)S(1)}, bf16[4,96,640]{2,1,0:T(8,128)(2,1)}, u32[]{:S(2)}) copy-start(bf16[4,96,640]{2,1,0:T(8,128)(2,1)} %get-tuple-element.159) | copy-start | bytes 1474564
  481.3 1.9 copy-start.9
  485.5 0.9 copy-start.17
  485.5 1.2 copy-start.18
  485.5 2.2 copy-start.4
  485.6 2.2 copy-start.5
  487.7 1.6 copy-start.6
  487.7 1.9 copy-start.7
  489.9 4.5 copy-start.14
  489.9 5.2 %copy-start.15 = (bf16[256,768]{1,0:T(8,128)(2,1)S(1)}, bf16[256,768]{1,0:T(8,128)(2,1)}, u32[]{:S(2)}) copy-start(bf16[256,768]{1,0:T(8,128)(2,1)} %get-tuple-element.233) | copy-start | bytes 1179652
  489.9 6.0 %copy-start.1 = (f32[20,768]{1,0:T(8,128)S(1)}, f32[20,768]{1,0:T(8,128)}, u32[]{:S(2)}) copy-start(f32[20,768]{1,0:T(8,128)} %param.20) | copy-start | bytes 184324

commit v7 on v6

--- a/solution.py
+++ b/solution.py
@@ -65,6 +65,18 @@
     return chunk + half * (3 - 2 * chunk)
 
 
+def mark_path(parent_ref, flag_ref, c):
+    for half, first in enumerate((c, 3 - c)):
+        path = [first]
+        for _ in range(3):
+            path.append(parent_ref[0, path[-1]])
+        for other in range(4):
+            found = path[0] == other
+            for segment in path[1:]:
+                found = found | (segment == other)
+            flag_ref[half, other] = found.astype(jnp.int32)
+
+
 def dma(*shape):
     return pltpu.SemaphoreType.DMA(shape)
 
@@ -369,10 +381,16 @@
         scratch = list(scratch)
         self.rides, self.hops, self.late, self.hopped = [], [], [], []
         self.firsts, self.seconds, self.begun, self.turned, self.sums = [], [], [], [], {}
+        self.stores, self.stored = [], 0
         for rider, target in zip(riders, targets):
             own = [scratch.pop(0) for _ in rider.scratch]
             chained = isinstance(rider.array, int)
             source = targets[rider.array] if chained else sources.pop(0)
+            if rider.make is None:
+                terms, total, sem = own
+                fetch = pltpu.make_async_copy(source, terms, sem.at[0])
+                self.stores.append((self.rides[rider.array], fetch, terms, total, total_copy(total, target, sem)))
+                continue
             if rider.summed is not None:
                 terms, total, sem = (scratch.pop(0) for _ in range(3))
                 self.sums[len(self.seconds)] = (pltpu.make_async_copy(source, terms, sem.at[0]), terms, total)
@@ -461,12 +479,30 @@
             self.turned.append(second)
             second.turn()
 
+    def store(self, count):
+        batch = self.stores[self.stored : self.stored + count]
+        for first, fetch, *_ in batch:
+            first.arrive()
+            fetch.start()
+        for _, fetch, terms, total, put in batch:
+            fetch.wait()
+            total[...] = jnp.sum(terms[...].astype(F32), axis=0).astype(total.dtype)
+            put.start()
+        self.stored += count
+
     def finish(self):
         for ride in self.rides:
             if ride not in self.turned:
                 ride.turn()
+        self.store(len(self.stores))
         for ride in self.rides:
             ride.finish()
+        for store in self.stores:
+            store[4].wait()
+
+
+def total_copy(total, target, sem):
+    return pltpu.make_async_copy(total, target, sem.at[1])
 
 
 def guarded(when, action):
@@ -696,6 +732,12 @@
         self.stays().wait()
 
 
+def stored_sum(first, terms):
+    total = sds(*terms.shape[1:], dtype=terms.dtype)
+    scratch = [pltpu.VMEM(terms.shape, terms.dtype), pltpu.VMEM(total.shape, total.dtype), dma(2)]
+    return Rider(first, total, None, scratch)
+
+
 def small_sum(own, size, first=None):
     many = 4 * size - 1
     scratch = [
@@ -730,15 +772,16 @@
 
 
 def inner_kernel(
-    fetch, ride, flag_ref, x_ref, w_ref, b_ref, xg_ref, qw_ref, kv_ref, o_ref, lse_ref, *rest
+    fetch, ride, parent_ref, x_ref, w_ref, b_ref, xg_ref, qw_ref, kv_ref, o_ref, lse_ref, *rest
 ):
     if fetch:
         full_ref, w_send, w_recv, *rest = rest
     (
         qbuf, qm_ref, m_ref, acc_ref, vt_ref, x_recv, x_right, x_left,
-        k1_send, k1_recv, k2_send, k2_recv, kf_send, kf_recv, q_send, q_recv,
+        k1_send, k1_recv, k2_send, k2_recv, kf_send, kf_recv, q_send, q_recv, flag_ref,
     ) = rest
     c = lax.axis_index("ctx")
+    mark_path(parent_ref, flag_ref, c)
     t = lax.axis_index("tp")
     f, size = lax.axis_index("fsdp"), lax.axis_size("fsdp")
     barrier = pltpu.get_barrier_semaphore()
@@ -973,7 +1016,7 @@
     ride.finish()
 
 
-def inner(x, w, b, flags, cid, riders=(), fetch=False):
+def inner(x, w, b, parents, cid, riders=(), fetch=False):
     outs = [
         sds(4, 256, 768), sds(4, 256, 256), sds(4, 4, 256, 384), sds(4, 256, 192), sds(4, 8, 256, dtype=F32),
     ]
@@ -982,7 +1025,7 @@
         pltpu.VMEM((3, 4, 256, 128), BF16), pltpu.VMEM((4, 8, 256), F32), pltpu.VMEM((4, 3, 80, 256), F32),
         pltpu.VMEM((4, 4, 3, 80, 256), BF16),
         dma(4), dma(3), dma(3),
-        dma(4), dma(4), dma(4), dma(4), dma(4), dma(4), dma(2), dma(2),
+        dma(4), dma(4), dma(4), dma(4), dma(4), dma(4), dma(2), dma(2), pltpu.SMEM((2, 4), jnp.int32),
     ]
     if fetch:
         size = lax.axis_size("fsdp")
@@ -990,7 +1033,7 @@
         scratch = [dma(size - 1), dma(size - 1)] + scratch
     cost = (2 * 1024 * 768 * 640 + 5 * 512 * 1024 * 64 * 12, 14 << 20, 5 * 512 * 1024 * 3)
     kernel = functools.partial(inner_kernel, fetch)
-    res, ridden = call(kernel, (flags, x, w, b), outs, scratch, cid, "inner", cost, riders, smem=(0,))
+    res, ridden = call(kernel, (parents, x, w, b), outs, scratch, cid, "inner", cost, riders, smem=(0,))
     full = res[5].reshape(768, 640) if fetch else w
     xg, qw, kv, o, lse = res[:5]
     return (
@@ -1375,14 +1418,15 @@
 
 
 def inner_back_kernel(
-    ride, flag_ref, qw_ref, kv_ref, do_ref, o_ref, lse_ref, w_ref, back_ref, xg_ref, mark_ref,
+    ride, parent_ref, qw_ref, kv_ref, do_ref, o_ref, lse_ref, w_ref, back_ref, xg_ref, mark_ref,
     grad_ref, low_ref, din_ref, sum_out_ref, mem_ref,
     qm_ref, dm_ref, row_ref, acc_ref, wide_ref, dkv_ref, dqs_ref,
     w_send, w_recv, term_ref, all_in_ref, dq_ref, own_ref, part_ref,
     near_ref, join_ref, sum_ref, far_ref, pass_ref, take_ref,
-    q_send, q_recv, n_send, n_recv, j_send, j_recv, f_send, f_recv, p_send, p_recv,
+    q_send, q_recv, n_send, n_recv, j_send, j_recv, f_send, f_recv, p_send, p_recv, flag_ref,
 ):
     c = lax.axis_index("ctx")
+    mark_path(parent_ref, flag_ref, c)
     t = lax.axis_index("tp")
     f, size = lax.axis_index("fsdp"), lax.axis_size("fsdp")
     depth = din_ref.shape[0]
@@ -1641,6 +1685,7 @@
     sum_out_ref[0:1, 0:256] = jnp.sum(query.astype(F32), axis=0, keepdims=True)
     sum_out_ref[0:1, 256:640] = jnp.sum(own.astype(F32), axis=0, keepdims=True)
     ride.put(sum_out_ref)
+    ride.store(1)
     grad_ref[...] = part_ref[t] + back_ref[...]
 
     for side, there in ((0, t < 3), (1, t > 0)):
@@ -1686,7 +1731,7 @@
 RIDE_HOPS = (8, 11, 14, 17)
 
 
-def inner_back(qw, kv, do, o, lse, flags, w, back_one, xg, marks, cid, riders=()):
+def inner_back(qw, kv, do, o, lse, parents, w, back_one, xg, marks, cid, riders=()):
     size = lax.axis_size("fsdp")
     depth = 768 // size
     f = functools.partial(sds, dtype=F32)
@@ -1702,23 +1747,12 @@
         pltpu.VMEM((4, 256, 384), BF16), pltpu.VMEM((4, 256, 384), BF16),
         pltpu.VMEM((4, 256, 768), BF16), pltpu.VMEM((2, 4, 256, 768), BF16),
         dma(2), dma(2), dma(4), dma(4), dma(4), dma(4), dma(4), dma(4), dma(4, 2), dma(2, 4, 2),
+        pltpu.SMEM((2, 4), jnp.int32),
     ]
     cost = (5 * 512 * 1024 * 64 * 30 + 4 * 1024 * 768 * 640, 16 << 20, 5 * 512 * 1024 * 3)
-    operands = (flags, qw, kv.reshape(4, 4, 256, 384), do, o, lse, w, back_one, xg, marks)
+    operands = (parents, qw, kv.reshape(4, 4, 256, 384), do, o, lse, w, back_one, xg, marks)
     res, ridden = call(inner_back_kernel, operands, outs, scratch, cid, "inner_back", cost, riders, smem=(0,))
     return (*res[:3], res[3][0], res[4], ridden)
-
-
-def ancestry(parent_row):
-    seg_count = parent_row.shape[0]
-    segment_ids = jnp.arange(seg_count, dtype=jnp.int32)
-    parent_hop = (parent_row[:, None] == segment_ids[None, :]).astype(jnp.int32)
-    reached = (segment_ids[:, None] == segment_ids[None, :]).astype(jnp.int32)
-    on_path = reached
-    for hop_number in range(seg_count - 1):
-        reached = jnp.dot(reached, parent_hop)
-        on_path = jnp.maximum(on_path, reached)
-    return on_path
 
 
 def joined(query, key, value, gap):
@@ -1762,10 +1796,7 @@
     stream = hidden.astype(F32) + jnp.dot(
         marks, memory, precision=lax.Precision.HIGHEST, preferred_element_type=F32
     )
-    on_path = ancestry(parents[0])
     ids = jnp.arange(4, dtype=jnp.int32)
-    pick = lambda seg: jnp.sum(on_path * (ids == seg).astype(jnp.int32)[:, None], axis=0)
-    flags = jnp.stack([pick(c), pick(3 - c)])
 
     gap = jnp.zeros(wq.shape[:2] + (64,), BF16)
     own_in = joined(wq, wk, wv, gap)
@@ -1783,7 +1814,7 @@
     rounded = low(stream)
     riders = [plane_gather(out_piece[0], size), ctx_gather(sds(4, size, piece, 192), axis=2, first=0)]
     riders += [flip_gather(w1[0], size).later(), tp_flip(down_turned[0]).later(hopped=True), tp_flip(ffn_bias)]
-    xg, qw, kv, o, lse, w_in, got = inner(rounded, own_in[0], in_bias[0][None], flags, 0, riders, fetch=True)
+    xg, qw, kv, o, lse, w_in, got = inner(rounded, own_in[0], in_bias[0][None], parents, 0, riders, fetch=True)
     _, out, w_up, down, units = got
     for n in range(layers):
         last = n == layers - 1
@@ -1805,7 +1836,7 @@
             up, out, w_in = got
             riders = [ctx_gather(out, axis=2), tp_flip(down_turned[n + 1]).later(), fsdp_gather(up, size)]
             xg, qw, kv, o, lse, w_in, (out, down, w_up) = inner(
-                rounded, w_in.reshape(768, 640), in_bias[n + 1][None], flags, 16 * n + 16, riders
+                rounded, w_in.reshape(768, 640), in_bias[n + 1][None], parents, 16 * n + 16, riders
             )
     output = rounded
 
@@ -1830,21 +1861,22 @@
             ctx_scatter(d_out.reshape(4, size, 4, piece, 192), axis=2),
             ctx_scatter(quarters, first=0), ctx_scatter(quarters, first=1),
         ]
+        riders += [stored_sum(at, riders[at].out) for at in (2, 3, 4)]
         if above is not None:
             done[n + 1] = tuple(got[2:4])
             riders += [ctx_gather(above["up"]), ctx_gather(above["down"])]
         grad, low_grad, d_in, sums, memory_part, got = inner_back(
-            qw, kv, do, o, lse, flags, w_in, back_one, xg, marks, 16 * n + 4, riders
+            qw, kv, do, o, lse, parents, w_in, back_one, xg, marks, 16 * n + 4, riders
         )
         if above is not None:
-            done[n + 1] = (done[n + 1][1], done[n + 1][0], got[5], got[6])
+            done[n + 1] = (done[n + 1][1], done[n + 1][0], got[8], got[9])
         d_query_bias, _, d_value_bias = parted(sums)
         heads[n] = jnp.stack([d_query_bias, d_value_bias])
         above = {
-            "up": low(added(got[3])),
-            "down": low(added(got[4])),
+            "up": got[6],
+            "down": got[7],
             "in": d_in.reshape(4, depth // 4, 640),
-            "out": low(added(got[2])),
+            "out": got[5],
         }
     hidden_grad = low_grad
     small = jnp.stack(small)

time: 504 us -> 499 us (0.990)
  other arithmetic: 18.3 us -> 9.97 us
    reduce_sum x6 -> x0, other arithmetic: 7.74 us -> none  [added(): return jnp.sum(terms.astype(F32), axis=axes)]
where the time goes in v7:
time: 499 us; the launch traced here: 491 us
  Pallas kernels  453 us (91%)
  local copies, waits for them, and re-layouts  23.2 us (5%)
  other arithmetic  9.97 us (2%)
    pallas_call x9, Pallas kernels, call(): pl.pallas_call(body, out_shape=list(out_shapes) + [rider.out for rider in...  453 us

profile of v7, /device:TPU:0, one launch (start us, length us, event | category | flops | bytes accessed | tf_op | source)
XLA Modules:
  0.0 490.8 jit_solution(3420780178274876059)
XLA Ops:
  0.7 0.8 copy-done
  1.5 2.6 fusion.8
  5.4 0.6 concatenate.36
  6.0 1.1 slice_bitcast_fusion.3
  7.3 0.6 fusion.6
  7.9 1.2 copy.54
  9.1 0.6 dynamic-slice_bitcast_fusion
  9.8 1.1 slice_bitcast_fusion.2
  10.9 0.6 copy.55
  11.5 1.1 slice_bitcast_fusion
  12.6 71.0 %inner.2 = (bf16[4,256,768]{2,1,0:T(8,128)(2,1)}, bf16[4,256,256]{2,1,0:T(8,128)(2,1)}, bf16[4,4,256,384]{3,2,1,0:T(8,128)(2,1)}, bf16[4,256,192]{2,1,0:T(8,128)...) custom-call(s32[1,4]{1,0:T(1,128)} %refs_0_.7, ...), custom_call_target="tpu_custom_call" | custom-call | flops 3019898880 | bytes 14680064 | tf_op jit(solution)/shard_map/inner/pallas_call | solution.py:549
  83.6 1.4 fusion.5
  85.0 0.6 concatenate.38.refs_5_
  85.6 43.9 %block.2 = (f32[256,768]{1,0:T(8,128)}, bf16[256,768]{1,0:T(8,128)(2,1)}, f32[256,768]{1,0:T(8,128)}, f32[256,128]{1,0:T(8,128)}, f32[256,768]{1,0:T(8,128)}, /*...) custom-call(bf16[4,256,192]{2,1,0:T(8,128)(2,1)} %get-tuple-element., ...), custom_call_target="tpu_custom_call" | custom-call | flops 2717908992 | bytes 16777216 | tf_op jit(solution)/shard_map/block/pallas_call | solution.py:549
  129.5 52.1 %inner.3 = (bf16[4,256,768]{2,1,0:T(8,128)(2,1)}, bf16[4,256,256]{2,1,0:T(8,128)(2,1)}, bf16[4,4,256,384]{3,2,1,0:T(8,128)(2,1)}, bf16[4,256,192]{2,1,0:T(8,128)...) custom-call(s32[1,4]{1,0:T(1,128)} %refs_0_.7, ...), custom_call_target="tpu_custom_call" | custom-call | flops 3019898880 | bytes 14680064 | tf_op jit(solution)/shard_map/inner/pallas_call | solution.py:549
  181.6 0.6 concatenate.39.refs_5_
  182.2 37.6 %block.3 = (f32[256,768]{1,0:T(8,128)}, bf16[256,768]{1,0:T(8,128)(2,1)}, f32[256,768]{1,0:T(8,128)}, f32[256,128]{1,0:T(8,128)}, f32[256,768]{1,0:T(8,128)}, /*...) custom-call(bf16[4,256,192]{2,1,0:T(8,128)(2,1)} %get-tuple-element., ...), custom_call_target="tpu_custom_call" | custom-call | flops 2717908992 | bytes 16777216 | tf_op jit(solution)/shard_map/block/pallas_call | solution.py:549
  219.8 0.9 convert_element_type.44.refs_0_
  220.7 37.1 %block_back.2 = (f32[256,768]{1,0:T(8,128)}, bf16[4,256,192]{2,1,0:T(8,128)(2,1)}, f32[8,768]{1,0:T(8,128)}, bf16[384,768]{1,0:T(8,128)(2,1)}, bf16[768,768]{1,0:T(8,128)(2,1)}, /*index=5*/bf16[4,768,192]{2,1,0:T(8,128)(2,1)}) custom-call(f32[256,768]{1,0:T(8,128)} %convert_element_type.44.refs_0_, f32[256,768]{1,0:T(8,128)} %get-tuple-element.109.refs_1_, ...), custom_call_target="tpu_custom_call" | custom-call | flops 5435817984 | bytes 20971520 | tf_op jit(solution)/shard_map/block_back/pallas_call | solution.py:549
  257.8 0.8 compare_convert_fusion.refs_9_
  258.6 71.1 %inner_back.2 = (f32[256,768]{1,0:T(8,128)}, bf16[256,768]{1,0:T(8,128)(2,1)}, bf16[384,640]{1,0:T(8,128)(2,1)}, f32[8,640]{1,0:T(8,128)}, f32[20,768]{1,0:T(8,1...) custom-call(s32[1,4]{1,0:T(1,128)} %refs_0_.7, ...), custom_call_target="tpu_custom_call" | custom-call | flops 7046430720 | bytes 16777216 | tf_op jit(solution)/shard_map/inner_back/pallas_call | solution.py:549
  329.8 43.5 %block_back.3 = (f32[256,768]{1,0:T(8,128)}, bf16[4,256,192]{2,1,0:T(8,128)(2,1)}, f32[8,768]{1,0:T(8,128)}, bf16[384,768]{1,0:T(8,128)(2,1)}, bf16[768,768]{1,0...) custom-call(f32[256,768]{1,0:T(8,128)} %get-tuple-element.125.refs_0, ...), custom_call_target="tpu_custom_call" | custom-call | flops 5435817984 | bytes 20971520 | tf_op jit(solution)/shard_map/block_back/pallas_call | solution.py:549
  373.2 68.2 %inner_back.3 = (f32[256,768]{1,0:T(8,128)}, bf16[256,768]{1,0:T(8,128)(2,1)}, bf16[384,640]{1,0:T(8,128)(2,1)}, f32[8,640]{1,0:T(8,128)}, f32[20,768]{1,0:T(8,1...) custom-call(s32[1,4]{1,0:T(1,128)} %refs_0_.7, ...), custom_call_target="tpu_custom_call" | custom-call | flops 7046430720 | bytes 16777216 | tf_op jit(solution)/shard_map/inner_back/pallas_call | solution.py:549
  441.9 0.8 slice_bitcast_fusion.18
  442.6 0.7 slice_bitcast_fusion.19
  443.3 0.8 slice_bitcast_fusion.22
  444.1 0.7 slice_bitcast_fusion.23
  445.1 1.0 concatenate.44
  446.1 0.7 reshape.216.refs_2_
  446.8 28.9 %carry.1 = (bf16[3,96,640]{2,1,0:T(8,128)(2,1)}, bf16[4,2,96,192]{3,2,1,0:T(8,128)(2,1)}, f32[4,2,6,768]{3,2,1,0:T(8,128)}, bf16[4,96,768]{2,1,0:T(8,128)(2,1)},...) custom-call(bf16[4,96,640]{2,1,0:T(8,128)(2,1)} %bitcast.136, ...), custom_call_target="tpu_custom_call" | custom-call | flops 1048576 | bytes 1048576 | tf_op jit(solution)/shard_map/carry/pallas_call | solution.py:549
  475.8 1.0 reshape.217
  476.8 0.6 slice.289
  477.4 0.3 copy.57
  477.7 0.3 copy.56
  478.2 0.9 pad_maximum_fusion
  479.1 0.9 pad_maximum_fusion.1
  480.0 0.9 pad_maximum_fusion.2
  481.3 0.9 maximum_convert_fusion.3
  482.1 1.6 maximum_convert_fusion
  483.7 0.3 copy.61
  484.0 0.3 copy.60
  484.4 1.6 maximum_convert_fusion.1
  486.0 0.7 multiply_reduce_fusion.1
  486.7 0.7 multiply_reduce_fusion
  487.4 0.8 slice_bitcast_fusion.5
  488.2 0.6 fusion.4
  488.8 0.7 copy.77
  489.6 0.7 copy.78
  (109 shorter events, 2.8 us)
Async XLA Ops:
  0.6 0.9 copy-start
  0.7 3.5 slice-start
  0.7 3.6 slice-start.1
  1.5 3.0 slice-start.2
  1.5 3.1 slice-start.4
  4.1 0.9 slice-start.3
  4.1 1.1 slice-start.5
  6.0 1.1 copy-start.20
  6.0 3.8 copy-start.2
  7.9 3.0 copy-start.3
  12.6 72.3 %copy-start.17 = (f32[2,2,768]{2,1,0:T(2,128)S(1)}, f32[2,2,768]{2,1,0:T(2,128)}, u32[]{:S(2)}) copy-start(f32[2,2,768]{2,1,0:T(2,128)} %param.29) | copy-start | bytes 36868
  12.6 72.3 %copy-start.18 = (f32[2,2,768]{2,1,0:T(2,128)S(1)}, f32[2,2,768]{2,1,0:T(2,128)}, u32[]{:S(2)}) copy-start(f32[2,2,768]{2,1,0:T(2,128)} %param.31) | copy-start | bytes 36868
  12.6 72.4 %copy-start.19 = (f32[2,2,768]{2,1,0:T(2,128)S(1)}, f32[2,2,768]{2,1,0:T(2,128)}, u32[]{:S(2)}) copy-start(f32[2,2,768]{2,1,0:T(2,128)} %param.30) | copy-start | bytes 36868
  182.2 37.6 %copy-start.12 = (bf16[256,768]{1,0:T(8,128)(2,1)S(1)}, bf16[256,768]{1,0:T(8,128)(2,1)}, u32[]{:S(2)}) copy-start(bf16[256,768]{1,0:T(8,128)(2,1)} %param.17) | copy-start | bytes 1179652
  220.7 37.1 %copy-start.21 = (s32[1,1,20]{2,1,0:T(1,128)S(1)}, s32[1,1,20]{2,1,0:T(1,128)}, u32[]{:S(2)}) copy-start(s32[1,1,20]{2,1,0:T(1,128)} %param.18) | copy-start | bytes 244
  373.2 68.3 %copy-start.15 = (f32[8,768]{1,0:T(8,128)S(1)}, f32[8,768]{1,0:T(8,128)}, u32[]{:S(2)}) copy-start(f32[8,768]{1,0:T(8,128)} %get-tuple-element.151) | copy-start | bytes 73732
  373.2 68.3 %copy-start.16 = (f32[8,768]{1,0:T(8,128)S(1)}, f32[8,768]{1,0:T(8,128)}, u32[]{:S(2)}) copy-start(f32[8,768]{1,0:T(8,128)} %get-tuple-element.150) | copy-start | bytes 73732
  441.5 35.9 %copy-start.8 = (bf16[4,96,640]{2,1,0:T(8,128)(2,1)S(1)}, bf16[4,96,640]{2,1,0:T(8,128)(2,1)}, u32[]{:S(2)}) copy-start(bf16[4,96,640]{2,1,0:T(8,128)(2,1)} %get-tuple-element.159) | copy-start | bytes 1474564
  475.7 1.9 copy-start.9
  479.9 0.9 copy-start.13
  479.9 1.2 copy-start.14
  479.9 2.2 copy-start.4
  480.0 2.2 copy-start.5
  482.1 1.6 copy-start.6
  482.1 1.9 copy-start.7
  484.3 4.5 copy-start.10
  484.3 5.2 %copy-start.11 = (bf16[256,768]{1,0:T(8,128)(2,1)S(1)}, bf16[256,768]{1,0:T(8,128)(2,1)}, u32[]{:S(2)}) copy-start(bf16[256,768]{1,0:T(8,128)(2,1)} %get-tuple-element.229) | copy-start | bytes 1179652
  484.3 6.0 %copy-start.1 = (f32[20,768]{1,0:T(8,128)S(1)}, f32[20,768]{1,0:T(8,128)}, u32[]{:S(2)}) copy-start(f32[20,768]{1,0:T(8,128)} %param.20) | copy-start | bytes 184324

commit v8 on v7

--- a/solution.py
+++ b/solution.py
@@ -1418,7 +1418,7 @@
 
 
 def inner_back_kernel(
-    ride, parent_ref, qw_ref, kv_ref, do_ref, o_ref, lse_ref, w_ref, back_ref, xg_ref, mark_ref,
+    lowest, ride, parent_ref, qw_ref, kv_ref, do_ref, o_ref, lse_ref, w_ref, back_ref, xg_ref, mark_ref,
     grad_ref, low_ref, din_ref, sum_out_ref, mem_ref,
     qm_ref, dm_ref, row_ref, acc_ref, wide_ref, dkv_ref, dqs_ref,
     w_send, w_recv, term_ref, all_in_ref, dq_ref, own_ref, part_ref,
@@ -1686,23 +1686,6 @@
     sum_out_ref[0:1, 256:640] = jnp.sum(own.astype(F32), axis=0, keepdims=True)
     ride.put(sum_out_ref)
     ride.store(1)
-    grad_ref[...] = part_ref[t] + back_ref[...]
-
-    for side, there in ((0, t < 3), (1, t > 0)):
-
-        @pl.when(there)
-        def _():
-            for p in range(2):
-                passed(side, t, p)
-                grad_ref[pieces[p]] += take_ref[side, t, pieces[p]].astype(F32)
-
-    low_ref[...] = grad_ref[...].astype(BF16)
-    ride.put(grad_ref, low_ref)
-    mem_ref[...] = lax.dot_general(
-        mark_ref[...], grad_ref[...], (((0,), (0,)), ((), ())),
-        precision=lax.Precision.HIGHEST, preferred_element_type=F32,
-    )
-    ride.put(mem_ref)
     total = all_in_ref[slice_of(f)].astype(F32)
     for k in range(1, size):
         for span in range(3):
@@ -1710,6 +1693,27 @@
         total += term_ref[k - 1].astype(F32)
     din_ref[...] = total.astype(BF16)
     ride.put(din_ref)
+    ride.store(2)
+    grad_ref[...] = part_ref[t] + back_ref[...]
+
+    for side, there in ((0, t < 3), (1, t > 0)):
+
+        @pl.when(there)
+        def _():
+            for p in range(2):
+                passed(side, t, p)
+                grad_ref[pieces[p]] += take_ref[side, t, pieces[p]].astype(F32)
+
+    low_ref[...] = grad_ref[...].astype(BF16)
+    ride.put(grad_ref, low_ref)
+    if lowest:
+        mem_ref[...] = lax.dot_general(
+            mark_ref[...], grad_ref[...], (((0,), (0,)), ((), ())),
+            precision=lax.Precision.HIGHEST, preferred_element_type=F32,
+        )
+    else:
+        mem_ref[...] = jnp.zeros_like(mem_ref)
+    ride.put(mem_ref)
     for k in range(1, size):
         for span in range(3):
             term(k, span).wait_send()
@@ -1731,7 +1735,7 @@
 RIDE_HOPS = (8, 11, 14, 17)
 
 
-def inner_back(qw, kv, do, o, lse, parents, w, back_one, xg, marks, cid, riders=()):
+def inner_back(qw, kv, do, o, lse, parents, w, back_one, xg, marks, lowest, cid, riders=()):
     size = lax.axis_size("fsdp")
     depth = 768 // size
     f = functools.partial(sds, dtype=F32)
@@ -1751,7 +1755,7 @@
     ]
     cost = (5 * 512 * 1024 * 64 * 30 + 4 * 1024 * 768 * 640, 16 << 20, 5 * 512 * 1024 * 3)
     operands = (parents, qw, kv.reshape(4, 4, 256, 384), do, o, lse, w, back_one, xg, marks)
-    res, ridden = call(inner_back_kernel, operands, outs, scratch, cid, "inner_back", cost, riders, smem=(0,))
+    res, ridden = call(functools.partial(inner_back_kernel, lowest), operands, outs, scratch, cid, "inner_back", cost, riders, smem=(0,))
     return (*res[:3], res[3][0], res[4], ridden)
 
 
@@ -1866,7 +1870,7 @@
             done[n + 1] = tuple(got[2:4])
             riders += [ctx_gather(above["up"]), ctx_gather(above["down"])]
         grad, low_grad, d_in, sums, memory_part, got = inner_back(
-            qw, kv, do, o, lse, parents, w_in, back_one, xg, marks, 16 * n + 4, riders
+            qw, kv, do, o, lse, parents, w_in, back_one, xg, marks, n == 0, 16 * n + 4, riders
         )
         if above is not None:
             done[n + 1] = (done[n + 1][1], done[n + 1][0], got[8], got[9])

time: 499 us -> 500 us (level)
  no operation moved by 1% of the time
where the time goes in v8:
time: 500 us; the launch traced here: 492 us
  Pallas kernels  455 us (91%)
  local copies, waits for them, and re-layouts  23.2 us (5%)
  other arithmetic  9.97 us (2%)
    pallas_call x9, Pallas kernels, call(): pl.pallas_call(body, out_shape=list(out_shapes) + [rider.out for rider in...  455 us

profile of v8, /device:TPU:0, one launch (start us, length us, event | category | flops | bytes accessed | tf_op | source)
XLA Modules:
  0.0 492.1 jit_solution(10154638752675411668)
XLA Ops:
  0.7 0.8 copy-done
  1.5 2.6 fusion.8
  5.4 0.6 concatenate.36
  6.0 1.1 slice_bitcast_fusion.3
  7.3 0.6 fusion.6
  7.9 1.2 copy.54
  9.1 0.6 dynamic-slice_bitcast_fusion
  9.8 1.1 slice_bitcast_fusion.2
  10.9 0.6 copy.55
  11.5 1.1 slice_bitcast_fusion
  12.6 71.0 %inner.2 = (bf16[4,256,768]{2,1,0:T(8,128)(2,1)}, bf16[4,256,256]{2,1,0:T(8,128)(2,1)}, bf16[4,4,256,384]{3,2,1,0:T(8,128)(2,1)}, bf16[4,256,192]{2,1,0:T(8,128)...) custom-call(s32[1,4]{1,0:T(1,128)} %refs_0_.7, ...), custom_call_target="tpu_custom_call" | custom-call | flops 3019898880 | bytes 14680064 | tf_op jit(solution)/shard_map/inner/pallas_call | solution.py:549
  83.6 1.4 fusion.5
  85.0 0.6 concatenate.38.refs_5_
  85.6 43.9 %block.2 = (f32[256,768]{1,0:T(8,128)}, bf16[256,768]{1,0:T(8,128)(2,1)}, f32[256,768]{1,0:T(8,128)}, f32[256,128]{1,0:T(8,128)}, f32[256,768]{1,0:T(8,128)}, /*...) custom-call(bf16[4,256,192]{2,1,0:T(8,128)(2,1)} %get-tuple-element., ...), custom_call_target="tpu_custom_call" | custom-call | flops 2717908992 | bytes 16777216 | tf_op jit(solution)/shard_map/block/pallas_call | solution.py:549
  129.5 52.1 %inner.3 = (bf16[4,256,768]{2,1,0:T(8,128)(2,1)}, bf16[4,256,256]{2,1,0:T(8,128)(2,1)}, bf16[4,4,256,384]{3,2,1,0:T(8,128)(2,1)}, bf16[4,256,192]{2,1,0:T(8,128)...) custom-call(s32[1,4]{1,0:T(1,128)} %refs_0_.7, ...), custom_call_target="tpu_custom_call" | custom-call | flops 3019898880 | bytes 14680064 | tf_op jit(solution)/shard_map/inner/pallas_call | solution.py:549
  181.6 0.6 concatenate.39.refs_5_
  182.2 37.6 %block.3 = (f32[256,768]{1,0:T(8,128)}, bf16[256,768]{1,0:T(8,128)(2,1)}, f32[256,768]{1,0:T(8,128)}, f32[256,128]{1,0:T(8,128)}, f32[256,768]{1,0:T(8,128)}, /*...) custom-call(bf16[4,256,192]{2,1,0:T(8,128)(2,1)} %get-tuple-element., ...), custom_call_target="tpu_custom_call" | custom-call | flops 2717908992 | bytes 16777216 | tf_op jit(solution)/shard_map/block/pallas_call | solution.py:549
  219.8 0.9 convert_element_type.44.refs_0_
  220.7 37.1 %block_back.2 = (f32[256,768]{1,0:T(8,128)}, bf16[4,256,192]{2,1,0:T(8,128)(2,1)}, f32[8,768]{1,0:T(8,128)}, bf16[384,768]{1,0:T(8,128)(2,1)}, bf16[768,768]{1,0:T(8,128)(2,1)}, /*index=5*/bf16[4,768,192]{2,1,0:T(8,128)(2,1)}) custom-call(f32[256,768]{1,0:T(8,128)} %convert_element_type.44.refs_0_, f32[256,768]{1,0:T(8,128)} %get-tuple-element.109.refs_1_, ...), custom_call_target="tpu_custom_call" | custom-call | flops 5435817984 | bytes 20971520 | tf_op jit(solution)/shard_map/block_back/pallas_call | solution.py:549
  257.8 0.8 compare_convert_fusion.refs_9_
  258.6 69.5 %inner_back.2 = (f32[256,768]{1,0:T(8,128)}, bf16[256,768]{1,0:T(8,128)(2,1)}, bf16[384,640]{1,0:T(8,128)(2,1)}, f32[8,640]{1,0:T(8,128)}, f32[20,768]{1,0:T(8,1...) custom-call(s32[1,4]{1,0:T(1,128)} %refs_0_.7, ...), custom_call_target="tpu_custom_call" | custom-call | flops 7046430720 | bytes 16777216 | tf_op jit(solution)/shard_map/inner_back/pallas_call | solution.py:549
  328.1 46.1 %block_back.3 = (f32[256,768]{1,0:T(8,128)}, bf16[4,256,192]{2,1,0:T(8,128)(2,1)}, f32[8,768]{1,0:T(8,128)}, bf16[384,768]{1,0:T(8,128)(2,1)}, bf16[768,768]{1,0...) custom-call(f32[256,768]{1,0:T(8,128)} %get-tuple-element.125.refs_0, ...), custom_call_target="tpu_custom_call" | custom-call | flops 5435817984 | bytes 20971520 | tf_op jit(solution)/shard_map/block_back/pallas_call | solution.py:549
  374.2 67.5 %inner_back.3 = (f32[256,768]{1,0:T(8,128)}, bf16[256,768]{1,0:T(8,128)(2,1)}, bf16[384,640]{1,0:T(8,128)(2,1)}, f32[8,640]{1,0:T(8,128)}, f32[20,768]{1,0:T(8,1...) custom-call(s32[1,4]{1,0:T(1,128)} %refs_0_.7, ...), custom_call_target="tpu_custom_call" | custom-call | flops 7046430720 | bytes 16777216 | tf_op jit(solution)/shard_map/inner_back/pallas_call | solution.py:549
  442.1 0.8 slice_bitcast_fusion.18
  442.8 0.7 slice_bitcast_fusion.19
  443.6 0.8 slice_bitcast_fusion.22
  444.3 0.7 slice_bitcast_fusion.23
  445.3 1.0 concatenate.44
  446.4 0.7 reshape.216.refs_2_
  447.1 29.9 %carry.1 = (bf16[3,96,640]{2,1,0:T(8,128)(2,1)}, bf16[4,2,96,192]{3,2,1,0:T(8,128)(2,1)}, f32[4,2,6,768]{3,2,1,0:T(8,128)}, bf16[4,96,768]{2,1,0:T(8,128)(2,1)},...) custom-call(bf16[4,96,640]{2,1,0:T(8,128)(2,1)} %bitcast.136, ...), custom_call_target="tpu_custom_call" | custom-call | flops 1048576 | bytes 1048576 | tf_op jit(solution)/shard_map/carry/pallas_call | solution.py:549
  477.0 1.0 reshape.217
  478.0 0.6 slice.289
  478.6 0.3 copy.57
  478.9 0.3 copy.56
  479.4 0.9 pad_maximum_fusion
  480.3 0.9 pad_maximum_fusion.1
  481.2 0.9 pad_maximum_fusion.2
  482.5 0.9 maximum_convert_fusion.3
  483.4 1.6 maximum_convert_fusion
  484.9 0.3 copy.61
  485.2 0.3 copy.60
  485.6 1.6 maximum_convert_fusion.1
  487.2 0.7 multiply_reduce_fusion.1
  487.9 0.7 multiply_reduce_fusion
  488.6 0.8 slice_bitcast_fusion.5
  489.4 0.6 fusion.4
  490.1 0.7 copy.77
  490.8 0.7 copy.78
  (109 shorter events, 2.8 us)
Async XLA Ops:
  0.6 0.9 copy-start
  0.7 3.5 slice-start
  0.7 3.6 slice-start.1
  1.5 3.0 slice-start.2
  1.5 3.1 slice-start.4
  4.1 0.9 slice-start.3
  4.1 1.1 slice-start.5
  6.0 1.1 copy-start.20
  6.0 3.8 copy-start.2
  7.9 3.0 copy-start.3
  12.6 72.3 %copy-start.17 = (f32[2,2,768]{2,1,0:T(2,128)S(1)}, f32[2,2,768]{2,1,0:T(2,128)}, u32[]{:S(2)}) copy-start(f32[2,2,768]{2,1,0:T(2,128)} %param.29) | copy-start | bytes 36868
  12.6 72.3 %copy-start.18 = (f32[2,2,768]{2,1,0:T(2,128)S(1)}, f32[2,2,768]{2,1,0:T(2,128)}, u32[]{:S(2)}) copy-start(f32[2,2,768]{2,1,0:T(2,128)} %param.31) | copy-start | bytes 36868
  12.6 72.4 %copy-start.19 = (f32[2,2,768]{2,1,0:T(2,128)S(1)}, f32[2,2,768]{2,1,0:T(2,128)}, u32[]{:S(2)}) copy-start(f32[2,2,768]{2,1,0:T(2,128)} %param.30) | copy-start | bytes 36868
  182.2 37.6 %copy-start.12 = (bf16[256,768]{1,0:T(8,128)(2,1)S(1)}, bf16[256,768]{1,0:T(8,128)(2,1)}, u32[]{:S(2)}) copy-start(bf16[256,768]{1,0:T(8,128)(2,1)} %param.17) | copy-start | bytes 1179652
  220.7 37.1 %copy-start.21 = (s32[1,1,20]{2,1,0:T(1,128)S(1)}, s32[1,1,20]{2,1,0:T(1,128)}, u32[]{:S(2)}) copy-start(s32[1,1,20]{2,1,0:T(1,128)} %param.18) | copy-start | bytes 244
  374.2 67.6 %copy-start.15 = (f32[8,768]{1,0:T(8,128)S(1)}, f32[8,768]{1,0:T(8,128)}, u32[]{:S(2)}) copy-start(f32[8,768]{1,0:T(8,128)} %get-tuple-element.151) | copy-start | bytes 73732
  374.2 67.6 %copy-start.16 = (f32[8,768]{1,0:T(8,128)S(1)}, f32[8,768]{1,0:T(8,128)}, u32[]{:S(2)}) copy-start(f32[8,768]{1,0:T(8,128)} %get-tuple-element.150) | copy-start | bytes 73732
  441.7 36.9 %copy-start.8 = (bf16[4,96,640]{2,1,0:T(8,128)(2,1)S(1)}, bf16[4,96,640]{2,1,0:T(8,128)(2,1)}, u32[]{:S(2)}) copy-start(bf16[4,96,640]{2,1,0:T(8,128)(2,1)} %get-tuple-element.159) | copy-start | bytes 1474564
  477.0 1.9 copy-start.9
  481.1 0.9 copy-start.13
  481.1 1.2 copy-start.14
  481.2 2.2 copy-start.4
  481.2 2.2 copy-start.5
  483.4 1.6 copy-start.6
  483.4 1.9 copy-start.7
  485.6 4.5 copy-start.10
  485.6 5.2 %copy-start.11 = (bf16[256,768]{1,0:T(8,128)(2,1)S(1)}, bf16[256,768]{1,0:T(8,128)(2,1)}, u32[]{:S(2)}) copy-start(bf16[256,768]{1,0:T(8,128)(2,1)} %get-tuple-element.229) | copy-start | bytes 1179652
  485.6 6.0 %copy-start.1 = (f32[20,768]{1,0:T(8,128)S(1)}, f32[20,768]{1,0:T(8,128)}, u32[]{:S(2)}) copy-start(f32[20,768]{1,0:T(8,128)} %param.20) | copy-start | bytes 184324
